TPU v7x, 32 devices: a whole 2x2x4 slice. The times are simulated.
32 devices in a mesh: fsdp: 2 (over core), ctx: 4 (over y, x), tp: 4 (over z).
Axes of the slice: x: 2, y: 2, z: 4, core: 2. Of those that a mesh axis runs over, the one named last changes fastest.
Arguments:
- layer_input: float32 [4, 1024, 512], P('fsdp', 'ctx'), may hold values from -6 to 6
- timesteps: int32 [4], P('fsdp'), may hold values from 0 to 999
- segment_ids: int32 [4, 1024], P('fsdp'), may hold values from 0 to 15, never falling along the last dimension, each value on 1 to 512 neighbouring positions
- time_table: float32 [1000, 512], replicated, may hold values from -3 to 3
- ln1_gain: float32 [512], replicated, may hold values from 0.5 to 1.5
- ln1_bias: float32 [512], replicated, may hold values from -1.5 to 1.5
- w_qkv: float32 [3, 512, 512], P(None, 'fsdp', 'tp'), may hold values from -0.25 to 0.25
- b_qv: float32 [2, 512], P(None, 'tp'), may hold values from -1.5 to 1.5
- w_out_t: float32 [512, 512], P('fsdp', 'tp'), may hold values from -1 to 1
- b_out: float32 [512], replicated, may hold values from -1.5 to 1.5
- ln2_gain: float32 [512], replicated, may hold values from 0.5 to 1.5
- ln2_bias: float32 [512], replicated, may hold values from -1.5 to 1.5
- w_up: float32 [512, 2048], P('fsdp', 'tp'), may hold values from -0.25 to 0.25
- b_up: float32 [2048], P('tp'), may hold values from -1.5 to 1.5
- w_down_t: float32 [512, 2048], P('fsdp', 'tp'), may hold values from -0.125 to 0.125
- b_down: float32 [512], replicated, may hold values from -1.5 to 1.5
- out_grad: float32 [4, 1024, 512], P('fsdp', 'ctx'), may hold values from -6 to 6
Outputs:
- output: float32 [4, 1024, 512], P('fsdp', 'ctx')
- grad_input: float32 [4, 1024, 512], P('fsdp', 'ctx')
- grad_table: float32 [1000, 512], replicated
- grad_ln1_gain: float32 [512], replicated
- grad_ln1_bias: float32 [512], replicated
- grad_w_qkv: float32 [3, 512, 512], P(None, 'fsdp', 'tp')
- grad_b_qv: float32 [2, 512], P(None, 'tp')
- grad_w_out_t: float32 [512, 512], P('fsdp', 'tp')
- grad_b_out: float32 [512], replicated
- grad_ln2_gain: float32 [512], replicated
- grad_ln2_bias: float32 [512], replicated
- grad_w_up: float32 [512, 2048], P('fsdp', 'tp')
- grad_b_up: float32 [2048], P('tp')
- grad_w_down_t: float32 [512, 2048], P('fsdp', 'tp')
- grad_b_down: float32 [512], replicated
Inputs may be any that keep to these rules, and one draw needn't show every extreme that they name: `segment_ids`: in each sequence the ids never fall; each document has 1 to 512 characters and one has exactly 512.
All inputs are finite; a program needn't handle non-finite values.
Results may differ from a plain program's by a relative error of at most 0.011.
Values may be sent and summed in bfloat16 or wider, within the bound.
No kernel may reach another device: no remote copies, remote signals or barrier semaphores. Data moves between devices by JAX's collectives and lax.ppermute only.
A program may use at most 64 MiB of HBM per device.

v0:
```python
import jax
import jax.numpy as jnp
from jax import lax
from jax.sharding import PartitionSpec as P

HEAD_DIM = 64


EPSILON = 1e-05
NEGATIVE = -1e30
PRECISE = lax.Precision.HIGHEST


def layer_norm(values, norm_gain, norm_bias):
    centre = values - jnp.mean(values, axis=-1, keepdims=True)
    spread = jnp.mean(centre * centre, axis=-1, keepdims=True)
    return centre * lax.rsqrt(spread + EPSILON) * norm_gain + norm_bias


def contract_last(left, right):
    return lax.dot_general(
        left, right, (((1,), (1,)), ((), ())), preferred_element_type=jnp.float32
    )


def contract_first(left, right):
    return lax.dot_general(
        left, right, (((0,), (0,)), ((), ())), preferred_element_type=jnp.float32
    )


def per_device(
    layer_input,
    timesteps,
    segment_ids,
    time_table,
    ln1_gain,
    ln1_bias,
    w_qkv,
    b_qv,
    w_out_t,
    b_out,
    ln2_gain,
    ln2_bias,
    w_up,
    b_up,
    w_down_t,
    b_down,
    out_grad,
):
    seq_count, span_len, model_width = layer_input.shape
    tok_rows = seq_count * span_len
    seq_len = segment_ids.shape[1]
    step_count = time_table.shape[0]
    ctx_index = lax.axis_index("ctx")
    masters = (
        w_qkv.astype(jnp.bfloat16),
        w_out_t.astype(jnp.bfloat16),
        w_up.astype(jnp.bfloat16),
        w_down_t.astype(jnp.bfloat16),
    )
    qkv_mat, out_mat, up_mat, down_mat = (
        lax.all_gather(masters[0], "fsdp", axis=1, tiled=True),
        lax.all_gather(masters[1], "fsdp", axis=0, tiled=True),
        lax.all_gather(masters[2], "fsdp", axis=0, tiled=True),
        lax.all_gather(masters[3], "fsdp", axis=0, tiled=True),
    )
    steps_hot = (timesteps[:, None] == jnp.arange(step_count, dtype=jnp.int32)[None, :]).astype(
        jnp.float32
    )
    embedded = jnp.dot(steps_hot, time_table, precision=PRECISE)
    stream = (layer_input + embedded[:, None, :]).reshape(tok_rows, model_width)
    normed, norm_one_pull = jax.vjp(layer_norm, stream, ln1_gain, ln1_bias)
    normed_low = normed.astype(jnp.bfloat16)
    projected = jnp.einsum("rd,kdc->krc", normed_low, qkv_mat, preferred_element_type=jnp.float32)
    local_cols = projected.shape[2]
    heads_here = local_cols // HEAD_DIM
    query = (projected[0] + b_qv[0]).astype(jnp.bfloat16)
    key_local = projected[1].astype(jnp.bfloat16).reshape(seq_count, span_len, local_cols)
    value_local = (
        (projected[2] + b_qv[1]).astype(jnp.bfloat16).reshape(seq_count, span_len, local_cols)
    )
    key_all, value_all = (
        lax.all_gather(key_local, "ctx", axis=1, tiled=True),
        lax.all_gather(value_local, "ctx", axis=1, tiled=True),
    )
    query_ids = lax.dynamic_slice_in_dim(segment_ids, ctx_index * span_len, span_len, 1)
    same_doc = (query_ids[:, :, None] == segment_ids[:, None, :])[:, None]
    query_heads = query.reshape(seq_count, span_len, heads_here, HEAD_DIM)
    key_heads = key_all.reshape(seq_count, seq_len, heads_here, HEAD_DIM)
    value_heads = value_all.reshape(seq_count, seq_len, heads_here, HEAD_DIM)
    scale = HEAD_DIM ** (-0.5)

    def score_block():
        raw_scores = jnp.einsum(
            "sqhd,skhd->shqk", query_heads, key_heads, preferred_element_type=jnp.float32
        )
        return jnp.where(same_doc, raw_scores * scale, NEGATIVE)

    scores = score_block()
    row_top = jnp.max(scores, axis=-1, keepdims=True)
    expd = jnp.exp(scores - row_top)
    row_total = jnp.sum(expd, axis=-1, keepdims=True)
    probs = expd / row_total
    log_total = row_top + jnp.log(row_total)
    mixed = jnp.einsum(
        "shqk,skhd->sqhd",
        probs.astype(jnp.bfloat16),
        value_heads,
        preferred_element_type=jnp.float32,
    )
    mixed = mixed.reshape(tok_rows, local_cols).astype(jnp.bfloat16)
    attn_terms = contract_last(mixed, out_mat)
    attn = lax.psum(attn_terms, "tp")
    resid = stream + attn + b_out
    normed_two, norm_two_pull = jax.vjp(layer_norm, resid, ln2_gain, ln2_bias)
    normed_two_low = normed_two.astype(jnp.bfloat16)
    pre_act = jnp.dot(normed_two_low, up_mat, preferred_element_type=jnp.float32) + b_up
    activ, gelu_pull = jax.vjp(jax.nn.gelu, pre_act)
    activ_low = activ.astype(jnp.bfloat16)
    ffn_terms = contract_last(activ_low, down_mat)
    ffn = lax.psum(ffn_terms.astype(jnp.bfloat16), "tp").astype(jnp.float32)
    output = (resid + ffn + b_down).reshape(seq_count, span_len, model_width)
    cotan = out_grad.reshape(tok_rows, model_width)
    cotan_low = cotan.astype(jnp.bfloat16)
    grad_down = contract_first(cotan_low, activ_low)
    grad_act = jnp.dot(cotan_low, down_mat, preferred_element_type=jnp.float32)
    (grad_pre,) = gelu_pull(grad_act)
    grad_pre_low = grad_pre.astype(jnp.bfloat16)
    grad_upmat = contract_first(normed_two_low, grad_pre_low)
    back_two = lax.psum(contract_last(grad_pre_low, up_mat), "tp")
    resid_back, grad_gain_two, grad_bias_two = norm_two_pull(back_two)
    grad_resid = cotan + resid_back
    grad_resid_low = grad_resid.astype(jnp.bfloat16)
    grad_outmat = contract_first(grad_resid_low, mixed)
    grad_mixed = jnp.dot(grad_resid_low, out_mat, preferred_element_type=jnp.float32).astype(
        jnp.bfloat16
    )
    probs_again = jnp.exp(score_block() - log_total)
    mixed_heads = grad_mixed.reshape(seq_count, span_len, heads_here, HEAD_DIM)
    grad_probs = jnp.einsum(
        "sqhd,skhd->shqk", mixed_heads, value_heads, preferred_element_type=jnp.float32
    )
    inner = jnp.sum(probs_again * grad_probs, axis=-1, keepdims=True)
    grad_raw = (probs_again * (grad_probs - inner) * scale).astype(jnp.bfloat16)
    grad_query = jnp.einsum(
        "shqk,skhd->sqhd", grad_raw, key_heads, preferred_element_type=jnp.float32
    ).reshape(tok_rows, local_cols)
    grad_key_all = jnp.einsum(
        "shqk,sqhd->skhd", grad_raw, query_heads, preferred_element_type=jnp.float32
    ).reshape(seq_count, seq_len, local_cols)
    grad_value_all = jnp.einsum(
        "shqk,sqhd->skhd",
        probs_again.astype(jnp.bfloat16),
        mixed_heads,
        preferred_element_type=jnp.float32,
    ).reshape(seq_count, seq_len, local_cols)
    grad_key, grad_value = (
        lax.psum_scatter(grad_key_all, "ctx", scatter_dimension=1, tiled=True),
        lax.psum_scatter(grad_value_all, "ctx", scatter_dimension=1, tiled=True),
    )
    grad_key = grad_key.reshape(tok_rows, local_cols)
    grad_value = grad_value.reshape(tok_rows, local_cols)
    grad_stack = jnp.stack(
        [
            grad_query.astype(jnp.bfloat16),
            grad_key.astype(jnp.bfloat16),
            grad_value.astype(jnp.bfloat16),
        ]
    )
    grad_qkvmat = jnp.einsum(
        "rd,krc->kdc", normed_low, grad_stack, preferred_element_type=jnp.float32
    )
    back_one = lax.psum(
        jnp.einsum("krc,kdc->rd", grad_stack, qkv_mat, preferred_element_type=jnp.float32), "tp"
    )
    stream_back, grad_gain_one, grad_bias_one = norm_one_pull(back_one)
    grad_input = grad_resid + stream_back
    per_sequence = jnp.sum(grad_input.reshape(seq_count, span_len, model_width), axis=1)
    qv_terms = jnp.stack([jnp.sum(grad_query, axis=0), jnp.sum(grad_value, axis=0)])
    small = lax.psum(
        (
            grad_gain_one,
            grad_bias_one,
            grad_gain_two,
            grad_bias_two,
            qv_terms,
            jnp.sum(grad_pre, axis=0),
            jnp.sum(grad_resid, axis=0),
            jnp.sum(cotan, axis=0),
        ),
        ("fsdp", "ctx"),
    )
    (
        gain_one_sum,
        bias_one_sum,
        gain_two_sum,
        bias_two_sum,
        qv_sum,
        up_bias_sum,
        out_bias_sum,
        down_bias_sum,
    ) = small
    table_terms = jnp.dot(steps_hot.T, per_sequence, precision=PRECISE)
    table_sum = lax.psum(table_terms, ("fsdp", "ctx"))
    weight_terms = (grad_qkvmat, grad_outmat, grad_upmat, grad_down)
    summed = lax.psum((weight_terms[0], weight_terms[1], weight_terms[2], weight_terms[3]), "ctx")
    owned = (
        lax.psum_scatter(summed[0], "fsdp", scatter_dimension=1, tiled=True),
        lax.psum_scatter(summed[1], "fsdp", scatter_dimension=0, tiled=True),
        lax.psum_scatter(summed[2], "fsdp", scatter_dimension=0, tiled=True),
        lax.psum_scatter(summed[3], "fsdp", scatter_dimension=0, tiled=True),
    )
    qkv_owned, out_owned, up_owned, down_owned = owned
    return (
        output,
        grad_input.reshape(seq_count, span_len, model_width),
        table_sum,
        gain_one_sum,
        bias_one_sum,
        qkv_owned,
        qv_sum,
        out_owned,
        out_bias_sum,
        gain_two_sum,
        bias_two_sum,
        up_owned,
        up_bias_sum,
        down_owned,
        down_bias_sum,
    )


def solution(mesh):
    placed = (
        P("fsdp", "ctx", None),
        P("fsdp"),
        P("fsdp", None),
        P(),
        P(),
        P(),
        P(None, "fsdp", "tp"),
        P(None, "tp"),
        P("fsdp", "tp"),
        P(),
        P(),
        P(),
        P("fsdp", "tp"),
        P("tp"),
        P("fsdp", "tp"),
        P(),
        P("fsdp", "ctx", None),
    )
    return jax.shard_map(
        per_device,
        mesh=mesh,
        in_specs=placed,
        out_specs=(
            P("fsdp", "ctx", None),
            P("fsdp", "ctx", None),
            P(),
            P(),
            P(),
            P(None, "fsdp", "tp"),
            P(None, "tp"),
            P("fsdp", "tp"),
            P(),
            P(),
            P(),
            P("fsdp", "tp"),
            P("tp"),
            P("fsdp", "tp"),
            P(),
        ),
        check_vma=False,
    )
```

profile of v0, /device:TPU:0, one launch (start us, length us, event | category | flops | bytes accessed | tf_op | source)
XLA Modules:
  0.0 526.8 jit_solution(3402038133135190457)
XLA Ops:
  7.3 1.2 convert_element_type.111
  8.4 2.2 all_gather.18
  10.6 1.4 fusion.44
  12.1 1.4 fusion.62
  17.8 2.0 all_gather.21
  19.8 1.2 broadcast_compare_fusion
  21.0 2.1 reshape.228
  23.0 1.9 copy.60
  25.0 13.5 %all_gather.20 = bf16[2,1024,128]{2,1,0:T(8,128)(2,1)} all-gather(bf16[2,256,128]{2,1,0:T(8,128)(2,1)} %bitcast.102), channel_id=1, replica_groups=mesh['fsdp'=2,'ctx'=4,'tp'=4] {'ctx'}, dimensions={1}, use_global_device_ids=true | all-gather | bytes 655360 | tf_op jit(solution)/shard_map/all_gather | solution.py:84
  38.5 2.0 copy.61
  41.5 9.8 %all_gather.19 = bf16[2,1024,128]{2,1,0:T(8,128)(2,1)} all-gather(bf16[2,256,128]{2,1,0:T(8,128)(2,1)S(1)} %add_convert_fusion.3), channel_id=1, replica_groups=mesh['fsdp'=2,'ctx'=4,'tp'=4] {'ctx'}, dimensions={1}, use_global_device_ids=true | all-gather | bytes 655360 | tf_op jit(solution)/shard_map/all_gather | solution.py:85
  51.3 2.0 copy.58
  53.4 2.5 fusion.67
  55.9 1.1 fusion.2
  56.9 1.1 fusion.26
  58.8 1.3 fusion.70
  60.2 1.1 convert_element_type.121
  61.3 1.1 convert_element_type.123
  62.4 2.3 all_gather.22
  64.7 2.3 all_gather.23
  67.0 1.5 fusion.63
  69.4 1.4 fusion.71
  70.8 41.6 %all-reduce.9.cloned.1.call-done = f32[512,512]{1,0:T(8,128)} async-done(((f32[512,512]{1,0:T(8,128)}), f32[512,512]{1,0:T(8,128)}) %all-reduce.9.cloned.1.call-update) | async-done | bytes 1048592 | tf_op jit(solution)/shard_map/psum | solution.py:114
  112.4 1.5 fusion.60
  114.3 2.7 fusion.55
  117.8 1.4 fusion.41
  119.3 2.7 convolution_convert_fusion
  122.3 48.4 %all-reduce.13.cloned.1.call-done = f32[512,512]{1,0:T(8,128)} async-done(((f32[512,512]{1,0:T(8,128)}), f32[512,512]{1,0:T(8,128)}) %all-reduce.13.cloned.1.call-update) | async-done | bytes 1048592 | tf_op jit(solution)/shard_map/psum | solution.py:131
  170.6 2.0 multiply_reduce_fusion.1
  172.6 38.1 %all-reduce.11.cloned.1.call-done = bf16[512,512]{1,0:T(8,128)(2,1)} async-done(((bf16[512,512]{1,0:T(8,128)(2,1)}), bf16[512,512]{1,0:T(8,128)(2,1)}) %all-reduce.11.cloned.1.call-update) | async-done | bytes 524304 | tf_op jit(solution)/shard_map/psum | solution.py:122
  210.7 3.2 fusion.59
  214.1 1.1 copy-done.3
  216.1 1.7 reshape.230
  217.9 1.7 copy.64
  219.6 4.1 fusion.12
  223.7 3.8 fusion.72
  227.6 12.8 %fusion.7 = f32[2,2,64,1024]{3,2,1,0:T(8,128)} fusion(f32[2,2,256,1024]{3,2,1,0:T(8,128)} %fusion.72, f32[2,2,256,1024]{3,2,1,0:T(8,128)} %copy-done.1, f32[2,2,256]{2,1,0:T(2,128)S(1)} %log_add_fusion, f32[2,256,2,64]{1,3,2,0:T(8,128)} %copy.60, f32[2,64]{1,0:T(2,128)S(1)} %add.179), kind=kOutput, calls=%fused_computation.10 | convolution fusion | flops 141690880 | bytes 9703936 | tf_op jit(solution)/shard_map/shqk,sqhd->skhd/dot_general | solution.py:149
  240.5 2.3 fusion.36
  242.8 2.9 convolution_bitcast_fusion
  245.8 3.1 fusion.39
  248.9 12.1 %fusion.65 = (f32[2,64]{1,0:T(2,128)S(1)}, bf16[2,256,2,64]{1,3,2,0:T(8,128)(2,1)}) fusion(bf16[2,1024,2,64]{1,3,2,0:T(8,128)(2,1)} %bitcast.90, f32[2,2,256,1024]{3,2,1,0:T(8,128)} %fusion.72, f32[2,2,256,1024]{3,2,1,0:T(8,128)} %copy-done.1, f32[2,2,256]{2,1,0:T(2,128)S(1)} %log_add_fusion), kind=kOutput, calls=%fused_computation.104 | convolution fusion | flops 141690752 | bytes 9048576 | tf_op jit(solution)/shard_map/shqk,skhd->sqhd/dot_general | solution.py:146
  261.0 1.8 copy.76
  262.8 1.8 reshape.229
  264.6 1.7 fusion.66
  266.3 1.7 copy.68
  268.0 14.4 %reduce-scatter.7.cloned.1.call-done = f32[2,256,128]{1,2,0:T(8,128)} async-done(((f32[2,1024,128]{1,2,0:T(8,128)}), f32[2,256,128]{1,2,0:T(8,128)}) %reduce-scatter.7.cloned.1.call-update) | async-done | bytes 262160 | tf_op jit(solution)/shard_map/reduce_scatter | solution.py:159
  282.4 1.6 convert_element_type.133
  284.0 1.7 copy.66
  285.6 2.5 convolution_bitcast_fusion.2
  288.2 2.5 convolution_bitcast_fusion.1
  290.8 1.9 reduce-scatter.13.cloned.1.call-done
  292.7 12.1 %reduce-scatter.17.cloned.1.call-done = f32[256,512]{0,1:T(8,128)} async-done(((f32[512,512]{0,1:T(8,128)}), f32[256,512]{0,1:T(8,128)}) %reduce-scatter.17.cloned.1.call-update) | async-done | bytes 524304 | tf_op jit(solution)/shard_map/reduce_scatter | solution.py:212
  304.8 12.0 %reduce-scatter.15.cloned.1.call-done = f32[256,512]{1,0:T(8,128)} async-done(((f32[512,512]{1,0:T(8,128)}), f32[256,512]{1,0:T(8,128)}) %reduce-scatter.15.cloned.1.call-update) | async-done | bytes 524304 | tf_op jit(solution)/shard_map/reduce_scatter | solution.py:211
  316.7 12.3 %reduce-scatter.11.cloned.1.call-done = f32[3,256,128]{1,2,0:T(8,128)} async-done(((f32[3,512,128]{1,2,0:T(8,128)}), f32[3,256,128]{1,2,0:T(8,128)}) %reduce-scatter.11.cloned.1.call-update) | async-done | bytes 393232 | tf_op jit(solution)/shard_map/reduce_scatter | solution.py:209
  329.4 55.5 %all-reduce.15.cloned.1.call-done = f32[512,512]{1,0:T(8,128)} async-done(((f32[512,512]{1,0:T(8,128)}), f32[512,512]{1,0:T(8,128)}) %all-reduce.15.cloned.1.call-update) | async-done | bytes 1048592 | tf_op jit(solution)/shard_map/psum | solution.py:174
  384.9 1.8 multiply_reduce_fusion.2
  386.7 1.8 fusion.58
  388.7 2.4 fusion.43
  391.2 27.6 %all-reduce = (f32[512]{0:T(512)}, f32[512]{0:T(512)}, f32[2,128]{1,0:T(2,128)}, f32[512]{0:T(512)}, f32[512]{0:T(512)}, /*index=5*/f32[512]{0:T(512)}, f32[512]{0:T(512)}, f32[512]{0:T(512)}) all-reduce(f32[512]{0:T(512)S(1)} %get-tuple-element.62, ...), channel_id=1, replica_groups=mesh['fsdp'=2,'ctx'=4,'tp'=4] {'fsdp','ctx'}, use_global_device_ids=true, to_apply=%region_20.21 | all-reduce | flops 3840 | bytes 30720 | tf_op jit(solution)/shard_map/psum | solution.py:181
  418.9 31.2 %all-reduce.19.cloned.1.call-done = (f32[3,256,128]{1,2,0:T(8,128)}, f32[256,128]{1,0:T(8,128)}, f32[256,512]{1,0:T(8,128)}, f32[256,512]{0,1:T(8,128)}) async-done(((f32[3,256,128]{1,2,0:T(8,128)}, f32[256,128]{1,0:T(8,128)}, f32[256,512]{1,0:T(8,128)}, f32[256,512]{0,1:T(8,128)}), (f32[3,256,128]{1,2,0:T(8,128)}, f32[256,128]{1,0:T(8,128)}, f32[256,512]{1,0:T(8,128)}, ...) | async-done | bytes 1572880 | tf_op jit(solution)/shard_map/psum | solution.py:207
  450.1 1.9 copy.71
  452.1 2.0 copy.72
  454.1 61.3 %all-reduce.17.cloned.1.call-done = f32[1000,512]{1,0:T(8,128)} async-done(((f32[1000,512]{1,0:T(8,128)}), f32[1000,512]{1,0:T(8,128)}) %all-reduce.17.cloned.1.call-update) | async-done | bytes 2048016 | tf_op jit(solution)/shard_map/psum | solution.py:205
  515.4 3.1 copy.92
  (119 shorter events, 12.1 us)
Async XLA Ops:
  7.2 3.4 copy-start
  7.2 6.6 %copy-start.20 = (f32[512]{0:T(512)S(1)}, f32[512]{0:T(512)}, u32[]{:S(2)}) copy-start(f32[512]{0:T(512)} %param.21) | copy-start | bytes 6148
  7.2 6.6 %copy-start.22 = (f32[512]{0:T(512)S(1)}, f32[512]{0:T(512)}, u32[]{:S(2)}) copy-start(f32[512]{0:T(512)} %param.22) | copy-start | bytes 6148
  7.2 105.2 %all-reduce.9.cloned.1.call-start = ((), (), s32[]{:S(2)}) async-start(), calls=%async_computation.6 | async-start | bytes 2097152 | tf_op jit(solution)/shard_map/psum | solution.py:114
  12.0 4.7 copy-start.29
  12.0 7.8 %copy-start.21 = (s32[2,1024]{1,0:T(2,128)S(1)}, s32[2,1024]{1,0:T(2,128)}, u32[]{:S(2)}) copy-start(s32[2,1024]{1,0:T(2,128)} %param.19) | copy-start | bytes 24580
  14.0 0.8 copy-start.5
  53.4 3.6 copy-start.8
  55.8 2.2 copy-start.1
  56.9 1.9 copy-start.13
  58.2 0.7 copy-start.15
  60.1 52.3 %copy-start.23 = (f32[512]{0:T(512)S(1)}, f32[512]{0:T(512)}, u32[]{:S(2)}) copy-start(f32[512]{0:T(512)} %param.26) | copy-start | bytes 6148
  60.2 110.5 %all-reduce.13.cloned.1.call-start = ((), (), s32[]{:S(2)}) async-start(), calls=%async_computation.8 | async-start | bytes 2097152 | tf_op jit(solution)/shard_map/psum | solution.py:131
  64.7 49.5 %copy-start.19 = (f32[512]{0:T(512)S(1)}, f32[512]{0:T(512)}, u32[]{:S(2)}) copy-start(f32[512]{0:T(512)} %param.27) | copy-start | bytes 6148
  64.7 49.6 %copy-start.25 = (f32[512]{0:T(512)S(1)}, f32[512]{0:T(512)}, u32[]{:S(2)}) copy-start(f32[512]{0:T(512)} %param.28) | copy-start | bytes 6148
  64.7 49.6 %copy-start.30 = (f32[512]{0:T(512)S(1)}, f32[512]{0:T(512)}, u32[]{:S(2)}) copy-start(f32[512]{0:T(512)} %param.30) | copy-start | bytes 6148
  67.0 1.6 copy-start.11
  68.6 0.8 copy-start.10
  112.4 1.9 copy-start.12
  112.4 1.9 copy-start.16
  113.9 3.0 copy-start.2
  117.0 0.8 copy-start.9
  117.8 92.9 %copy-start.24 = (f32[512]{0:T(512)S(1)}, f32[512]{0:T(512)}, u32[]{:S(2)}) copy-start(f32[512]{0:T(512)} %param.32) | copy-start | bytes 6148
  119.3 91.4 %all-reduce.11.cloned.1.call-start = ((), (), s32[]{:S(2)}) async-start(), calls=%async_computation.7 | async-start | bytes 1048576 | tf_op jit(solution)/shard_map/psum | solution.py:122
  122.0 142.5 %reduce-scatter.9.cloned.1.call-start = ((), (), s32[]{:S(2)}) async-start(), calls=%async_computation.10 | async-start | bytes 1310720 | tf_op jit(solution)/shard_map/reduce_scatter | solution.py:160
  210.7 3.2 copy-start.6
  210.7 4.5 copy-start.14
  214.1 1.1 copy-start.3
  223.7 58.7 %reduce-scatter.7.cloned.1.call-start = ((), (), s32[]{:S(2)}) async-start(), calls=%async_computation.9 | async-start | bytes 1310720 | tf_op jit(solution)/shard_map/reduce_scatter | solution.py:159
  240.4 5.4 %copy-start.26 = (f32[512]{0:T(512)S(1)}, f32[512]{0:T(512)}, u32[]{:S(2)}) copy-start(f32[512]{0:T(512)} %param.28) | copy-start | bytes 6148
  240.4 52.3 %reduce-scatter.13.cloned.1.call-start = ((), (), s32[]{:S(2)}) async-start(), calls=%async_computation.14 | async-start | bytes 393216 | tf_op jit(solution)/shard_map/reduce_scatter | solution.py:210
  242.7 62.0 %reduce-scatter.17.cloned.1.call-start = ((), (), s32[]{:S(2)}) async-start(), calls=%async_computation.16 | async-start | bytes 1572864 | tf_op jit(solution)/shard_map/reduce_scatter | solution.py:212
  245.7 71.0 %reduce-scatter.15.cloned.1.call-start = ((), (), s32[]{:S(2)}) async-start(), calls=%async_computation.15 | async-start | bytes 1572864 | tf_op jit(solution)/shard_map/reduce_scatter | solution.py:211
  248.9 80.2 %reduce-scatter.11.cloned.1.call-start = ((), (), s32[]{:S(2)}) async-start(), calls=%async_computation.13 | async-start | bytes 1179648 | tf_op jit(solution)/shard_map/reduce_scatter | solution.py:209
  288.2 96.7 %all-reduce.15.cloned.1.call-start = ((), (), s32[]{:S(2)}) async-start(), calls=%async_computation.11 | async-start | bytes 2097152 | tf_op jit(solution)/shard_map/psum | solution.py:174
  290.7 159.4 %all-reduce.19.cloned.1.call-start = ((), (), s32[]{:S(2)}) async-start(), calls=%async_computation.17 | async-start | bytes 3145728 | tf_op jit(solution)/shard_map/psum | solution.py:207
  329.1 186.3 %all-reduce.17.cloned.1.call-start = ((), (), s32[]{:S(2)}) async-start(), calls=%async_computation.12 | async-start | bytes 4096000 | tf_op jit(solution)/shard_map/psum | solution.py:205
  384.9 3.6 copy-start.4
  386.6 2.1 copy-start.27
  388.4 2.8 copy-start.28
  388.6 129.9 %copy-start.7 = (f32[512,512]{1,0:T(8,128)}, f32[512,512]{1,0:T(8,128)S(1)}, u32[]{:S(2)}) copy-start(f32[512,512]{1,0:T(8,128)S(1)} %add_add_fusion.2) | copy-start | bytes 3145732
  450.1 68.4 %copy-start.18 = (f32[256,128]{1,0:T(8,128)S(1)}, f32[256,128]{1,0:T(8,128)}, u32[]{:S(2)}) copy-start(f32[256,128]{1,0:T(8,128)} %get-tuple-element.117) | copy-start | bytes 393220
  515.4 3.8 copy-start.17
Sparse Core Ops, SparseCore 0:
  60.3 52.0 all-reduce.8
  119.4 51.1 all-reduce.12
  173.0 37.6 all-reduce.10
  223.8 27.7 reduce-scatter.8
  254.6 27.7 reduce-scatter.6
  285.0 7.6 reduce-scatter.12
  295.0 9.6 reduce-scatter.16
  307.0 9.6 reduce-scatter.14
  319.7 9.3 reduce-scatter.10
  331.9 52.9 all-reduce.14
  388.6 61.4 all-reduce.18
  453.8 61.5 all-reduce.16
where the time goes:
time: 528 us; the launch traced here: 527 us
  waiting for transfers between devices  329 us (62%)
  matrix products  64.3 us (12%)
  blocking collectives  59.8 us (11%)
  local copies, waits for them, and re-layouts  33 us (6%)
  other arithmetic  25.2 us (5%)
  between operations  14.6 us (3%)
    psum x1, waiting for transfers between devices, per_device(): table_sum = lax.psum(table_terms, ('fsdp', 'ctx'))  61.3 us
    psum x1, waiting for transfers between devices, per_device(): lax.psum(jnp.einsum('krc,kdc->rd', grad_stack, qkv_mat, preferred_element...  55.5 us
    psum x1, waiting for transfers between devices, per_device(): back_two = lax.psum(contract_last(grad_pre_low, up_mat), 'tp')  48.4 us
    psum x1, waiting for transfers between devices, per_device(): attn = lax.psum(attn_terms, 'tp')  41.6 us
    psum x1, waiting for transfers between devices, per_device(): ffn = lax.psum(ffn_terms.astype(jnp.bfloat16), 'tp').astype(jnp.float32)  38.1 us
    psum x1, waiting for transfers between devices, per_device(): lax.psum((weight_terms[0], weight_terms[1], weight_terms[2], weight_terms...  31.2 us
    psum x1, blocking collectives, per_device(): lax.psum((grad_gain_one, grad_bias_one, grad_gain_two, grad_bias_two, qv_...  27.6 us
    reduce_scatter x1, waiting for transfers between devices, per_device(): lax.psum_scatter(grad_key_all, 'ctx', scatter_dimension=1, tiled=True)  14.4 us
  transfers between devices with their start and end apart: 12, of which 11 were waited for; matrix products, arithmetic and copies ran while one was open for 14% of the time, Pallas kernels for 0%

commit v1 on v0

v1 whole, which is shorter than its diff:
```python
import functools
import jax
import jax.numpy as jnp
from jax import lax
from jax.experimental import pallas as pl
from jax.experimental.pallas import tpu as pltpu
from jax.sharding import PartitionSpec as P

HEAD_DIM = 64
SCALE = HEAD_DIM ** (-0.5)
EPSILON = 1e-05
NEGATIVE = -1e30
F32 = jnp.float32
BF16 = jnp.bfloat16


def xor_pairs(size, bits):
    return [(i, i ^ bits) for i in range(size)]


def dot_nn(left, right):
    return lax.dot_general(left, right, (((1,), (0,)), ((), ())), preferred_element_type=F32)


def dot_nt(left, right):
    return lax.dot_general(left, right, (((1,), (1,)), ((), ())), preferred_element_type=F32)


def dot_tn(left, right):
    return lax.dot_general(left, right, (((0,), (0,)), ((), ())), preferred_element_type=F32)


def norm_parts(values):
    centre = values - jnp.mean(values, axis=-1, keepdims=True)
    spread = jnp.mean(centre * centre, axis=-1, keepdims=True)
    inverse = lax.rsqrt(spread + EPSILON)
    return centre * inverse, inverse


def norm_back(grad, hat, inverse, gain):
    scaled = grad * gain
    mean_one = jnp.mean(scaled, axis=-1, keepdims=True)
    mean_two = jnp.mean(scaled * hat, axis=-1, keepdims=True)
    return inverse * (scaled - mean_one - hat * mean_two)


def mask_biases(where_ref, seg_ref, span):
    chunk = where_ref[0]
    count = seg_ref.shape[1] // span

    def ids_of(step):
        start = pl.multiple_of((chunk ^ step) * span, span)
        return seg_ref[:, pl.ds(start, span)]

    own = jnp.broadcast_to(ids_of(0), (span, span)).T
    return [
        jnp.where(own == jnp.broadcast_to(ids_of(step), (span, span)), 0.0, NEGATIVE)
        for step in range(count)
    ]


def lane_mask(shape, head):
    lanes = lax.broadcasted_iota(jnp.int32, shape, 1)
    return (lanes // HEAD_DIM) == head


def attend_forward_kernel(where_ref, seg_ref, q_ref, kv0, kv1, kv2, kv3, mixed_ref, lse_ref):
    span, width = q_ref.shape
    biases = mask_biases(where_ref, seg_ref, span)
    kvs = (kv0, kv1, kv2, kv3)
    query = q_ref[...]
    mixed, lse = None, None
    for head in range(width // HEAD_DIM):
        mine = lane_mask((span, width), head)
        masked = jnp.where(mine, query, jnp.zeros_like(query))
        scores = [
            dot_nt(masked, kv[:, :width]) * SCALE + bias for kv, bias in zip(kvs, biases)
        ]
        top = functools.reduce(
            jnp.maximum, [jnp.max(block, axis=-1, keepdims=True) for block in scores]
        )
        grown = [jnp.exp(block - top) for block in scores]
        total = functools.reduce(
            jnp.add, [jnp.sum(block, axis=-1, keepdims=True) for block in grown]
        )
        share = 1.0 / total
        out = functools.reduce(
            jnp.add,
            [dot_nn((block * share).astype(BF16), kv[:, width:]) for block, kv in zip(grown, kvs)],
        )
        log_total = jnp.broadcast_to(top + jnp.log(total), (span, width))
        mixed = out if head == 0 else jnp.where(mine, out, mixed)
        lse = log_total if head == 0 else jnp.where(mine, log_total, lse)
    mixed_ref[...] = mixed.astype(BF16)
    lse_ref[...] = lse


def attend_backward_kernel(
    where_ref, seg_ref, q_ref, g_ref, lse_ref, kv0, kv1, kv2, kv3,
    dq_ref, own_ref, out1, out2, out3,
):
    span, width = q_ref.shape
    biases = mask_biases(where_ref, seg_ref, span)
    kvs = (kv0, kv1, kv2, kv3)
    outs = (own_ref, out1, out2, out3)
    query, grad = q_ref[...], g_ref[...]
    dq, dks, dvs = None, [None] * 4, [None] * 4
    for head in range(width // HEAD_DIM):
        mine = lane_mask((span, width), head)
        masked_q = jnp.where(mine, query, jnp.zeros_like(query))
        masked_g = jnp.where(mine, grad, jnp.zeros_like(grad))
        lse = lse_ref[:, head * HEAD_DIM : head * HEAD_DIM + 1]
        probs = [
            jnp.exp(dot_nt(masked_q, kv[:, :width]) * SCALE + bias - lse)
            for kv, bias in zip(kvs, biases)
        ]
        grads = [dot_nt(masked_g, kv[:, width:]) for kv in kvs]
        inner = functools.reduce(
            jnp.add,
            [jnp.sum(p * g, axis=-1, keepdims=True) for p, g in zip(probs, grads)],
        )
        raws = [(p * (g - inner) * SCALE).astype(BF16) for p, g in zip(probs, grads)]
        head_dq = functools.reduce(
            jnp.add, [dot_nn(raw, kv[:, :width]) for raw, kv in zip(raws, kvs)]
        )
        dq = head_dq if head == 0 else jnp.where(mine, head_dq, dq)
        for step in range(4):
            head_dk = dot_tn(raws[step], query)
            head_dv = dot_tn(probs[step].astype(BF16), grad)
            dks[step] = head_dk if head == 0 else jnp.where(mine, head_dk, dks[step])
            dvs[step] = head_dv if head == 0 else jnp.where(mine, head_dv, dvs[step])
    dq_ref[...] = dq
    for step in range(4):
        outs[step][:, :width] = dks[step].astype(outs[step].dtype)
        outs[step][:, width:] = dvs[step].astype(outs[step].dtype)


def vmem_specs(count):
    return [pl.BlockSpec(memory_space=pltpu.VMEM)] * count


def attend_forward(where, seg, query, kvs):
    span, width = query.shape
    return pl.pallas_call(
        attend_forward_kernel,
        out_shape=(
            jax.ShapeDtypeStruct((span, width), BF16),
            jax.ShapeDtypeStruct((span, width), F32),
        ),
        in_specs=[pl.BlockSpec(memory_space=pltpu.SMEM)] + vmem_specs(6),
        out_specs=tuple(vmem_specs(2)),
        compiler_params=pltpu.CompilerParams(vmem_limit_bytes=40 << 20),
        cost_estimate=pl.CostEstimate(
            flops=4 * 2 * 4 * span * span * width, bytes_accessed=2 << 20, transcendentals=8 * span * span
        ),
    )(where, seg, query, *kvs)


def attend_backward(where, seg, query, grad, lse, kvs):
    span, width = query.shape
    return pl.pallas_call(
        attend_backward_kernel,
        out_shape=(
            jax.ShapeDtypeStruct((span, width), F32),
            jax.ShapeDtypeStruct((span, 2 * width), F32),
        )
        + (jax.ShapeDtypeStruct((span, 2 * width), BF16),) * 3,
        in_specs=[pl.BlockSpec(memory_space=pltpu.SMEM)] + vmem_specs(8),
        out_specs=tuple(vmem_specs(5)),
        compiler_params=pltpu.CompilerParams(vmem_limit_bytes=40 << 20),
        cost_estimate=pl.CostEstimate(
            flops=10 * 2 * 4 * span * span * width, bytes_accessed=3 << 20, transcendentals=8 * span * span
        ),
    )(where, seg, query, grad, lse, *kvs)


def swap(values, axis, size, bits):
    return lax.ppermute(values, axis, xor_pairs(size, bits))


def gather_rows(part, parts, place):
    if parts != 2:
        return lax.all_gather(part, "fsdp", axis=0, tiled=True)
    other = swap(part, "fsdp", 2, 1)
    return jnp.where(
        place == 0, jnp.concatenate([part, other]), jnp.concatenate([other, part])
    )


def scatter_rows(whole, parts, place):
    if parts != 2:
        return lax.psum_scatter(whole, "fsdp", scatter_dimension=0, tiled=True)
    rows = whole.shape[0] // 2
    given = lax.dynamic_slice_in_dim(whole, (1 - place) * rows, rows, 0).astype(BF16)
    kept = lax.dynamic_slice_in_dim(whole, place * rows, rows, 0)
    return kept + swap(given, "fsdp", 2, 1).astype(F32)


def sum_four(values, axis):
    got = [swap(values, axis, 4, bits) for bits in (1, 2, 3)]
    return (values + got[0]) + (got[1] + got[2])


def scatter_four(values, axis, place):
    rows = values.shape[0] // 4

    def quarter(bits):
        return lax.dynamic_slice_in_dim(values, (place ^ bits) * rows, rows, 0)

    got = [swap(quarter(bits).astype(BF16), axis, 4, bits).astype(F32) for bits in (1, 2, 3)]
    return (quarter(0) + got[0]) + (got[1] + got[2])


def gather_four(part, axis, place):
    pieces = [part] + [swap(part, axis, 4, bits) for bits in (1, 2, 3)]
    out = []
    for spot in range(4):
        bits = place ^ spot
        low = jnp.where(bits == 0, pieces[0], pieces[1])
        high = jnp.where(bits == 2, pieces[2], pieces[3])
        out.append(jnp.where(bits < 2, low, high))
    return jnp.concatenate(out)


def per_device(
    layer_input,
    timesteps,
    segment_ids,
    time_table,
    ln1_gain,
    ln1_bias,
    w_qkv,
    b_qv,
    w_out_t,
    b_out,
    ln2_gain,
    ln2_bias,
    w_up,
    b_up,
    w_down_t,
    b_down,
    out_grad,
    *,
    parts,
):
    span, model_width = layer_input.shape[1:]
    step_count = time_table.shape[0]
    cols = w_qkv.shape[2]
    hidden = w_up.shape[1]
    half = span // 2
    core = lax.axis_index("fsdp")
    chunk = lax.axis_index("ctx")
    shard = lax.axis_index("tp")
    pair, bit = shard // 2, shard % 2

    qkv_part = jnp.concatenate([w_qkv[0], w_qkv[1], w_qkv[2]], axis=1).astype(BF16)
    rest_part = jnp.concatenate([w_out_t, w_up, w_down_t], axis=1).astype(BF16)
    bias_part = jnp.concatenate([b_qv[0], b_qv[1], b_up])[None]
    qkv_own = gather_rows(qkv_part, parts, core)
    bias_other = swap(bias_part, "tp", 4, 2)
    qkv_other = gather_rows(swap(qkv_part, "tp", 4, 2), parts, core)
    rest_far = swap(rest_part, "tp", 4, 2)
    rest_both = gather_rows(jnp.concatenate([rest_part, rest_far], axis=1), parts, core)
    rest = cols + 2 * hidden
    out_mat = jnp.concatenate([rest_both[:, :cols], rest_both[:, rest : rest + cols]], axis=1)
    up_mat = jnp.concatenate(
        [rest_both[:, cols : cols + hidden], rest_both[:, rest + cols : rest + cols + hidden]],
        axis=1,
    )
    down_mat = jnp.concatenate(
        [rest_both[:, cols + hidden : rest], rest_both[:, rest + cols + hidden :]], axis=1
    )
    up_bias = jnp.concatenate([b_up, bias_other[0, 2 * cols :]])

    def of_pair(values):
        return lax.dynamic_index_in_dim(values, pair, 0, keepdims=False)

    step_at = of_pair(timesteps)
    embedded = lax.dynamic_slice(time_table, (step_at, 0), (1, model_width))
    stream = of_pair(layer_input) + embedded
    seg = of_pair(segment_ids)[None]
    cotan = of_pair(out_grad)
    where = chunk.astype(jnp.int32).reshape(1)

    hat_one, inverse_one = norm_parts(stream)
    normed = (hat_one * ln1_gain + ln1_bias).astype(BF16)

    def project(weights, q_bias, v_bias):
        raw = dot_nn(normed, weights)
        query = (raw[:, :cols] + q_bias).astype(BF16)
        value = (raw[:, 2 * cols :] + v_bias).astype(BF16)
        return query, jnp.concatenate([raw[:, cols : 2 * cols].astype(BF16), value], axis=1)

    def spread_kv(kv):
        return [kv] + [swap(kv, "ctx", 4, bits) for bits in (1, 2, 3)]

    query_own, kv_own = project(qkv_own, b_qv[0], b_qv[1])
    kvs_own = spread_kv(kv_own)
    query_other, kv_other = project(
        qkv_other, bias_other[0, :cols], bias_other[0, cols : 2 * cols]
    )
    kvs_other = spread_kv(kv_other)
    mixed_own, lse_own = attend_forward(where, seg, query_own, kvs_own)
    mixed_other, lse_other = attend_forward(where, seg, query_other, kvs_other)
    mixed = jnp.concatenate([mixed_own, mixed_other], axis=1)

    attn_terms = dot_nt(mixed, out_mat)
    resid = stream + (attn_terms + swap(attn_terms.astype(BF16), "tp", 4, 1).astype(F32)) + b_out
    hat_two, inverse_two = norm_parts(resid)
    normed_two = (hat_two * ln2_gain + ln2_bias).astype(BF16)
    pre_act = dot_nn(normed_two, up_mat) + up_bias
    activ, gelu_pull = jax.vjp(jax.nn.gelu, pre_act)
    activ_low = activ.astype(BF16)
    cotan_low = cotan.astype(BF16)
    (grad_pre,) = gelu_pull(dot_nn(cotan_low, down_mat))
    grad_pre_low = grad_pre.astype(BF16)
    back_two = dot_nt(grad_pre_low, up_mat)
    ffn_terms = dot_nt(activ_low, down_mat)

    def half_of(values, which):
        return lax.dynamic_slice_in_dim(values, which * half, half, 0)

    def scatter_pair(values):
        got = swap(half_of(values, 1 - bit).astype(BF16), "tp", 4, 1)
        return half_of(values, bit) + got.astype(F32)

    norm_grad = scatter_pair(back_two)
    hat_half, inverse_half = half_of(hat_two, bit), half_of(inverse_two, bit)
    cotan_half = half_of(cotan, bit)
    grad_resid = cotan_half + norm_back(norm_grad, hat_half, inverse_half, ln2_gain)
    resid_low = grad_resid.astype(BF16)
    resid_far = swap(resid_low, "tp", 4, 1)
    resid_all = jnp.where(
        bit == 0,
        jnp.concatenate([resid_low, resid_far]),
        jnp.concatenate([resid_far, resid_low]),
    )
    grad_mixed = dot_nn(resid_all, out_mat).astype(BF16)

    out_half = half_of(resid, bit) + scatter_pair(ffn_terms) + b_down
    output = gather_four(out_half.astype(BF16), "tp", shard).astype(F32)

    def reduce_weights(terms):
        mine = scatter_rows(terms, parts, core)
        quarter = scatter_four(mine, "ctx", chunk)
        width = quarter.shape[1] // 2
        summed = quarter[:, :width] + swap(quarter[:, width:].astype(BF16), "tp", 4, 2).astype(F32)
        return gather_four(summed.astype(BF16), "ctx", chunk).astype(F32)

    grad_up = dot_tn(normed_two, grad_pre_low)
    grad_down = dot_tn(cotan_low, activ_low)
    grad_out = dot_tn(resid_all, mixed)
    rest_terms = jnp.concatenate(
        [
            grad_out[:, :cols],
            grad_up[:, :hidden],
            grad_down[:, :hidden],
            grad_out[:, cols:],
            grad_up[:, hidden:],
            grad_down[:, hidden:],
        ],
        axis=1,
    )
    rest_owned = reduce_weights(rest_terms)

    def attend_pull(query, grad, lse, kvs):
        dq, kept, *given = attend_backward(where, seg, query, grad, lse, kvs)
        got = [swap(piece, "ctx", 4, bits + 1).astype(F32) for bits, piece in enumerate(given)]
        grad_kv = (kept + got[0]) + (got[1] + got[2])
        sums = jnp.stack([jnp.sum(dq, axis=0), jnp.sum(grad_kv[:, cols:], axis=0)])
        return jnp.concatenate([dq, grad_kv], axis=1).astype(BF16), sums

    pulled_own, qv_own = attend_pull(query_own, grad_mixed[:, :cols], lse_own, kvs_own)
    pulled_other, qv_other = attend_pull(query_other, grad_mixed[:, cols:], lse_other, kvs_other)

    back_one = dot_nt(pulled_own, qkv_own) + dot_nt(pulled_other, qkv_other)
    gain_one = jnp.sum(back_one * hat_one, axis=0)
    bias_one = jnp.sum(back_one, axis=0)
    stream_terms = norm_back(back_one, hat_one, inverse_one, ln1_gain)
    sequence_sum = jnp.sum(stream_terms, axis=0) + jnp.sum(grad_resid, axis=0)
    input_half = grad_resid + scatter_pair(stream_terms)
    grad_input = gather_four(input_half.astype(BF16), "tp", shard).astype(F32)

    qkv_terms = jnp.concatenate(
        [dot_tn(normed, pulled_own), dot_tn(normed, pulled_other)], axis=1
    )
    qkv_owned = reduce_weights(qkv_terms)

    seqs = 2 * parts
    place = 2 * core + pair
    rows = lambda *values: jnp.stack(values)
    fixed = rows(
        gain_one,
        bias_one,
        jnp.sum(norm_grad * hat_half, axis=0),
        jnp.sum(norm_grad, axis=0),
        jnp.sum(grad_resid, axis=0),
        jnp.sum(cotan_half, axis=0),
    )
    seq_hot = (jnp.arange(seqs) == place).astype(F32)
    seq_rows = seq_hot[:, None] * sequence_sum[None]
    first = jnp.logical_and(chunk == 0, bit == 0).astype(F32)
    step_row = jnp.pad(seq_hot * step_at.astype(F32) * first, (0, model_width - seqs))[None]
    four = jnp.arange(4)[:, None]
    near, far = (four == shard).astype(F32), (four == shard ^ 2).astype(F32)
    up_sum = jnp.sum(grad_pre, axis=0)
    up_rows = near * up_sum[None, :hidden] + far * up_sum[None, hidden:]
    qv_rows = (near[None] * qv_own[:, None] + far[None] * qv_other[:, None]).reshape(
        2, 4 * cols
    )
    small = jnp.concatenate([fixed, seq_rows, step_row, up_rows, qv_rows])
    small = small + swap(small, "fsdp", 2, 1) if parts == 2 else lax.psum(small, "fsdp")
    small = sum_four(sum_four(small, "ctx"), "tp")
    seq_sums = small[6 : 6 + seqs]
    steps = small[6 + seqs, :seqs].astype(jnp.int32)
    hot = (jnp.arange(step_count, dtype=jnp.int32)[:, None] == steps[None]).astype(F32)
    grad_table = jnp.dot(hot, seq_sums, precision=lax.Precision.HIGHEST)
    up_at, qv_at = 7 + seqs, 11 + seqs
    grad_b_up = lax.dynamic_index_in_dim(small[up_at : up_at + 4], shard, 0, keepdims=False)
    grad_b_qv = lax.dynamic_slice_in_dim(small[qv_at : qv_at + 2], shard * cols, cols, 1)

    shape = layer_input.shape
    return (
        output.reshape(shape),
        grad_input.reshape(shape),
        grad_table,
        small[0],
        small[1],
        jnp.stack([qkv_owned[:, i * cols : (i + 1) * cols] for i in range(3)]),
        grad_b_qv,
        rest_owned[:, :cols],
        small[4],
        small[2],
        small[3],
        rest_owned[:, cols : cols + hidden],
        grad_b_up,
        rest_owned[:, cols + hidden :],
        small[5],
    )


def solution(mesh):
    placed = (
        P("fsdp", "ctx", None),
        P("fsdp"),
        P("fsdp", None),
        P(),
        P(),
        P(),
        P(None, "fsdp", "tp"),
        P(None, "tp"),
        P("fsdp", "tp"),
        P(),
        P(),
        P(),
        P("fsdp", "tp"),
        P("tp"),
        P("fsdp", "tp"),
        P(),
        P("fsdp", "ctx", None),
    )
    return jax.shard_map(
        functools.partial(per_device, parts=mesh.shape["fsdp"]),
        mesh=mesh,
        in_specs=placed,
        out_specs=(
            P("fsdp", "ctx", None),
            P("fsdp", "ctx", None),
            P(),
            P(),
            P(),
            P(None, "fsdp", "tp"),
            P(None, "tp"),
            P("fsdp", "tp"),
            P(),
            P(),
            P(),
            P("fsdp", "tp"),
            P("tp"),
            P("fsdp", "tp"),
            P(),
        ),
        check_vma=False,
    )
```

time: 528 us -> 217 us (0.41)
  waiting for transfers between devices: 329 us -> 65.1 us
  starting transfers between devices: 0.89 us -> 65.1 us
  blocking collectives: 59.8 us -> 0 us
  matrix products: 64.3 us -> 16 us
  between operations: 14.6 us -> 4.68 us
  local copies, waits for them, and re-layouts: 33 us -> 25.3 us
  Pallas kernels: 0 us -> 7.59 us
  other arithmetic: 25.2 us -> 32.3 us
    psum x6 -> x0, waiting for transfers between devices: 276 us -> none  [the longest x1 61.3 us: per_device(): table_sum = lax.psum(table_terms, ('fsdp', 'ctx'))]
    ppermute x0 -> x52, waiting for transfers between devices: none -> 65.1 us  [swap(): return lax.ppermute(values, axis, xor_pairs(size, bits))]
    ppermute x0 -> x52, starting transfers between devices: none -> 65.1 us  [swap(): return lax.ppermute(values, axis, xor_pairs(size, bits))]
    reduce_scatter x6 -> x0, waiting for transfers between devices: 52.7 us -> none  [the longest x1 14.4 us: per_device(): lax.psum_scatter(grad_key_all, 'ctx', scatter_dimension=1, tiled=True)]
    dot_general x20 -> x16, matrix products: 64.3 us -> 16 us  [the longest x5 4.71 us: dot_tn(): lax.dot_general(left, right, (((0,), (0,)), ((), ())), preferred_element_...]
    all_gather x6 -> x0, blocking collectives: 32.2 us -> none  [the longest x1 13.5 us: per_device(): lax.all_gather(key_local, 'ctx', axis=1, tiled=True)]
    psum x1 -> x0, blocking collectives: 27.6 us -> none  [per_device(): lax.psum((grad_gain_one, grad_bias_one, grad_gain_two, grad_bias_two, qv_...]
    reduce_sum x12 -> x11, other arithmetic: 16.6 us -> 3.7 us  [the longest x1 1.58 us: per_device(): jnp.sum(cotan_half, axis=0)]
  transfers between devices with their start and end apart: 12 -> 52, of which waited for: 11 -> 24; matrix products, arithmetic and copies ran while one was open for 14% -> 22% of each run, Pallas kernels for 0% -> 4%
where the time goes in v1:
time: 217 us; the launch traced here: 216 us
  starting transfers between devices  65.1 us (30%)
  waiting for transfers between devices  65.1 us (30%)
  other arithmetic  32.3 us (15%)
  local copies, waits for them, and re-layouts  25.3 us (12%)
  matrix products  16 us (7%)
  Pallas kernels  7.59 us (3%)
  between operations  4.68 us (2%)
    ppermute x52, waiting for transfers between devices, swap(): return lax.ppermute(values, axis, xor_pairs(size, bits))  65.1 us
    ppermute x52, starting transfers between devices, swap(): return lax.ppermute(values, axis, xor_pairs(size, bits))  65.1 us
    select_n x1, other arithmetic, gather_rows(): jnp.where(place == 0, jnp.concatenate([part, other]), jnp.concatenate([ot...  8.69 us
    unnamed x137, local copies, waits for them, and re-layouts  8.06 us
    pallas_call x2, Pallas kernels, attend_backward(): pl.pallas_call(attend_backward_kernel, out_shape=(jax.ShapeDtypeStruct((s...  4.79 us
    dot_general x5, matrix products, dot_tn(): lax.dot_general(left, right, (((0,), (0,)), ((), ())), preferred_element_...  4.71 us
    dot_general x5, matrix products, dot_nn(): lax.dot_general(left, right, (((1,), (0,)), ((), ())), preferred_element_...  4.53 us
    dot_general x5, matrix products, dot_nt(): lax.dot_general(left, right, (((1,), (1,)), ((), ())), preferred_element_...  4.48 us
  transfers between devices with their start and end apart: 52, of which 24 were waited for; matrix products, arithmetic and copies ran while one was open for 22% of the time, Pallas kernels for 4%

profile of v1, /device:TPU:0, one launch (start us, length us, event | category | flops | bytes accessed | tf_op | source)
XLA Modules:
  0.0 216.0 jit_solution(11518478677255195248)
XLA Ops:
  0.7 1.2 convert.46
  2.6 4.0 %collective-permute-start.4 = (bf16[256,384]{1,0:T(8,128)(2,1)}, bf16[256,384]{1,0:T(8,128)(2,1)}, u32[]{:S(2)}, u32[]{:S(2)}) collective-permute-start(bf16[256,384]{1,0:T(8,128)(2,1)} %pad_maximum_fusion.17), channel_id=1, source_target_pairs={{0,2},{1,3},{2,0},{3,1},{4,6},{5,7},{6,4},{7,5},{8,10},{9,11},{10,... | collective-permute-start | bytes 589832 | tf_op jit(solution)/shard_map/ppermute | solution.py:178
  12.4 2.9 %collective-permute-start.10 = (bf16[256,1152]{1,0:T(8,128)(2,1)}, bf16[256,1152]{1,0:T(8,128)(2,1)}, u32[]{:S(2)}, u32[]{:S(2)}) collective-permute-start(bf16[256,1152]{1,0:T(8,128)(2,1)} %pad_maximum_fusion.9), channel_id=1, source_target_pairs={{0,2},{1,3},{2,0},{3,1},{4,6},{5,7},{6,4},{7,5},{8,10},{9,11},{10,... | collective-permute-start | bytes 1769480 | tf_op jit(solution)/shard_map/ppermute | solution.py:178
  15.3 1.2 dynamic_slice.92
  20.7 1.3 broadcast_bitcast_fusion.2
  22.1 1.3 broadcast_bitcast_fusion.3
  24.1 1.2 add_convert_fusion.1
  26.1 1.6 dynamic-slice_reduce_fusion
  29.7 1.4 fusion.55
  31.1 10.9 %collective-permute-done.10 = bf16[256,1152]{1,0:T(8,128)(2,1)} collective-permute-done((bf16[256,1152]{1,0:T(8,128)(2,1)}, bf16[256,1152]{1,0:T(8,128)(2,1)}, u32[]{:S(2)}, u32[]{:S(2)}) %collective-permute-start.10) | collective-permute-done | bytes 589856 | tf_op jit(solution)/shard_map/ppermute | solution.py:178
  43.4 2.6 %collective-permute-start.3 = (bf16[256,256]{1,0:T(8,128)(2,1)S(1)}, bf16[256,256]{1,0:T(8,128)(2,1)S(1)}, u32[]{:S(2)}, u32[]{:S(2)}) collective-permute-start(bf16[256,256]{1,0:T(8,128)(2,1)S(1)} %pad_maximum_fusion.22.kv0), channel_id=1, source_target_pairs={{0,12},{4,8},{8,4},{12,0},{1,13},{5,9},{9,5},{13,1},{2,14},{6,10},... | collective-permute-start | bytes 393224 | tf_op jit(solution)/shard_map/ppermute | solution.py:178
  47.0 1.5 fusion.35
  48.6 2.6 %collective-permute-start.9 = (bf16[256,256]{1,0:T(8,128)(2,1)S(1)}, bf16[256,256]{1,0:T(8,128)(2,1)S(1)}, u32[]{:S(2)}, u32[]{:S(2)}) collective-permute-start(bf16[256,256]{1,0:T(8,128)(2,1)S(1)} %pad_maximum_fusion.23.kv0), channel_id=1, source_target_pairs={{0,12},{4,8},{8,4},{12,0},{1,13},{5,9},{9,5},{13,1},{2,14},{6,10},... | collective-permute-start | bytes 393224 | tf_op jit(solution)/shard_map/ppermute | solution.py:178
  51.1 1.2 collective-permute-start.8
  52.3 1.6 collective-permute-done.2.kv2
  53.9 1.2 collective-permute-start.7
  55.1 1.4 shard_map.280
  56.6 2.1 collective-permute-done.8.kv2
  59.2 1.4 shard_map.281
  60.7 8.7 %maximum_select_fusion = bf16[512,2304]{1,0:T(8,128)(2,1)S(1)} fusion(bf16[256,2304]{1,0:T(8,128)(2,1)S(1)} %collective-permute-done.11, bf16[256,1152]{1,0:T(8,128)(2,1)} %collective-permute-done.10, bf16[256,512]{1,0:T(8,128)(2,1)S(1)} %copy-done.20, bf16[256,512]{1,0:T(8,128)(2,1)S(1)} %copy-done.17, bf16[256,128]{1,0:T(8,128)(2,1)S(1)} %copy-done.29, ...), kind=kLoop, calls=%fused_computation | loop fusion | flops 24772608 | bytes 4718593 | tf_op jit(solution)/shard_map/jit(_where)/select_n | solution.py:185
  70.7 6.8 %collective-permute-done.12 = bf16[256,512]{1,0:T(8,128)(2,1)S(1)} collective-permute-done((bf16[256,512]{1,0:T(8,128)(2,1)S(1)}, bf16[256,512]{1,0:T(8,128)(2,1)S(1)}, u32[]{:S(2)}, u32[]{:S(2)}) %collective-permute-start.12) | collective-permute-done | bytes 262176 | tf_op jit(solution)/shard_map/ppermute | solution.py:178
  80.8 2.0 fusion.32
  83.3 1.8 fusion.18
  86.0 1.3 collective-permute-start.17
  87.4 4.7 %collective-permute-done.17 = bf16[128,512]{1,0:T(8,128)(2,1)S(1)} collective-permute-done((bf16[128,512]{1,0:T(8,128)(2,1)S(1)}, bf16[128,512]{1,0:T(8,128)(2,1)S(1)}, u32[]{:S(2)}, u32[]{:S(2)}) %collective-permute-start.17) | collective-permute-done | bytes 131104 | tf_op jit(solution)/shard_map/ppermute | solution.py:178
  94.0 3.4 %collective-permute-start.16 = (bf16[128,512]{1,0:T(8,128)(2,1)}, bf16[128,512]{1,0:T(8,128)(2,1)}, u32[]{:S(2)}, u32[]{:S(2)}) collective-permute-start(bf16[128,512]{1,0:T(8,128)(2,1)} %add_convert_fusion.3), channel_id=1, source_target_pairs={{0,3},{1,2},{2,1},{3,0},{4,7},{5,6},{6,5},{7,4},{8,11},{9,10},{10,... | collective-permute-start | bytes 393224 | tf_op jit(solution)/shard_map/ppermute | solution.py:178
  98.4 1.3 collective-permute-done.18
  101.1 1.8 copy.33
  105.6 2.7 %shard_map.283 = (f32[256,128]{1,0:T(8,128)S(1)}, f32[256,256]{1,0:T(8,128)S(1)}, bf16[256,256]{1,0:T(8,128)(2,1)}, bf16[256,256]{1,0:T(8,128)(2,1)}, bf16[256,256]{1,0:T(8,128)(2,1)S(1)}) custom-call(s32[1]{0:T(128)} %bitcast.3.where_ref, s32[1,1024]{1,0:T(1,128)S(1)} %constant_dynamic-slice_fusion.2.seg_ref, ...), custom_call_target="tpu_custom_call" | custom-call | flops 671088640 | bytes 3145728 | tf_op jit(solution)/shard_map/pallas_call | solution.py:161
  108.9 1.4 collective-permute-start.22
  111.3 1.8 copy.32
  114.0 2.1 shard_map.282
  116.2 1.2 collective-permute-start.24
  117.4 1.4 collective-permute-start.19
  124.6 1.2 collective-permute-start.21
  126.9 3.6 %collective-permute-done.21 = bf16[256,256]{1,0:T(8,128)(2,1)S(1)} collective-permute-done((bf16[256,256]{1,0:T(8,128)(2,1)S(1)}, bf16[256,256]{1,0:T(8,128)(2,1)S(1)}, u32[]{:S(2)}, u32[]{:S(2)}) %collective-permute-start.21) | collective-permute-done | bytes 131104 | tf_op jit(solution)/shard_map/ppermute | solution.py:178
  131.1 1.4 fusion.31
  132.6 1.8 multiply_reduce_fusion
  137.1 1.2 collective-permute-start.32
  138.3 1.4 collective-permute-start.31
  143.9 5.3 %collective-permute-start.35 = (f32[17,512]{1,0:T(8,128)S(1)}, f32[17,512]{1,0:T(8,128)S(1)}, u32[]{:S(2)}, u32[]{:S(2)}) collective-permute-start(f32[17,512]{1,0:T(8,128)S(1)} %add_add_fusion.6), channel_id=1, source_target_pairs={{0,3},{1,2},{2,1},{3,0},{4,7},{5,6},{6,5},{7,4},{8,11},{9,10},{10,... | collective-permute-start | bytes 104456 | tf_op jit(solution)/shard_map/ppermute | solution.py:178
  149.8 2.4 %collective-permute-done.35 = f32[17,512]{1,0:T(8,128)S(1)} collective-permute-done((f32[17,512]{1,0:T(8,128)S(1)}, f32[17,512]{1,0:T(8,128)S(1)}, u32[]{:S(2)}, u32[]{:S(2)}) %collective-permute-start.35) | collective-permute-done | bytes 34848 | tf_op jit(solution)/shard_map/ppermute | solution.py:178
  152.3 1.9 collective-permute-done.34
  154.8 2.2 %fusion.14 = f32[1000,512]{1,0:T(8,128)} fusion(s32[4]{0:T(128)S(1)} %fusion.42, f32[17,512]{1,0:T(8,128)S(1)} %add_add_fusion.5), kind=kOutput, calls=%fused_computation.51 | convolution fusion | flops 24580000 | bytes 2056704 | tf_op jit(solution)/shard_map/dot_general | solution.py:417
  158.3 1.9 collective-permute-start.28
  160.4 2.3 %collective-permute-start.26 = (bf16[128,512]{1,0:T(8,128)(2,1)S(1)}, bf16[128,512]{1,0:T(8,128)(2,1)S(1)}, u32[]{:S(2)}, u32[]{:S(2)}) collective-permute-start(bf16[128,512]{1,0:T(8,128)(2,1)S(1)} %add_convert_fusion.2), channel_id=1, source_target_pairs={{0,1},{1,0},{2,3},{3,2},{4,5},{5,4},{6,7},{7,6},{8,9},{9,8},{10,11... | collective-permute-start | bytes 393224 | tf_op jit(solution)/shard_map/ppermute | solution.py:178
  163.1 1.6 collective-permute-start.37
  164.7 1.8 collective-permute-done.28
  166.6 1.5 collective-permute-start.39
  168.1 3.1 %collective-permute-done.27 = bf16[128,512]{1,0:T(8,128)(2,1)S(1)} collective-permute-done((bf16[128,512]{1,0:T(8,128)(2,1)S(1)}, bf16[128,512]{1,0:T(8,128)(2,1)S(1)}, u32[]{:S(2)}, u32[]{:S(2)}) %collective-permute-start.27) | collective-permute-done | bytes 131104 | tf_op jit(solution)/shard_map/ppermute | solution.py:178
  173.2 4.2 %collective-permute-done.38 = bf16[64,768]{0,1:T(8,128)(2,1)S(1)} collective-permute-done((bf16[64,768]{0,1:T(8,128)(2,1)S(1)}, bf16[64,768]{0,1:T(8,128)(2,1)S(1)}, u32[]{:S(2)}, u32[]{:S(2)}) %collective-permute-start.38) | collective-permute-done | bytes 98336 | tf_op jit(solution)/shard_map/ppermute | solution.py:178
  177.6 2.9 %collective-permute-start.40 = (bf16[64,384]{0,1:T(8,128)(2,1)S(1)}, bf16[64,384]{0,1:T(8,128)(2,1)S(1)}, u32[]{:S(2)}, u32[]{:S(2)}) collective-permute-start(bf16[64,384]{0,1:T(8,128)(2,1)S(1)} %slice.306), channel_id=1, source_target_pairs={{0,2},{1,3},{2,0},{3,1},{4,6},{5,7},{6,4},{7,5},{8,10},{9,11},{10,... | collective-permute-start | bytes 147464 | tf_op jit(solution)/shard_map/ppermute | solution.py:178
  180.5 1.5 convert_add_fusion
  183.1 1.5 collective-permute-start.47
  186.9 1.6 collective-permute-start.43
  189.3 2.7 %collective-permute-done.45 = bf16[64,2304]{1,0:T(8,128)(2,1)S(1)} collective-permute-done((bf16[64,2304]{1,0:T(8,128)(2,1)S(1)}, bf16[64,2304]{1,0:T(8,128)(2,1)S(1)}, u32[]{:S(2)}, u32[]{:S(2)}) %collective-permute-start.45) | collective-permute-done | bytes 294944 | tf_op jit(solution)/shard_map/ppermute | solution.py:178
  193.1 3.1 %collective-permute-done.47 = bf16[64,2304]{1,0:T(8,128)(2,1)S(1)} collective-permute-done((bf16[64,2304]{1,0:T(8,128)(2,1)S(1)}, bf16[64,2304]{1,0:T(8,128)(2,1)S(1)}, u32[]{:S(2)}, u32[]{:S(2)}) %collective-permute-start.47) | collective-permute-done | bytes 294944 | tf_op jit(solution)/shard_map/ppermute | solution.py:178
  196.2 2.4 %collective-permute-done.46 = bf16[64,2304]{1,0:T(8,128)(2,1)S(1)} collective-permute-done((bf16[64,2304]{1,0:T(8,128)(2,1)S(1)}, bf16[64,2304]{1,0:T(8,128)(2,1)S(1)}, u32[]{:S(2)}, u32[]{:S(2)}) %collective-permute-start.46) | collective-permute-done | bytes 294944 | tf_op jit(solution)/shard_map/ppermute | solution.py:178
  198.7 2.7 %collective-permute-start.48 = (bf16[64,1152]{1,0:T(8,128)(2,1)S(1)}, bf16[64,1152]{1,0:T(8,128)(2,1)S(1)}, u32[]{:S(2)}, u32[]{:S(2)}) collective-permute-start(bf16[64,1152]{1,0:T(8,128)(2,1)S(1)} %slice.305), channel_id=1, source_target_pairs={{0,2},{1,3},{2,0},{3,1},{4,6},{5,7},{6,4},{7,5},{8,10},{9,11},{10,... | collective-permute-start | bytes 442376 | tf_op jit(solution)/shard_map/ppermute | solution.py:178
  201.6 4.8 %collective-permute-done.48 = bf16[64,1152]{1,0:T(8,128)(2,1)S(1)} collective-permute-done((bf16[64,1152]{1,0:T(8,128)(2,1)S(1)}, bf16[64,1152]{1,0:T(8,128)(2,1)S(1)}, u32[]{:S(2)}, u32[]{:S(2)}) %collective-permute-start.48) | collective-permute-done | bytes 147488 | tf_op jit(solution)/shard_map/ppermute | solution.py:178
  206.4 1.5 collective-permute-start.51
  207.9 2.1 collective-permute-start.49
  211.0 1.7 collective-permute-done.51
  212.6 1.5 collective-permute-done.50
  (307 shorter events, 57.4 us)
Async XLA Ops:
  0.6 19.7 %copy-start = (f32[1000,512]{1,0:T(8,128)S(1)}, f32[1000,512]{1,0:T(8,128)}, u32[]{:S(2)}) copy-start(f32[1000,512]{1,0:T(8,128)} %param.20) | copy-start | bytes 6144004
  0.7 19.7 %copy-start.13 = (f32[2,256,512]{2,1,0:T(8,128)S(1)}, f32[2,256,512]{2,1,0:T(8,128)}, u32[]{:S(2)}) copy-start(f32[2,256,512]{2,1,0:T(8,128)} %param.17) | copy-start | bytes 3145732
  1.9 27.8 %copy-start.34 = (bf16[256,128]{1,0:T(8,128)(2,1)}, bf16[256,128]{1,0:T(8,128)(2,1)S(1)}, u32[]{:S(2)}) copy-start(bf16[256,128]{1,0:T(8,128)(2,1)S(1)} %get-tuple-element.116) | copy-start | bytes 196612
  1.9 27.8 %copy-start.36 = (bf16[256,128]{1,0:T(8,128)(2,1)}, bf16[256,128]{1,0:T(8,128)(2,1)S(1)}, u32[]{:S(2)}) copy-start(bf16[256,128]{1,0:T(8,128)(2,1)S(1)} %get-tuple-element.117) | copy-start | bytes 196612
  2.6 27.0 %collective-permute-start.4 = (bf16[256,384]{1,0:T(8,128)(2,1)}, bf16[256,384]{1,0:T(8,128)(2,1)}, u32[]{:S(2)}, u32[]{:S(2)}) collective-permute-start(bf16[256,384]{1,0:T(8,128)(2,1)} %pad_maximum_fusion.17), channel_id=1, source_target_pairs={{0,2},{1,3},{2,0},{3,1},{4,6},{5,7},{6,4},{7,5},{8,10},{9,11},{10,... | collective-permute-start | bytes 589832 | tf_op jit(solution)/shard_map/ppermute | solution.py:178
  6.7 23.0 %collective-permute-start = (bf16[256,384]{1,0:T(8,128)(2,1)}, bf16[256,384]{1,0:T(8,128)(2,1)}, u32[]{:S(2)}, u32[]{:S(2)}) collective-permute-start(bf16[256,384]{1,0:T(8,128)(2,1)} %pad_maximum_fusion.17), channel_id=1, source_target_pairs={{0,16},{16,0},{1,17},{17,1},{2,18},{18,2},{3,19},{19,3},{4,20},{20... | collective-permute-start | bytes 589832 | tf_op jit(solution)/shard_map/ppermute | solution.py:178
  8.7 19.0 %collective-permute-start.6 = (f32[1,768]{1,0:T(1,128)}, f32[1,768]{1,0:T(1,128)}, u32[]{:S(2)}, u32[]{:S(2)}) collective-permute-start(f32[1,768]{1,0:T(1,128)} %broadcast_in_dim.4), channel_id=1, source_target_pairs={{0,2},{1,3},{2,0},{3,1},{4,6},{5,7},{6,4},{7,5},{8,10},{9,11},{10,... | collective-permute-start | bytes 9224 | tf_op jit(solution)/shard_map/ppermute | solution.py:178
  9.6 32.4 %copy-start.28 = (bf16[256,128]{1,0:T(8,128)(2,1)}, bf16[256,128]{1,0:T(8,128)(2,1)S(1)}, u32[]{:S(2)}) copy-start(bf16[256,128]{1,0:T(8,128)(2,1)S(1)} %convert.49) | copy-start | bytes 196612
  10.8 31.3 %copy-start.16 = (bf16[256,512]{1,0:T(8,128)(2,1)}, bf16[256,512]{1,0:T(8,128)(2,1)S(1)}, u32[]{:S(2)}) copy-start(bf16[256,512]{1,0:T(8,128)(2,1)S(1)} %convert.50) | copy-start | bytes 786436
  12.4 29.6 %collective-permute-start.10 = (bf16[256,1152]{1,0:T(8,128)(2,1)}, bf16[256,1152]{1,0:T(8,128)(2,1)}, u32[]{:S(2)}, u32[]{:S(2)}) collective-permute-start(bf16[256,1152]{1,0:T(8,128)(2,1)} %pad_maximum_fusion.9), channel_id=1, source_target_pairs={{0,2},{1,3},{2,0},{3,1},{4,6},{5,7},{6,4},{7,5},{8,10},{9,11},{10,... | collective-permute-start | bytes 1769480 | tf_op jit(solution)/shard_map/ppermute | solution.py:178
  20.7 21.3 %copy-start.19 = (bf16[256,512]{1,0:T(8,128)(2,1)S(1)}, bf16[256,512]{1,0:T(8,128)(2,1)}, u32[]{:S(2)}) copy-start(bf16[256,512]{1,0:T(8,128)(2,1)} %copy-done.18) | copy-start | bytes 786436
  20.7 22.5 %copy-start.45 = (f32[256]{0:T(256)}, f32[256]{0:T(256)S(1)}, u32[]{:S(2)}) copy-start(f32[256]{0:T(256)S(1)} %add_rsqrt_fusion.1) | copy-start | bytes 3076
  25.4 18.0 %copy-start.23 = (bf16[256,512]{1,0:T(8,128)(2,1)}, bf16[256,512]{1,0:T(8,128)(2,1)S(1)}, u32[]{:S(2)}) copy-start(bf16[256,512]{1,0:T(8,128)(2,1)S(1)} %add_convert_fusion.1) | copy-start | bytes 786436
  29.6 17.4 %collective-permute-start.5 = (bf16[256,384]{1,0:T(8,128)(2,1)}, bf16[256,384]{1,0:T(8,128)(2,1)S(1)}, u32[]{:S(2)}, u32[]{:S(2)}) collective-permute-start(bf16[256,384]{1,0:T(8,128)(2,1)} %collective-permute-done.4), channel_id=1, source_target_pairs={{0,16},{16,0},{1,17},{17,1},{2,18},{18,2},{3,19},{19,3},{4,20},{20... | collective-permute-start | bytes 589832 | tf_op jit(solution)/shard_map/ppermute | solution.py:178
  43.2 17.4 %collective-permute-start.11 = (bf16[256,2304]{1,0:T(8,128)(2,1)S(1)}, bf16[256,2304]{1,0:T(8,128)(2,1)S(1)}, u32[]{:S(2)}, u32[]{:S(2)}) collective-permute-start(bf16[256,2304]{1,0:T(8,128)(2,1)S(1)} %pad_maximum_fusion), channel_id=1, source_target_pairs={{0,16},{16,0},{1,17},{17,1},{2,18},{18,2},{3,19},{19,3},{4,20},{20... | collective-permute-start | bytes 3538952 | tf_op jit(solution)/shard_map/ppermute | solution.py:178
  43.4 7.7 %collective-permute-start.3 = (bf16[256,256]{1,0:T(8,128)(2,1)S(1)}, bf16[256,256]{1,0:T(8,128)(2,1)S(1)}, u32[]{:S(2)}, u32[]{:S(2)}) collective-permute-start(bf16[256,256]{1,0:T(8,128)(2,1)S(1)} %pad_maximum_fusion.22.kv0), channel_id=1, source_target_pairs={{0,12},{4,8},{8,4},{12,0},{1,13},{5,9},{9,5},{13,1},{2,14},{6,10},... | collective-permute-start | bytes 393224 | tf_op jit(solution)/shard_map/ppermute | solution.py:178
  46.0 7.9 %collective-permute-start.2 = (bf16[256,256]{1,0:T(8,128)(2,1)S(1)}, bf16[256,256]{1,0:T(8,128)(2,1)S(1)}, u32[]{:S(2)}, u32[]{:S(2)}) collective-permute-start(bf16[256,256]{1,0:T(8,128)(2,1)S(1)} %pad_maximum_fusion.22.kv0), channel_id=1, source_target_pairs={{0,8},{4,12},{8,0},{12,4},{1,9},{5,13},{9,1},{13,5},{2,10},{6,14},... | collective-permute-start | bytes 393224 | tf_op jit(solution)/shard_map/ppermute | solution.py:178
  46.5 8.6 %collective-permute-start.1 = (bf16[256,256]{1,0:T(8,128)(2,1)S(1)}, bf16[256,256]{1,0:T(8,128)(2,1)S(1)}, u32[]{:S(2)}, u32[]{:S(2)}) collective-permute-start(bf16[256,256]{1,0:T(8,128)(2,1)S(1)} %pad_maximum_fusion.22.kv0), channel_id=1, source_target_pairs={{0,4},{4,0},{8,12},{12,8},{1,5},{5,1},{9,13},{13,9},{2,6},{6,2},{1... | collective-permute-start | bytes 393224 | tf_op jit(solution)/shard_map/ppermute | solution.py:178
  48.6 8.0 %collective-permute-start.9 = (bf16[256,256]{1,0:T(8,128)(2,1)S(1)}, bf16[256,256]{1,0:T(8,128)(2,1)S(1)}, u32[]{:S(2)}, u32[]{:S(2)}) collective-permute-start(bf16[256,256]{1,0:T(8,128)(2,1)S(1)} %pad_maximum_fusion.23.kv0), channel_id=1, source_target_pairs={{0,12},{4,8},{8,4},{12,0},{1,13},{5,9},{9,5},{13,1},{2,14},{6,10},... | collective-permute-start | bytes 393224 | tf_op jit(solution)/shard_map/ppermute | solution.py:178
  51.1 7.6 %collective-permute-start.8 = (bf16[256,256]{1,0:T(8,128)(2,1)S(1)}, bf16[256,256]{1,0:T(8,128)(2,1)S(1)}, u32[]{:S(2)}, u32[]{:S(2)}) collective-permute-start(bf16[256,256]{1,0:T(8,128)(2,1)S(1)} %pad_maximum_fusion.23.kv0), channel_id=1, source_target_pairs={{0,8},{4,12},{8,0},{12,4},{1,9},{5,13},{9,1},{13,5},{2,10},{6,14},... | collective-permute-start | bytes 393224 | tf_op jit(solution)/shard_map/ppermute | solution.py:178
  53.9 5.3 %collective-permute-start.7 = (bf16[256,256]{1,0:T(8,128)(2,1)S(1)}, bf16[256,256]{1,0:T(8,128)(2,1)S(1)}, u32[]{:S(2)}, u32[]{:S(2)}) collective-permute-start(bf16[256,256]{1,0:T(8,128)(2,1)S(1)} %pad_maximum_fusion.23.kv0), channel_id=1, source_target_pairs={{0,4},{4,0},{8,12},{12,8},{1,5},{5,1},{9,13},{13,9},{2,6},{6,2},{1... | collective-permute-start | bytes 393224 | tf_op jit(solution)/shard_map/ppermute | solution.py:178
  69.8 7.8 %collective-permute-start.12 = (bf16[256,512]{1,0:T(8,128)(2,1)S(1)}, bf16[256,512]{1,0:T(8,128)(2,1)S(1)}, u32[]{:S(2)}, u32[]{:S(2)}) collective-permute-start(bf16[256,512]{1,0:T(8,128)(2,1)S(1)} %get-tuple-element.137), channel_id=1, source_target_pairs={{0,1},{1,0},{2,3},{3,2},{4,5},{5,4},{6,7},{7,6},{8,9},{9,8},{10,11... | collective-permute-start | bytes 786440 | tf_op jit(solution)/shard_map/ppermute | solution.py:178
  85.2 8.0 %collective-permute-start.13 = (bf16[128,512]{1,0:T(8,128)(2,1)S(1)}, bf16[128,512]{1,0:T(8,128)(2,1)S(1)}, u32[]{:S(2)}, u32[]{:S(2)}) collective-permute-start(bf16[128,512]{1,0:T(8,128)(2,1)S(1)} %dynamic-slice_convert_fusion.10), channel_id=1, source_target_pairs={{0,1},{1,0},{2,3},{3,2},{4,5},{5,4},{6,7},{7,6},{8,9},{9,8},{10,11... | collective-permute-start | bytes 393224 | tf_op jit(solution)/shard_map/ppermute | solution.py:178
  86.0 6.1 %collective-permute-start.17 = (bf16[128,512]{1,0:T(8,128)(2,1)S(1)}, bf16[128,512]{1,0:T(8,128)(2,1)S(1)}, u32[]{:S(2)}, u32[]{:S(2)}) collective-permute-start(bf16[128,512]{1,0:T(8,128)(2,1)S(1)} %dynamic-slice_convert_fusion.9), channel_id=1, source_target_pairs={{0,1},{1,0},{2,3},{3,2},{4,5},{5,4},{6,7},{7,6},{8,9},{9,8},{10,11... | collective-permute-start | bytes 393224 | tf_op jit(solution)/shard_map/ppermute | solution.py:178
  92.4 7.3 %collective-permute-start.18 = (bf16[128,512]{1,0:T(8,128)(2,1)S(1)}, bf16[128,512]{1,0:T(8,128)(2,1)S(1)}, u32[]{:S(2)}, u32[]{:S(2)}) collective-permute-start(bf16[128,512]{1,0:T(8,128)(2,1)S(1)} %convert_element_type.235), channel_id=1, source_target_pairs={{0,1},{1,0},{2,3},{3,2},{4,5},{5,4},{6,7},{7,6},{8,9},{9,8},{10,11... | collective-permute-start | bytes 393224 | tf_op jit(solution)/shard_map/ppermute | solution.py:178
  94.0 22.2 %collective-permute-start.16 = (bf16[128,512]{1,0:T(8,128)(2,1)}, bf16[128,512]{1,0:T(8,128)(2,1)}, u32[]{:S(2)}, u32[]{:S(2)}) collective-permute-start(bf16[128,512]{1,0:T(8,128)(2,1)} %add_convert_fusion.3), channel_id=1, source_target_pairs={{0,3},{1,2},{2,1},{3,0},{4,7},{5,6},{6,5},{7,4},{8,11},{9,10},{10,... | collective-permute-start | bytes 393224 | tf_op jit(solution)/shard_map/ppermute | solution.py:178
  97.4 20.0 %collective-permute-start.15 = (bf16[128,512]{1,0:T(8,128)(2,1)}, bf16[128,512]{1,0:T(8,128)(2,1)}, u32[]{:S(2)}, u32[]{:S(2)}) collective-permute-start(bf16[128,512]{1,0:T(8,128)(2,1)} %add_convert_fusion.3), channel_id=1, source_target_pairs={{0,2},{1,3},{2,0},{3,1},{4,6},{5,7},{6,4},{7,5},{8,10},{9,11},{10,... | collective-permute-start | bytes 393224 | tf_op jit(solution)/shard_map/ppermute | solution.py:178
  97.4 21.4 %collective-permute-start.14 = (bf16[128,512]{1,0:T(8,128)(2,1)}, bf16[128,512]{1,0:T(8,128)(2,1)}, u32[]{:S(2)}, u32[]{:S(2)}) collective-permute-start(bf16[128,512]{1,0:T(8,128)(2,1)} %add_convert_fusion.3), channel_id=1, source_target_pairs={{0,1},{1,0},{2,3},{3,2},{4,5},{5,4},{6,7},{7,6},{8,9},{9,8},{10,11... | collective-permute-start | bytes 393224 | tf_op jit(solution)/shard_map/ppermute | solution.py:178
  108.9 15.6 %collective-permute-start.22 = (bf16[256,256]{1,0:T(8,128)(2,1)}, bf16[256,256]{1,0:T(8,128)(2,1)}, u32[]{:S(2)}, u32[]{:S(2)}) collective-permute-start(bf16[256,256]{1,0:T(8,128)(2,1)} %get-tuple-element.40), channel_id=1, source_target_pairs={{0,4},{4,0},{8,12},{12,8},{1,5},{5,1},{9,13},{13,9},{2,6},{6,2},{1... | collective-permute-start | bytes 393224 | tf_op jit(solution)/shard_map/ppermute | solution.py:178
  110.4 15.4 %collective-permute-start.23 = (bf16[256,256]{1,0:T(8,128)(2,1)}, bf16[256,256]{1,0:T(8,128)(2,1)}, u32[]{:S(2)}, u32[]{:S(2)}) collective-permute-start(bf16[256,256]{1,0:T(8,128)(2,1)} %get-tuple-element.41), channel_id=1, source_target_pairs={{0,8},{4,12},{8,0},{12,4},{1,9},{5,13},{9,1},{13,5},{2,10},{6,14},... | collective-permute-start | bytes 393224 | tf_op jit(solution)/shard_map/ppermute | solution.py:178
  116.2 9.6 %collective-permute-start.24 = (bf16[256,256]{1,0:T(8,128)(2,1)S(1)}, bf16[256,256]{1,0:T(8,128)(2,1)S(1)}, u32[]{:S(2)}, u32[]{:S(2)}) collective-permute-start(bf16[256,256]{1,0:T(8,128)(2,1)S(1)} %copy-done.6), channel_id=1, source_target_pairs={{0,12},{4,8},{8,4},{12,0},{1,13},{5,9},{9,5},{13,1},{2,14},{6,10},... | collective-permute-start | bytes 393224 | tf_op jit(solution)/shard_map/ppermute | solution.py:178
  117.4 9.5 %collective-permute-start.19 = (bf16[256,256]{1,0:T(8,128)(2,1)S(1)}, bf16[256,256]{1,0:T(8,128)(2,1)S(1)}, u32[]{:S(2)}, u32[]{:S(2)}) collective-permute-start(bf16[256,256]{1,0:T(8,128)(2,1)S(1)} %get-tuple-element.34), channel_id=1, source_target_pairs={{0,4},{4,0},{8,12},{12,8},{1,5},{5,1},{9,13},{13,9},{2,6},{6,2},{1... | collective-permute-start | bytes 393224 | tf_op jit(solution)/shard_map/ppermute | solution.py:178
  118.8 8.1 %collective-permute-start.20 = (bf16[256,256]{1,0:T(8,128)(2,1)S(1)}, bf16[256,256]{1,0:T(8,128)(2,1)S(1)}, u32[]{:S(2)}, u32[]{:S(2)}) collective-permute-start(bf16[256,256]{1,0:T(8,128)(2,1)S(1)} %get-tuple-element.35), channel_id=1, source_target_pairs={{0,8},{4,12},{8,0},{12,4},{1,9},{5,13},{9,1},{13,5},{2,10},{6,14},... | collective-permute-start | bytes 393224 | tf_op jit(solution)/shard_map/ppermute | solution.py:178
  124.6 5.9 %collective-permute-start.21 = (bf16[256,256]{1,0:T(8,128)(2,1)S(1)}, bf16[256,256]{1,0:T(8,128)(2,1)S(1)}, u32[]{:S(2)}, u32[]{:S(2)}) collective-permute-start(bf16[256,256]{1,0:T(8,128)(2,1)S(1)} %get-tuple-element.36), channel_id=1, source_target_pairs={{0,12},{4,8},{8,4},{12,0},{1,13},{5,9},{9,5},{13,1},{2,14},{6,10},... | collective-permute-start | bytes 393224 | tf_op jit(solution)/shard_map/ppermute | solution.py:178
  125.8 54.7 %collective-permute-start.44 = (bf16[256,2304]{1,0:T(8,128)(2,1)}, bf16[256,2304]{1,0:T(8,128)(2,1)}, u32[]{:S(2)}, u32[]{:S(2)}) collective-permute-start(bf16[256,2304]{1,0:T(8,128)(2,1)} %dynamic-slice_convert_fusion), channel_id=1, source_target_pairs={{0,16},{16,0},{1,17},{17,1},{2,18},{18,2},{3,19},{19,3},{4,20},{20... | collective-permute-start | bytes 3538952 | tf_op jit(solution)/shard_map/ppermute | solution.py:178
  135.8 1.3 collective-permute-start.29
  137.1 5.2 %collective-permute-start.32 = (f32[17,512]{1,0:T(8,128)S(1)}, f32[17,512]{1,0:T(8,128)S(1)}, u32[]{:S(2)}, u32[]{:S(2)}) collective-permute-start(f32[17,512]{1,0:T(8,128)S(1)} %add.351), channel_id=1, source_target_pairs={{0,12},{4,8},{8,4},{12,0},{1,13},{5,9},{9,5},{13,1},{2,14},{6,10},... | collective-permute-start | bytes 104456 | tf_op jit(solution)/shard_map/ppermute | solution.py:178
  138.3 4.6 %collective-permute-start.31 = (f32[17,512]{1,0:T(8,128)S(1)}, f32[17,512]{1,0:T(8,128)S(1)}, u32[]{:S(2)}, u32[]{:S(2)}) collective-permute-start(f32[17,512]{1,0:T(8,128)S(1)} %add.351), channel_id=1, source_target_pairs={{0,8},{4,12},{8,0},{12,4},{1,9},{5,13},{9,1},{13,5},{2,10},{6,14},... | collective-permute-start | bytes 104456 | tf_op jit(solution)/shard_map/ppermute | solution.py:178
  139.8 4.1 %collective-permute-start.30 = (f32[17,512]{1,0:T(8,128)S(1)}, f32[17,512]{1,0:T(8,128)S(1)}, u32[]{:S(2)}, u32[]{:S(2)}) collective-permute-start(f32[17,512]{1,0:T(8,128)S(1)} %add.351), channel_id=1, source_target_pairs={{0,4},{4,0},{8,12},{12,8},{1,5},{5,1},{9,13},{13,9},{2,6},{6,2},{1... | collective-permute-start | bytes 104456 | tf_op jit(solution)/shard_map/ppermute | solution.py:178
  140.7 17.5 %copy-start.26 = (f32[128,512]{1,0:T(8,128)S(1)}, f32[128,512]{1,0:T(8,128)}, u32[]{:S(2)}) copy-start(f32[128,512]{1,0:T(8,128)} %copy-done.25) | copy-start | bytes 786436
  140.7 17.5 %copy-start.27 = (f32[256,512]{1,0:T(8,128)S(1)}, f32[256,512]{1,0:T(8,128)}, u32[]{:S(2)}) copy-start(f32[256,512]{1,0:T(8,128)} %get-tuple-element.67) | copy-start | bytes 1572868
  141.7 16.5 %collective-permute-start.25 = (bf16[128,512]{1,0:T(8,128)(2,1)S(1)}, bf16[128,512]{1,0:T(8,128)(2,1)S(1)}, u32[]{:S(2)}, u32[]{:S(2)}) collective-permute-start(bf16[128,512]{1,0:T(8,128)(2,1)S(1)} %dynamic-slice_convert_fusion.8), channel_id=1, source_target_pairs={{0,1},{1,0},{2,3},{3,2},{4,5},{5,4},{6,7},{7,6},{8,9},{9,8},{10,11... | collective-permute-start | bytes 393224 | tf_op jit(solution)/shard_map/ppermute | solution.py:178
  143.9 8.4 %collective-permute-start.35 = (f32[17,512]{1,0:T(8,128)S(1)}, f32[17,512]{1,0:T(8,128)S(1)}, u32[]{:S(2)}, u32[]{:S(2)}) collective-permute-start(f32[17,512]{1,0:T(8,128)S(1)} %add_add_fusion.6), channel_id=1, source_target_pairs={{0,3},{1,2},{2,1},{3,0},{4,7},{5,6},{6,5},{7,4},{8,11},{9,10},{10,... | collective-permute-start | bytes 104456 | tf_op jit(solution)/shard_map/ppermute | solution.py:178
  149.1 5.0 %collective-permute-start.34 = (f32[17,512]{1,0:T(8,128)S(1)}, f32[17,512]{1,0:T(8,128)S(1)}, u32[]{:S(2)}, u32[]{:S(2)}) collective-permute-start(f32[17,512]{1,0:T(8,128)S(1)} %add_add_fusion.6), channel_id=1, source_target_pairs={{0,2},{1,3},{2,0},{3,1},{4,6},{5,7},{6,4},{7,5},{8,10},{9,11},{10,... | collective-permute-start | bytes 104456 | tf_op jit(solution)/shard_map/ppermute | solution.py:178
  149.2 5.0 %collective-permute-start.33 = (f32[17,512]{1,0:T(8,128)S(1)}, f32[17,512]{1,0:T(8,128)S(1)}, u32[]{:S(2)}, u32[]{:S(2)}) collective-permute-start(f32[17,512]{1,0:T(8,128)S(1)} %add_add_fusion.6), channel_id=1, source_target_pairs={{0,1},{1,0},{2,3},{3,2},{4,5},{5,4},{6,7},{7,6},{8,9},{9,8},{10,11... | collective-permute-start | bytes 104456 | tf_op jit(solution)/shard_map/ppermute | solution.py:178
  152.3 10.5 %collective-permute-start.36 = (bf16[256,768]{0,1:T(8,128)(2,1)S(1)}, bf16[256,768]{0,1:T(8,128)(2,1)S(1)}, u32[]{:S(2)}, u32[]{:S(2)}) collective-permute-start(bf16[256,768]{0,1:T(8,128)(2,1)S(1)} %fusion.7), channel_id=1, source_target_pairs={{0,16},{16,0},{1,17},{17,1},{2,18},{18,2},{3,19},{19,3},{4,20},{20... | collective-permute-start | bytes 1179656 | tf_op jit(solution)/shard_map/ppermute | solution.py:178
  158.3 8.3 %collective-permute-start.28 = (bf16[128,512]{1,0:T(8,128)(2,1)S(1)}, bf16[128,512]{1,0:T(8,128)(2,1)S(1)}, u32[]{:S(2)}, u32[]{:S(2)}) collective-permute-start(bf16[128,512]{1,0:T(8,128)(2,1)S(1)} %add_convert_fusion.2), channel_id=1, source_target_pairs={{0,3},{1,2},{2,1},{3,0},{4,7},{5,6},{6,5},{7,4},{8,11},{9,10},{10,... | collective-permute-start | bytes 393224 | tf_op jit(solution)/shard_map/ppermute | solution.py:178
  160.2 11.0 %collective-permute-start.27 = (bf16[128,512]{1,0:T(8,128)(2,1)S(1)}, bf16[128,512]{1,0:T(8,128)(2,1)S(1)}, u32[]{:S(2)}, u32[]{:S(2)}) collective-permute-start(bf16[128,512]{1,0:T(8,128)(2,1)S(1)} %add_convert_fusion.2), channel_id=1, source_target_pairs={{0,2},{1,3},{2,0},{3,1},{4,6},{5,7},{6,4},{7,5},{8,10},{9,11},{10,... | collective-permute-start | bytes 393224 | tf_op jit(solution)/shard_map/ppermute | solution.py:178
  160.4 11.7 %collective-permute-start.26 = (bf16[128,512]{1,0:T(8,128)(2,1)S(1)}, bf16[128,512]{1,0:T(8,128)(2,1)S(1)}, u32[]{:S(2)}, u32[]{:S(2)}) collective-permute-start(bf16[128,512]{1,0:T(8,128)(2,1)S(1)} %add_convert_fusion.2), channel_id=1, source_target_pairs={{0,1},{1,0},{2,3},{3,2},{4,5},{5,4},{6,7},{7,6},{8,9},{9,8},{10,11... | collective-permute-start | bytes 393224 | tf_op jit(solution)/shard_map/ppermute | solution.py:178
  162.7 17.8 %copy-start.22 = (f32[512,2304]{1,0:T(8,128)S(1)}, f32[512,2304]{1,0:T(8,128)}, u32[]{:S(2)}) copy-start(f32[512,2304]{1,0:T(8,128)} %copy-done.21) | copy-start | bytes 14155780
  163.1 9.1 %collective-permute-start.37 = (bf16[64,768]{0,1:T(8,128)(2,1)S(1)}, bf16[64,768]{0,1:T(8,128)(2,1)S(1)}, u32[]{:S(2)}, u32[]{:S(2)}) collective-permute-start(bf16[64,768]{0,1:T(8,128)(2,1)S(1)} %get-tuple-element.86), channel_id=1, source_target_pairs={{0,4},{4,0},{8,12},{12,8},{1,5},{5,1},{9,13},{13,9},{2,6},{6,2},{1... | collective-permute-start | bytes 294920 | tf_op jit(solution)/shard_map/ppermute | solution.py:178
  166.6 6.6 %collective-permute-start.39 = (bf16[64,768]{0,1:T(8,128)(2,1)S(1)}, bf16[64,768]{0,1:T(8,128)(2,1)S(1)}, u32[]{:S(2)}, u32[]{:S(2)}) collective-permute-start(bf16[64,768]{0,1:T(8,128)(2,1)S(1)} %get-tuple-element.87), channel_id=1, source_target_pairs={{0,12},{4,8},{8,4},{12,0},{1,13},{5,9},{9,5},{13,1},{2,14},{6,10},... | collective-permute-start | bytes 294920 | tf_op jit(solution)/shard_map/ppermute | solution.py:178
  171.2 6.2 %collective-permute-start.38 = (bf16[64,768]{0,1:T(8,128)(2,1)S(1)}, bf16[64,768]{0,1:T(8,128)(2,1)S(1)}, u32[]{:S(2)}, u32[]{:S(2)}) collective-permute-start(bf16[64,768]{0,1:T(8,128)(2,1)S(1)} %get-tuple-element.88), channel_id=1, source_target_pairs={{0,8},{4,12},{8,0},{12,4},{1,9},{5,13},{9,1},{13,5},{2,10},{6,14},... | collective-permute-start | bytes 294920 | tf_op jit(solution)/shard_map/ppermute | solution.py:178
  177.6 9.3 %collective-permute-start.40 = (bf16[64,384]{0,1:T(8,128)(2,1)S(1)}, bf16[64,384]{0,1:T(8,128)(2,1)S(1)}, u32[]{:S(2)}, u32[]{:S(2)}) collective-permute-start(bf16[64,384]{0,1:T(8,128)(2,1)S(1)} %slice.306), channel_id=1, source_target_pairs={{0,2},{1,3},{2,0},{3,1},{4,6},{5,7},{6,4},{7,5},{8,10},{9,11},{10,... | collective-permute-start | bytes 147464 | tf_op jit(solution)/shard_map/ppermute | solution.py:178
  182.1 9.9 %collective-permute-start.45 = (bf16[64,2304]{1,0:T(8,128)(2,1)S(1)}, bf16[64,2304]{1,0:T(8,128)(2,1)S(1)}, u32[]{:S(2)}, u32[]{:S(2)}) collective-permute-start(bf16[64,2304]{1,0:T(8,128)(2,1)S(1)} %get-tuple-element.77), channel_id=1, source_target_pairs={{0,4},{4,0},{8,12},{12,8},{1,5},{5,1},{9,13},{13,9},{2,6},{6,2},{1... | collective-permute-start | bytes 884744 | tf_op jit(solution)/shard_map/ppermute | solution.py:178
  183.1 13.1 %collective-permute-start.47 = (bf16[64,2304]{1,0:T(8,128)(2,1)S(1)}, bf16[64,2304]{1,0:T(8,128)(2,1)S(1)}, u32[]{:S(2)}, u32[]{:S(2)}) collective-permute-start(bf16[64,2304]{1,0:T(8,128)(2,1)S(1)} %get-tuple-element.78), channel_id=1, source_target_pairs={{0,12},{4,8},{8,4},{12,0},{1,13},{5,9},{9,5},{13,1},{2,14},{6,10},... | collective-permute-start | bytes 884744 | tf_op jit(solution)/shard_map/ppermute | solution.py:178
  184.6 13.9 %collective-permute-start.46 = (bf16[64,2304]{1,0:T(8,128)(2,1)S(1)}, bf16[64,2304]{1,0:T(8,128)(2,1)S(1)}, u32[]{:S(2)}, u32[]{:S(2)}) collective-permute-start(bf16[64,2304]{1,0:T(8,128)(2,1)S(1)} %get-tuple-element.79), channel_id=1, source_target_pairs={{0,8},{4,12},{8,0},{12,4},{1,9},{5,13},{9,1},{13,5},{2,10},{6,14},... | collective-permute-start | bytes 884744 | tf_op jit(solution)/shard_map/ppermute | solution.py:178
  186.9 14.5 %collective-permute-start.43 = (bf16[64,384]{0,1:T(8,128)(2,1)S(1)}, bf16[64,384]{0,1:T(8,128)(2,1)S(1)}, u32[]{:S(2)}, u32[]{:S(2)}) collective-permute-start(bf16[64,384]{0,1:T(8,128)(2,1)S(1)} %fusion.22), channel_id=1, source_target_pairs={{0,12},{4,8},{8,4},{12,0},{1,13},{5,9},{9,5},{13,1},{2,14},{6,10},... | collective-permute-start | bytes 147464 | tf_op jit(solution)/shard_map/ppermute | solution.py:178
  188.4 12.9 %collective-permute-start.42 = (bf16[64,384]{0,1:T(8,128)(2,1)S(1)}, bf16[64,384]{0,1:T(8,128)(2,1)S(1)}, u32[]{:S(2)}, u32[]{:S(2)}) collective-permute-start(bf16[64,384]{0,1:T(8,128)(2,1)S(1)} %fusion.22), channel_id=1, source_target_pairs={{0,8},{4,12},{8,0},{12,4},{1,9},{5,13},{9,1},{13,5},{2,10},{6,14},... | collective-permute-start | bytes 147464 | tf_op jit(solution)/shard_map/ppermute | solution.py:178
  192.0 9.3 %collective-permute-start.41 = (bf16[64,384]{0,1:T(8,128)(2,1)S(1)}, bf16[64,384]{0,1:T(8,128)(2,1)S(1)}, u32[]{:S(2)}, u32[]{:S(2)}) collective-permute-start(bf16[64,384]{0,1:T(8,128)(2,1)S(1)} %fusion.22), channel_id=1, source_target_pairs={{0,4},{4,0},{8,12},{12,8},{1,5},{5,1},{9,13},{13,9},{2,6},{6,2},{1... | collective-permute-start | bytes 147464 | tf_op jit(solution)/shard_map/ppermute | solution.py:178
  198.7 7.7 %collective-permute-start.48 = (bf16[64,1152]{1,0:T(8,128)(2,1)S(1)}, bf16[64,1152]{1,0:T(8,128)(2,1)S(1)}, u32[]{:S(2)}, u32[]{:S(2)}) collective-permute-start(bf16[64,1152]{1,0:T(8,128)(2,1)S(1)} %slice.305), channel_id=1, source_target_pairs={{0,2},{1,3},{2,0},{3,1},{4,6},{5,7},{6,4},{7,5},{8,10},{9,11},{10,... | collective-permute-start | bytes 442376 | tf_op jit(solution)/shard_map/ppermute | solution.py:178
  206.4 6.2 %collective-permute-start.51 = (bf16[64,1152]{1,0:T(8,128)(2,1)S(1)}, bf16[64,1152]{1,0:T(8,128)(2,1)S(1)}, u32[]{:S(2)}, u32[]{:S(2)}) collective-permute-start(bf16[64,1152]{1,0:T(8,128)(2,1)S(1)} %fusion.15), channel_id=1, source_target_pairs={{0,12},{4,8},{8,4},{12,0},{1,13},{5,9},{9,5},{13,1},{2,14},{6,10},... | collective-permute-start | bytes 442376 | tf_op jit(solution)/shard_map/ppermute | solution.py:178
  207.9 6.2 %collective-permute-start.50 = (bf16[64,1152]{1,0:T(8,128)(2,1)S(1)}, bf16[64,1152]{1,0:T(8,128)(2,1)S(1)}, u32[]{:S(2)}, u32[]{:S(2)}) collective-permute-start(bf16[64,1152]{1,0:T(8,128)(2,1)S(1)} %fusion.15), channel_id=1, source_target_pairs={{0,8},{4,12},{8,0},{12,4},{1,9},{5,13},{9,1},{13,5},{2,10},{6,14},... | collective-permute-start | bytes 442376 | tf_op jit(solution)/shard_map/ppermute | solution.py:178
  207.9 6.2 %collective-permute-start.49 = (bf16[64,1152]{1,0:T(8,128)(2,1)S(1)}, bf16[64,1152]{1,0:T(8,128)(2,1)S(1)}, u32[]{:S(2)}, u32[]{:S(2)}) collective-permute-start(bf16[64,1152]{1,0:T(8,128)(2,1)S(1)} %fusion.15), channel_id=1, source_target_pairs={{0,4},{4,0},{8,12},{12,8},{1,5},{5,1},{9,13},{13,9},{2,6},{6,2},{1... | collective-permute-start | bytes 442376 | tf_op jit(solution)/shard_map/ppermute | solution.py:178
  (52 other events, 319.7 us)

commit v2 on v0

v2 whole, which is shorter than its diff:
```python
import functools
import jax
import jax.numpy as jnp
from jax import lax
from jax.experimental import pallas as pl
from jax.experimental.pallas import tpu as pltpu
from jax.sharding import PartitionSpec as P

HEAD_DIM = 64
SCALE = HEAD_DIM ** (-0.5)
EPSILON = 1e-05
NEGATIVE = -1e30
F32 = jnp.float32
BF16 = jnp.bfloat16
BIAS_ROWS = 16
CUBE = 0.044715
ROOT = 0.7978845608028654
COST = 20_000_000_000
VMEM = pl.BlockSpec(memory_space=pltpu.VMEM)
SMEM = pl.BlockSpec(memory_space=pltpu.SMEM)


def dot_nn(left, right):
    return lax.dot_general(left, right, (((1,), (0,)), ((), ())), preferred_element_type=F32)


def dot_nt(left, right):
    return lax.dot_general(left, right, (((1,), (1,)), ((), ())), preferred_element_type=F32)


def dot_tn(left, right):
    return lax.dot_general(left, right, (((0,), (0,)), ((), ())), preferred_element_type=F32)


def total(values):
    return functools.reduce(jnp.add, values)


def norm_parts(values):
    centre = values - jnp.mean(values, axis=-1, keepdims=True)
    spread = jnp.mean(centre * centre, axis=-1, keepdims=True)
    inverse = lax.rsqrt(spread + EPSILON)
    return centre * inverse, inverse


def norm_back(grad, hat, inverse, gain):
    scaled = grad * gain
    mean_one = jnp.mean(scaled, axis=-1, keepdims=True)
    mean_two = jnp.mean(scaled * hat, axis=-1, keepdims=True)
    return inverse * (scaled - mean_one - hat * mean_two)


def column_sum(values):
    return jnp.sum(values, axis=0, keepdims=True)


def window(index, size):
    return pl.ds(pl.multiple_of(index * size, size), size)


def halves(spot_ref, size):
    return window(spot_ref[0], size), window(1 - spot_ref[0], size)


def hold(*values):
    return lax.optimization_barrier(values)


class Order:
    def __init__(self, spot):
        self.spot = spot

    def call(self, kernel, outs, operands, *, far=(), scratch=(), limit=12):
        scalars = [SMEM if operand.ndim == 1 else None for operand in operands]
        specs = [
            pl.BlockSpec(memory_space=pltpu.HBM) if i in far else scalars[i] or VMEM
            for i in range(len(operands))
        ]
        operands = [
            pltpu.with_memory_space_constraint(operand, pltpu.HBM) if i in far else operand
            for i, operand in enumerate(operands)
        ]
        results = pl.pallas_call(
            kernel,
            out_shape=tuple(jax.ShapeDtypeStruct(shape, dtype) for shape, dtype in outs),
            in_specs=[SMEM] + specs,
            out_specs=(VMEM,) * len(outs),
            scratch_shapes=list(scratch),
            compiler_params=pltpu.CompilerParams(vmem_limit_bytes=limit << 20),
            cost_estimate=pl.CostEstimate(
                flops=COST, bytes_accessed=1 << 16, transcendentals=0
            ),
        )(self.spot, *operands)
        first, self.spot = hold(results[0], self.spot)
        return [first, *results[1:]]

    def swap(self, values, axis, bits):
        values, self.spot = hold(values, self.spot)
        size = 2 if axis == "fsdp" else 4
        with jax.named_scope("swap_%s_%d" % (axis, bits)):
            return lax.ppermute(values, axis, [(i, i ^ bits) for i in range(size)])

    def swap_three(self, values, axis):
        return [self.swap(values, axis, bits) for bits in (1, 2, 3)]

    def swap_turn(self, values, turn):
        values, self.spot = hold(values, self.spot)
        pairs = [
            (4 * core + i, 4 * core + (i ^ (1 + (core + turn) % 2)))
            for core in range(2)
            for i in range(4)
        ]
        with jax.named_scope("swap_turn_%d" % turn):
            return lax.ppermute(values, ("fsdp", "ctx"), pairs)


def fetch(copies, sems):
    started = [
        pltpu.make_async_copy(source, target, sems.at[i])
        for i, (source, target) in enumerate(copies)
    ]
    for copy in started:
        copy.start()
    for copy in started:
        copy.wait()


def split_three(values):
    high = values.astype(BF16)
    rest = values - high.astype(F32)
    middle = rest.astype(BF16)
    return [high, middle, (rest - middle.astype(F32)).astype(BF16)]


def pack_first_kernel(
    spot_ref, steps_ref, w_hbm, out_hbm, qv_hbm, up_hbm, pack_ref, w_ref, o_ref, qv_ref, up_ref,
    sems,
):
    rows, cols = w_ref.shape[1:]
    fetch([(w_hbm, w_ref), (out_hbm, o_ref), (qv_hbm, qv_ref), (up_hbm, up_ref)], sems)
    for i in range(3):
        pack_ref[:rows, i * cols : (i + 1) * cols] = w_ref[i].astype(BF16)
    pack_ref[:rows, 3 * cols :] = o_ref[...].astype(BF16)
    lanes = lax.broadcasted_iota(jnp.int32, (1, cols), 1)
    steps = jnp.zeros((1, cols), F32)
    for i in range(steps_ref.shape[0]):
        steps = jnp.where(lanes == i, steps_ref[i].astype(F32), steps)
    fill = jnp.zeros((1, cols), F32)
    line = jnp.concatenate([qv_ref[0:1], qv_ref[1:2], steps, fill], axis=1)
    parts = split_three(jnp.concatenate([line, up_ref[...]], axis=0))
    fill = jnp.zeros((BIAS_ROWS - 6, 4 * cols), F32)
    stack = jnp.concatenate([v.astype(F32) for v in parts] + [fill], axis=0)
    pack_ref[rows:, :] = stack.astype(BF16)


def bias_lines(pack_ref, row):
    bits = pack_ref[row : row + BIAS_ROWS, :].astype(F32)
    lines = bits[0:2] + bits[2:4] + bits[4:6]
    return lines[0:1], lines[1:2]


def pack_rest_kernel(
    spot_ref, up_hbm, down_hbm, cotan_hbm, pack_ref, half_ref, cotan_ref, up_ref, down_ref, sems
):
    hidden = up_ref.shape[1]
    pair = spot_ref[2] // 2
    fetch([(up_hbm, up_ref), (down_hbm, down_ref), (cotan_hbm.at[pair], cotan_ref)], sems)
    pack_ref[:, :hidden] = up_ref[...].astype(BF16)
    pack_ref[:, hidden:] = down_ref[...].astype(BF16)
    mine = window(spot_ref[1] % 2, half_ref.shape[0])
    half_ref[:, :hidden] = up_ref[mine, :].astype(BF16)
    half_ref[:, hidden:] = down_ref[mine, :].astype(BF16)


def join_kernel(spot_ref, *refs, place, keep):
    pieces, out_ref = refs[:-1], refs[-1]
    rows = pieces[0].shape[0]
    for bits, piece in enumerate(pieces):
        at = window((spot_ref[place] & keep) ^ bits, rows)
        out_ref[at, :] = piece[...].astype(out_ref.dtype)


def join(order, place, pieces, dtype):
    rows, cols = pieces[0].shape
    kernel = functools.partial(join_kernel, place=place, keep=len(pieces) - 1)
    return order.call(kernel, [((rows * len(pieces), cols), dtype)], pieces)[0]


def stream_kernel(
    spot_ref, steps_ref, x_hbm, table_hbm, seg_hbm, g1, b1, g2, b2, bo, bd,
    stream_ref, normed_ref, seg_ref, lines_ref, x_ref, table_ref, ids_ref, line_ref, sems,
):
    pair = spot_ref[2] // 2
    step = steps_ref[pair]
    block = pl.multiple_of(step // 8 * 8, 8)
    copies = [
        (x_hbm.at[pair], x_ref),
        (table_hbm.at[pl.ds(block, 8), :], table_ref),
        (seg_hbm, ids_ref),
    ]
    vectors = (g1, b1, g2, b2, bo, bd)
    fetch(copies + [(v, line_ref.at[i]) for i, v in enumerate(vectors)], sems)
    for i in range(len(vectors)):
        lines_ref[i : i + 1, :] = line_ref[i]
    seg_ref[...] = ids_ref[pl.ds(pair, 1), :]
    stream = x_ref[...] + table_ref[pl.ds(step % 8, 1), :]
    hat, _ = norm_parts(stream)
    stream_ref[...] = stream
    normed_ref[...] = (hat * line_ref[0] + line_ref[1]).astype(BF16)


def project_kernel(spot_ref, normed_ref, one_ref, two_ref, bias_ref, q_ref, kv_ref, *, row):
    cols = q_ref.shape[1]
    size = normed_ref.shape[1] // 2
    one, two = halves(spot_ref, size)
    raw = dot_nn(normed_ref[:, one], one_ref[:size, : 3 * cols])
    raw = raw + dot_nn(normed_ref[:, two], two_ref[:size, : 3 * cols])
    line, _ = bias_lines(bias_ref, row)
    q_bias, v_bias = line[:, :cols], line[:, cols : 2 * cols]
    q_ref[...] = (raw[:, :cols] + q_bias).astype(BF16)
    kv_ref[:, :cols] = raw[:, cols : 2 * cols].astype(BF16)
    kv_ref[:, cols:] = (raw[:, 2 * cols :] + v_bias).astype(BF16)


def mask_biases(spot_ref, seg_ref, span):
    chunk = spot_ref[1]
    ids = [seg_ref[:, window(chunk ^ step, span)] for step in range(seg_ref.shape[1] // span)]
    own = jnp.broadcast_to(ids[0], (span, span)).T
    return [
        jnp.where(own == jnp.broadcast_to(step_ids, (span, span)), 0.0, NEGATIVE)
        for step_ids in ids
    ]


def lane_mask(shape, head):
    return (lax.broadcasted_iota(jnp.int32, shape, 1) // HEAD_DIM) == head


def attend_forward(spot_ref, seg_ref, q_ref, kvs, mixed_ref, lse_ref):
    span, width = q_ref.shape
    biases = mask_biases(spot_ref, seg_ref, span)
    query = q_ref[...]
    mixed, lse = None, None
    for head in range(width // HEAD_DIM):
        mine = lane_mask((span, width), head)
        masked = jnp.where(mine, query, jnp.zeros_like(query))
        scores = [dot_nt(masked, kv[:, :width]) * SCALE + bias for kv, bias in zip(kvs, biases)]
        top = functools.reduce(
            jnp.maximum, [jnp.max(block, axis=-1, keepdims=True) for block in scores]
        )
        grown = [jnp.exp(block - top) for block in scores]
        mass = total([jnp.sum(block, axis=-1, keepdims=True) for block in grown])
        share = 1.0 / mass
        out = total(
            [dot_nn((block * share).astype(BF16), kv[:, width:]) for block, kv in zip(grown, kvs)]
        )
        log_mass = jnp.broadcast_to(top + jnp.log(mass), (span, width))
        mixed = out if head == 0 else jnp.where(mine, out, mixed)
        lse = log_mass if head == 0 else jnp.where(mine, log_mass, lse)
    mixed_ref[...] = mixed.astype(BF16)
    lse_ref[...] = lse


def attend_one_kernel(spot_ref, seg_ref, q_ref, kv0, kv1, kv2, kv3, mixed_ref, lse_ref):
    attend_forward(spot_ref, seg_ref, q_ref, (kv0, kv1, kv2, kv3), mixed_ref, lse_ref)


def attend_two_kernel(
    spot_ref, seg_ref, q_ref, kv0, kv1, kv2, kv3, near_ref, one_n, two_n, one_f, two_f,
    mixed_ref, lse_ref, terms_ref, given_ref,
):
    attend_forward(spot_ref, seg_ref, q_ref, (kv0, kv1, kv2, kv3), mixed_ref, lse_ref)
    size, cols = terms_ref.shape[1] // 2, q_ref.shape[1]
    one, two = halves(spot_ref, size)
    near, far = near_ref[...], mixed_ref[...]
    for columns, near_w, far_w in ((one, one_n, one_f), (two, two_n, two_f)):
        terms = dot_nt(near, near_w[:size, 3 * cols :]) + dot_nt(far, far_w[:size, 3 * cols :])
        terms_ref[:, columns] = terms
        given_ref[:, columns] = terms.astype(BF16)


def gelu_parts(x):
    square = x * x
    curve = jnp.tanh(ROOT * (x + CUBE * (x * square)))
    half = 0.5 * (1.0 + curve)
    slope = half + 0.5 * x * (1.0 - curve * curve) * (ROOT * (1.0 + 3.0 * CUBE * square))
    return x * half, slope


def ffn_kernel(
    spot_ref, stream_ref, terms_ref, got_ref, cotan_ref, lines_ref, near_pack, far_pack,
    one_n, two_n, *refs, row,
):
    count = len(refs) - 14
    pieces, refs = refs[:count], refs[count:]
    if count == 2:
        (one_f, two_f), refs = pieces, refs[:-2]
    else:
        (one_f, two_f), refs = refs[-2:], refs[:-2]
        rows = pieces[0].shape[0]
        for target, mine, other in ((one_f, 0, 1), (two_f, 2, 3)):
            target[window(spot_ref[1] % 2, rows), :] = pieces[mine][...]
            target[window(1 - spot_ref[1] % 2, rows), :] = pieces[other][...]
    ffn_body(
        spot_ref, stream_ref, terms_ref, got_ref, cotan_ref, lines_ref, near_pack, far_pack,
        one_n, two_n, one_f, two_f, *refs, row=row,
    )


def ffn_body(
    spot_ref, stream_ref, terms_ref, got_ref, cotan_ref, lines_ref, near_pack, far_pack,
    one_n, two_n, one_f, two_f,
    back_given, back_kept, ffn_given, out_kept, resid_ref, normed_ref, act_ref, pre_ref, low_ref,
    sum_ref, back_all, resid_all, *, row,
):
    span, width = stream_ref.shape
    hidden = one_n.shape[1] // 2
    half = span // 2
    bit = spot_ref[2] % 2
    one, two = halves(spot_ref, width // 2)
    resid = stream_ref[...] + (terms_ref[...] + got_ref[...].astype(F32)) + lines_ref[4:5, :]
    resid_all[...] = resid
    hat, _ = norm_parts(resid)
    normed_ref[...] = (hat * lines_ref[2:3, :] + lines_ref[3:4, :]).astype(BF16)
    low_ref[...] = cotan_ref[...].astype(BF16)
    biases = [bias_lines(pack, row)[1] for pack in (near_pack, far_pack)]
    back_one = back_two = ffn_one = ffn_two = None
    for side, (first, second) in enumerate(((one_n, two_n), (one_f, two_f))):
        bias = biases[side]
        at = slice(side * hidden, (side + 1) * hidden)
        pre = dot_nn(normed_ref[:, one], first[:, :hidden])
        pre = pre + dot_nn(normed_ref[:, two], second[:, :hidden]) + bias
        value, slope = gelu_parts(pre)
        grad = dot_nn(low_ref[:, one], first[:, hidden:])
        grad = (grad + dot_nn(low_ref[:, two], second[:, hidden:])) * slope
        sum_ref[:, at] = column_sum(grad)
        act_ref[:, at] = value.astype(BF16)
        pre_ref[:, at] = grad.astype(BF16)
        act, pre_low = act_ref[:, at], pre_ref[:, at]
        terms = [
            dot_nt(pre_low, first[:, :hidden]),
            dot_nt(pre_low, second[:, :hidden]),
            dot_nt(act, first[:, hidden:]),
            dot_nt(act, second[:, hidden:]),
        ]
        if side == 0:
            back_one, back_two, ffn_one, ffn_two = terms
    back_all[:, one] = back_one + terms[0]
    back_all[:, two] = back_two + terms[1]
    given, kept = window(1 - bit, half), window(bit, half)
    back_given[...] = back_all[given, :].astype(BF16)
    back_kept[...] = back_all[kept, :]
    back_all[:, one] = ffn_one + terms[2]
    back_all[:, two] = ffn_two + terms[3]
    ffn_given[...] = back_all[given, :].astype(BF16)
    resid_ref[...] = resid_all[kept, :]
    out_kept[...] = resid_all[kept, :] + back_all[kept, :] + lines_ref[5:6, :]


def ffn_grads_kernel(spot_ref, normed_ref, low_ref, act_ref, pre_ref, kept_ref, given_ref):
    hidden = act_ref.shape[1] // 2
    one, two = halves(spot_ref, normed_ref.shape[1] // 2)
    for columns, out_ref in ((two, given_ref), (one, kept_ref)):
        normed, low = normed_ref[:, columns], low_ref[:, columns]
        for side in range(2):
            at = slice(side * hidden, (side + 1) * hidden)
            start = 2 * side * hidden
            up = dot_tn(normed, pre_ref[:, at])
            out_ref[:, start : start + hidden] = up.astype(out_ref.dtype)
            down = dot_tn(low, act_ref[:, at])
            out_ref[:, start + hidden : start + 2 * hidden] = down.astype(out_ref.dtype)


def resid_kernel(
    spot_ref, kept_ref, got_ref, resid_ref, cotan_ref, lines_ref, grad_ref, low_ref, rows_ref
):
    half = kept_ref.shape[0]
    bit = spot_ref[2] % 2
    grad = kept_ref[...] + got_ref[...].astype(F32)
    hat, inverse = norm_parts(resid_ref[...])
    cotan = cotan_ref[window(bit, half), :]
    resid_grad = cotan + norm_back(grad, hat, inverse, lines_ref[2:3, :])
    grad_ref[...] = resid_grad
    low_ref[...] = resid_grad.astype(BF16)
    sums = [grad * hat, grad, resid_grad, cotan]
    rows_ref[...] = jnp.concatenate([column_sum(v) for v in sums], axis=0)


def attend_backward(spot_ref, seg_ref, q_ref, grad, lse_ref, kvs, dq_ref, outs, side):
    span, width = q_ref.shape
    biases = mask_biases(spot_ref, seg_ref, span)
    query = q_ref[...]
    dq, dks, dvs = None, [None] * 4, [None] * 4
    for head in range(width // HEAD_DIM):
        mine = lane_mask((span, width), head)
        masked_q = jnp.where(mine, query, jnp.zeros_like(query))
        masked_g = jnp.where(mine, grad, jnp.zeros_like(grad))
        lse = lse_ref[:, head * HEAD_DIM : head * HEAD_DIM + 1]
        probs = [
            jnp.exp(dot_nt(masked_q, kv[:, :width]) * SCALE + bias - lse)
            for kv, bias in zip(kvs, biases)
        ]
        grads = [dot_nt(masked_g, kv[:, width:]) for kv in kvs]
        inner = total([jnp.sum(p * g, axis=-1, keepdims=True) for p, g in zip(probs, grads)])
        raws = [(p * (g - inner) * SCALE).astype(BF16) for p, g in zip(probs, grads)]
        head_dq = total([dot_nn(raw, kv[:, :width]) for raw, kv in zip(raws, kvs)])
        dq = head_dq if head == 0 else jnp.where(mine, head_dq, dq)
        for step in range(4):
            head_dk = dot_tn(raws[step], query)
            head_dv = dot_tn(probs[step].astype(BF16), grad)
            dks[step] = head_dk if head == 0 else jnp.where(mine, head_dk, dks[step])
            dvs[step] = head_dv if head == 0 else jnp.where(mine, head_dv, dvs[step])
    dq_ref[:, side * width : (side + 1) * width] = dq
    at = 2 * side * width
    for step in range(4):
        outs[step][:, at : at + width] = dks[step].astype(outs[step].dtype)
        outs[step][:, at + width : at + 2 * width] = dvs[step].astype(outs[step].dtype)


def pull_kernel(
    spot_ref, seg_ref, q_n, lse_n, n0, n1, n2, n3, q_f, lse_f, f0, f1, f2, f3, mine_ref, got_ref,
    one_n, two_n, one_f, two_f,
    dq_ref, own_ref, out1, out2, out3, low_ref,
):
    half, cols = mine_ref.shape[0], q_n.shape[1]
    size = low_ref.shape[1] // 2
    bit = spot_ref[2] % 2
    low_ref[window(bit, half), :] = mine_ref[...]
    low_ref[window(1 - bit, half), :] = got_ref[...]
    one, two = halves(spot_ref, size)
    outs = (own_ref, out1, out2, out3)
    sides = ((q_n, lse_n, (n0, n1, n2, n3), one_n, two_n), (q_f, lse_f, (f0, f1, f2, f3), one_f, two_f))
    for side, (q_ref, lse_ref, kvs, first, second) in enumerate(sides):
        grad = dot_nn(low_ref[:, one], first[:size, 3 * cols :])
        grad = grad + dot_nn(low_ref[:, two], second[:size, 3 * cols :])
        attend_backward(
            spot_ref, seg_ref, q_ref, grad.astype(BF16), lse_ref, kvs, dq_ref, outs, side
        )


def input_kernel(
    spot_ref, stream_ref, lines_ref, resid_ref, rows_ref, up_sum_ref, dq_ref, own_ref, g1, g2, g3,
    one_n, two_n, one_f, two_f, normed_ref, low_ref, near_ref, far_ref,
    kept_ref, given_ref, small_ref, w_kept_ref, w_given_ref, pulled_ref, terms_ref,
):
    span, width = stream_ref.shape
    cols = dq_ref.shape[1] // 2
    hidden = up_sum_ref.shape[1] // 2
    half, size = span // 2, width // 2
    shard, slot = spot_ref[2], spot_ref[3]
    bit, far = shard % 2, shard ^ 2
    one, two = halves(spot_ref, size)
    small_ref[...] = jnp.zeros_like(small_ref)
    got = (own_ref[...] + g1[...].astype(F32)) + (g2[...].astype(F32) + g3[...].astype(F32))
    for side, place in enumerate((shard, far)):
        dq = dq_ref[:, side * cols : (side + 1) * cols]
        dkv = got[:, 2 * side * cols : 2 * (side + 1) * cols]
        at = side * 3 * cols
        pulled_ref[:, at : at + cols] = dq.astype(BF16)
        pulled_ref[:, at + cols : at + 3 * cols] = dkv.astype(BF16)
        small_ref[6:7, window(place, cols)] = column_sum(dq)
        small_ref[7:8, window(place, cols)] = column_sum(dkv[:, cols:])
        small_ref[pl.ds(8 + place, 1), :] = up_sum_ref[:, side * hidden : (side + 1) * hidden]
    for columns, near_w, far_w in ((one, one_n, one_f), (two, two_n, two_f)):
        back = dot_nt(pulled_ref[:, : 3 * cols], near_w[:size, : 3 * cols])
        back = back + dot_nt(pulled_ref[:, 3 * cols :], far_w[:size, : 3 * cols])
        terms_ref[:, columns] = back
    back = terms_ref[...]
    hat, inverse = norm_parts(stream_ref[...])
    small_ref[0:1, :] = column_sum(back * hat)
    small_ref[1:2, :] = column_sum(back)
    small_ref[2:6, :] = rows_ref[...]
    grad = norm_back(back, hat, inverse, lines_ref[0:1, :])
    small_ref[pl.ds(12 + slot, 1), :] = column_sum(grad) + rows_ref[2:3, :]
    terms_ref[...] = grad
    given_ref[...] = terms_ref[window(1 - bit, half), :].astype(BF16)
    kept_ref[...] = resid_ref[...] + terms_ref[window(bit, half), :]
    for columns, out_ref in ((two, w_given_ref), (one, w_kept_ref)):
        normed, low = normed_ref[:, columns], low_ref[:, columns]
        for side, mixed in enumerate((near_ref, far_ref)):
            at, start = side * 3 * cols, side * 4 * cols
            qkv = dot_tn(normed, pulled_ref[:, at : at + 3 * cols])
            out_ref[:, start : start + 3 * cols] = qkv.astype(out_ref.dtype)
            out = dot_tn(low, mixed[...])
            out_ref[:, start + 3 * cols : start + 4 * cols] = out.astype(out_ref.dtype)


def turn_bits(spot_ref):
    return 1 + spot_ref[0], 2 - spot_ref[0]


def split_two(values):
    high = values.astype(BF16)
    return high, (values - high.astype(F32)).astype(BF16)


def both(high, low):
    return high.astype(F32) + low.astype(F32)


def cut_kernel(spot_ref, kept_ref, got_ref, *refs):
    small_ref = refs[0] if len(refs) == 3 else None
    own_ref, send_ref = refs[-2:]
    rows = own_ref.shape[0] // 2
    chunk = spot_ref[1]
    first, second = turn_bits(spot_ref)
    for spot, place in enumerate((chunk, chunk ^ second)):
        at, to = window(place, rows), slice(spot * rows, (spot + 1) * rows)
        own_ref[to, :] = kept_ref[at, :] + got_ref[at, :].astype(F32)
        at = window(place ^ first, rows)
        send_ref[to, :] = (kept_ref[at, :] + got_ref[at, :].astype(F32)).astype(BF16)
    if small_ref is not None:
        width = small_ref.shape[1]
        send_ref[2 * rows :, :width], send_ref[2 * rows :, width:] = split_two(small_ref[...])


def middle_kernel(spot_ref, kept_ref, sent_ref, got_ref, own_ref, send_ref):
    rows = own_ref.shape[0]
    own_ref[...] = kept_ref[:rows, :] + got_ref[:rows, :].astype(F32)
    more = kept_ref[rows:, :] + got_ref[rows : 2 * rows, :].astype(F32)
    send_ref[:rows, :] = more.astype(BF16)
    if send_ref.shape[0] > rows:
        width = own_ref.shape[1] // 2
        mine, far = sent_ref[2 * rows :, :], got_ref[2 * rows :, :]
        small = both(mine[:, :width], mine[:, width:]) + both(far[:, :width], far[:, width:])
        send_ref[rows:, :width], send_ref[rows:, width:] = split_two(small)


def shards_kernel(spot_ref, own_ref, sent_ref, got_ref, kept_ref, send_ref):
    rows, width = kept_ref.shape
    values = own_ref[...] + got_ref[:rows, :].astype(F32)
    kept_ref[...] = values[:, :width]
    send_ref[:rows, :] = values[:, width:].astype(BF16)
    count = got_ref.shape[0] - rows
    if count:
        mine, far = sent_ref[rows:, :], got_ref[rows:, :]
        small = both(mine[:, :width], mine[:, width:]) + both(far[:, :width], far[:, width:])
        send_ref[rows : rows + count, :], send_ref[rows + count :, :] = split_two(small)


def owned_kernel(spot_ref, kept_ref, sent_ref, got_ref, out_ref, *small):
    rows = out_ref.shape[0]
    out_ref[...] = (kept_ref[...] + got_ref[:rows, :].astype(F32)).astype(BF16)
    if small:
        count = small[0].shape[0]
        top, end = slice(rows, rows + count), slice(rows + count, rows + 2 * count)
        mine = both(sent_ref[top, :], sent_ref[end, :])
        small[0][...] = mine + both(got_ref[top, :], got_ref[end, :])


def stack_kernel(spot_ref, one_ref, two_ref, out_ref):
    rows = one_ref.shape[0]
    out_ref[:rows, :] = one_ref[...]
    out_ref[rows:, :] = two_ref[...]


def places(spot_ref, rows):
    first, second = turn_bits(spot_ref)
    chunk = spot_ref[1]
    return [window(chunk ^ bits, rows) for bits in (0, second, first, 3)]


def own_ffn_kernel(spot_ref, p0, p1, p2, up_ref, down_ref):
    rows, hidden = p0.shape[0], up_ref.shape[1]
    pieces = (p0[...], p1[...], p2[:rows, :], p2[rows:, :])
    for at, piece in zip(places(spot_ref, rows), pieces):
        up_ref[at, :] = piece[:, :hidden].astype(F32)
        down_ref[at, :] = piece[:, hidden:].astype(F32)


def own_attention_kernel(spot_ref, p0, p1, p2, qkv_ref, out_ref):
    rows, cols = p0.shape[0], out_ref.shape[1]
    pieces = (p0[...], p1[...], p2[:rows, :], p2[rows:, :])
    for at, piece in zip(places(spot_ref, rows), pieces):
        for i in range(3):
            qkv_ref[i, at, :] = piece[:, i * cols : (i + 1) * cols].astype(F32)
        out_ref[at, :] = piece[:, 3 * cols :].astype(F32)


def add_low_kernel(spot_ref, kept_ref, got_ref, out_ref):
    out_ref[...] = (kept_ref[...] + got_ref[...].astype(F32)).astype(BF16)


def add_kernel(spot_ref, own_ref, got_ref, out_ref):
    out_ref[...] = own_ref[...] + got_ref[...]


def sums_kernel(spot_ref, steps_ref, own_ref, got_ref, table_ref, rows_ref, up_ref, qv_ref):
    cols = qv_ref.shape[1]
    shard = spot_ref[2]
    rows_ref[...] = own_ref[...] + got_ref[...]
    table_ref[...] = jnp.zeros_like(table_ref)
    for place in range(steps_ref.shape[0]):
        at = pl.ds(steps_ref[place], 1)
        table_ref[at, :] = table_ref[at, :] + rows_ref[12 + place : 13 + place, :]
    up_ref[...] = rows_ref[pl.ds(8 + shard, 1), :]
    qv_ref[...] = rows_ref[6:8, window(shard, cols)]


class Reduction:
    def __init__(self, order, kept, small=None):
        self.order, self.small = order, small
        self.rows, self.width = kept.shape[0] // 4, kept.shape[1]
        self.more = 0 if small is None else small.shape[0]
        self.kept = kept

    def cut(self, got):
        rows, width = self.rows, self.width
        extra = [] if self.small is None else [self.small]
        self.own, self.sent = self.order.call(
            cut_kernel,
            [((2 * rows, width), F32), ((2 * rows + self.more, width), BF16)],
            [self.kept, got, *extra],
        )
        self.got = self.order.swap_turn(self.sent, 0)

    def middle(self):
        rows, width = self.rows, self.width
        self.own, self.sent = self.order.call(
            middle_kernel,
            [((rows, width), F32), ((rows + self.more, width), BF16)],
            [self.own, self.sent, self.got],
        )
        self.got = self.order.swap_turn(self.sent, 1)

    def shards(self):
        rows, width = self.rows, self.width // 2
        self.own, self.sent = self.order.call(
            shards_kernel,
            [((rows, width), F32), ((rows + 2 * self.more, width), BF16)],
            [self.own, self.sent, self.got],
        )
        self.got = self.order.swap(self.sent, "tp", 2)

    def owned(self):
        rows, width = self.rows, self.width // 2
        extra = [] if self.small is None else [(self.small.shape, F32)]
        self.own, *small = self.order.call(
            owned_kernel,
            [((rows, width), BF16)] + extra,
            [self.own, self.sent, self.got],
        )
        self.small = small[0] if small else None
        self.got = self.order.swap_turn(self.own, 1)

    def stack(self):
        both_rows = self.order.call(
            stack_kernel, [((2 * self.rows, self.width // 2), BF16)], [self.own, self.got]
        )[0]
        self.last = self.order.swap_turn(both_rows, 0)

    def finish(self, kernel, shapes):
        return self.order.call(
            kernel, [(shape, F32) for shape in shapes], [self.own, self.got, self.last]
        )


def reduce_plainly(kept, given, chunk):
    whole = jnp.concatenate([kept, given.astype(F32)])
    mine = lax.psum_scatter(whole, "fsdp", scatter_dimension=0, tiled=True)
    quarter = lax.psum_scatter(mine, "ctx", scatter_dimension=0, tiled=True)
    width = quarter.shape[1] // 2
    far = lax.ppermute(quarter[:, width:], "tp", [(i, i ^ 2) for i in range(4)])
    return lax.all_gather(quarter[:, :width] + far, "ctx", axis=0, tiled=True)


def pieces_of(order, part, parts, rows):
    if parts == 2:
        return part, order.swap(part, "fsdp", 1)
    whole = lax.all_gather(part[:rows], "fsdp", axis=0, tiled=True)
    size = whole.shape[0] // 2
    return whole[:size], whole[size:]


def per_device(
    layer_input,
    timesteps,
    segment_ids,
    time_table,
    ln1_gain,
    ln1_bias,
    w_qkv,
    b_qv,
    w_out_t,
    b_out,
    ln2_gain,
    ln2_bias,
    w_up,
    b_up,
    w_down_t,
    b_down,
    out_grad,
    *,
    parts,
):
    span, width = layer_input.shape[1:]
    rows, cols = w_qkv.shape[1:]
    hidden = w_up.shape[1]
    half, size = span // 2, width // 2
    core = lax.axis_index("fsdp")
    chunk = lax.axis_index("ctx")
    shard = lax.axis_index("tp")
    place = core if parts == 2 else 0 * core
    spot = jnp.stack([place, chunk, shard, 2 * core + shard // 2]).astype(jnp.int32)
    order = Order(spot)
    line = lambda values: values.reshape(1, -1)
    dma = lambda count: pltpu.SemaphoreType.DMA((count,))

    pack = order.call(
        pack_first_kernel,
        [((rows + BIAS_ROWS, 4 * cols), BF16)],
        [timesteps, w_qkv, w_out_t, b_qv, line(b_up)],
        far=(1, 2, 3, 4),
        scratch=[
            pltpu.VMEM(w_qkv.shape, F32),
            pltpu.VMEM(w_out_t.shape, F32),
            pltpu.VMEM(b_qv.shape, F32),
            pltpu.VMEM((1, hidden), F32),
            dma(4),
        ],
    )[0]
    near = pieces_of(order, pack, parts, rows)
    pack_far = order.swap(pack, "tp", 2)
    stream, normed, seg, lines = order.call(
        stream_kernel,
        [
            ((span, width), F32), ((span, width), BF16), ((1, segment_ids.shape[1]), jnp.int32),
            ((8, width), F32),
        ],
        [timesteps, layer_input, time_table, segment_ids]
        + [line(v) for v in (ln1_gain, ln1_bias, ln2_gain, ln2_bias, b_out, b_down)],
        far=range(1, 10),
        scratch=[
            pltpu.VMEM((span, width), F32),
            pltpu.VMEM((8, width), F32),
            pltpu.VMEM(segment_ids.shape, jnp.int32),
            pltpu.VMEM((6, 1, width), F32),
            dma(9),
        ],
    )
    projected = [((span, cols), BF16), ((span, 2 * cols), BF16)]
    project = functools.partial(project_kernel, row=rows)
    q_near, kv_near = order.call(project, projected, [normed, *near, pack])
    kvs_near = [kv_near] + order.swap_three(kv_near, "ctx")

    rest, rest_half, cotan = order.call(
        pack_rest_kernel,
        [((rows, 2 * hidden), BF16), ((rows // 2, 2 * hidden), BF16), ((span, width), F32)],
        [w_up, w_down_t, out_grad],
        far=(0, 1, 2),
        scratch=[pltpu.VMEM(w_up.shape, F32), pltpu.VMEM(w_down_t.shape, F32), dma(3)],
    )
    rest_near = pieces_of(order, rest, parts, rows)
    rest_far = order.swap(rest_half if parts == 2 else rest, "tp", 2)

    pack_far, *kvs_near[1:] = hold(pack_far, *kvs_near[1:])
    far = pieces_of(order, pack_far, parts, rows)
    q_far, kv_far = order.call(project, projected, [normed, *far, pack_far])
    kvs_far = [kv_far] + order.swap_three(kv_far, "ctx")
    attended = [((span, cols), BF16), ((span, cols), F32)]
    mixed_near, lse_near = order.call(attend_one_kernel, attended, [seg, q_near, *kvs_near])
    if parts == 2:
        rest_more = order.swap(rest_far, "ctx", 1)
        rest_far = [rest_far, rest_more, order.swap(rest_far, "fsdp", 1)]
    else:
        rest_far = pieces_of(order, rest_far, parts, rows)
    mixed_far, lse_far, terms, given = order.call(
        attend_two_kernel,
        attended + [((span, width), F32), ((span, width), BF16)],
        [seg, q_far, *kvs_far, mixed_near, *near, *far],
    )
    got = order.swap(given, "tp", 1)
    if parts == 2:
        rest_far.append(order.swap(rest_more, "fsdp", 1))

    (
        back_given, back_kept, ffn_given, out_kept, resid, normed_two, act, pre, low, up_sum,
    ) = order.call(
        functools.partial(ffn_kernel, row=rows),
        [
            ((half, width), BF16), ((half, width), F32), ((half, width), BF16),
            ((half, width), F32), ((half, width), F32), ((span, width), BF16),
            ((span, 2 * hidden), BF16), ((span, 2 * hidden), BF16), ((span, width), BF16),
            ((1, 2 * hidden), F32),
        ],
        [stream, terms, got, cotan, lines, pack, pack_far, *rest_near, *rest_far],
        scratch=[pltpu.VMEM((span, width), F32)] * 2
        + [pltpu.VMEM((size, 2 * hidden), BF16)] * 2,
        limit=24,
    )
    back_got = order.swap(back_given, "tp", 1)
    ffn_kept, ffn_sent = order.call(
        ffn_grads_kernel,
        [((size, 4 * hidden), F32), ((size, 4 * hidden), BF16)],
        [normed_two, low, act, pre],
    )
    if parts == 2:
        ffn_far = order.swap(ffn_sent, "fsdp", 1)
    resid_grad, resid_low, resid_rows = order.call(
        resid_kernel,
        [((half, width), F32), ((half, width), BF16), ((4, width), F32)],
        [back_kept, back_got, resid, cotan, lines],
    )
    resid_got = order.swap(resid_low, "tp", 1)
    if parts == 2:
        ffn_sum = Reduction(order, ffn_kept)
        ffn_sum.cut(ffn_far)
    dq, own, *shares, low_all = order.call(
        pull_kernel,
        [((span, 2 * cols), F32), ((span, 4 * cols), F32)]
        + [((span, 4 * cols), BF16)] * 3
        + [((span, width), BF16)],
        [
            seg, q_near, lse_near, *kvs_near, q_far, lse_far, *kvs_far, resid_low, resid_got,
            *near, *far,
        ],
    )
    shared = [order.swap(piece, "ctx", bits + 1) for bits, piece in enumerate(shares)]

    ffn_got = order.swap(ffn_given, "tp", 1)
    if parts == 2:
        ffn_sum.middle()
    out_half = order.call(add_low_kernel, [((half, width), BF16)], [out_kept, ffn_got])[0]
    out_halves = [out_half] + order.swap_three(out_half, "tp")

    seqs = 2 * parts
    small_rows = -(-(12 + seqs) // 16) * 16
    in_kept, in_given, small, attention_kept, attention_sent = order.call(
        input_kernel,
        [
            ((half, width), F32), ((half, width), BF16), ((small_rows, width), F32),
            ((size, 8 * cols), F32), ((size, 8 * cols), BF16),
        ],
        [
            stream, lines, resid_grad, resid_rows, up_sum, dq, own, *shared, *near, *far,
            normed, low_all, mixed_near, mixed_far,
        ],
        scratch=[pltpu.VMEM((span, 6 * cols), BF16), pltpu.VMEM((span, width), F32)],
    )
    if parts == 2:
        attention_far = order.swap(attention_sent, "fsdp", 1)
    in_got = order.swap(in_given, "tp", 1)
    if parts == 2:
        attention_sum = Reduction(order, attention_kept, small)
        ffn_sum.shards()
        attention_sum.cut(attention_far)
    in_half = order.call(add_low_kernel, [((half, width), BF16)], [in_kept, in_got])[0]
    in_halves = [in_half] + order.swap_three(in_half, "tp")
    if parts == 2:
        ffn_sum.owned()
        attention_sum.middle()
        output = join(order, 2, out_halves, F32)
        ffn_sum.stack()
        attention_sum.shards()
        grads_up, grads_down = ffn_sum.finish(own_ffn_kernel, [(rows, hidden)] * 2)
        attention_sum.owned()
        small = attention_sum.small
        small_got = order.swap(small, "tp", 1)
        attention_sum.stack()
        small = order.call(add_kernel, [(small.shape, F32)], [small, small_got])[0]
        small_got = order.swap(small, "fsdp", 1)
        grad_input = join(order, 2, in_halves, F32)
        bits = near[1][rows : rows + 6 : 2, 2 * cols : 2 * cols + 2].astype(F32)
        far_steps = jnp.sum(bits, axis=0).astype(jnp.int32)
        steps = jnp.where(
            core == 0,
            jnp.concatenate([timesteps, far_steps]),
            jnp.concatenate([far_steps, timesteps]),
        )
    else:
        output = join(order, 2, out_halves, F32)
        grad_input = join(order, 2, in_halves, F32)
        both_grads = reduce_plainly(ffn_kept, ffn_sent, chunk)
        grads_up, grads_down = both_grads[:, :hidden], both_grads[:, hidden:]
        small = lax.psum(small, ("fsdp", "ctx", "tp"))
        small_got = jnp.zeros_like(small)
        steps = lax.all_gather(timesteps, "fsdp", axis=0, tiled=True)
    table, sums, up_line, qv_lines = order.call(
        sums_kernel,
        [(time_table.shape, F32), (small.shape, F32), ((1, hidden), F32), ((2, cols), F32)],
        [steps, small, small_got],
    )
    if parts == 2:
        grads_qkv, grads_out = attention_sum.finish(
            own_attention_kernel, [(3, rows, cols), (rows, cols)]
        )
    else:
        every = reduce_plainly(attention_kept, attention_sent, chunk)
        grads_qkv = jnp.stack([every[:, i * cols : (i + 1) * cols] for i in range(3)])
        grads_out = every[:, 3 * cols :]

    shape = layer_input.shape
    return (
        output.reshape(shape),
        grad_input.reshape(shape),
        table,
        sums[0],
        sums[1],
        grads_qkv,
        qv_lines,
        grads_out,
        sums[4],
        sums[2],
        sums[3],
        grads_up,
        up_line.reshape(-1),
        grads_down,
        sums[5],
    )


def solution(mesh):
    placed = (
        P("fsdp", "ctx", None),
        P("fsdp"),
        P("fsdp", None),
        P(),
        P(),
        P(),
        P(None, "fsdp", "tp"),
        P(None, "tp"),
        P("fsdp", "tp"),
        P(),
        P(),
        P(),
        P("fsdp", "tp"),
        P("tp"),
        P("fsdp", "tp"),
        P(),
        P("fsdp", "ctx", None),
    )
    return jax.shard_map(
        functools.partial(per_device, parts=mesh.shape["fsdp"]),
        mesh=mesh,
        in_specs=placed,
        out_specs=(
            P("fsdp", "ctx", None),
            P("fsdp", "ctx", None),
            P(),
            P(),
            P(),
            P(None, "fsdp", "tp"),
            P(None, "tp"),
            P("fsdp", "tp"),
            P(),
            P(),
            P(),
            P("fsdp", "tp"),
            P("tp"),
            P("fsdp", "tp"),
            P(),
        ),
        check_vma=False,
    )
```

time: 528 us -> 142 us (0.27)
  waiting for transfers between devices: 329 us -> 54.7 us
  matrix products: 64.3 us -> 0 us
  blocking collectives: 59.8 us -> 0 us
  Pallas kernels: 0 us -> 39.6 us
  starting transfers between devices: 0.89 us -> 36 us
  other arithmetic: 25.2 us -> 0.69 us
  local copies, waits for them, and re-layouts: 33 us -> 8.89 us
  between operations: 14.6 us -> 1.21 us
    psum x6 -> x0, waiting for transfers between devices: 276 us -> none  [the longest x1 61.3 us: per_device(): table_sum = lax.psum(table_terms, ('fsdp', 'ctx'))]
    dot_general x20 -> x0, matrix products: 64.3 us -> none  [the longest x1 12.8 us: per_device(): jnp.einsum('shqk,sqhd->skhd', grad_raw, query_heads, preferred_element_ty...]
    ppermute x0 -> x42, waiting for transfers between devices: none -> 54.7 us  [the longest x34 49 us: swap(): return lax.ppermute(values, axis, [(i, i ^ bits) for i in range(size)])]
    reduce_scatter x6 -> x0, waiting for transfers between devices: 52.7 us -> none  [the longest x1 14.4 us: per_device(): lax.psum_scatter(grad_key_all, 'ctx', scatter_dimension=1, tiled=True)]
    pallas_call x0 -> x30, Pallas kernels: none -> 39.6 us  [call(): pl.pallas_call(kernel, out_shape=tuple((jax.ShapeDtypeStruct(shape, dtype...]
    ppermute x0 -> x42, starting transfers between devices: none -> 36 us  [the longest x34 28.4 us: swap(): return lax.ppermute(values, axis, [(i, i ^ bits) for i in range(size)])]
    all_gather x6 -> x0, blocking collectives: 32.2 us -> none  [the longest x1 13.5 us: per_device(): lax.all_gather(key_local, 'ctx', axis=1, tiled=True)]
    psum x1 -> x0, blocking collectives: 27.6 us -> none  [per_device(): lax.psum((grad_gain_one, grad_bias_one, grad_gain_two, grad_bias_two, qv_...]
  transfers between devices with their start and end apart: 12 -> 42, of which waited for: 11 -> 20; matrix products, arithmetic and copies ran while one was open for 14% -> 1% of each run, Pallas kernels for 0% -> 24%
where the time goes in v2:
time: 142 us; the launch traced here: 141 us
  waiting for transfers between devices  54.7 us (39%)
  Pallas kernels  39.6 us (28%)
  starting transfers between devices  36 us (25%)
  local copies, waits for them, and re-layouts  8.89 us (6%)
    ppermute x34, waiting for transfers between devices, swap(): return lax.ppermute(values, axis, [(i, i ^ bits) for i in range(size)])  49 us
    pallas_call x30, Pallas kernels, call(): pl.pallas_call(kernel, out_shape=tuple((jax.ShapeDtypeStruct(shape, dtype...  39.6 us
    ppermute x34, starting transfers between devices, swap(): return lax.ppermute(values, axis, [(i, i ^ bits) for i in range(size)])  28.4 us
    unnamed x80, local copies, waits for them, and re-layouts  8.26 us
    ppermute x8, starting transfers between devices, swap_turn(): return lax.ppermute(values, ('fsdp', 'ctx'), pairs)  7.55 us
    ppermute x8, waiting for transfers between devices, swap_turn(): return lax.ppermute(values, ('fsdp', 'ctx'), pairs)  5.77 us
  transfers between devices with their start and end apart: 42, of which 20 were waited for; matrix products, arithmetic and copies ran while one was open for 1% of the time, Pallas kernels for 24%

profile of v2, /device:TPU:0, one launch (start us, length us, event | category | flops | bytes accessed | tf_op | source)
XLA Modules:
  0.0 141.1 jit_solution(304702475785602396)
XLA Ops:
  0.7 0.7 copy-done
  1.4 1.6 %shard_map.280.one_ref.bias_ref.one_n.near_pack = bf16[272,512]{1,0:T(8,128)(2,1)S(1)} custom-call(s32[4]{0:T(128)S(1)} %pad_add_fusion.spot_ref, s32[2]{0:T(128)S(1)} %copy-done, f32[3,256,128]{2,1,0:T(8,128)} %w_hbm.1, f32[256,128]{1,0:T(8,128)} %out_hbm.1, f32[2,128]{1,0:T(2,128)} %qv_hbm.1, f32[1,512]{1,0:T(1,128)} %bitcast.26), custom_call_target="tpu_custom_call" | custom-call | flops 20000000000 | bytes 65536 | tf_op jit(solution)/shard_map/pallas_call | solution.py:83
  3.1 4.1 %collective-permute-start.2 = (bf16[272,512]{1,0:T(8,128)(2,1)S(1)}, bf16[272,512]{1,0:T(8,128)(2,1)S(1)}, u32[]{:S(2)}, u32[]{:S(2)}) collective-permute-start(bf16[272,512]{1,0:T(8,128)(2,1)S(1)} %shard_map.280.one_ref.bias_ref.one_n.near_pack), channel_id=1, source_target_pairs={{0,2},{1,3},{2,0},{3,1},{4,6},{5,7},{6,4},{7,5},{8,10},{9,11},{10,... | collective-permute-start | bytes 835592 | tf_op jit(solution)/shard_map/swap_tp_2/ppermute | solution.py:101
  7.2 1.9 %shard_map.281 = (f32[256,512]{1,0:T(8,128)S(1)}, bf16[256,512]{1,0:T(8,128)(2,1)S(1)}, s32[1,1024]{1,0:T(1,128)S(1)}, f32[8,512]{1,0:T(8,128)S(1)}) custom-call(s32[4]{0:T(128)S(1)} %pad_add_fusion.spot_ref, s32[2]{0:T(128)S(1)} %copy-done, f32[2,256,512]{2,1,0:T(8,128)} %x_hbm.1, f32[1000,512]{1,0:T(8,128)} %table_hbm.1, s32[2,1024]{1,0:T(2,128)} %seg_hbm.1, ...), custom_call_target="tpu_custom_call" | custom-call | flops 20000000000 | bytes 65536 | tf_op jit(solution)/shard_map/pallas_call | solution.py:83
  9.1 0.8 copy-done.18
  9.9 0.8 shard_map.282
  10.8 2.5 %collective-permute-start.5 = (bf16[256,256]{1,0:T(8,128)(2,1)S(1)}, bf16[256,256]{1,0:T(8,128)(2,1)S(1)}, u32[]{:S(2)}, u32[]{:S(2)}) collective-permute-start(bf16[256,256]{1,0:T(8,128)(2,1)S(1)} %get-tuple-element.234.kv0.n0), channel_id=1, source_target_pairs={{0,12},{4,8},{8,4},{12,0},{1,13},{5,9},{9,5},{13,1},{2,14},{6,10},... | collective-permute-start | bytes 393224 | tf_op jit(solution)/shard_map/swap_ctx_3/ppermute | solution.py:101
  14.3 2.0 %shard_map.283 = (bf16[256,1024]{1,0:T(8,128)(2,1)S(1)}, bf16[128,1024]{1,0:T(8,128)(2,1)S(1)}, f32[256,512]{1,0:T(8,128)S(1)}) custom-call(s32[4]{0:T(128)S(1)} %pad_add_fusion.spot_ref, f32[256,512]{1,0:T(8,128)} %up_hbm.1, f32[256,512]{1,0:T(8,128)} %down_hbm.1, f32[2,256,512]{2,1,0:T(8,128)} %cotan_hbm.1), custom_call_target="tpu_custom_call" | custom-call | flops 20000000000 | bytes 65536 | tf_op jit(solution)/shard_map/pallas_call | solution.py:83
  16.4 0.8 copy-done.20
  17.2 2.6 %collective-permute-done.2.one_ref.bias_ref.one_f.far_pack = bf16[272,512]{1,0:T(8,128)(2,1)S(1)} collective-permute-done((bf16[272,512]{1,0:T(8,128)(2,1)S(1)}, bf16[272,512]{1,0:T(8,128)(2,1)S(1)}, u32[]{:S(2)}, u32[]{:S(2)}) %collective-permute-start.2) | collective-permute-done | bytes 278560 | tf_op jit(solution)/shard_map/swap_tp_2/ppermute | solution.py:101
  19.8 0.7 collective-permute-done.4.kv2.n2
  21.1 1.0 collective-permute-done.6.two_ref.two_f
  22.1 0.8 shard_map.284
  23.0 1.9 %collective-permute-start.10 = (bf16[256,256]{1,0:T(8,128)(2,1)S(1)}, bf16[256,256]{1,0:T(8,128)(2,1)S(1)}, u32[]{:S(2)}, u32[]{:S(2)}) collective-permute-start(bf16[256,256]{1,0:T(8,128)(2,1)S(1)} %get-tuple-element.258.kv0.f0), channel_id=1, source_target_pairs={{0,12},{4,8},{8,4},{12,0},{1,13},{5,9},{9,5},{13,1},{2,14},{6,10},... | collective-permute-start | bytes 393224 | tf_op jit(solution)/shard_map/swap_ctx_3/ppermute | solution.py:101
  24.9 1.1 collective-permute-start.9
  26.6 1.9 %shard_map.285 = (bf16[256,128]{1,0:T(8,128)(2,1)S(1)}, f32[256,128]{1,0:T(8,128)S(1)}) custom-call(s32[4]{0:T(128)S(1)} %pad_add_fusion.spot_ref, s32[1,1024]{1,0:T(1,128)S(1)} %get-tuple-element.245.seg_ref, bf16[256,128]{1,0:T(8,128)(2,1)S(1)} %get-tuple-element.246.q_ref.q_n, bf16[256,256]{1,0:T(8,128)(2,1)S(1)} %get-tuple-element.234.kv0.n0, ...), custom_call_target="tpu_custom_call" | custom-call | flops 20000000000 | bytes 65536 | tf_op jit(solution)/shard_map/pallas_call | solution.py:83
  28.5 7.3 %collective-permute-done.1.refs_0_ = bf16[128,1024]{1,0:T(8,128)(2,1)S(1)} collective-permute-done((bf16[128,1024]{1,0:T(8,128)(2,1)S(1)}, bf16[128,1024]{1,0:T(8,128)(2,1)S(1)}, u32[]{:S(2)}, u32[]{:S(2)}) %collective-permute-start.1) | collective-permute-done | bytes 262176 | tf_op jit(solution)/shard_map/swap_tp_2/ppermute | solution.py:101
  35.8 1.6 %collective-permute-start.7 = (bf16[128,1024]{1,0:T(8,128)(2,1)S(1)}, bf16[128,1024]{1,0:T(8,128)(2,1)S(1)}, u32[]{:S(2)}, u32[]{:S(2)}) collective-permute-start(bf16[128,1024]{1,0:T(8,128)(2,1)S(1)} %collective-permute-done.1.refs_0_), channel_id=1, source_target_pairs={{0,4},{4,0},{8,12},{12,8},{1,5},{5,1},{9,13},{13,9},{2,6},{6,2},{1... | collective-permute-start | bytes 786440 | tf_op jit(solution)/shard_map/swap_ctx_1/ppermute | solution.py:101
  37.4 2.9 %shard_map.286 = (bf16[256,128]{1,0:T(8,128)(2,1)S(1)}, f32[256,128]{1,0:T(8,128)S(1)}, f32[256,512]{1,0:T(8,128)S(1)}, bf16[256,512]{1,0:T(8,128)(2,1)}) custom-call(s32[4]{0:T(128)S(1)} %pad_add_fusion.spot_ref, s32[1,1024]{1,0:T(1,128)S(1)} %get-tuple-element.245.seg_ref, bf16[256,128]{1,0:T(8,128)(2,1)S(1)} %get-tuple-element.255.q_ref.q_f, ...), custom_call_target="tpu_custom_call" | custom-call | flops 20000000000 | bytes 65536 | tf_op jit(solution)/shard_map/pallas_call | solution.py:83
  40.4 0.8 copy-done.22
  42.4 2.1 %collective-permute-done.7.refs_1_ = bf16[128,1024]{1,0:T(8,128)(2,1)S(1)} collective-permute-done((bf16[128,1024]{1,0:T(8,128)(2,1)S(1)}, bf16[128,1024]{1,0:T(8,128)(2,1)S(1)}, u32[]{:S(2)}, u32[]{:S(2)}) %collective-permute-start.7) | collective-permute-done | bytes 262176 | tf_op jit(solution)/shard_map/swap_ctx_1/ppermute | solution.py:101
  45.1 5.9 %collective-permute-done.11.got_ref = bf16[256,512]{1,0:T(8,128)(2,1)S(1)} collective-permute-done((bf16[256,512]{1,0:T(8,128)(2,1)}, bf16[256,512]{1,0:T(8,128)(2,1)S(1)}, u32[]{:S(2)}, u32[]{:S(2)}) %collective-permute-start.11) | collective-permute-done | bytes 262176 | tf_op jit(solution)/shard_map/swap_tp_1/ppermute | solution.py:101
  51.0 1.0 copy-done.19
  52.0 1.0 copy-done.21
  53.1 1.0 copy-done.23
  54.1 0.7 copy-done.37
  54.8 2.8 %shard_map.287 = (bf16[128,512]{1,0:T(8,128)(2,1)S(1)}, f32[128,512]{1,0:T(8,128)S(1)}, bf16[128,512]{1,0:T(8,128)(2,1)S(1)}, f32[128,512]{1,0:T(8,128)S(1)}, f3...) custom-call(s32[4]{0:T(128)S(1)} %pad_add_fusion.spot_ref, ...), custom_call_target="tpu_custom_call" | custom-call | flops 20000000000 | bytes 65536 | tf_op jit(solution)/shard_map/pallas_call | solution.py:83
  58.1 1.3 shard_map.288
  59.4 3.3 %collective-permute-done.15.got_ref = bf16[128,512]{1,0:T(8,128)(2,1)S(1)} collective-permute-done((bf16[128,512]{1,0:T(8,128)(2,1)S(1)}, bf16[128,512]{1,0:T(8,128)(2,1)S(1)}, u32[]{:S(2)}, u32[]{:S(2)}) %collective-permute-start.15) | collective-permute-done | bytes 131104 | tf_op jit(solution)/shard_map/swap_tp_1/ppermute | solution.py:101
  62.7 0.9 shard_map.289
  64.2 0.7 shard_map.290
  65.5 3.3 %collective-permute-done.17.got_ref = bf16[128,512]{1,0:T(8,128)(2,1)S(1)} collective-permute-done((bf16[128,512]{1,0:T(8,128)(2,1)S(1)}, bf16[128,512]{1,0:T(8,128)(2,1)S(1)}, u32[]{:S(2)}, u32[]{:S(2)}) %collective-permute-start.17) | collective-permute-done | bytes 131104 | tf_op jit(solution)/shard_map/swap_tp_1/ppermute | solution.py:101
  68.9 4.9 %shard_map.291 = (f32[256,256]{1,0:T(8,128)S(1)}, f32[256,512]{1,0:T(8,128)S(1)}, bf16[256,512]{1,0:T(8,128)(2,1)S(1)}, bf16[256,512]{1,0:T(8,128)(2,1)S(1)}, bf...) custom-call(s32[4]{0:T(128)S(1)} %pad_add_fusion.spot_ref, s32[1,1024]{1,0:T(1,128)S(1)} %get-tuple-element.245.seg_ref, ...), custom_call_target="tpu_custom_call" | custom-call | flops 20000000000 | bytes 65536 | tf_op jit(solution)/shard_map/pallas_call | solution.py:83
  74.2 1.5 %collective-permute-start.22 = (bf16[256,512]{1,0:T(8,128)(2,1)S(1)}, bf16[256,512]{1,0:T(8,128)(2,1)S(1)}, u32[]{:S(2)}, u32[]{:S(2)}) collective-permute-start(bf16[256,512]{1,0:T(8,128)(2,1)S(1)} %get-tuple-element.329), channel_id=1, source_target_pairs={{0,12},{4,8},{8,4},{12,0},{1,13},{5,9},{9,5},{13,1},{2,14},{6,10},... | collective-permute-start | bytes 786440 | tf_op jit(solution)/shard_map/swap_ctx_3/ppermute | solution.py:101
  76.2 1.5 %collective-permute-start.20 = (bf16[256,512]{1,0:T(8,128)(2,1)S(1)}, bf16[256,512]{1,0:T(8,128)(2,1)S(1)}, u32[]{:S(2)}, u32[]{:S(2)}) collective-permute-start(bf16[256,512]{1,0:T(8,128)(2,1)S(1)} %get-tuple-element.327), channel_id=1, source_target_pairs={{0,4},{4,0},{8,12},{12,8},{1,5},{5,1},{9,13},{13,9},{2,6},{6,2},{1... | collective-permute-start | bytes 786440 | tf_op jit(solution)/shard_map/swap_ctx_1/ppermute | solution.py:101
  79.4 1.0 collective-permute-start.23
  80.4 4.0 %collective-permute-done.22.g3 = bf16[256,512]{1,0:T(8,128)(2,1)S(1)} collective-permute-done((bf16[256,512]{1,0:T(8,128)(2,1)S(1)}, bf16[256,512]{1,0:T(8,128)(2,1)S(1)}, u32[]{:S(2)}, u32[]{:S(2)}) %collective-permute-start.22) | collective-permute-done | bytes 262176 | tf_op jit(solution)/shard_map/swap_ctx_3/ppermute | solution.py:101
  84.4 1.9 %collective-permute-done.21.g2 = bf16[256,512]{1,0:T(8,128)(2,1)S(1)} collective-permute-done((bf16[256,512]{1,0:T(8,128)(2,1)S(1)}, bf16[256,512]{1,0:T(8,128)(2,1)S(1)}, u32[]{:S(2)}, u32[]{:S(2)}) %collective-permute-start.21) | collective-permute-done | bytes 262176 | tf_op jit(solution)/shard_map/swap_ctx_2/ppermute | solution.py:101
  86.3 2.3 %collective-permute-done.20.g1 = bf16[256,512]{1,0:T(8,128)(2,1)S(1)} collective-permute-done((bf16[256,512]{1,0:T(8,128)(2,1)S(1)}, bf16[256,512]{1,0:T(8,128)(2,1)S(1)}, u32[]{:S(2)}, u32[]{:S(2)}) %collective-permute-start.20) | collective-permute-done | bytes 262176 | tf_op jit(solution)/shard_map/swap_ctx_1/ppermute | solution.py:101
  88.6 1.8 %shard_map.294 = (f32[128,512]{1,0:T(8,128)S(1)}, bf16[128,512]{1,0:T(8,128)(2,1)S(1)}, f32[16,512]{1,0:T(8,128)S(1)}, f32[256,1024]{1,0:T(8,128)S(1)}, bf16[256,1024]{1,0:T(8,128)(2,1)S(1)}) custom-call(s32[4]{0:T(128)S(1)} %pad_add_fusion.spot_ref, f32[256,512]{1,0:T(8,128)S(1)} %copy-done.19, f32[8,512]{1,0:T(8,128)S(1)} %copy-done.38, ...), custom_call_target="tpu_custom_call" | custom-call | flops 20000000000 | bytes 65536 | tf_op jit(solution)/shard_map/pallas_call | solution.py:83
  90.4 1.3 collective-permute-start.25
  91.7 1.3 collective-permute-start.30
  93.0 1.0 collective-permute-start.29
  94.0 2.2 %collective-permute-start.28 = (bf16[128,512]{1,0:T(8,128)(2,1)S(1)}, bf16[128,512]{1,0:T(8,128)(2,1)S(1)}, u32[]{:S(2)}, u32[]{:S(2)}) collective-permute-start(bf16[128,512]{1,0:T(8,128)(2,1)S(1)} %shard_map.293.refs_0_), channel_id=1, source_target_pairs={{0,1},{1,0},{2,3},{3,2},{4,5},{5,4},{6,7},{7,6},{8,9},{9,8},{10,11... | collective-permute-start | bytes 393224 | tf_op jit(solution)/shard_map/swap_tp_1/ppermute | solution.py:101
  96.7 1.3 collective-permute-done.24.got_ref
  98.0 0.7 shard_map.296
  99.3 1.0 collective-permute-start.27
  100.3 7.4 %collective-permute-done.26.got_ref = bf16[64,1024]{1,0:T(8,128)(2,1)S(1)} collective-permute-done((bf16[64,1024]{1,0:T(8,128)(2,1)S(1)}, bf16[64,1024]{1,0:T(8,128)(2,1)S(1)}, u32[]{:S(2)}, u32[]{:S(2)}) %collective-permute-start.26) | collective-permute-done | bytes 131104 | tf_op jit(solution)/shard_map/swap_tp_2/ppermute | solution.py:101
  108.2 1.0 collective-permute-start.31
  109.8 1.2 collective-permute-start.32
  111.0 1.6 %shard_map.300 = f32[512,512]{1,0:T(8,128)} custom-call(s32[4]{0:T(128)S(1)} %pad_add_fusion.spot_ref, bf16[128,512]{1,0:T(8,128)(2,1)S(1)} %shard_map.293.refs_0_, bf16[128,512]{1,0:T(8,128)(2,1)S(1)} %collective-permute-done.28.refs_1_, bf16[128,512]{1,0:T(8,128)(2,1)S(1)} %collective-permute-done.29.refs_2_, ...), custom_call_target="tpu_custom_call" | custom-call | flops 20000000000 | bytes 65536 | tf_op jit(solution)/shard_map/pallas_call | solution.py:83
  112.6 0.7 collective-permute-done.31.two_ref.p1
  114.5 1.0 collective-permute-done.32.got_ref
  116.1 4.1 %collective-permute-done.33.p2 = bf16[128,1024]{1,0:T(8,128)(2,1)S(1)} collective-permute-done((bf16[128,1024]{1,0:T(8,128)(2,1)S(1)}, bf16[128,1024]{1,0:T(8,128)(2,1)S(1)}, u32[]{:S(2)}, u32[]{:S(2)}) %collective-permute-start.33) | collective-permute-done | bytes 262176 | tf_op jit(solution)/shard_map/swap_turn_0/ppermute | solution.py:114
  120.3 1.6 %shard_map.303 = (f32[256,512]{1,0:T(8,128)}, f32[256,512]{1,0:T(8,128)}) custom-call(s32[4]{0:T(128)S(1)} %pad_add_fusion.spot_ref, bf16[64,1024]{1,0:T(8,128)(2,1)S(1)} %shard_map.298.one_ref.p0, bf16[64,1024]{1,0:T(8,128)(2,1)S(1)} %collective-permute-done.31.two_ref.p1, bf16[128,1024]{1,0:T(8,128)(2,1)S(1)} %collective-permute-done.33.p2), custom_call_target="tpu_custom_call" | custom-call | flops 20000000000 | bytes 65536 | tf_op jit(solution)/shard_map/pallas_call | solution.py:83
  122.4 1.2 collective-permute-start.35
  123.7 1.9 %collective-permute-start.39 = (bf16[128,512]{1,0:T(8,128)(2,1)S(1)}, bf16[128,512]{1,0:T(8,128)(2,1)S(1)}, u32[]{:S(2)}, u32[]{:S(2)}) collective-permute-start(bf16[128,512]{1,0:T(8,128)(2,1)S(1)} %shard_map.297.refs_0_), channel_id=1, source_target_pairs={{0,3},{1,2},{2,1},{3,0},{4,7},{5,6},{6,5},{7,4},{8,11},{9,10},{10,... | collective-permute-start | bytes 393224 | tf_op jit(solution)/shard_map/swap_tp_3/ppermute | solution.py:101
  125.6 2.5 %collective-permute-start.37 = (bf16[128,512]{1,0:T(8,128)(2,1)S(1)}, bf16[128,512]{1,0:T(8,128)(2,1)S(1)}, u32[]{:S(2)}, u32[]{:S(2)}) collective-permute-start(bf16[128,512]{1,0:T(8,128)(2,1)S(1)} %shard_map.297.refs_0_), channel_id=1, source_target_pairs={{0,1},{1,0},{2,3},{3,2},{4,5},{5,4},{6,7},{7,6},{8,9},{9,8},{10,11... | collective-permute-start | bytes 393224 | tf_op jit(solution)/shard_map/swap_tp_1/ppermute | solution.py:101
  128.6 4.4 %collective-permute-done.36.got_ref = f32[16,512]{1,0:T(8,128)S(1)} collective-permute-done((f32[16,512]{1,0:T(8,128)S(1)}, f32[16,512]{1,0:T(8,128)S(1)}, u32[]{:S(2)}, u32[]{:S(2)}) %collective-permute-start.36) | collective-permute-done | bytes 32800 | tf_op jit(solution)/shard_map/swap_tp_1/ppermute | solution.py:101
  133.7 1.0 collective-permute-start.41
  134.7 0.8 collective-permute-done.38.refs_2_
  135.6 1.6 %shard_map.307 = f32[512,512]{1,0:T(8,128)} custom-call(s32[4]{0:T(128)S(1)} %pad_add_fusion.spot_ref, bf16[128,512]{1,0:T(8,128)(2,1)S(1)} %shard_map.297.refs_0_, bf16[128,512]{1,0:T(8,128)(2,1)S(1)} %collective-permute-done.37.refs_1_, bf16[128,512]{1,0:T(8,128)(2,1)S(1)} %collective-permute-done.38.refs_2_, ...), custom_call_target="tpu_custom_call" | custom-call | flops 20000000000 | bytes 65536 | tf_op jit(solution)/shard_map/pallas_call | solution.py:83
  137.2 2.0 %shard_map.308 = (f32[1000,512]{1,0:T(8,128)}, f32[16,512]{1,0:T(8,128)S(1)}, f32[1,512]{1,0:T(1,128)}, f32[2,128]{1,0:T(2,128)}) custom-call(s32[4]{0:T(128)S(1)} %pad_add_fusion.spot_ref, s32[4]{0:T(128)S(1)} %broadcast_select_fusion.steps_ref, f32[16,512]{1,0:T(8,128)S(1)} %shard_map.306.own_ref, f32[16,512]{1,0:T(8,128)S(1)} %collective-permute-done.40.got_ref), custom_call_target="tpu_custom_call" | custom-call | flops 20000000000 | bytes 65536 | tf_op jit(solution)/shard_map/pallas_call | solution.py:83
  139.8 1.4 shard_map.309
  (136 shorter events, 15.1 us)
Async XLA Ops:
  3.1 16.7 %collective-permute-start.2 = (bf16[272,512]{1,0:T(8,128)(2,1)S(1)}, bf16[272,512]{1,0:T(8,128)(2,1)S(1)}, u32[]{:S(2)}, u32[]{:S(2)}) collective-permute-start(bf16[272,512]{1,0:T(8,128)(2,1)S(1)} %shard_map.280.one_ref.bias_ref.one_n.near_pack), channel_id=1, source_target_pairs={{0,2},{1,3},{2,0},{3,1},{4,6},{5,7},{6,4},{7,5},{8,10},{9,11},{10,... | collective-permute-start | bytes 835592 | tf_op jit(solution)/shard_map/swap_tp_2/ppermute | solution.py:101
  7.2 2.8 %collective-permute-start = (bf16[272,512]{1,0:T(8,128)(2,1)S(1)}, bf16[272,512]{1,0:T(8,128)(2,1)S(1)}, u32[]{:S(2)}, u32[]{:S(2)}) collective-permute-start(bf16[272,512]{1,0:T(8,128)(2,1)S(1)} %shard_map.280.one_ref.bias_ref.one_n.near_pack), channel_id=1, source_target_pairs={{0,16},{16,0},{1,17},{17,1},{2,18},{18,2},{3,19},{19,3},{4,20},{20... | collective-permute-start | bytes 835592 | tf_op jit(solution)/shard_map/swap_fsdp_1/ppermute | solution.py:101
  9.9 12.2 %copy-start.24 = (bf16[256,512]{1,0:T(8,128)(2,1)}, bf16[256,512]{1,0:T(8,128)(2,1)S(1)}, u32[]{:S(2)}) copy-start(bf16[256,512]{1,0:T(8,128)(2,1)S(1)} %get-tuple-element.219.normed_ref) | copy-start | bytes 786436
  10.8 15.8 %copy-start.2 = (bf16[256,256]{1,0:T(8,128)(2,1)}, bf16[256,256]{1,0:T(8,128)(2,1)S(1)}, u32[]{:S(2)}) copy-start(bf16[256,256]{1,0:T(8,128)(2,1)S(1)} %get-tuple-element.234.kv0.n0) | copy-start | bytes 393220
  10.8 15.8 %copy-start.32 = (bf16[256,128]{1,0:T(8,128)(2,1)}, bf16[256,128]{1,0:T(8,128)(2,1)S(1)}, u32[]{:S(2)}) copy-start(bf16[256,128]{1,0:T(8,128)(2,1)S(1)} %get-tuple-element.246.q_ref.q_n) | copy-start | bytes 196612
  10.8 9.0 %collective-permute-start.5 = (bf16[256,256]{1,0:T(8,128)(2,1)S(1)}, bf16[256,256]{1,0:T(8,128)(2,1)S(1)}, u32[]{:S(2)}, u32[]{:S(2)}) collective-permute-start(bf16[256,256]{1,0:T(8,128)(2,1)S(1)} %get-tuple-element.234.kv0.n0), channel_id=1, source_target_pairs={{0,12},{4,8},{8,4},{12,0},{1,13},{5,9},{9,5},{13,1},{2,14},{6,10},... | collective-permute-start | bytes 393224 | tf_op jit(solution)/shard_map/swap_ctx_3/ppermute | solution.py:101
  13.3 7.2 %collective-permute-start.4 = (bf16[256,256]{1,0:T(8,128)(2,1)S(1)}, bf16[256,256]{1,0:T(8,128)(2,1)S(1)}, u32[]{:S(2)}, u32[]{:S(2)}) collective-permute-start(bf16[256,256]{1,0:T(8,128)(2,1)S(1)} %get-tuple-element.234.kv0.n0), channel_id=1, source_target_pairs={{0,8},{4,12},{8,0},{12,4},{1,9},{5,13},{9,1},{13,5},{2,10},{6,14},... | collective-permute-start | bytes 393224 | tf_op jit(solution)/shard_map/swap_ctx_2/ppermute | solution.py:101
  13.8 6.8 %collective-permute-start.3 = (bf16[256,256]{1,0:T(8,128)(2,1)S(1)}, bf16[256,256]{1,0:T(8,128)(2,1)S(1)}, u32[]{:S(2)}, u32[]{:S(2)}) collective-permute-start(bf16[256,256]{1,0:T(8,128)(2,1)S(1)} %get-tuple-element.234.kv0.n0), channel_id=1, source_target_pairs={{0,4},{4,0},{8,12},{12,8},{1,5},{5,1},{9,13},{13,9},{2,6},{6,2},{1... | collective-permute-start | bytes 393224 | tf_op jit(solution)/shard_map/swap_ctx_1/ppermute | solution.py:101
  19.8 6.8 %copy-start.4 = (bf16[256,256]{1,0:T(8,128)(2,1)}, bf16[256,256]{1,0:T(8,128)(2,1)S(1)}, u32[]{:S(2)}) copy-start(bf16[256,256]{1,0:T(8,128)(2,1)S(1)} %collective-permute-done.5.kv3.n3) | copy-start | bytes 393220
  20.5 6.1 %copy-start.6 = (bf16[256,256]{1,0:T(8,128)(2,1)}, bf16[256,256]{1,0:T(8,128)(2,1)S(1)}, u32[]{:S(2)}) copy-start(bf16[256,256]{1,0:T(8,128)(2,1)S(1)} %collective-permute-done.4.kv2.n2) | copy-start | bytes 393220
  20.6 6.0 %copy-start.8 = (bf16[256,256]{1,0:T(8,128)(2,1)}, bf16[256,256]{1,0:T(8,128)(2,1)S(1)}, u32[]{:S(2)}) copy-start(bf16[256,256]{1,0:T(8,128)(2,1)S(1)} %collective-permute-done.3.kv1.n1) | copy-start | bytes 393220
  20.6 1.6 %collective-permute-start.6 = (bf16[272,512]{1,0:T(8,128)(2,1)S(1)}, bf16[272,512]{1,0:T(8,128)(2,1)S(1)}, u32[]{:S(2)}, u32[]{:S(2)}) collective-permute-start(bf16[272,512]{1,0:T(8,128)(2,1)S(1)} %collective-permute-done.2.one_ref.bias_ref.one_f.far_pack), channel_id=1, source_target_pairs={{0,16},{16,0},{1,17},{17,1},{2,18},{18,2},{3,19},{19,3},{4,20},{20... | collective-permute-start | bytes 835592 | tf_op jit(solution)/shard_map/swap_fsdp_1/ppermute | solution.py:101
  20.6 15.2 %collective-permute-start.1 = (bf16[128,1024]{1,0:T(8,128)(2,1)S(1)}, bf16[128,1024]{1,0:T(8,128)(2,1)S(1)}, u32[]{:S(2)}, u32[]{:S(2)}) collective-permute-start(bf16[128,1024]{1,0:T(8,128)(2,1)S(1)} %get-tuple-element.230), channel_id=1, source_target_pairs={{0,2},{1,3},{2,0},{3,1},{4,6},{5,7},{6,4},{7,5},{8,10},{9,11},{10,... | collective-permute-start | bytes 786440 | tf_op jit(solution)/shard_map/swap_tp_2/ppermute | solution.py:101
  20.9 24.2 %collective-permute-start.12 = (bf16[256,1024]{1,0:T(8,128)(2,1)S(1)}, bf16[256,1024]{1,0:T(8,128)(2,1)S(1)}, u32[]{:S(2)}, u32[]{:S(2)}) collective-permute-start(bf16[256,1024]{1,0:T(8,128)(2,1)S(1)} %get-tuple-element.271.one_n), channel_id=1, source_target_pairs={{0,16},{16,0},{1,17},{17,1},{2,18},{18,2},{3,19},{19,3},{4,20},{20... | collective-permute-start | bytes 1572872 | tf_op jit(solution)/shard_map/swap_fsdp_1/ppermute | solution.py:101
  23.0 14.4 %copy-start.10 = (bf16[256,256]{1,0:T(8,128)(2,1)}, bf16[256,256]{1,0:T(8,128)(2,1)S(1)}, u32[]{:S(2)}) copy-start(bf16[256,256]{1,0:T(8,128)(2,1)S(1)} %get-tuple-element.258.kv0.f0) | copy-start | bytes 393220
  23.0 14.4 %copy-start.34 = (bf16[256,128]{1,0:T(8,128)(2,1)}, bf16[256,128]{1,0:T(8,128)(2,1)S(1)}, u32[]{:S(2)}) copy-start(bf16[256,128]{1,0:T(8,128)(2,1)S(1)} %get-tuple-element.255.q_ref.q_f) | copy-start | bytes 196612
  23.0 12.8 %collective-permute-start.10 = (bf16[256,256]{1,0:T(8,128)(2,1)S(1)}, bf16[256,256]{1,0:T(8,128)(2,1)S(1)}, u32[]{:S(2)}, u32[]{:S(2)}) collective-permute-start(bf16[256,256]{1,0:T(8,128)(2,1)S(1)} %get-tuple-element.258.kv0.f0), channel_id=1, source_target_pairs={{0,12},{4,8},{8,4},{12,0},{1,13},{5,9},{9,5},{13,1},{2,14},{6,10},... | collective-permute-start | bytes 393224 | tf_op jit(solution)/shard_map/swap_ctx_3/ppermute | solution.py:101
  24.9 12.5 %collective-permute-start.9 = (bf16[256,256]{1,0:T(8,128)(2,1)S(1)}, bf16[256,256]{1,0:T(8,128)(2,1)S(1)}, u32[]{:S(2)}, u32[]{:S(2)}) collective-permute-start(bf16[256,256]{1,0:T(8,128)(2,1)S(1)} %get-tuple-element.258.kv0.f0), channel_id=1, source_target_pairs={{0,8},{4,12},{8,0},{12,4},{1,9},{5,13},{9,1},{13,5},{2,10},{6,14},... | collective-permute-start | bytes 393224 | tf_op jit(solution)/shard_map/swap_ctx_2/ppermute | solution.py:101
  26.0 11.4 %collective-permute-start.8 = (bf16[256,256]{1,0:T(8,128)(2,1)S(1)}, bf16[256,256]{1,0:T(8,128)(2,1)S(1)}, u32[]{:S(2)}, u32[]{:S(2)}) collective-permute-start(bf16[256,256]{1,0:T(8,128)(2,1)S(1)} %get-tuple-element.258.kv0.f0), channel_id=1, source_target_pairs={{0,4},{4,0},{8,12},{12,8},{1,5},{5,1},{9,13},{13,9},{2,6},{6,2},{1... | collective-permute-start | bytes 393224 | tf_op jit(solution)/shard_map/swap_ctx_1/ppermute | solution.py:101
  28.5 11.8 %copy-start.26 = (f32[256,128]{1,0:T(8,128)}, f32[256,128]{1,0:T(8,128)S(1)}, u32[]{:S(2)}) copy-start(f32[256,128]{1,0:T(8,128)S(1)} %get-tuple-element.298.lse_n) | copy-start | bytes 393220
  35.8 9.3 %collective-permute-start.13 = (bf16[128,1024]{1,0:T(8,128)(2,1)S(1)}, bf16[128,1024]{1,0:T(8,128)(2,1)S(1)}, u32[]{:S(2)}, u32[]{:S(2)}) collective-permute-start(bf16[128,1024]{1,0:T(8,128)(2,1)S(1)} %collective-permute-done.1.refs_0_), channel_id=1, source_target_pairs={{0,16},{16,0},{1,17},{17,1},{2,18},{18,2},{3,19},{19,3},{4,20},{20... | collective-permute-start | bytes 786440 | tf_op jit(solution)/shard_map/swap_fsdp_1/ppermute | solution.py:101
  35.8 8.7 %collective-permute-start.7 = (bf16[128,1024]{1,0:T(8,128)(2,1)S(1)}, bf16[128,1024]{1,0:T(8,128)(2,1)S(1)}, u32[]{:S(2)}, u32[]{:S(2)}) collective-permute-start(bf16[128,1024]{1,0:T(8,128)(2,1)S(1)} %collective-permute-done.1.refs_0_), channel_id=1, source_target_pairs={{0,4},{4,0},{8,12},{12,8},{1,5},{5,1},{9,13},{13,9},{2,6},{6,2},{1... | collective-permute-start | bytes 786440 | tf_op jit(solution)/shard_map/swap_ctx_1/ppermute | solution.py:101
  42.4 8.6 %collective-permute-start.11 = (bf16[256,512]{1,0:T(8,128)(2,1)}, bf16[256,512]{1,0:T(8,128)(2,1)S(1)}, u32[]{:S(2)}, u32[]{:S(2)}) collective-permute-start(bf16[256,512]{1,0:T(8,128)(2,1)} %get-tuple-element.267), channel_id=1, source_target_pairs={{0,1},{1,0},{2,3},{3,2},{4,5},{5,4},{6,7},{7,6},{8,9},{9,8},{10,11... | collective-permute-start | bytes 786440 | tf_op jit(solution)/shard_map/swap_tp_1/ppermute | solution.py:101
  44.5 6.5 %collective-permute-start.14 = (bf16[128,1024]{1,0:T(8,128)(2,1)S(1)}, bf16[128,1024]{1,0:T(8,128)(2,1)S(1)}, u32[]{:S(2)}, u32[]{:S(2)}) collective-permute-start(bf16[128,1024]{1,0:T(8,128)(2,1)S(1)} %collective-permute-done.7.refs_1_), channel_id=1, source_target_pairs={{0,16},{16,0},{1,17},{17,1},{2,18},{18,2},{3,19},{19,3},{4,20},{20... | collective-permute-start | bytes 786440 | tf_op jit(solution)/shard_map/swap_fsdp_1/ppermute | solution.py:101
  57.7 5.0 %collective-permute-start.15 = (bf16[128,512]{1,0:T(8,128)(2,1)S(1)}, bf16[128,512]{1,0:T(8,128)(2,1)S(1)}, u32[]{:S(2)}, u32[]{:S(2)}) collective-permute-start(bf16[128,512]{1,0:T(8,128)(2,1)S(1)} %get-tuple-element.286), channel_id=1, source_target_pairs={{0,1},{1,0},{2,3},{3,2},{4,5},{5,4},{6,7},{7,6},{8,9},{9,8},{10,11... | collective-permute-start | bytes 393224 | tf_op jit(solution)/shard_map/swap_tp_1/ppermute | solution.py:101
  59.3 4.8 %collective-permute-start.16 = (bf16[256,2048]{1,0:T(8,128)(2,1)S(1)}, bf16[256,2048]{1,0:T(8,128)(2,1)S(1)}, u32[]{:S(2)}, u32[]{:S(2)}) collective-permute-start(bf16[256,2048]{1,0:T(8,128)(2,1)S(1)} %get-tuple-element.293), channel_id=1, source_target_pairs={{0,16},{16,0},{1,17},{17,1},{2,18},{18,2},{3,19},{19,3},{4,20},{20... | collective-permute-start | bytes 3145736 | tf_op jit(solution)/shard_map/swap_fsdp_1/ppermute | solution.py:101
  63.6 5.2 %copy-start.3 = (bf16[256,256]{1,0:T(8,128)(2,1)S(1)}, bf16[256,256]{1,0:T(8,128)(2,1)}, u32[]{:S(2)}) copy-start(bf16[256,256]{1,0:T(8,128)(2,1)} %copy-done.2) | copy-start | bytes 393220
  63.6 5.2 %copy-start.5 = (bf16[256,256]{1,0:T(8,128)(2,1)S(1)}, bf16[256,256]{1,0:T(8,128)(2,1)}, u32[]{:S(2)}) copy-start(bf16[256,256]{1,0:T(8,128)(2,1)} %copy-done.4) | copy-start | bytes 393220
  63.6 5.1 %copy-start.7 = (bf16[256,256]{1,0:T(8,128)(2,1)S(1)}, bf16[256,256]{1,0:T(8,128)(2,1)}, u32[]{:S(2)}) copy-start(bf16[256,256]{1,0:T(8,128)(2,1)} %copy-done.6) | copy-start | bytes 393220
  63.6 5.1 %copy-start.9 = (bf16[256,256]{1,0:T(8,128)(2,1)S(1)}, bf16[256,256]{1,0:T(8,128)(2,1)}, u32[]{:S(2)}) copy-start(bf16[256,256]{1,0:T(8,128)(2,1)} %copy-done.8) | copy-start | bytes 393220
  63.6 5.1 %copy-start.11 = (bf16[256,256]{1,0:T(8,128)(2,1)S(1)}, bf16[256,256]{1,0:T(8,128)(2,1)}, u32[]{:S(2)}) copy-start(bf16[256,256]{1,0:T(8,128)(2,1)} %copy-done.10) | copy-start | bytes 393220
  63.7 5.1 %copy-start.13 = (bf16[256,256]{1,0:T(8,128)(2,1)S(1)}, bf16[256,256]{1,0:T(8,128)(2,1)}, u32[]{:S(2)}) copy-start(bf16[256,256]{1,0:T(8,128)(2,1)} %copy-done.12) | copy-start | bytes 393220
  63.7 5.1 %copy-start.15 = (bf16[256,256]{1,0:T(8,128)(2,1)S(1)}, bf16[256,256]{1,0:T(8,128)(2,1)}, u32[]{:S(2)}) copy-start(bf16[256,256]{1,0:T(8,128)(2,1)} %copy-done.14) | copy-start | bytes 393220
  63.7 5.1 %copy-start.17 = (bf16[256,256]{1,0:T(8,128)(2,1)S(1)}, bf16[256,256]{1,0:T(8,128)(2,1)}, u32[]{:S(2)}) copy-start(bf16[256,256]{1,0:T(8,128)(2,1)} %copy-done.16) | copy-start | bytes 393220
  63.7 5.1 %copy-start.27 = (f32[256,128]{1,0:T(8,128)S(1)}, f32[256,128]{1,0:T(8,128)}, u32[]{:S(2)}) copy-start(f32[256,128]{1,0:T(8,128)} %copy-done.26) | copy-start | bytes 393220
  63.7 5.1 %copy-start.29 = (f32[256,128]{1,0:T(8,128)S(1)}, f32[256,128]{1,0:T(8,128)}, u32[]{:S(2)}) copy-start(f32[256,128]{1,0:T(8,128)} %copy-done.28) | copy-start | bytes 393220
  63.7 5.0 %collective-permute-start.17 = (bf16[128,512]{1,0:T(8,128)(2,1)S(1)}, bf16[128,512]{1,0:T(8,128)(2,1)S(1)}, u32[]{:S(2)}, u32[]{:S(2)}) collective-permute-start(bf16[128,512]{1,0:T(8,128)(2,1)S(1)} %get-tuple-element.300.mine_ref), channel_id=1, source_target_pairs={{0,1},{1,0},{2,3},{3,2},{4,5},{5,4},{6,7},{7,6},{8,9},{9,8},{10,11... | collective-permute-start | bytes 393224 | tf_op jit(solution)/shard_map/swap_tp_1/ppermute | solution.py:101
  64.9 12.8 %collective-permute-start.18 = (bf16[128,2048]{1,0:T(8,128)(2,1)S(1)}, bf16[128,2048]{1,0:T(8,128)(2,1)S(1)}, u32[]{:S(2)}, u32[]{:S(2)}) collective-permute-start(bf16[128,2048]{1,0:T(8,128)(2,1)S(1)} %get-tuple-element.311.sent_ref), channel_id=1, source_target_pairs={{0,4},{4,0},{8,12},{12,8},{16,24},{20,28},{24,16},{28,20},{1,5},{5... | collective-permute-start | bytes 1572872 | tf_op jit(solution)/shard_map/swap_turn_0/ppermute | solution.py:114
  73.8 5.0 %collective-permute-start.19 = (bf16[128,512]{1,0:T(8,128)(2,1)S(1)}, bf16[128,512]{1,0:T(8,128)(2,1)S(1)}, u32[]{:S(2)}, u32[]{:S(2)}) collective-permute-start(bf16[128,512]{1,0:T(8,128)(2,1)S(1)} %get-tuple-element.317), channel_id=1, source_target_pairs={{0,1},{1,0},{2,3},{3,2},{4,5},{5,4},{6,7},{7,6},{8,9},{9,8},{10,11... | collective-permute-start | bytes 393224 | tf_op jit(solution)/shard_map/swap_tp_1/ppermute | solution.py:101
  74.2 10.1 %collective-permute-start.22 = (bf16[256,512]{1,0:T(8,128)(2,1)S(1)}, bf16[256,512]{1,0:T(8,128)(2,1)S(1)}, u32[]{:S(2)}, u32[]{:S(2)}) collective-permute-start(bf16[256,512]{1,0:T(8,128)(2,1)S(1)} %get-tuple-element.329), channel_id=1, source_target_pairs={{0,12},{4,8},{8,4},{12,0},{1,13},{5,9},{9,5},{13,1},{2,14},{6,10},... | collective-permute-start | bytes 786440 | tf_op jit(solution)/shard_map/swap_ctx_3/ppermute | solution.py:101
  75.7 10.5 %collective-permute-start.21 = (bf16[256,512]{1,0:T(8,128)(2,1)S(1)}, bf16[256,512]{1,0:T(8,128)(2,1)S(1)}, u32[]{:S(2)}, u32[]{:S(2)}) collective-permute-start(bf16[256,512]{1,0:T(8,128)(2,1)S(1)} %get-tuple-element.328), channel_id=1, source_target_pairs={{0,8},{4,12},{8,0},{12,4},{1,9},{5,13},{9,1},{13,5},{2,10},{6,14},... | collective-permute-start | bytes 786440 | tf_op jit(solution)/shard_map/swap_ctx_2/ppermute | solution.py:101
  76.2 12.4 %collective-permute-start.20 = (bf16[256,512]{1,0:T(8,128)(2,1)S(1)}, bf16[256,512]{1,0:T(8,128)(2,1)S(1)}, u32[]{:S(2)}, u32[]{:S(2)}) collective-permute-start(bf16[256,512]{1,0:T(8,128)(2,1)S(1)} %get-tuple-element.327), channel_id=1, source_target_pairs={{0,4},{4,0},{8,12},{12,8},{1,5},{5,1},{9,13},{13,9},{2,6},{6,2},{1... | collective-permute-start | bytes 786440 | tf_op jit(solution)/shard_map/swap_ctx_1/ppermute | solution.py:101
  78.8 9.8 %copy-start.25 = (bf16[256,512]{1,0:T(8,128)(2,1)S(1)}, bf16[256,512]{1,0:T(8,128)(2,1)}, u32[]{:S(2)}) copy-start(bf16[256,512]{1,0:T(8,128)(2,1)} %copy-done.24) | copy-start | bytes 786436
  78.8 9.8 %copy-start.31 = (bf16[256,128]{1,0:T(8,128)(2,1)S(1)}, bf16[256,128]{1,0:T(8,128)(2,1)}, u32[]{:S(2)}) copy-start(bf16[256,128]{1,0:T(8,128)(2,1)} %copy-done.30) | copy-start | bytes 196612
  78.8 9.8 %copy-start.38 = (f32[8,512]{1,0:T(8,128)S(1)}, f32[8,512]{1,0:T(8,128)}, u32[]{:S(2)}) copy-start(f32[8,512]{1,0:T(8,128)} %copy-done.36) | copy-start | bytes 49156
  79.4 16.7 %collective-permute-start.23 = (bf16[64,2048]{1,0:T(8,128)(2,1)S(1)}, bf16[64,2048]{1,0:T(8,128)(2,1)S(1)}, u32[]{:S(2)}, u32[]{:S(2)}) collective-permute-start(bf16[64,2048]{1,0:T(8,128)(2,1)S(1)} %get-tuple-element.339.sent_ref), channel_id=1, source_target_pairs={{0,8},{4,12},{8,0},{12,4},{16,20},{20,16},{24,28},{28,24},{1,9},{5... | collective-permute-start | bytes 786440 | tf_op jit(solution)/shard_map/swap_turn_1/ppermute | solution.py:114
  90.4 8.3 %collective-permute-start.25 = (bf16[128,512]{1,0:T(8,128)(2,1)S(1)}, bf16[128,512]{1,0:T(8,128)(2,1)S(1)}, u32[]{:S(2)}, u32[]{:S(2)}) collective-permute-start(bf16[128,512]{1,0:T(8,128)(2,1)S(1)} %get-tuple-element.352), channel_id=1, source_target_pairs={{0,1},{1,0},{2,3},{3,2},{4,5},{5,4},{6,7},{7,6},{8,9},{9,8},{10,11... | collective-permute-start | bytes 393224 | tf_op jit(solution)/shard_map/swap_tp_1/ppermute | solution.py:101
  91.7 19.3 %collective-permute-start.30 = (bf16[128,512]{1,0:T(8,128)(2,1)S(1)}, bf16[128,512]{1,0:T(8,128)(2,1)S(1)}, u32[]{:S(2)}, u32[]{:S(2)}) collective-permute-start(bf16[128,512]{1,0:T(8,128)(2,1)S(1)} %shard_map.293.refs_0_), channel_id=1, source_target_pairs={{0,3},{1,2},{2,1},{3,0},{4,7},{5,6},{6,5},{7,4},{8,11},{9,10},{10,... | collective-permute-start | bytes 393224 | tf_op jit(solution)/shard_map/swap_tp_3/ppermute | solution.py:101
  93.0 18.0 %collective-permute-start.29 = (bf16[128,512]{1,0:T(8,128)(2,1)S(1)}, bf16[128,512]{1,0:T(8,128)(2,1)S(1)}, u32[]{:S(2)}, u32[]{:S(2)}) collective-permute-start(bf16[128,512]{1,0:T(8,128)(2,1)S(1)} %shard_map.293.refs_0_), channel_id=1, source_target_pairs={{0,2},{1,3},{2,0},{3,1},{4,6},{5,7},{6,4},{7,5},{8,10},{9,11},{10,... | collective-permute-start | bytes 393224 | tf_op jit(solution)/shard_map/swap_tp_2/ppermute | solution.py:101
  94.0 17.0 %collective-permute-start.28 = (bf16[128,512]{1,0:T(8,128)(2,1)S(1)}, bf16[128,512]{1,0:T(8,128)(2,1)S(1)}, u32[]{:S(2)}, u32[]{:S(2)}) collective-permute-start(bf16[128,512]{1,0:T(8,128)(2,1)S(1)} %shard_map.293.refs_0_), channel_id=1, source_target_pairs={{0,1},{1,0},{2,3},{3,2},{4,5},{5,4},{6,7},{7,6},{8,9},{9,8},{10,11... | collective-permute-start | bytes 393224 | tf_op jit(solution)/shard_map/swap_tp_1/ppermute | solution.py:101
  96.1 1.9 %collective-permute-start.24 = (bf16[256,1024]{1,0:T(8,128)(2,1)S(1)}, bf16[256,1024]{1,0:T(8,128)(2,1)S(1)}, u32[]{:S(2)}, u32[]{:S(2)}) collective-permute-start(bf16[256,1024]{1,0:T(8,128)(2,1)S(1)} %get-tuple-element.345), channel_id=1, source_target_pairs={{0,16},{16,0},{1,17},{17,1},{2,18},{18,2},{3,19},{19,3},{4,20},{20... | collective-permute-start | bytes 1572872 | tf_op jit(solution)/shard_map/swap_fsdp_1/ppermute | solution.py:101
  98.0 9.6 %collective-permute-start.26 = (bf16[64,1024]{1,0:T(8,128)(2,1)S(1)}, bf16[64,1024]{1,0:T(8,128)(2,1)S(1)}, u32[]{:S(2)}, u32[]{:S(2)}) collective-permute-start(bf16[64,1024]{1,0:T(8,128)(2,1)S(1)} %get-tuple-element.358.sent_ref), channel_id=1, source_target_pairs={{0,2},{1,3},{2,0},{3,1},{4,6},{5,7},{6,4},{7,5},{8,10},{9,11},{10,... | collective-permute-start | bytes 393224 | tf_op jit(solution)/shard_map/swap_tp_2/ppermute | solution.py:101
  99.3 9.9 %collective-permute-start.27 = (bf16[144,1024]{1,0:T(8,128)(2,1)S(1)}, bf16[144,1024]{1,0:T(8,128)(2,1)S(1)}, u32[]{:S(2)}, u32[]{:S(2)}) collective-permute-start(bf16[144,1024]{1,0:T(8,128)(2,1)S(1)} %get-tuple-element.361.sent_ref), channel_id=1, source_target_pairs={{0,4},{4,0},{8,12},{12,8},{16,24},{20,28},{24,16},{28,20},{1,5},{5... | collective-permute-start | bytes 884744 | tf_op jit(solution)/shard_map/swap_turn_0/ppermute | solution.py:114
  108.2 5.0 %collective-permute-start.31 = (bf16[64,1024]{1,0:T(8,128)(2,1)S(1)}, bf16[64,1024]{1,0:T(8,128)(2,1)S(1)}, u32[]{:S(2)}, u32[]{:S(2)}) collective-permute-start(bf16[64,1024]{1,0:T(8,128)(2,1)S(1)} %shard_map.298.one_ref.p0), channel_id=1, source_target_pairs={{0,8},{4,12},{8,0},{12,4},{16,20},{20,16},{24,28},{28,24},{1,9},{5... | collective-permute-start | bytes 393224 | tf_op jit(solution)/shard_map/swap_turn_1/ppermute | solution.py:114
  109.8 5.6 %collective-permute-start.32 = (bf16[80,1024]{1,0:T(8,128)(2,1)S(1)}, bf16[80,1024]{1,0:T(8,128)(2,1)S(1)}, u32[]{:S(2)}, u32[]{:S(2)}) collective-permute-start(bf16[80,1024]{1,0:T(8,128)(2,1)S(1)} %get-tuple-element.375.sent_ref), channel_id=1, source_target_pairs={{0,8},{4,12},{8,0},{12,4},{16,20},{20,16},{24,28},{28,24},{1,9},{5... | collective-permute-start | bytes 491528 | tf_op jit(solution)/shard_map/swap_turn_1/ppermute | solution.py:114
  113.8 6.4 %collective-permute-start.33 = (bf16[128,1024]{1,0:T(8,128)(2,1)S(1)}, bf16[128,1024]{1,0:T(8,128)(2,1)S(1)}, u32[]{:S(2)}, u32[]{:S(2)}) collective-permute-start(bf16[128,1024]{1,0:T(8,128)(2,1)S(1)} %shard_map.301), channel_id=1, source_target_pairs={{0,4},{4,0},{8,12},{12,8},{16,24},{20,28},{24,16},{28,20},{1,5},{5... | collective-permute-start | bytes 786440 | tf_op jit(solution)/shard_map/swap_turn_0/ppermute | solution.py:114
  116.0 5.8 %collective-permute-start.34 = (bf16[96,512]{1,0:T(8,128)(2,1)S(1)}, bf16[96,512]{1,0:T(8,128)(2,1)S(1)}, u32[]{:S(2)}, u32[]{:S(2)}) collective-permute-start(bf16[96,512]{1,0:T(8,128)(2,1)S(1)} %get-tuple-element.384.sent_ref), channel_id=1, source_target_pairs={{0,2},{1,3},{2,0},{3,1},{4,6},{5,7},{6,4},{7,5},{8,10},{9,11},{10,... | collective-permute-start | bytes 294920 | tf_op jit(solution)/shard_map/swap_tp_2/ppermute | solution.py:101
  122.4 5.7 %collective-permute-start.35 = (bf16[64,512]{1,0:T(8,128)(2,1)S(1)}, bf16[64,512]{1,0:T(8,128)(2,1)S(1)}, u32[]{:S(2)}, u32[]{:S(2)}) collective-permute-start(bf16[64,512]{1,0:T(8,128)(2,1)S(1)} %get-tuple-element.390.one_ref.p0), channel_id=1, source_target_pairs={{0,8},{4,12},{8,0},{12,4},{16,20},{20,16},{24,28},{28,24},{1,9},{5... | collective-permute-start | bytes 196616 | tf_op jit(solution)/shard_map/swap_turn_1/ppermute | solution.py:114
  123.7 11.1 %collective-permute-start.39 = (bf16[128,512]{1,0:T(8,128)(2,1)S(1)}, bf16[128,512]{1,0:T(8,128)(2,1)S(1)}, u32[]{:S(2)}, u32[]{:S(2)}) collective-permute-start(bf16[128,512]{1,0:T(8,128)(2,1)S(1)} %shard_map.297.refs_0_), channel_id=1, source_target_pairs={{0,3},{1,2},{2,1},{3,0},{4,7},{5,6},{6,5},{7,4},{8,11},{9,10},{10,... | collective-permute-start | bytes 393224 | tf_op jit(solution)/shard_map/swap_tp_3/ppermute | solution.py:101
  125.6 10.0 %collective-permute-start.38 = (bf16[128,512]{1,0:T(8,128)(2,1)S(1)}, bf16[128,512]{1,0:T(8,128)(2,1)S(1)}, u32[]{:S(2)}, u32[]{:S(2)}) collective-permute-start(bf16[128,512]{1,0:T(8,128)(2,1)S(1)} %shard_map.297.refs_0_), channel_id=1, source_target_pairs={{0,2},{1,3},{2,0},{3,1},{4,6},{5,7},{6,4},{7,5},{8,10},{9,11},{10,... | collective-permute-start | bytes 393224 | tf_op jit(solution)/shard_map/swap_tp_2/ppermute | solution.py:101
  125.6 10.0 %collective-permute-start.37 = (bf16[128,512]{1,0:T(8,128)(2,1)S(1)}, bf16[128,512]{1,0:T(8,128)(2,1)S(1)}, u32[]{:S(2)}, u32[]{:S(2)}) collective-permute-start(bf16[128,512]{1,0:T(8,128)(2,1)S(1)} %shard_map.297.refs_0_), channel_id=1, source_target_pairs={{0,1},{1,0},{2,3},{3,2},{4,5},{5,4},{6,7},{7,6},{8,9},{9,8},{10,11... | collective-permute-start | bytes 393224 | tf_op jit(solution)/shard_map/swap_tp_1/ppermute | solution.py:101
  128.1 5.0 %collective-permute-start.36 = (f32[16,512]{1,0:T(8,128)S(1)}, f32[16,512]{1,0:T(8,128)S(1)}, u32[]{:S(2)}, u32[]{:S(2)}) collective-permute-start(f32[16,512]{1,0:T(8,128)S(1)} %get-tuple-element.392.own_ref), channel_id=1, source_target_pairs={{0,1},{1,0},{2,3},{3,2},{4,5},{5,4},{6,7},{7,6},{8,9},{9,8},{10,11... | collective-permute-start | bytes 98312 | tf_op jit(solution)/shard_map/swap_tp_1/ppermute | solution.py:101
  133.6 3.5 %collective-permute-start.40 = (f32[16,512]{1,0:T(8,128)S(1)}, f32[16,512]{1,0:T(8,128)S(1)}, u32[]{:S(2)}, u32[]{:S(2)}) collective-permute-start(f32[16,512]{1,0:T(8,128)S(1)} %shard_map.306.own_ref), channel_id=1, source_target_pairs={{0,16},{16,0},{1,17},{17,1},{2,18},{18,2},{3,19},{19,3},{4,20},{20... | collective-permute-start | bytes 98312 | tf_op jit(solution)/shard_map/swap_fsdp_1/ppermute | solution.py:101
  133.7 6.1 %collective-permute-start.41 = (bf16[128,512]{1,0:T(8,128)(2,1)S(1)}, bf16[128,512]{1,0:T(8,128)(2,1)S(1)}, u32[]{:S(2)}, u32[]{:S(2)}) collective-permute-start(bf16[128,512]{1,0:T(8,128)(2,1)S(1)} %shard_map.305), channel_id=1, source_target_pairs={{0,4},{4,0},{8,12},{12,8},{16,24},{20,28},{24,16},{28,20},{1,5},{5... | collective-permute-start | bytes 393224 | tf_op jit(solution)/shard_map/swap_turn_0/ppermute | solution.py:114
  (18 other events, 33.2 us)

commit v3 on v2

v3 whole, which is shorter than its diff:
```python
import functools
import jax
import jax.numpy as jnp
from jax import lax
from jax.experimental import pallas as pl
from jax.experimental.pallas import tpu as pltpu
from jax.sharding import PartitionSpec as P

HEAD_DIM = 64
SCALE = HEAD_DIM ** (-0.5)
EPSILON = 1e-05
NEGATIVE = -1e30
F32 = jnp.float32
BF16 = jnp.bfloat16
BIAS_ROWS = 16
PAD = 16
CUBE = 0.044715
ROOT = 0.7978845608028654
COST, QUICK, LONG = 8_000_000_000, 1_000, 20_000_000_000
VMEM = pl.BlockSpec(memory_space=pltpu.VMEM)
SMEM = pl.BlockSpec(memory_space=pltpu.SMEM)


def dot_nn(left, right):
    return lax.dot_general(left, right, (((1,), (0,)), ((), ())), preferred_element_type=F32)


def dot_nt(left, right):
    return lax.dot_general(left, right, (((1,), (1,)), ((), ())), preferred_element_type=F32)


def dot_tn(left, right):
    return lax.dot_general(left, right, (((0,), (0,)), ((), ())), preferred_element_type=F32)


def total(values):
    return functools.reduce(jnp.add, values)


def norm_parts(values):
    centre = values - jnp.mean(values, axis=-1, keepdims=True)
    spread = jnp.mean(centre * centre, axis=-1, keepdims=True)
    inverse = lax.rsqrt(spread + EPSILON)
    return centre * inverse, inverse


def norm_back(grad, hat, inverse, gain):
    scaled = grad * gain
    mean_one = jnp.mean(scaled, axis=-1, keepdims=True)
    mean_two = jnp.mean(scaled * hat, axis=-1, keepdims=True)
    return inverse * (scaled - mean_one - hat * mean_two)


def column_sum(values):
    return jnp.sum(values, axis=0, keepdims=True)


def window(index, size):
    return pl.ds(pl.multiple_of(index * size, size), size)


def halves(spot_ref, size):
    return window(spot_ref[0], size), window(1 - spot_ref[0], size)


def hold(*values):
    return lax.optimization_barrier(values)


class Order:
    def __init__(self, spot, parts):
        self.spot, self.parts, self.cost = spot, parts, COST

    def call(self, kernel, outs, operands, *, far=(), scratch=(), limit=5, cost=None):
        specs = [
            SMEM if operand.ndim == 1
            else pl.BlockSpec(memory_space=pltpu.HBM if i in far else pltpu.VMEM)
            for i, operand in enumerate(operands)
        ]
        operands = [
            pltpu.with_memory_space_constraint(operand, pltpu.HBM) if i in far else operand
            for i, operand in enumerate(operands)
        ]
        count = len(operands)

        def body(*refs):
            kernel(refs[count], *refs[:count], *refs[count + 1 :])

        results = pl.pallas_call(
            body,
            out_shape=tuple(jax.ShapeDtypeStruct(shape, dtype) for shape, dtype in outs),
            in_specs=specs + [SMEM],
            out_specs=(VMEM,) * len(outs),
            scratch_shapes=list(scratch),
            compiler_params=pltpu.CompilerParams(vmem_limit_bytes=limit << 20),
            cost_estimate=pl.CostEstimate(
                flops=cost or self.cost, bytes_accessed=1 << 16, transcendentals=0
            ),
        )(*operands, self.spot)
        first, self.spot = hold(results[0], self.spot)
        return [first, *results[1:]]

    def swap(self, values, axis, bits):
        values, self.spot = hold(values, self.spot)
        size = 2 if axis == "fsdp" else 4
        with jax.named_scope("swap_%s_%d" % (axis, bits)):
            return lax.ppermute(values, axis, [(i, i ^ bits) for i in range(size)])

    def swap_three(self, values, axis):
        return [self.swap(values, axis, bits) for bits in (1, 2, 3)]

    def swap_turn(self, values, turn):
        if self.parts != 2:
            return self.swap(values, "ctx", 1 + turn)
        values, self.spot = hold(values, self.spot)
        pairs = [
            (4 * core + i, 4 * core + (i ^ (1 + (core + turn) % 2)))
            for core in range(2)
            for i in range(4)
        ]
        with jax.named_scope("swap_turn_%d" % turn):
            return lax.ppermute(values, ("fsdp", "ctx"), pairs)


def clear_below(ref, rows):
    if ref.shape[0] > rows:
        ref[rows:, :] = jnp.zeros((ref.shape[0] - rows, ref.shape[1]), ref.dtype)


def fetch(copies, sems):
    started = [
        pltpu.make_async_copy(source, target, sems.at[i])
        for i, (source, target) in enumerate(copies)
    ]
    for copy in started:
        copy.start()
    for copy in started:
        copy.wait()


def split_three(values):
    high = values.astype(BF16)
    rest = values - high.astype(F32)
    middle = rest.astype(BF16)
    return [high, middle, (rest - middle.astype(F32)).astype(BF16)]


def pack_kernel(
    spot_ref, steps_ref, w_hbm, out_hbm, qv_hbm, up_bias_hbm, up_hbm, down_hbm,
    pack_ref, rest_ref, quarter_ref,
    w_ref, o_ref, qv_ref, up_bias_ref, up_ref, down_ref, sems,
):
    rows, cols = w_ref.shape[1:]
    hidden = up_ref.shape[1]
    fetch(
        [
            (w_hbm, w_ref), (out_hbm, o_ref), (qv_hbm, qv_ref), (up_bias_hbm, up_bias_ref),
            (up_hbm, up_ref), (down_hbm, down_ref),
        ],
        sems,
    )
    for i in range(3):
        pack_ref[:rows, i * cols : (i + 1) * cols] = w_ref[i].astype(BF16)
    pack_ref[:rows, 3 * cols :] = o_ref[...].astype(BF16)
    lanes = lax.broadcasted_iota(jnp.int32, (1, cols), 1)
    steps = jnp.zeros((1, cols), F32)
    for i in range(steps_ref.shape[0]):
        steps = jnp.where(lanes == i, steps_ref[i].astype(F32), steps)
    fill = jnp.zeros((1, cols), F32)
    up_bias = up_bias_ref[...]
    lines = [
        jnp.concatenate([qv_ref[0:1], qv_ref[1:2], steps, fill], axis=1),
        jnp.concatenate([up_bias[:, : 2 * cols], fill, fill], axis=1),
        jnp.concatenate([up_bias[:, 2 * cols :], fill, fill], axis=1),
    ]
    parts = split_three(jnp.concatenate(lines, axis=0))
    fill = jnp.zeros((BIAS_ROWS - 9, 4 * cols), F32)
    stack = jnp.concatenate([v.astype(F32) for v in parts] + [fill], axis=0)
    pack_ref[rows:, :] = stack.astype(BF16)
    rest_ref[:, :hidden] = up_ref[...].astype(BF16)
    rest_ref[:, hidden:] = down_ref[...].astype(BF16)
    quarter = rows // 4
    mine = window(spot_ref[1], quarter)
    quarter_ref[:quarter, :hidden] = up_ref[mine, :].astype(BF16)
    quarter_ref[:quarter, hidden:] = down_ref[mine, :].astype(BF16)
    clear_below(quarter_ref, quarter)


def bias_lines(pack_ref, row):
    bits = pack_ref[row : row + BIAS_ROWS, :].astype(F32)
    lines = bits[0:3] + bits[3:6] + bits[6:9]
    half = 4 * HEAD_DIM
    return lines[0:1], jnp.concatenate([lines[1:2, :half], lines[2:3, :half]], axis=1)


def out_part(ref, size):
    cols = 2 * HEAD_DIM
    return ref[:size, ref.shape[1] - cols :]


def pair_kernel(spot_ref, own_ref, got_ref, out_ref):
    pair, span = spot_ref[2] // 2, own_ref.shape[0]
    out_ref[window(pair, span), :] = own_ref[...].astype(F32)
    out_ref[window(1 - pair, span), :] = got_ref[...].astype(F32)


def add_pair_kernel(spot_ref, base_ref, own_ref, got_ref, out_ref):
    span = base_ref.shape[0]
    terms = own_ref[:span, :].astype(F32) + got_ref[:span, :].astype(F32)
    out_ref[...] = (base_ref[...] + terms).astype(BF16)


def stream_kernel(
    spot_ref, steps_ref, x_hbm, table_hbm, seg_hbm, cotan_hbm, g1, b1, g2, b2, bo, bd,
    stream_ref, normed_ref, seg_ref, lines_ref, cotan_ref, x_ref, table_ref, ids_ref, line_ref,
    sems,
):
    pair = spot_ref[2] // 2
    step = steps_ref[pair]
    block = pl.multiple_of(step // 8 * 8, 8)
    copies = [
        (x_hbm.at[pair], x_ref),
        (table_hbm.at[pl.ds(block, 8), :], table_ref),
        (seg_hbm, ids_ref),
        (cotan_hbm.at[pair], cotan_ref),
    ]
    vectors = (g1, b1, g2, b2, bo, bd)
    fetch(copies + [(v, line_ref.at[i]) for i, v in enumerate(vectors)], sems)
    for i in range(len(vectors)):
        lines_ref[i : i + 1, :] = line_ref[i]
    seg_ref[...] = ids_ref[pl.ds(pair, 1), :]
    stream = x_ref[...] + table_ref[pl.ds(step % 8, 1), :]
    hat, _ = norm_parts(stream)
    stream_ref[...] = stream
    normed_ref[...] = (hat * line_ref[0] + line_ref[1]).astype(BF16)


def project_kernel(spot_ref, normed_ref, one_ref, two_ref, bias_ref, q_ref, kv_ref, *, row):
    span, cols = q_ref.shape
    size = normed_ref.shape[1] // 2
    one, two = halves(spot_ref, size)
    raw = dot_nn(normed_ref[:, one], one_ref[:size, : 3 * cols])
    raw = raw + dot_nn(normed_ref[:, two], two_ref[:size, : 3 * cols])
    line, _ = bias_lines(bias_ref, row)
    q_bias, v_bias = line[:, :cols], line[:, cols : 2 * cols]
    q_ref[...] = (raw[:, :cols] + q_bias).astype(BF16)
    kv_ref[:span, :cols] = raw[:, cols : 2 * cols].astype(BF16)
    kv_ref[:span, cols:] = (raw[:, 2 * cols :] + v_bias).astype(BF16)
    clear_below(kv_ref, span)


def mask_biases(spot_ref, seg_ref, span):
    chunk = spot_ref[1]
    ids = [seg_ref[:, window(chunk ^ step, span)] for step in range(seg_ref.shape[1] // span)]
    own = jnp.broadcast_to(ids[0], (span, span)).T
    return [
        jnp.where(own == jnp.broadcast_to(step_ids, (span, span)), 0.0, NEGATIVE)
        for step_ids in ids
    ]


def lane_mask(shape, head):
    return (lax.broadcasted_iota(jnp.int32, shape, 1) // HEAD_DIM) == head


def attend_forward(spot_ref, seg_ref, q_ref, kvs, mixed_ref, lse_ref):
    span, width = q_ref.shape
    biases = mask_biases(spot_ref, seg_ref, span)
    query = q_ref[...]
    mixed, lse = None, None
    for head in range(width // HEAD_DIM):
        mine = lane_mask((span, width), head)
        masked = jnp.where(mine, query, jnp.zeros_like(query))
        scores = [
            dot_nt(masked, kv[:span, :width]) * SCALE + bias for kv, bias in zip(kvs, biases)
        ]
        top = functools.reduce(
            jnp.maximum, [jnp.max(block, axis=-1, keepdims=True) for block in scores]
        )
        grown = [jnp.exp(block - top) for block in scores]
        mass = total([jnp.sum(block, axis=-1, keepdims=True) for block in grown])
        share = 1.0 / mass
        out = total(
            [
                dot_nn((block * share).astype(BF16), kv[:span, width:])
                for block, kv in zip(grown, kvs)
            ]
        )
        log_mass = jnp.broadcast_to(top + jnp.log(mass), (span, width))
        mixed = out if head == 0 else jnp.where(mine, out, mixed)
        lse = log_mass if head == 0 else jnp.where(mine, log_mass, lse)
    mixed_ref[...] = mixed.astype(BF16)
    lse_ref[...] = lse


def attend_one_kernel(spot_ref, seg_ref, q_ref, kv0, kv1, kv2, kv3, mixed_ref, lse_ref):
    attend_forward(spot_ref, seg_ref, q_ref, (kv0, kv1, kv2, kv3), mixed_ref, lse_ref)


def attend_two_kernel(
    spot_ref, seg_ref, q_ref, kv0, kv1, kv2, kv3, near_ref, one_n, two_n, one_f, two_f,
    mixed_ref, lse_ref, given_ref,
):
    attend_forward(spot_ref, seg_ref, q_ref, (kv0, kv1, kv2, kv3), mixed_ref, lse_ref)
    size = given_ref.shape[1] // 2
    one, two = halves(spot_ref, size)
    near, far = near_ref[...], mixed_ref[...]
    for columns, near_w, far_w in ((one, one_n, one_f), (two, two_n, two_f)):
        terms = dot_nt(near, out_part(near_w, size)) + dot_nt(far, out_part(far_w, size))
        given_ref[: near.shape[0], columns] = terms.astype(BF16)
    clear_below(given_ref, near.shape[0])


def stack_kernel(spot_ref, one_ref, two_ref, out_ref):
    rows = out_ref.shape[0] // 2
    out_ref[:rows, :] = one_ref[:rows, :]
    out_ref[rows:, :] = two_ref[:rows, :]


def gelu_parts(x):
    square = x * x
    curve = jnp.tanh(ROOT * (x + CUBE * (x * square)))
    half = 0.5 * (1.0 + curve)
    slope = half + 0.5 * x * (1.0 - curve * curve) * (ROOT * (1.0 + 3.0 * CUBE * square))
    return x * half, slope


def ffn_side(
    normed_ref, low_ref, bias, first, second, columns, act_ref, pre_ref, sum_ref, *sums
):
    hidden = act_ref.shape[1]
    one, two = columns
    pre = dot_nn(normed_ref[:, one], first[:, :hidden])
    pre = pre + dot_nn(normed_ref[:, two], second[:, :hidden]) + bias
    value, slope = gelu_parts(pre)
    grad = dot_nn(low_ref[:, one], first[:, hidden:])
    grad = (grad + dot_nn(low_ref[:, two], second[:, hidden:])) * slope
    sum_ref[...] = column_sum(grad)
    act_ref[...] = value.astype(BF16)
    pre_ref[...] = grad.astype(BF16)
    act, pre_low = act_ref[...], pre_ref[...]
    for at, weights in zip(columns, (first, second)):
        back = dot_nt(pre_low, weights[:, :hidden])
        down = dot_nt(act, weights[:, hidden:])
        if len(sums) == 2:
            back_ref, out_ref = sums
        else:
            back_near, out_near, back_ref, out_ref = sums
            back, down = back + back_near[:, at], down + out_near[:, at]
        back_ref[: act.shape[0], at] = back.astype(back_ref.dtype)
        out_ref[: act.shape[0], at] = down.astype(out_ref.dtype)
    clear_below(sums[-2], act.shape[0])
    clear_below(sums[-1], act.shape[0])


def ffn_near_kernel(
    spot_ref, stream_ref, mine_ref, got_ref, cotan_ref, lines_ref, pack_ref, first, second,
    back_ref, ffn_ref, out_ref, resid_ref, normed_ref, act_ref, pre_ref, low_ref, sum_ref, *, row,
):
    span = stream_ref.shape[0]
    terms = mine_ref[:span, :].astype(F32) + got_ref[:span, :].astype(F32)
    resid = stream_ref[...] + terms + lines_ref[4:5, :]
    resid_ref[...] = resid
    out_ref[...] = resid + lines_ref[5:6, :]
    hat, _ = norm_parts(resid)
    normed_ref[...] = (hat * lines_ref[2:3, :] + lines_ref[3:4, :]).astype(BF16)
    low_ref[...] = cotan_ref[...].astype(BF16)
    ffn_side(
        normed_ref, low_ref, bias_lines(pack_ref, row)[1], first, second,
        halves(spot_ref, first.shape[0]), act_ref, pre_ref, sum_ref, back_ref, ffn_ref,
    )


def ffn_far_kernel(spot_ref, normed_ref, low_ref, back_near, ffn_near, pack_ref, *refs, row):
    count = len(refs) - 7
    pieces, outs, (first, second) = refs[:count], refs[count:-2], refs[-2:]
    if count == 2:
        first, second = pieces
    else:
        rows = pieces[0].shape[0] // 2
        turn, other = turn_bits(spot_ref)
        for target, pairs, bits in (
            (first, pieces[:2], (0, turn, other, 3)),
            (second, pieces[2:], (0, other, turn, 3)),
        ):
            for i in range(4):
                block = pairs[i // 2][i % 2 * rows : (i % 2 + 1) * rows, :]
                target[window(spot_ref[1] ^ bits[i], rows), :] = block
    act_ref, pre_ref, sum_ref, back_ref, ffn_ref = outs
    ffn_side(
        normed_ref, low_ref, bias_lines(pack_ref, row)[1], first, second,
        halves(spot_ref, first.shape[0]), act_ref, pre_ref, sum_ref, back_near, ffn_near,
        back_ref, ffn_ref,
    )


def ffn_grads_kernel(
    spot_ref, normed_ref, low_ref, act_n, pre_n, act_f, pre_f, kept_ref, *given
):
    hidden = act_n.shape[1]
    one, two = halves(spot_ref, normed_ref.shape[1] // 2)
    for columns in (two, one):
        normed, low = normed_ref[:, columns], low_ref[:, columns]
        for i, (left, right) in enumerate(((normed, pre_n), (low, act_n), (normed, pre_f), (low, act_f))):
            grads = dot_tn(left, right[...])
            if columns is one:
                kept_ref[:, i * hidden : (i + 1) * hidden] = grads
            else:
                given[i][...] = grads.astype(BF16)


def resid_part(
    spot_ref, mine_ref, got_ref, resid_ref, cotan_ref, lines_ref, grad_ref, low_ref, rows_ref,
    work_ref,
):
    half = resid_ref.shape[0] // 2
    mine = window(spot_ref[2] % 2, half)
    span = resid_ref.shape[0]
    grad = mine_ref[:span, :].astype(F32) + got_ref[:span, :].astype(F32)
    hat, inverse = norm_parts(resid_ref[...])
    resid_grad = cotan_ref[...] + norm_back(grad, hat, inverse, lines_ref[2:3, :])
    grad_ref[...] = resid_grad
    low_ref[...] = resid_grad.astype(BF16)
    work_ref[0] = grad * hat
    work_ref[1] = grad
    sums = [work_ref[0, mine, :], work_ref[1, mine, :], grad_ref[mine, :], cotan_ref[mine, :]]
    rows_ref[...] = jnp.concatenate([column_sum(v) for v in sums], axis=0)


def attend_backward(spot_ref, seg_ref, q_ref, grad, lse_ref, kvs, dq_ref, outs, side):
    span, width = q_ref.shape
    biases = mask_biases(spot_ref, seg_ref, span)
    query = q_ref[...]
    dq, dks, dvs = None, [None] * 4, [None] * 4
    for head in range(width // HEAD_DIM):
        mine = lane_mask((span, width), head)
        masked_q = jnp.where(mine, query, jnp.zeros_like(query))
        masked_g = jnp.where(mine, grad, jnp.zeros_like(grad))
        lse = lse_ref[:, head * HEAD_DIM : head * HEAD_DIM + 1]
        probs = [
            jnp.exp(dot_nt(masked_q, kv[:span, :width]) * SCALE + bias - lse)
            for kv, bias in zip(kvs, biases)
        ]
        grads = [dot_nt(masked_g, kv[:span, width:]) for kv in kvs]
        inner = total([jnp.sum(p * g, axis=-1, keepdims=True) for p, g in zip(probs, grads)])
        raws = [(p * (g - inner) * SCALE).astype(BF16) for p, g in zip(probs, grads)]
        head_dq = total([dot_nn(raw, kv[:span, :width]) for raw, kv in zip(raws, kvs)])
        dq = head_dq if head == 0 else jnp.where(mine, head_dq, dq)
        for step in range(4):
            head_dk = dot_tn(raws[step], query)
            head_dv = dot_tn(probs[step].astype(BF16), grad)
            dks[step] = head_dk if head == 0 else jnp.where(mine, head_dk, dks[step])
            dvs[step] = head_dv if head == 0 else jnp.where(mine, head_dv, dvs[step])
    dq_ref[:, side * width : (side + 1) * width] = dq
    at = 2 * side * width
    for step in range(4):
        outs[step][:span, at : at + width] = dks[step].astype(outs[step].dtype)
        outs[step][:span, at + width : at + 2 * width] = dvs[step].astype(outs[step].dtype)


def pull_kernel(
    spot_ref, seg_ref, q_n, lse_n, n0, n1, n2, n3, q_f, lse_f, f0, f1, f2, f3,
    mine_ref, got_ref, resid_ref, cotan_ref, lines_ref, one_n, two_n, one_f, two_f,
    dq_ref, own_ref, out1, out2, out3, grad_ref, low_ref, rows_ref, work_ref,
):
    size = low_ref.shape[1] // 2
    resid_part(
        spot_ref, mine_ref, got_ref, resid_ref, cotan_ref, lines_ref, grad_ref, low_ref, rows_ref,
        work_ref,
    )
    one, two = halves(spot_ref, size)
    outs = (own_ref, out1, out2, out3)
    near = (q_n, lse_n, (n0, n1, n2, n3), one_n, two_n)
    far = (q_f, lse_f, (f0, f1, f2, f3), one_f, two_f)
    for side, (q_ref, lse_ref, kvs, first, second) in enumerate((near, far)):
        grad = dot_nn(low_ref[:, one], out_part(first, size))
        grad = grad + dot_nn(low_ref[:, two], out_part(second, size))
        attend_backward(
            spot_ref, seg_ref, q_ref, grad.astype(BF16), lse_ref, kvs, dq_ref, outs, side
        )
    for out_ref in (out1, out2, out3):
        clear_below(out_ref, q_n.shape[0])


def input_kernel(
    spot_ref, stream_ref, lines_ref, rows_ref, up_near, up_far, dq_ref, own_ref, g1, g2, g3,
    one_n, two_n, one_f, two_f, normed_ref, low_ref, near_ref, far_ref,
    given_ref, small_ref, w_kept_ref, w_near_ref, w_far_ref, pulled_ref, terms_ref,
):
    span, width = stream_ref.shape
    cols = dq_ref.shape[1] // 2
    size = width // 2
    shard, slot = spot_ref[2], spot_ref[3]
    far = shard ^ 2
    one, two = halves(spot_ref, size)
    small_ref[...] = jnp.zeros_like(small_ref)
    parts = [ref[:span, :].astype(F32) for ref in (g1, g2, g3)]
    got = (own_ref[...] + parts[0]) + (parts[1] + parts[2])
    for side, (place, up_sum) in enumerate(((shard, up_near), (far, up_far))):
        dq = dq_ref[:, side * cols : (side + 1) * cols]
        dkv = got[:, 2 * side * cols : 2 * (side + 1) * cols]
        at = side * 3 * cols
        pulled_ref[:, at : at + cols] = dq.astype(BF16)
        pulled_ref[:, at + cols : at + 3 * cols] = dkv.astype(BF16)
        small_ref[6:7, window(place, cols)] = column_sum(dq)
        small_ref[7:8, window(place, cols)] = column_sum(dkv[:, cols:])
        small_ref[pl.ds(8 + place, 1), :] = up_sum[...]
    for columns, near_w, far_w in ((one, one_n, one_f), (two, two_n, two_f)):
        back = dot_nt(pulled_ref[:, : 3 * cols], near_w[:size, : 3 * cols])
        back = back + dot_nt(pulled_ref[:, 3 * cols :], far_w[:size, : 3 * cols])
        terms_ref[:, columns] = back
    back = terms_ref[...]
    hat, inverse = norm_parts(stream_ref[...])
    small_ref[0:1, :] = column_sum(back * hat)
    small_ref[1:2, :] = column_sum(back)
    small_ref[2:6, :] = rows_ref[...]
    grad = norm_back(back, hat, inverse, lines_ref[0:1, :])
    small_ref[pl.ds(12 + slot, 1), :] = column_sum(grad) + rows_ref[2:3, :]
    given_ref[...] = grad.astype(BF16)
    given = (w_near_ref, w_far_ref)
    for columns in (two, one):
        normed, low = normed_ref[:, columns], low_ref[:, columns]
        for side, mixed in enumerate((near_ref, far_ref)):
            at, start = side * 3 * cols, side * 4 * cols
            qkv = dot_tn(normed, pulled_ref[:, at : at + 3 * cols])
            out = dot_tn(low, mixed[...])
            if columns is one:
                w_kept_ref[:, start : start + 3 * cols] = qkv
                w_kept_ref[:, start + 3 * cols : start + 4 * cols] = out
            else:
                given[side][:size, : 3 * cols] = qkv.astype(BF16)
                given[side][:size, 3 * cols :] = out.astype(BF16)
    w_near_ref[size:, :], w_far_ref[size:, :] = split_two(small_ref[...])


def turn_bits(spot_ref):
    return 1 + spot_ref[0], 2 - spot_ref[0]


def split_two(values):
    high = values.astype(BF16)
    return high, (values - high.astype(F32)).astype(BF16)


def both(high, low):
    return high.astype(F32) + low.astype(F32)


def cut_kernel(spot_ref, kept_ref, *refs):
    got, (own_ref, send_ref) = refs[:4], refs[4:]
    rows, width = own_ref.shape[0] // 2, got[0].shape[1]
    chunk = spot_ref[1]
    first, second = turn_bits(spot_ref)
    for spot, place in enumerate((chunk, chunk ^ second)):
        to = slice(spot * rows, (spot + 1) * rows)
        for i, piece in enumerate(got):
            columns = slice(i * width, (i + 1) * width)
            at = window(place, rows)
            own_ref[to, columns] = kept_ref[at, columns] + piece[at, :].astype(F32)
            at = window(place ^ first, rows)
            values = kept_ref[at, columns] + piece[at, :].astype(F32)
            send_ref[to, columns] = values.astype(BF16)


def middle_kernel(
    spot_ref, kept_ref, got_ref, base_ref, own_terms, got_terms, near_ref, send_ref, out_ref
):
    rows, width = near_ref.shape
    span = base_ref.shape[0]
    values = kept_ref[...] + got_ref[...].astype(F32)
    near_ref[...] = values[:, :width]
    terms = own_terms[:span, :].astype(F32) + got_terms[:span, :].astype(F32)
    out_ref[...] = (base_ref[...] + terms).astype(BF16)
    send_ref[: span // 2, :] = out_ref[window(spot_ref[2] % 2, span // 2), :]
    half = send_ref.shape[1]
    for i in range(width // half):
        at = span // 2 + i * rows
        columns = slice(width + i * half, width + (i + 1) * half)
        send_ref[at : at + rows, :] = values[:, columns].astype(BF16)


def settle_kernel(spot_ref, near_ref, got_ref, out_ref, own_ref, send_ref):
    rows, width = own_ref.shape
    span = out_ref.shape[0]
    out_ref[...] = got_ref[:span, :]
    half = got_ref.shape[1]
    for i in range(width // half):
        at, columns = span + 2 * i * rows, slice(i * half, (i + 1) * half)
        own_ref[:, columns] = near_ref[:rows, columns] + got_ref[at : at + rows, :].astype(F32)
        more = near_ref[rows:, columns] + got_ref[at + rows : at + 2 * rows, :].astype(F32)
        send_ref[:, columns] = more.astype(BF16)


def rows_kernel(spot_ref, own_ref, one_ref, two_ref, in_own, in_got, out_ref, in_ref):
    pair, bit, span = spot_ref[2] // 2, spot_ref[2] % 2, own_ref.shape[0]
    half = span // 2
    out_ref[window(pair, span), :] = own_ref[...].astype(F32)
    out_ref[window(2 * (1 - pair) + bit, half), :] = one_ref[...].astype(F32)
    out_ref[window(2 * (1 - pair) + 1 - bit, half), :] = two_ref[...].astype(F32)
    in_ref[window(pair, span), :] = in_own[...].astype(F32)
    in_ref[window(1 - pair, span), :] = in_got[...].astype(F32)


def cut_small_kernel(
    spot_ref, kept_ref, got_near, got_far, small_ref, own_ref, o1, o2, o3, sum_ref
):
    rows, width = own_ref.shape[0], small_ref.shape[1]
    whole = kept_ref.shape[0]
    for bits, out_ref in enumerate((own_ref, o1, o2, o3)):
        at = window(spot_ref[1] ^ bits, rows)
        for side, got_ref in enumerate((got_near, got_far)):
            columns = slice(side * width, (side + 1) * width)
            values = kept_ref[at, columns] + got_ref[at, :].astype(F32)
            out_ref[:rows, columns] = values.astype(out_ref.dtype)
    mine = both(*split_two(small_ref[...]))
    high, low = split_two(mine + both(got_near[whole:, :], got_far[whole:, :]))
    for out_ref in (o1, o2, o3):
        out_ref[rows:, :width] = high
        out_ref[rows:, width:] = low
    sum_ref[...] = both(high, low)


def shards_small_kernel(spot_ref, own_ref, g1, g2, g3, small_ref, kept_ref, send_ref):
    rows, width = kept_ref.shape
    got = [piece[:rows, :].astype(F32) for piece in (g1, g2, g3)]
    values = (own_ref[...] + got[0]) + (got[1] + got[2])
    kept_ref[...] = values[:, :width]
    send_ref[:rows, :] = values[:, width:].astype(BF16)
    count = small_ref.shape[0]
    got = [both(piece[rows:, :width], piece[rows:, width:]) for piece in (g1, g2, g3)]
    high, low = split_two((small_ref[...] + got[0]) + (got[1] + got[2]))
    send_ref[rows : rows + count, :] = high
    send_ref[rows + count :, :] = low


def owned_kernel(
    spot_ref, ffn_kept, ffn_got, kept_ref, sent_ref, got_ref, out_ref, small_ref
):
    rows, width = ffn_kept.shape
    out_ref[:, :width] = (ffn_kept[...] + ffn_got[...].astype(F32)).astype(BF16)
    out_ref[:, width:] = (kept_ref[...] + got_ref[:rows, :].astype(F32)).astype(BF16)
    count = small_ref.shape[0]
    top, end = slice(rows, rows + count), slice(rows + count, rows + 2 * count)
    mine = both(sent_ref[top, :], sent_ref[end, :])
    small_ref[...] = mine + both(got_ref[top, :], got_ref[end, :])


def own_kernel(spot_ref, p0, p1, p2, p3, up_ref, down_ref, qkv_ref, out_ref):
    rows, hidden, cols = p0.shape[0], up_ref.shape[1], out_ref.shape[1]
    for bits, piece in enumerate((p0, p1, p2, p3)):
        at = window(spot_ref[1] ^ bits, rows)
        up_ref[at, :] = piece[:, :hidden].astype(F32)
        down_ref[at, :] = piece[:, hidden : 2 * hidden].astype(F32)
        start = 2 * hidden
        for i in range(3):
            qkv_ref[i, at, :] = piece[:, start + i * cols : start + (i + 1) * cols].astype(F32)
        out_ref[at, :] = piece[:, start + 3 * cols :].astype(F32)


def sums_kernel(spot_ref, steps_ref, own_ref, got_ref, table_ref, up_ref, qv_ref, *refs):
    lines, rows_ref = refs[:-1], refs[-1]
    cols = qv_ref.shape[1]
    shard = spot_ref[2]
    rows_ref[...] = own_ref[...] + got_ref[...]
    table_ref[...] = jnp.zeros_like(table_ref)
    for place in range(steps_ref.shape[0]):
        at = pl.ds(steps_ref[place], 1)
        table_ref[at, :] = table_ref[at, :] + rows_ref[12 + place : 13 + place, :]
    up_ref[...] = rows_ref[pl.ds(8 + shard, 1), :]
    qv_ref[...] = rows_ref[6:8, window(shard, cols)]
    for i, line_ref in enumerate(lines):
        line_ref[...] = rows_ref[i : i + 1, :]


class Reduction:
    def __init__(self, order, kept, small):
        self.order, self.kept, self.small = order, kept, small
        self.rows, self.width = kept.shape[0] // 4, kept.shape[1]

    def cut(self, got):
        rows, width, more = self.rows, self.width, self.small.shape[0]
        self.own, *cuts, self.small = self.order.call(
            cut_small_kernel,
            [((rows, width), F32)]
            + [((rows + more, width), BF16)] * 3
            + [(self.small.shape, F32)],
            [self.kept, *got, self.small],
        )
        self.got = [self.order.swap(cuts[bits - 1], "ctx", bits) for bits in (1, 2, 3)]

    def shards(self):
        rows, width, more = self.rows, self.width // 2, 2 * self.small.shape[0]
        self.own, self.sent = self.order.call(
            shards_small_kernel,
            [((rows, width), F32), ((rows + more, width), BF16)],
            [self.own, *self.got, self.small],
        )
        self.got = self.order.swap(self.sent, "tp", 2)


def reduce_plainly(kept, given, chunk):
    whole = jnp.concatenate([kept, given.astype(F32)])
    mine = lax.psum_scatter(whole, "fsdp", scatter_dimension=0, tiled=True)
    quarter = lax.psum_scatter(mine, "ctx", scatter_dimension=0, tiled=True)
    width = quarter.shape[1] // 2
    far = lax.ppermute(quarter[:, width:], "tp", [(i, i ^ 2) for i in range(4)])
    return lax.all_gather(quarter[:, :width] + far, "ctx", axis=0, tiled=True)


def pieces_of(order, part, parts, rows):
    if parts == 2:
        return part, order.swap(part, "fsdp", 1)
    whole = lax.all_gather(part[:rows], "fsdp", axis=0, tiled=True)
    size = whole.shape[0] // 2
    return whole[:size], whole[size:]


def per_device(
    layer_input,
    timesteps,
    segment_ids,
    time_table,
    ln1_gain,
    ln1_bias,
    w_qkv,
    b_qv,
    w_out_t,
    b_out,
    ln2_gain,
    ln2_bias,
    w_up,
    b_up,
    w_down_t,
    b_down,
    out_grad,
    *,
    parts,
):
    span, width = layer_input.shape[1:]
    rows, cols = w_qkv.shape[1:]
    hidden = w_up.shape[1]
    size = width // 2
    core = lax.axis_index("fsdp")
    chunk = lax.axis_index("ctx")
    shard = lax.axis_index("tp")
    place = core if parts == 2 else 0 * core
    spot = jnp.stack([place, chunk, shard, 2 * core + shard // 2]).astype(jnp.int32)
    order = Order(spot, parts)
    line = lambda values: values.reshape(1, -1)
    dma = lambda count: pltpu.SemaphoreType.DMA((count,))

    pack, rest, quarter = order.call(
        pack_kernel,
        [
            ((rows + BIAS_ROWS, 4 * cols), BF16), ((rows, 2 * hidden), BF16),
            ((rows // 4 + PAD * (parts == 2), 2 * hidden), BF16),
        ],
        [timesteps, w_qkv, w_out_t, b_qv, line(b_up), w_up, w_down_t],
        far=range(7),
        scratch=[
            pltpu.VMEM(w_qkv.shape, F32),
            pltpu.VMEM(w_out_t.shape, F32),
            pltpu.VMEM(b_qv.shape, F32),
            pltpu.VMEM((1, hidden), F32),
            pltpu.VMEM(w_up.shape, F32),
            pltpu.VMEM(w_down_t.shape, F32),
            dma(6),
        ],
    )
    near = pieces_of(order, pack, parts, rows)
    pack_far = order.swap(pack, "tp", 2)
    stream, normed, seg, lines, cotan = order.call(
        stream_kernel,
        [
            ((span, width), F32), ((span, width), BF16), ((1, segment_ids.shape[1]), jnp.int32),
            ((8, width), F32), ((span, width), F32),
        ],
        [timesteps, layer_input, time_table, segment_ids, out_grad]
        + [line(v) for v in (ln1_gain, ln1_bias, ln2_gain, ln2_bias, b_out, b_down)],
        far=range(11),
        scratch=[
            pltpu.VMEM((span, width), F32),
            pltpu.VMEM((8, width), F32),
            pltpu.VMEM(segment_ids.shape, jnp.int32),
            pltpu.VMEM((6, 1, width), F32),
            dma(10),
        ],
    )
    projected = [((span, cols), BF16), ((span, 2 * cols), BF16)]
    more = [((span, cols), BF16), ((span + PAD, 2 * cols), BF16)]
    project = functools.partial(project_kernel, row=rows)
    q_near, kv_near = order.call(project, projected, [normed, *near, pack])
    kvs_near = [kv_near] + order.swap_three(kv_near, "ctx")
    rest_far = order.swap(quarter if parts == 2 else rest, "tp", 2)
    rest_near = pieces_of(order, rest, parts, rows)

    attended = [((span, cols), BF16), ((span, cols), F32)]
    pack_far, *kvs_near[1:] = hold(pack_far, *kvs_near[1:])
    far = pieces_of(order, pack_far, parts, rows)
    mixed_near, lse_near = order.call(
        attend_one_kernel, attended, [seg, q_near, *kvs_near], cost=QUICK
    )
    q_far, kv_far = order.call(project, more, [normed, *far, pack_far], cost=QUICK)
    kvs_far = [kv_far] + order.swap_three(kv_far, "ctx")
    if parts == 2:
        rest_turn = order.swap_turn(rest_far, 0)
    mixed_far, lse_far, given = order.call(
        attend_two_kernel,
        attended + [((span + PAD, width), BF16)],
        [seg, q_far, *kvs_far, mixed_near, *near, *far],
    )
    got = order.swap(given, "tp", 1)
    if parts == 2:
        rest_one = order.call(
            stack_kernel, [((rows // 2, 2 * hidden), BF16)], [rest_far, rest_turn], cost=QUICK
        )[0]
        rest_two = order.swap_turn(rest_one, 1)
        rest_far = [
            rest_one, rest_two, order.swap(rest_one, "fsdp", 1), order.swap(rest_two, "fsdp", 1)
        ]
    else:
        rest_far = pieces_of(order, rest_far, parts, rows)

    acts = [((span, hidden), BF16), ((span, hidden), BF16)]
    back_near, ffn_near, out_base, resid, normed_two, act_n, pre_n, low, up_near = order.call(
        functools.partial(ffn_near_kernel, row=rows),
        [((span, width), F32)] * 4
        + [((span, width), BF16), *acts, ((span, width), BF16), ((1, hidden), F32)],
        [stream, given, got, cotan, lines, pack, *rest_near],
    )
    act_f, pre_f, up_far, back, ffn_terms = order.call(
        functools.partial(ffn_far_kernel, row=rows),
        [*acts, ((1, hidden), F32), ((span + PAD, width), BF16), ((span, width), BF16)],
        [normed_two, low, back_near, ffn_near, pack_far, *rest_far],
        scratch=[pltpu.VMEM((size, 2 * hidden), BF16)] * 2,
    )
    back_got = order.swap(back, "tp", 1)
    ffn_kept, *ffn_sent = order.call(
        ffn_grads_kernel,
        [((size, 4 * hidden), F32)] + [((size, hidden), BF16)] * 4,
        [normed_two, low, act_n, pre_n, act_f, pre_f],
    )
    if parts == 2:
        ffn_got = [order.swap(piece, "fsdp", 1) for piece in ffn_sent]
        ffn_own, ffn_cut = order.call(
            cut_kernel,
            [((rows // 2, 4 * hidden), F32), ((rows // 2, 4 * hidden), BF16)],
            [ffn_kept, *ffn_got],
            cost=QUICK,
        )
        ffn_turn = order.swap_turn(ffn_cut, 0)
    dq, own, *shares, resid_grad, low_all, resid_rows = order.call(
        pull_kernel,
        [((span, 2 * cols), F32), ((span, 4 * cols), F32)]
        + [((span + PAD, 4 * cols), BF16)] * 3
        + [((span, width), F32), ((span, width), BF16), ((4, width), F32)],
        [
            seg, q_near, lse_near, *kvs_near, q_far, lse_far, *kvs_far, back, back_got, resid,
            cotan, lines, *near, *far,
        ],
        scratch=[pltpu.VMEM((2, span, width), F32)],
        limit=6,
    )
    shared = [order.swap(shares[bits - 1], "ctx", bits) for bits in (1, 2, 3)]

    terms_got = order.swap(ffn_terms, "tp", 1)
    if parts == 2:
        ffn_near, sent, out_low = order.call(
            middle_kernel,
            [
                ((rows // 2, 2 * hidden), F32), ((span // 2 + rows, width), BF16),
                ((span, width), BF16),
            ],
            [ffn_own, ffn_turn, out_base, ffn_terms, terms_got],
            cost=QUICK,
        )
        sent_got = order.swap(sent, "tp", 2)
    else:
        out_low = order.call(
            add_pair_kernel, [((span, width), BF16)], [out_base, ffn_terms, terms_got]
        )[0]
        out_got = order.swap(out_low, "tp", 2)

    seqs = 2 * parts
    small_rows = -(-(12 + seqs) // 16) * 16
    in_terms, small, attention_kept, *attention_sent = order.call(
        input_kernel,
        [
            ((span, width), BF16), ((small_rows, width), F32),
            ((size, 8 * cols), F32), ((size + small_rows, 4 * cols), BF16),
            ((size + small_rows, 4 * cols), BF16),
        ],
        [
            stream, lines, resid_rows, up_near, up_far, dq, own, *shared, *near, *far,
            normed, low_all, mixed_near, mixed_far,
        ],
        scratch=[pltpu.VMEM((span, 6 * cols), BF16), pltpu.VMEM((span, width), F32)],
    )
    order.cost = QUICK
    if parts == 2:
        attention_far = [order.swap(piece, "fsdp", 1) for piece in attention_sent]
    in_got = order.swap(in_terms, "tp", 1)
    if parts == 2:
        attention_sum = Reduction(order, attention_kept, small)
        attention_sum.cut(attention_far)
        out_half, ffn_own, ffn_cut = order.call(
            settle_kernel,
            [
                ((span // 2, width), BF16), ((rows // 4, 2 * hidden), F32),
                ((rows // 4, 2 * hidden), BF16),
            ],
            [ffn_near, sent_got],
            cost=COST,
        )
        ffn_turn = order.swap_turn(ffn_cut, 1)
        out_more = order.swap(out_half, "tp", 1)
        attention_sum.shards()
    else:
        output = order.call(pair_kernel, [((2 * span, width), F32)], [out_low, out_got])[0]
    in_low = order.call(
        add_pair_kernel, [((span, width), BF16)], [resid_grad, in_terms, in_got]
    )[0]
    in_far = order.swap(in_low, "tp", 2)
    if parts == 2:
        attention = attention_sum
        owned, small = order.call(
            owned_kernel,
            [((rows // 4, 2 * hidden + 4 * cols), BF16), (small.shape, F32)],
            [ffn_own, ffn_turn, attention.own, attention.sent, attention.got],
        )
        small_got = order.swap(small, "tp", 1)
        pieces = [owned] + order.swap_three(owned, "ctx")
    if parts == 2:
        output, grad_input = order.call(
            rows_kernel,
            [((2 * span, width), F32)] * 2,
            [out_low, out_half, out_more, in_low, in_far],
        )
    else:
        grad_input = order.call(pair_kernel, [((2 * span, width), F32)], [in_low, in_far])[0]
    if parts == 2:
        bits = near[1][rows : rows + 9 : 3, 2 * cols : 2 * cols + 2].astype(F32)
        far_steps = jnp.sum(bits, axis=0).astype(jnp.int32)
        steps = jnp.where(
            core == 0,
            jnp.concatenate([timesteps, far_steps]),
            jnp.concatenate([far_steps, timesteps]),
        )
    else:
        ffn_sent = jnp.concatenate(ffn_sent, axis=1)
        both_grads = reduce_plainly(ffn_kept, ffn_sent, chunk)
        grads_up, grads_down = both_grads[:, :hidden], both_grads[:, hidden:]
        small = lax.psum(small, ("fsdp", "ctx", "tp"))
        small_got = jnp.zeros_like(small)
        steps = lax.all_gather(timesteps, "fsdp", axis=0, tiled=True)
    table, up_line, qv_lines, *sums = order.call(
        sums_kernel,
        [(time_table.shape, F32), ((1, hidden), F32), ((2, cols), F32)] + [((1, width), F32)] * 6,
        [steps, small, small_got],
        scratch=[pltpu.VMEM(small.shape, F32)],
    )
    sums = [values.reshape(-1) for values in sums]
    if parts == 2:
        grads_up, grads_down, grads_qkv, grads_out = order.call(
            own_kernel,
            [((rows, hidden), F32)] * 2 + [((3, rows, cols), F32), ((rows, cols), F32)],
            pieces,
        )
    else:
        attention_sent = jnp.concatenate(attention_sent, axis=1)[:size]
        every = reduce_plainly(attention_kept, attention_sent, chunk)
        grads_qkv = jnp.stack([every[:, i * cols : (i + 1) * cols] for i in range(3)])
        grads_out = every[:, 3 * cols :]

    shape = layer_input.shape
    return (
        output.reshape(shape),
        grad_input.reshape(shape),
        table,
        sums[0],
        sums[1],
        grads_qkv,
        qv_lines,
        grads_out,
        sums[4],
        sums[2],
        sums[3],
        grads_up,
        up_line.reshape(-1),
        grads_down,
        sums[5],
    )


def solution(mesh):
    placed = (
        P("fsdp", "ctx", None),
        P("fsdp"),
        P("fsdp", None),
        P(),
        P(),
        P(),
        P(None, "fsdp", "tp"),
        P(None, "tp"),
        P("fsdp", "tp"),
        P(),
        P(),
        P(),
        P("fsdp", "tp"),
        P("tp"),
        P("fsdp", "tp"),
        P(),
        P("fsdp", "ctx", None),
    )
    return jax.shard_map(
        functools.partial(per_device, parts=mesh.shape["fsdp"]),
        mesh=mesh,
        in_specs=placed,
        out_specs=(
            P("fsdp", "ctx", None),
            P("fsdp", "ctx", None),
            P(),
            P(),
            P(),
            P(None, "fsdp", "tp"),
            P(None, "tp"),
            P("fsdp", "tp"),
            P(),
            P(),
            P(),
            P("fsdp", "tp"),
            P("tp"),
            P("fsdp", "tp"),
            P(),
        ),
        check_vma=False,
    )
```

time: 142 us -> 123 us (0.87)
  local copies, waits for them, and re-layouts: 8.89 us -> 0.03 us
  Pallas kernels: 39.6 us -> 33.1 us
  waiting for transfers between devices: 54.7 us -> 51.2 us
  starting transfers between devices: 36 us -> 37.6 us
    unnamed x80 -> x2, local copies, waits for them, and re-layouts: 8.26 us -> 0.01 us
    pallas_call x30 -> x22, Pallas kernels: 39.6 us -> 33.1 us  [call(): pl.pallas_call(body, out_shape=tuple((jax.ShapeDtypeStruct(shape, dtype)...]
    ppermute x34 -> x37, starting transfers between devices: 28.4 us -> 31.5 us  [swap(): return lax.ppermute(values, axis, [(i, i ^ bits) for i in range(size)])]
    ppermute x34 -> x37, waiting for transfers between devices: 49 us -> 46.3 us  [swap(): return lax.ppermute(values, axis, [(i, i ^ bits) for i in range(size)])]
    ppermute x8 -> x4, starting transfers between devices: 7.55 us -> 6.07 us  [swap_turn(): return lax.ppermute(values, ('fsdp', 'ctx'), pairs)]
    ppermute x8 -> x4, waiting for transfers between devices: 5.77 us -> 4.86 us  [swap_turn(): return lax.ppermute(values, ('fsdp', 'ctx'), pairs)]
  transfers between devices with their start and end apart: 42 -> 41, of which waited for: 20 -> 22; matrix products, arithmetic and copies ran while one was open for 1% -> 0% of each run, Pallas kernels for 24% -> 22%
where the time goes in v3:
time: 123 us
  waiting for transfers between devices  51.2 us (42%)
  starting transfers between devices  37.6 us (31%)
  Pallas kernels  33.1 us (27%)
    ppermute x37, waiting for transfers between devices, swap(): return lax.ppermute(values, axis, [(i, i ^ bits) for i in range(size)])  46.3 us
    pallas_call x22, Pallas kernels, call(): pl.pallas_call(body, out_shape=tuple((jax.ShapeDtypeStruct(shape, dtype)...  33.1 us
    ppermute x37, starting transfers between devices, swap(): return lax.ppermute(values, axis, [(i, i ^ bits) for i in range(size)])  31.5 us
    ppermute x4, starting transfers between devices, swap_turn(): return lax.ppermute(values, ('fsdp', 'ctx'), pairs)  6.07 us
    ppermute x4, waiting for transfers between devices, swap_turn(): return lax.ppermute(values, ('fsdp', 'ctx'), pairs)  4.86 us
  transfers between devices with their start and end apart: 41, of which 22 were waited for; matrix products, arithmetic and copies ran while one was open for 0% of the time, Pallas kernels for 22%

profile of v3, /device:TPU:0, one launch (start us, length us, event | category | flops | bytes accessed | tf_op | source)
XLA Modules:
  0.0 123.0 jit_solution(7414849187933076631)
XLA Ops:
  0.7 2.2 %shard_map.280 = (bf16[272,512]{1,0:T(8,128)(2,1)S(1)}, bf16[256,1024]{1,0:T(8,128)(2,1)S(1)}, bf16[80,1024]{1,0:T(8,128)(2,1)S(1)}) custom-call(s32[2]{0:T(128)} %refs_0_.3, f32[3,256,128]{2,1,0:T(8,128)} %refs_1_.2, f32[256,128]{1,0:T(8,128)} %refs_2_.2, f32[2,128]{1,0:T(2,128)} %refs_3_.2, f32[1,512]{1,0:T(1,128)} %bitcast.22, f32[256,512]{1,0:T(8,128)} %refs_5_.1, ...), custom_call_target="tpu_custom_call" | custom-call | flops 8000000000 | bytes 65536 | tf_op jit(solution)/shard_map/pallas_call | solution.py:89
  3.0 0.5 collective-permute-start.1
  3.5 3.7 %collective-permute-start = (bf16[272,512]{1,0:T(8,128)(2,1)S(1)}, bf16[272,512]{1,0:T(8,128)(2,1)S(1)}, u32[]{:S(2)}, u32[]{:S(2)}) collective-permute-start(bf16[272,512]{1,0:T(8,128)(2,1)S(1)} %get-tuple-element.231.refs_1_.refs_3_.refs_7_.refs_5_.refs_18_.refs_10_), channel_id=1, source_target_pairs={{0,2},{1,3},{2,0},{3,1},{4,6},{5,7},{6,4},{7,5},{8,10},{9,11},{10,... | collective-permute-start | bytes 835592 | tf_op jit(solution)/shard_map/swap_tp_2/ppermute | solution.py:107
  7.2 2.3 %shard_map.281 = (f32[256,512]{1,0:T(8,128)S(1)}, bf16[256,512]{1,0:T(8,128)(2,1)S(1)}, s32[1,1024]{1,0:T(1,128)S(1)}, f32[8,512]{1,0:T(8,128)S(1)}, f32[256,512]{1,0:T(8,128)S(1)}) custom-call(s32[2]{0:T(128)} %refs_0_.3, f32[2,256,512]{2,1,0:T(8,128)} %refs_1_.3, f32[1000,512]{1,0:T(8,128)} %refs_2_.3, s32[2,1024]{1,0:T(2,128)} %refs_3_.3, ...), custom_call_target="tpu_custom_call" | custom-call | flops 8000000000 | bytes 65536 | tf_op jit(solution)/shard_map/pallas_call | solution.py:89
  9.5 0.8 shard_map.282
  10.3 2.5 %collective-permute-start.4 = (bf16[256,256]{1,0:T(8,128)(2,1)S(1)}, bf16[256,256]{1,0:T(8,128)(2,1)S(1)}, u32[]{:S(2)}, u32[]{:S(2)}) collective-permute-start(bf16[256,256]{1,0:T(8,128)(2,1)S(1)} %get-tuple-element.240.refs_2_.refs_3_), channel_id=1, source_target_pairs={{0,12},{4,8},{8,4},{12,0},{1,13},{5,9},{9,5},{13,1},{2,14},{6,10},... | collective-permute-start | bytes 393224 | tf_op jit(solution)/shard_map/swap_ctx_3/ppermute | solution.py:107
  12.8 0.5 collective-permute-start.3
  13.3 0.5 collective-permute-start.2
  13.9 6.5 %collective-permute-done.refs_1_.refs_3_.refs_9_.refs_4_.refs_20_.refs_12_ = bf16[272,512]{1,0:T(8,128)(2,1)S(1)} collective-permute-done((bf16[272,512]{1,0:T(8,128)(2,1)S(1)}, bf16[272,512]{1,0:T(8,128)(2,1)S(1)}, u32[]{:S(2)}, u32[]{:S(2)}) %collective-permute-start) | collective-permute-done | bytes 278560 | tf_op jit(solution)/shard_map/swap_tp_2/ppermute | solution.py:107
  20.6 1.9 %shard_map.283 = (bf16[256,128]{1,0:T(8,128)(2,1)S(1)}, f32[256,128]{1,0:T(8,128)S(1)}) custom-call(s32[1,1024]{1,0:T(1,128)S(1)} %get-tuple-element.228.refs_0_, bf16[256,128]{1,0:T(8,128)(2,1)S(1)} %get-tuple-element.248.refs_1_, bf16[256,256]{1,0:T(8,128)(2,1)S(1)} %get-tuple-element.240.refs_2_.refs_3_, ...), custom_call_target="tpu_custom_call" | custom-call | flops 1000 | bytes 65536 | tf_op jit(solution)/shard_map/pallas_call | solution.py:89
  22.5 0.8 shard_map.284
  23.3 2.6 %collective-permute-start.8 = (bf16[272,256]{1,0:T(8,128)(2,1)S(1)}, bf16[272,256]{1,0:T(8,128)(2,1)S(1)}, u32[]{:S(2)}, u32[]{:S(2)}) collective-permute-start(bf16[272,256]{1,0:T(8,128)(2,1)S(1)} %get-tuple-element.263.refs_2_.refs_9_), channel_id=1, source_target_pairs={{0,12},{4,8},{8,4},{12,0},{1,13},{5,9},{9,5},{13,1},{2,14},{6,10},... | collective-permute-start | bytes 417800 | tf_op jit(solution)/shard_map/swap_ctx_3/ppermute | solution.py:107
  25.9 0.5 collective-permute-start.7
  26.4 0.5 collective-permute-start.6
  26.9 4.6 %collective-permute-done.9.refs_0_ = bf16[80,1024]{1,0:T(8,128)(2,1)S(1)} collective-permute-done((bf16[80,1024]{1,0:T(8,128)(2,1)S(1)}, bf16[80,1024]{1,0:T(8,128)(2,1)S(1)}, u32[]{:S(2)}, u32[]{:S(2)}) %collective-permute-start.9) | collective-permute-done | bytes 163872 | tf_op jit(solution)/shard_map/swap_tp_2/ppermute | solution.py:107
  31.5 1.6 %collective-permute-start.12 = (bf16[80,1024]{1,0:T(8,128)(2,1)S(1)}, bf16[80,1024]{1,0:T(8,128)(2,1)S(1)}, u32[]{:S(2)}, u32[]{:S(2)}) collective-permute-start(bf16[80,1024]{1,0:T(8,128)(2,1)S(1)} %collective-permute-done.9.refs_0_), channel_id=1, source_target_pairs={{0,4},{4,0},{8,12},{12,8},{16,24},{20,28},{24,16},{28,20},{1,5},{5... | collective-permute-start | bytes 491528 | tf_op jit(solution)/shard_map/swap_turn_0/ppermute | solution.py:122
  33.5 2.2 %shard_map.285 = (bf16[256,128]{1,0:T(8,128)(2,1)S(1)}, f32[256,128]{1,0:T(8,128)S(1)}, bf16[272,512]{1,0:T(8,128)(2,1)S(1)}) custom-call(s32[1,1024]{1,0:T(1,128)S(1)} %get-tuple-element.228.refs_0_, bf16[256,128]{1,0:T(8,128)(2,1)S(1)} %get-tuple-element.256.refs_1_.refs_7_, bf16[272,256]{1,0:T(8,128)(2,1)S(1)} %get-tuple-element.263.refs_2_.refs_9_, ...), custom_call_target="tpu_custom_call" | custom-call | flops 8000000000 | bytes 65536 | tf_op jit(solution)/shard_map/pallas_call | solution.py:89
  35.6 3.8 %collective-permute-start.10 = (bf16[272,512]{1,0:T(8,128)(2,1)S(1)}, bf16[272,512]{1,0:T(8,128)(2,1)S(1)}, u32[]{:S(2)}, u32[]{:S(2)}) collective-permute-start(bf16[272,512]{1,0:T(8,128)(2,1)S(1)} %get-tuple-element.271.refs_1_), channel_id=1, source_target_pairs={{0,1},{1,0},{2,3},{3,2},{4,5},{5,4},{6,7},{7,6},{8,9},{9,8},{10,11... | collective-permute-start | bytes 835592 | tf_op jit(solution)/shard_map/swap_tp_1/ppermute | solution.py:107
  39.5 0.6 shard_map.286.refs_5_
  40.0 1.6 %collective-permute-start.13 = (bf16[128,1024]{1,0:T(8,128)(2,1)S(1)}, bf16[128,1024]{1,0:T(8,128)(2,1)S(1)}, u32[]{:S(2)}, u32[]{:S(2)}) collective-permute-start(bf16[128,1024]{1,0:T(8,128)(2,1)S(1)} %shard_map.286.refs_5_), channel_id=1, source_target_pairs={{0,8},{4,12},{8,0},{12,4},{16,20},{20,16},{24,28},{28,24},{1,9},{5... | collective-permute-start | bytes 786440 | tf_op jit(solution)/shard_map/swap_turn_1/ppermute | solution.py:122
  41.6 4.9 %collective-permute-done.13.refs_6_ = bf16[128,1024]{1,0:T(8,128)(2,1)S(1)} collective-permute-done((bf16[128,1024]{1,0:T(8,128)(2,1)S(1)}, bf16[128,1024]{1,0:T(8,128)(2,1)S(1)}, u32[]{:S(2)}, u32[]{:S(2)}) %collective-permute-start.13) | collective-permute-done | bytes 262176 | tf_op jit(solution)/shard_map/swap_turn_1/ppermute | solution.py:122
  46.5 1.9 %shard_map.287 = (f32[256,512]{1,0:T(8,128)S(1)}, f32[256,512]{1,0:T(8,128)S(1)}, f32[256,512]{1,0:T(8,128)S(1)}, f32[256,512]{1,0:T(8,128)S(1)}, bf16[256,512]{...) custom-call(f32[256,512]{1,0:T(8,128)S(1)} %get-tuple-element.227.re, ...), custom_call_target="tpu_custom_call" | custom-call | flops 8000000000 | bytes 65536 | tf_op jit(solution)/shard_map/pallas_call | solution.py:89
  48.4 1.6 %shard_map.288 = (bf16[256,512]{1,0:T(8,128)(2,1)S(1)}, bf16[256,512]{1,0:T(8,128)(2,1)S(1)}, f32[1,512]{1,0:T(1,128)S(1)}, bf16[272,512]{1,0:T(8,128)(2,1)S(1)}, bf16[256,512]{1,0:T(8,128)(2,1)S(1)}) custom-call(bf16[256,512]{1,0:T(8,128)(2,1)S(1)} %get-tuple-element.282.refs_0_, bf16[256,512]{1,0:T(8,128)(2,1)S(1)} %get-tuple-element.283.refs_1_, ...), custom_call_target="tpu_custom_call" | custom-call | flops 8000000000 | bytes 65536 | tf_op jit(solution)/shard_map/pallas_call | solution.py:89
  50.0 1.5 %collective-permute-start.21 = (bf16[272,512]{1,0:T(8,128)(2,1)S(1)}, bf16[272,512]{1,0:T(8,128)(2,1)S(1)}, u32[]{:S(2)}, u32[]{:S(2)}) collective-permute-start(bf16[272,512]{1,0:T(8,128)(2,1)S(1)} %get-tuple-element.322.refs_13_), channel_id=1, source_target_pairs={{0,1},{1,0},{2,3},{3,2},{4,5},{5,4},{6,7},{7,6},{8,9},{9,8},{10,11... | collective-permute-start | bytes 835592 | tf_op jit(solution)/shard_map/swap_tp_1/ppermute | solution.py:107
  51.5 1.3 %shard_map.289 = (f32[256,2048]{1,0:T(8,128)S(1)}, bf16[256,512]{1,0:T(8,128)(2,1)S(1)}, bf16[256,512]{1,0:T(8,128)(2,1)S(1)}, bf16[256,512]{1,0:T(8,128)(2,1)S(1)}, bf16[256,512]{1,0:T(8,128)(2,1)S(1)}) custom-call(bf16[256,512]{1,0:T(8,128)(2,1)S(1)} %get-tuple-element.282.refs_0_, bf16[256,512]{1,0:T(8,128)(2,1)S(1)} %get-tuple-element.283.refs_1_, ...), custom_call_target="tpu_custom_call" | custom-call | flops 8000000000 | bytes 65536 | tf_op jit(solution)/shard_map/pallas_call | solution.py:89
  52.9 0.5 collective-permute-start.18
  53.4 0.4 collective-permute-start.16
  53.9 0.5 collective-permute-done.19.refs_4_
  55.5 0.7 shard_map.290
  56.2 1.6 %collective-permute-start.20 = (bf16[128,2048]{1,0:T(8,128)(2,1)S(1)}, bf16[128,2048]{1,0:T(8,128)(2,1)S(1)}, u32[]{:S(2)}, u32[]{:S(2)}) collective-permute-start(bf16[128,2048]{1,0:T(8,128)(2,1)S(1)} %get-tuple-element.317), channel_id=1, source_target_pairs={{0,4},{4,0},{8,12},{12,8},{16,24},{20,28},{24,16},{28,20},{1,5},{5... | collective-permute-start | bytes 1572872 | tf_op jit(solution)/shard_map/swap_turn_0/ppermute | solution.py:122
  57.8 1.3 %collective-permute-done.21.refs_14_ = bf16[272,512]{1,0:T(8,128)(2,1)S(1)} collective-permute-done((bf16[272,512]{1,0:T(8,128)(2,1)S(1)}, bf16[272,512]{1,0:T(8,128)(2,1)S(1)}, u32[]{:S(2)}, u32[]{:S(2)}) %collective-permute-start.21) | collective-permute-done | bytes 278560 | tf_op jit(solution)/shard_map/swap_tp_1/ppermute | solution.py:107
  59.1 5.4 %shard_map.291 = (f32[256,256]{1,0:T(8,128)S(1)}, f32[256,512]{1,0:T(8,128)S(1)}, bf16[272,512]{1,0:T(8,128)(2,1)S(1)}, bf16[272,512]{1,0:T(8,128)(2,1)S(1)}, bf...) custom-call(s32[1,1024]{1,0:T(1,128)S(1)} %get-tuple-element.228.refs_, ...), custom_call_target="tpu_custom_call" | custom-call | flops 8000000000 | bytes 65536 | tf_op jit(solution)/shard_map/pallas_call | solution.py:89
  64.5 2.5 %collective-permute-start.26 = (bf16[272,512]{1,0:T(8,128)(2,1)S(1)}, bf16[272,512]{1,0:T(8,128)(2,1)S(1)}, u32[]{:S(2)}, u32[]{:S(2)}) collective-permute-start(bf16[272,512]{1,0:T(8,128)(2,1)S(1)} %get-tuple-element.348), channel_id=1, source_target_pairs={{0,12},{4,8},{8,4},{12,0},{1,13},{5,9},{9,5},{13,1},{2,14},{6,10},... | collective-permute-start | bytes 835592 | tf_op jit(solution)/shard_map/swap_ctx_3/ppermute | solution.py:107
  67.0 0.5 collective-permute-start.25
  67.5 0.5 collective-permute-start.24
  68.4 6.8 %collective-permute-done.22.refs_4_ = bf16[256,512]{1,0:T(8,128)(2,1)S(1)} collective-permute-done((bf16[256,512]{1,0:T(8,128)(2,1)S(1)}, bf16[256,512]{1,0:T(8,128)(2,1)S(1)}, u32[]{:S(2)}, u32[]{:S(2)}) %collective-permute-start.22) | collective-permute-done | bytes 262176 | tf_op jit(solution)/shard_map/swap_tp_1/ppermute | solution.py:107
  75.2 0.9 shard_map.292
  76.4 3.4 %collective-permute-done.25.refs_8_ = bf16[272,512]{1,0:T(8,128)(2,1)S(1)} collective-permute-done((bf16[272,512]{1,0:T(8,128)(2,1)S(1)}, bf16[272,512]{1,0:T(8,128)(2,1)S(1)}, u32[]{:S(2)}, u32[]{:S(2)}) %collective-permute-start.25) | collective-permute-done | bytes 278560 | tf_op jit(solution)/shard_map/swap_ctx_2/ppermute | solution.py:107
  79.8 1.7 %shard_map.293 = (bf16[256,512]{1,0:T(8,128)(2,1)S(1)}, f32[16,512]{1,0:T(8,128)S(1)}, f32[256,1024]{1,0:T(8,128)S(1)}, bf16[272,512]{1,0:T(8,128)(2,1)S(1)}, bf16[272,512]{1,0:T(8,128)(2,1)S(1)}) custom-call(f32[256,512]{1,0:T(8,128)S(1)} %get-tuple-element.227.refs_0_, f32[8,512]{1,0:T(8,128)S(1)} %get-tuple-element.273.refs_4_.refs_17_.refs_1_, ...), custom_call_target="tpu_custom_call" | custom-call | flops 8000000000 | bytes 65536 | tf_op jit(solution)/shard_map/pallas_call | solution.py:89
  81.6 0.5 collective-permute-start.27
  82.3 0.8 collective-permute-done.28.refs_2_
  83.1 0.4 collective-permute-done.27.refs_1_
  83.5 0.7 shard_map.294
  84.2 1.7 %collective-permute-start.33 = (bf16[80,1024]{1,0:T(8,128)(2,1)S(1)}, bf16[80,1024]{1,0:T(8,128)(2,1)S(1)}, u32[]{:S(2)}, u32[]{:S(2)}) collective-permute-start(bf16[80,1024]{1,0:T(8,128)(2,1)S(1)} %get-tuple-element.383), channel_id=1, source_target_pairs={{0,12},{4,8},{8,4},{12,0},{1,13},{5,9},{9,5},{13,1},{2,14},{6,10},... | collective-permute-start | bytes 491528 | tf_op jit(solution)/shard_map/swap_ctx_3/ppermute | solution.py:107
  85.9 1.3 %collective-permute-start.32 = (bf16[80,1024]{1,0:T(8,128)(2,1)S(1)}, bf16[80,1024]{1,0:T(8,128)(2,1)S(1)}, u32[]{:S(2)}, u32[]{:S(2)}) collective-permute-start(bf16[80,1024]{1,0:T(8,128)(2,1)S(1)} %get-tuple-element.382), channel_id=1, source_target_pairs={{0,8},{4,12},{8,0},{12,4},{1,9},{5,13},{9,1},{13,5},{2,10},{6,14},... | collective-permute-start | bytes 491528 | tf_op jit(solution)/shard_map/swap_ctx_2/ppermute | solution.py:107
  87.2 0.5 collective-permute-start.31
  87.7 6.6 %collective-permute-done.23.refs_1_ = bf16[384,512]{1,0:T(8,128)(2,1)S(1)} collective-permute-done((bf16[384,512]{1,0:T(8,128)(2,1)S(1)}, bf16[384,512]{1,0:T(8,128)(2,1)S(1)}, u32[]{:S(2)}, u32[]{:S(2)}) %collective-permute-start.23) | collective-permute-done | bytes 393248 | tf_op jit(solution)/shard_map/swap_tp_2/ppermute | solution.py:107
  94.4 0.6 shard_map.295
  95.0 1.4 %collective-permute-start.35 = (bf16[64,1024]{1,0:T(8,128)(2,1)S(1)}, bf16[64,1024]{1,0:T(8,128)(2,1)S(1)}, u32[]{:S(2)}, u32[]{:S(2)}) collective-permute-start(bf16[64,1024]{1,0:T(8,128)(2,1)S(1)} %get-tuple-element.393), channel_id=1, source_target_pairs={{0,8},{4,12},{8,0},{12,4},{16,20},{20,16},{24,28},{28,24},{1,9},{5... | collective-permute-start | bytes 393224 | tf_op jit(solution)/shard_map/swap_turn_1/ppermute | solution.py:122
  96.4 0.6 shard_map.296
  97.1 1.5 %collective-permute-done.30.refs_2_ = bf16[256,512]{1,0:T(8,128)(2,1)S(1)} collective-permute-done((bf16[256,512]{1,0:T(8,128)(2,1)S(1)}, bf16[256,512]{1,0:T(8,128)(2,1)S(1)}, u32[]{:S(2)}, u32[]{:S(2)}) %collective-permute-start.30) | collective-permute-done | bytes 262176 | tf_op jit(solution)/shard_map/swap_tp_1/ppermute | solution.py:107
  98.6 0.6 shard_map.297.refs_3_
  99.3 1.5 %collective-permute-start.34 = (bf16[256,512]{1,0:T(8,128)(2,1)S(1)}, bf16[256,512]{1,0:T(8,128)(2,1)S(1)}, u32[]{:S(2)}, u32[]{:S(2)}) collective-permute-start(bf16[256,512]{1,0:T(8,128)(2,1)S(1)} %shard_map.297.refs_3_), channel_id=1, source_target_pairs={{0,2},{1,3},{2,0},{3,1},{4,6},{5,7},{6,4},{7,5},{8,10},{9,11},{10,... | collective-permute-start | bytes 786440 | tf_op jit(solution)/shard_map/swap_tp_2/ppermute | solution.py:107
  100.7 8.9 %collective-permute-done.36.refs_4_ = bf16[96,512]{1,0:T(8,128)(2,1)S(1)} collective-permute-done((bf16[96,512]{1,0:T(8,128)(2,1)S(1)}, bf16[96,512]{1,0:T(8,128)(2,1)S(1)}, u32[]{:S(2)}, u32[]{:S(2)}) %collective-permute-start.36) | collective-permute-done | bytes 98336 | tf_op jit(solution)/shard_map/swap_tp_2/ppermute | solution.py:107
  109.7 0.6 shard_map.298
  110.3 1.2 collective-permute-start.40
  111.4 1.5 %collective-permute-start.39 = (bf16[64,1536]{1,0:T(8,128)(2,1)S(1)}, bf16[64,1536]{1,0:T(8,128)(2,1)S(1)}, u32[]{:S(2)}, u32[]{:S(2)}) collective-permute-start(bf16[64,1536]{1,0:T(8,128)(2,1)S(1)} %get-tuple-element.416.refs_0_), channel_id=1, source_target_pairs={{0,8},{4,12},{8,0},{12,4},{1,9},{5,13},{9,1},{13,5},{2,10},{6,14},... | collective-permute-start | bytes 589832 | tf_op jit(solution)/shard_map/swap_ctx_2/ppermute | solution.py:107
  112.9 0.9 collective-permute-start.38
  114.0 0.6 collective-permute-done.34.refs_4_
  114.7 2.0 %shard_map.299 = (f32[512,512]{1,0:T(8,128)}, f32[512,512]{1,0:T(8,128)}) custom-call(bf16[256,512]{1,0:T(8,128)(2,1)S(1)} %get-tuple-element.335.refs_0_, bf16[128,512]{1,0:T(8,128)(2,1)S(1)} %get-tuple-element.377.refs_1_, bf16[128,512]{1,0:T(8,128)(2,1)S(1)} %collective-permute-done.29.refs_2_, bf16[256,512]{1,0:T(8,128)(2,1)S(1)} %shard_map.297.refs_3_, ...), custom_call_target="tpu_custom_call" | custom-call | flops 1000 | bytes 65536 | tf_op jit(solution)/shard_map/pallas_call | solution.py:89
  116.6 1.2 collective-permute-done.37.refs_2_
  117.8 2.0 %shard_map.300 = (f32[1000,512]{1,0:T(8,128)}, f32[1,512]{1,0:T(1,128)}, f32[2,128]{1,0:T(2,128)}, f32[1,512]{1,0:T(1,128)}, f32[1,512]{1,0:T(1,128)}, /*index=5...) custom-call(s32[4]{0:T(128)S(1)} %broadcast_select_fusion.refs_0_, ...), custom_call_target="tpu_custom_call" | custom-call | flops 1000 | bytes 65536 | tf_op jit(solution)/shard_map/pallas_call | solution.py:89
  119.9 1.2 collective-permute-done.39.refs_2_
  121.3 1.8 %shard_map.301 = (f32[256,512]{1,0:T(8,128)}, f32[256,512]{1,0:T(8,128)}, f32[3,256,128]{2,1,0:T(8,128)}, f32[256,128]{1,0:T(8,128)}) custom-call(bf16[64,1536]{1,0:T(8,128)(2,1)S(1)} %get-tuple-element.416.refs_0_, bf16[64,1536]{1,0:T(8,128)(2,1)S(1)} %collective-permute-done.38.refs_1_, bf16[64,1536]{1,0:T(8,128)(2,1)S(1)} %collective-permute-done.39.refs_2_, ...), custom_call_target="tpu_custom_call" | custom-call | flops 1000 | bytes 65536 | tf_op jit(solution)/shard_map/pallas_call | solution.py:89
  (47 shorter events, 3.5 us)
Async XLA Ops:
  3.0 6.5 %collective-permute-start.1 = (bf16[272,512]{1,0:T(8,128)(2,1)S(1)}, bf16[272,512]{1,0:T(8,128)(2,1)S(1)}, u32[]{:S(2)}, u32[]{:S(2)}) collective-permute-start(bf16[272,512]{1,0:T(8,128)(2,1)S(1)} %get-tuple-element.231.refs_1_.refs_3_.refs_7_.refs_5_.refs_18_.refs_10_), channel_id=1, source_target_pairs={{0,16},{16,0},{1,17},{17,1},{2,18},{18,2},{3,19},{19,3},{4,20},{20... | collective-permute-start | bytes 835592 | tf_op jit(solution)/shard_map/swap_fsdp_1/ppermute | solution.py:107
  3.5 16.9 %collective-permute-start = (bf16[272,512]{1,0:T(8,128)(2,1)S(1)}, bf16[272,512]{1,0:T(8,128)(2,1)S(1)}, u32[]{:S(2)}, u32[]{:S(2)}) collective-permute-start(bf16[272,512]{1,0:T(8,128)(2,1)S(1)} %get-tuple-element.231.refs_1_.refs_3_.refs_7_.refs_5_.refs_18_.refs_10_), channel_id=1, source_target_pairs={{0,2},{1,3},{2,0},{3,1},{4,6},{5,7},{6,4},{7,5},{8,10},{9,11},{10,... | collective-permute-start | bytes 835592 | tf_op jit(solution)/shard_map/swap_tp_2/ppermute | solution.py:107
  10.3 10.1 %collective-permute-start.4 = (bf16[256,256]{1,0:T(8,128)(2,1)S(1)}, bf16[256,256]{1,0:T(8,128)(2,1)S(1)}, u32[]{:S(2)}, u32[]{:S(2)}) collective-permute-start(bf16[256,256]{1,0:T(8,128)(2,1)S(1)} %get-tuple-element.240.refs_2_.refs_3_), channel_id=1, source_target_pairs={{0,12},{4,8},{8,4},{12,0},{1,13},{5,9},{9,5},{13,1},{2,14},{6,10},... | collective-permute-start | bytes 393224 | tf_op jit(solution)/shard_map/swap_ctx_3/ppermute | solution.py:107
  12.8 7.6 %collective-permute-start.3 = (bf16[256,256]{1,0:T(8,128)(2,1)S(1)}, bf16[256,256]{1,0:T(8,128)(2,1)S(1)}, u32[]{:S(2)}, u32[]{:S(2)}) collective-permute-start(bf16[256,256]{1,0:T(8,128)(2,1)S(1)} %get-tuple-element.240.refs_2_.refs_3_), channel_id=1, source_target_pairs={{0,8},{4,12},{8,0},{12,4},{1,9},{5,13},{9,1},{13,5},{2,10},{6,14},... | collective-permute-start | bytes 393224 | tf_op jit(solution)/shard_map/swap_ctx_2/ppermute | solution.py:107
  13.3 7.1 %collective-permute-start.2 = (bf16[256,256]{1,0:T(8,128)(2,1)S(1)}, bf16[256,256]{1,0:T(8,128)(2,1)S(1)}, u32[]{:S(2)}, u32[]{:S(2)}) collective-permute-start(bf16[256,256]{1,0:T(8,128)(2,1)S(1)} %get-tuple-element.240.refs_2_.refs_3_), channel_id=1, source_target_pairs={{0,4},{4,0},{8,12},{12,8},{1,5},{5,1},{9,13},{13,9},{2,6},{6,2},{1... | collective-permute-start | bytes 393224 | tf_op jit(solution)/shard_map/swap_ctx_1/ppermute | solution.py:107
  20.4 2.1 %collective-permute-start.5 = (bf16[272,512]{1,0:T(8,128)(2,1)S(1)}, bf16[272,512]{1,0:T(8,128)(2,1)S(1)}, u32[]{:S(2)}, u32[]{:S(2)}) collective-permute-start(bf16[272,512]{1,0:T(8,128)(2,1)S(1)} %collective-permute-done.refs_1_.refs_3_.refs_9_.refs_4_.refs_20_.refs_12_), channel_id=1, source_target_pairs={{0,16},{16,0},{1,17},{17,1},{2,18},{18,2},{3,19},{19,3},{4,20},{20... | collective-permute-start | bytes 835592 | tf_op jit(solution)/shard_map/swap_fsdp_1/ppermute | solution.py:107
  20.5 11.0 %collective-permute-start.9 = (bf16[80,1024]{1,0:T(8,128)(2,1)S(1)}, bf16[80,1024]{1,0:T(8,128)(2,1)S(1)}, u32[]{:S(2)}, u32[]{:S(2)}) collective-permute-start(bf16[80,1024]{1,0:T(8,128)(2,1)S(1)} %get-tuple-element.265), channel_id=1, source_target_pairs={{0,2},{1,3},{2,0},{3,1},{4,6},{5,7},{6,4},{7,5},{8,10},{9,11},{10,... | collective-permute-start | bytes 491528 | tf_op jit(solution)/shard_map/swap_tp_2/ppermute | solution.py:107
  23.3 9.7 %collective-permute-start.8 = (bf16[272,256]{1,0:T(8,128)(2,1)S(1)}, bf16[272,256]{1,0:T(8,128)(2,1)S(1)}, u32[]{:S(2)}, u32[]{:S(2)}) collective-permute-start(bf16[272,256]{1,0:T(8,128)(2,1)S(1)} %get-tuple-element.263.refs_2_.refs_9_), channel_id=1, source_target_pairs={{0,12},{4,8},{8,4},{12,0},{1,13},{5,9},{9,5},{13,1},{2,14},{6,10},... | collective-permute-start | bytes 417800 | tf_op jit(solution)/shard_map/swap_ctx_3/ppermute | solution.py:107
  25.9 7.4 %collective-permute-start.7 = (bf16[272,256]{1,0:T(8,128)(2,1)S(1)}, bf16[272,256]{1,0:T(8,128)(2,1)S(1)}, u32[]{:S(2)}, u32[]{:S(2)}) collective-permute-start(bf16[272,256]{1,0:T(8,128)(2,1)S(1)} %get-tuple-element.263.refs_2_.refs_9_), channel_id=1, source_target_pairs={{0,8},{4,12},{8,0},{12,4},{1,9},{5,13},{9,1},{13,5},{2,10},{6,14},... | collective-permute-start | bytes 417800 | tf_op jit(solution)/shard_map/swap_ctx_2/ppermute | solution.py:107
  26.4 7.0 %collective-permute-start.6 = (bf16[272,256]{1,0:T(8,128)(2,1)S(1)}, bf16[272,256]{1,0:T(8,128)(2,1)S(1)}, u32[]{:S(2)}, u32[]{:S(2)}) collective-permute-start(bf16[272,256]{1,0:T(8,128)(2,1)S(1)} %get-tuple-element.263.refs_2_.refs_9_), channel_id=1, source_target_pairs={{0,4},{4,0},{8,12},{12,8},{1,5},{5,1},{9,13},{13,9},{2,6},{6,2},{1... | collective-permute-start | bytes 417800 | tf_op jit(solution)/shard_map/swap_ctx_1/ppermute | solution.py:107
  26.9 19.6 %collective-permute-start.11 = (bf16[256,1024]{1,0:T(8,128)(2,1)S(1)}, bf16[256,1024]{1,0:T(8,128)(2,1)S(1)}, u32[]{:S(2)}, u32[]{:S(2)}) collective-permute-start(bf16[256,1024]{1,0:T(8,128)(2,1)S(1)} %get-tuple-element.274.refs_6_), channel_id=1, source_target_pairs={{0,16},{16,0},{1,17},{17,1},{2,18},{18,2},{3,19},{19,3},{4,20},{20... | collective-permute-start | bytes 1572872 | tf_op jit(solution)/shard_map/swap_fsdp_1/ppermute | solution.py:107
  31.5 8.0 %collective-permute-start.12 = (bf16[80,1024]{1,0:T(8,128)(2,1)S(1)}, bf16[80,1024]{1,0:T(8,128)(2,1)S(1)}, u32[]{:S(2)}, u32[]{:S(2)}) collective-permute-start(bf16[80,1024]{1,0:T(8,128)(2,1)S(1)} %collective-permute-done.9.refs_0_), channel_id=1, source_target_pairs={{0,4},{4,0},{8,12},{12,8},{16,24},{20,28},{24,16},{28,20},{1,5},{5... | collective-permute-start | bytes 491528 | tf_op jit(solution)/shard_map/swap_turn_0/ppermute | solution.py:122
  35.6 10.8 %collective-permute-start.10 = (bf16[272,512]{1,0:T(8,128)(2,1)S(1)}, bf16[272,512]{1,0:T(8,128)(2,1)S(1)}, u32[]{:S(2)}, u32[]{:S(2)}) collective-permute-start(bf16[272,512]{1,0:T(8,128)(2,1)S(1)} %get-tuple-element.271.refs_1_), channel_id=1, source_target_pairs={{0,1},{1,0},{2,3},{3,2},{4,5},{5,4},{6,7},{7,6},{8,9},{9,8},{10,11... | collective-permute-start | bytes 835592 | tf_op jit(solution)/shard_map/swap_tp_1/ppermute | solution.py:107
  40.0 6.4 %collective-permute-start.13 = (bf16[128,1024]{1,0:T(8,128)(2,1)S(1)}, bf16[128,1024]{1,0:T(8,128)(2,1)S(1)}, u32[]{:S(2)}, u32[]{:S(2)}) collective-permute-start(bf16[128,1024]{1,0:T(8,128)(2,1)S(1)} %shard_map.286.refs_5_), channel_id=1, source_target_pairs={{0,8},{4,12},{8,0},{12,4},{16,20},{20,16},{24,28},{28,24},{1,9},{5... | collective-permute-start | bytes 786440 | tf_op jit(solution)/shard_map/swap_turn_1/ppermute | solution.py:122
  41.6 6.7 %collective-permute-start.14 = (bf16[128,1024]{1,0:T(8,128)(2,1)S(1)}, bf16[128,1024]{1,0:T(8,128)(2,1)S(1)}, u32[]{:S(2)}, u32[]{:S(2)}) collective-permute-start(bf16[128,1024]{1,0:T(8,128)(2,1)S(1)} %shard_map.286.refs_5_), channel_id=1, source_target_pairs={{0,16},{16,0},{1,17},{17,1},{2,18},{18,2},{3,19},{19,3},{4,20},{20... | collective-permute-start | bytes 786440 | tf_op jit(solution)/shard_map/swap_fsdp_1/ppermute | solution.py:107
  46.5 1.9 %collective-permute-start.15 = (bf16[128,1024]{1,0:T(8,128)(2,1)S(1)}, bf16[128,1024]{1,0:T(8,128)(2,1)S(1)}, u32[]{:S(2)}, u32[]{:S(2)}) collective-permute-start(bf16[128,1024]{1,0:T(8,128)(2,1)S(1)} %collective-permute-done.13.refs_6_), channel_id=1, source_target_pairs={{0,16},{16,0},{1,17},{17,1},{2,18},{18,2},{3,19},{19,3},{4,20},{20... | collective-permute-start | bytes 786440 | tf_op jit(solution)/shard_map/swap_fsdp_1/ppermute | solution.py:107
  50.0 9.1 %collective-permute-start.21 = (bf16[272,512]{1,0:T(8,128)(2,1)S(1)}, bf16[272,512]{1,0:T(8,128)(2,1)S(1)}, u32[]{:S(2)}, u32[]{:S(2)}) collective-permute-start(bf16[272,512]{1,0:T(8,128)(2,1)S(1)} %get-tuple-element.322.refs_13_), channel_id=1, source_target_pairs={{0,1},{1,0},{2,3},{3,2},{4,5},{5,4},{6,7},{7,6},{8,9},{9,8},{10,11... | collective-permute-start | bytes 835592 | tf_op jit(solution)/shard_map/swap_tp_1/ppermute | solution.py:107
  52.8 1.6 %collective-permute-start.19 = (bf16[256,512]{1,0:T(8,128)(2,1)S(1)}, bf16[256,512]{1,0:T(8,128)(2,1)S(1)}, u32[]{:S(2)}, u32[]{:S(2)}) collective-permute-start(bf16[256,512]{1,0:T(8,128)(2,1)S(1)} %get-tuple-element.311), channel_id=1, source_target_pairs={{0,16},{16,0},{1,17},{17,1},{2,18},{18,2},{3,19},{19,3},{4,20},{20... | collective-permute-start | bytes 786440 | tf_op jit(solution)/shard_map/swap_fsdp_1/ppermute | solution.py:107
  52.9 1.9 %collective-permute-start.18 = (bf16[256,512]{1,0:T(8,128)(2,1)S(1)}, bf16[256,512]{1,0:T(8,128)(2,1)S(1)}, u32[]{:S(2)}, u32[]{:S(2)}) collective-permute-start(bf16[256,512]{1,0:T(8,128)(2,1)S(1)} %get-tuple-element.308), channel_id=1, source_target_pairs={{0,16},{16,0},{1,17},{17,1},{2,18},{18,2},{3,19},{19,3},{4,20},{20... | collective-permute-start | bytes 786440 | tf_op jit(solution)/shard_map/swap_fsdp_1/ppermute | solution.py:107
  53.4 1.8 %collective-permute-start.17 = (bf16[256,512]{1,0:T(8,128)(2,1)S(1)}, bf16[256,512]{1,0:T(8,128)(2,1)S(1)}, u32[]{:S(2)}, u32[]{:S(2)}) collective-permute-start(bf16[256,512]{1,0:T(8,128)(2,1)S(1)} %get-tuple-element.305), channel_id=1, source_target_pairs={{0,16},{16,0},{1,17},{17,1},{2,18},{18,2},{3,19},{19,3},{4,20},{20... | collective-permute-start | bytes 786440 | tf_op jit(solution)/shard_map/swap_fsdp_1/ppermute | solution.py:107
  53.4 2.1 %collective-permute-start.16 = (bf16[256,512]{1,0:T(8,128)(2,1)S(1)}, bf16[256,512]{1,0:T(8,128)(2,1)S(1)}, u32[]{:S(2)}, u32[]{:S(2)}) collective-permute-start(bf16[256,512]{1,0:T(8,128)(2,1)S(1)} %get-tuple-element.302), channel_id=1, source_target_pairs={{0,16},{16,0},{1,17},{17,1},{2,18},{18,2},{3,19},{19,3},{4,20},{20... | collective-permute-start | bytes 786440 | tf_op jit(solution)/shard_map/swap_fsdp_1/ppermute | solution.py:107
  56.2 18.9 %collective-permute-start.20 = (bf16[128,2048]{1,0:T(8,128)(2,1)S(1)}, bf16[128,2048]{1,0:T(8,128)(2,1)S(1)}, u32[]{:S(2)}, u32[]{:S(2)}) collective-permute-start(bf16[128,2048]{1,0:T(8,128)(2,1)S(1)} %get-tuple-element.317), channel_id=1, source_target_pairs={{0,4},{4,0},{8,12},{12,8},{16,24},{20,28},{24,16},{28,20},{1,5},{5... | collective-permute-start | bytes 1572872 | tf_op jit(solution)/shard_map/swap_turn_0/ppermute | solution.py:122
  64.5 11.9 %collective-permute-start.26 = (bf16[272,512]{1,0:T(8,128)(2,1)S(1)}, bf16[272,512]{1,0:T(8,128)(2,1)S(1)}, u32[]{:S(2)}, u32[]{:S(2)}) collective-permute-start(bf16[272,512]{1,0:T(8,128)(2,1)S(1)} %get-tuple-element.348), channel_id=1, source_target_pairs={{0,12},{4,8},{8,4},{12,0},{1,13},{5,9},{9,5},{13,1},{2,14},{6,10},... | collective-permute-start | bytes 835592 | tf_op jit(solution)/shard_map/swap_ctx_3/ppermute | solution.py:107
  67.0 12.7 %collective-permute-start.25 = (bf16[272,512]{1,0:T(8,128)(2,1)S(1)}, bf16[272,512]{1,0:T(8,128)(2,1)S(1)}, u32[]{:S(2)}, u32[]{:S(2)}) collective-permute-start(bf16[272,512]{1,0:T(8,128)(2,1)S(1)} %get-tuple-element.347), channel_id=1, source_target_pairs={{0,8},{4,12},{8,0},{12,4},{1,9},{5,13},{9,1},{13,5},{2,10},{6,14},... | collective-permute-start | bytes 835592 | tf_op jit(solution)/shard_map/swap_ctx_2/ppermute | solution.py:107
  67.5 12.3 %collective-permute-start.24 = (bf16[272,512]{1,0:T(8,128)(2,1)S(1)}, bf16[272,512]{1,0:T(8,128)(2,1)S(1)}, u32[]{:S(2)}, u32[]{:S(2)}) collective-permute-start(bf16[272,512]{1,0:T(8,128)(2,1)S(1)} %get-tuple-element.346), channel_id=1, source_target_pairs={{0,4},{4,0},{8,12},{12,8},{1,5},{5,1},{9,13},{13,9},{2,6},{6,2},{1... | collective-permute-start | bytes 835592 | tf_op jit(solution)/shard_map/swap_ctx_1/ppermute | solution.py:107
  68.1 7.1 %collective-permute-start.22 = (bf16[256,512]{1,0:T(8,128)(2,1)S(1)}, bf16[256,512]{1,0:T(8,128)(2,1)S(1)}, u32[]{:S(2)}, u32[]{:S(2)}) collective-permute-start(bf16[256,512]{1,0:T(8,128)(2,1)S(1)} %get-tuple-element.333.refs_3_), channel_id=1, source_target_pairs={{0,1},{1,0},{2,3},{3,2},{4,5},{5,4},{6,7},{7,6},{8,9},{9,8},{10,11... | collective-permute-start | bytes 786440 | tf_op jit(solution)/shard_map/swap_tp_1/ppermute | solution.py:107
  76.0 18.4 %collective-permute-start.23 = (bf16[384,512]{1,0:T(8,128)(2,1)S(1)}, bf16[384,512]{1,0:T(8,128)(2,1)S(1)}, u32[]{:S(2)}, u32[]{:S(2)}) collective-permute-start(bf16[384,512]{1,0:T(8,128)(2,1)S(1)} %get-tuple-element.340), channel_id=1, source_target_pairs={{0,2},{1,3},{2,0},{3,1},{4,6},{5,7},{6,4},{7,5},{8,10},{9,11},{10,... | collective-permute-start | bytes 1179656 | tf_op jit(solution)/shard_map/swap_tp_2/ppermute | solution.py:107
  81.5 1.6 %collective-permute-start.28 = (bf16[272,512]{1,0:T(8,128)(2,1)S(1)}, bf16[272,512]{1,0:T(8,128)(2,1)S(1)}, u32[]{:S(2)}, u32[]{:S(2)}) collective-permute-start(bf16[272,512]{1,0:T(8,128)(2,1)S(1)} %get-tuple-element.359), channel_id=1, source_target_pairs={{0,16},{16,0},{1,17},{17,1},{2,18},{18,2},{3,19},{19,3},{4,20},{20... | collective-permute-start | bytes 835592 | tf_op jit(solution)/shard_map/swap_fsdp_1/ppermute | solution.py:107
  81.6 1.9 %collective-permute-start.27 = (bf16[272,512]{1,0:T(8,128)(2,1)S(1)}, bf16[272,512]{1,0:T(8,128)(2,1)S(1)}, u32[]{:S(2)}, u32[]{:S(2)}) collective-permute-start(bf16[272,512]{1,0:T(8,128)(2,1)S(1)} %get-tuple-element.356), channel_id=1, source_target_pairs={{0,16},{16,0},{1,17},{17,1},{2,18},{18,2},{3,19},{19,3},{4,20},{20... | collective-permute-start | bytes 835592 | tf_op jit(solution)/shard_map/swap_fsdp_1/ppermute | solution.py:107
  82.1 16.5 %collective-permute-start.30 = (bf16[256,512]{1,0:T(8,128)(2,1)S(1)}, bf16[256,512]{1,0:T(8,128)(2,1)S(1)}, u32[]{:S(2)}, u32[]{:S(2)}) collective-permute-start(bf16[256,512]{1,0:T(8,128)(2,1)S(1)} %get-tuple-element.379.refs_1_), channel_id=1, source_target_pairs={{0,1},{1,0},{2,3},{3,2},{4,5},{5,4},{6,7},{7,6},{8,9},{9,8},{10,11... | collective-permute-start | bytes 786440 | tf_op jit(solution)/shard_map/swap_tp_1/ppermute | solution.py:107
  84.2 12.2 %collective-permute-start.33 = (bf16[80,1024]{1,0:T(8,128)(2,1)S(1)}, bf16[80,1024]{1,0:T(8,128)(2,1)S(1)}, u32[]{:S(2)}, u32[]{:S(2)}) collective-permute-start(bf16[80,1024]{1,0:T(8,128)(2,1)S(1)} %get-tuple-element.383), channel_id=1, source_target_pairs={{0,12},{4,8},{8,4},{12,0},{1,13},{5,9},{9,5},{13,1},{2,14},{6,10},... | collective-permute-start | bytes 491528 | tf_op jit(solution)/shard_map/swap_ctx_3/ppermute | solution.py:107
  85.9 10.5 %collective-permute-start.32 = (bf16[80,1024]{1,0:T(8,128)(2,1)S(1)}, bf16[80,1024]{1,0:T(8,128)(2,1)S(1)}, u32[]{:S(2)}, u32[]{:S(2)}) collective-permute-start(bf16[80,1024]{1,0:T(8,128)(2,1)S(1)} %get-tuple-element.382), channel_id=1, source_target_pairs={{0,8},{4,12},{8,0},{12,4},{1,9},{5,13},{9,1},{13,5},{2,10},{6,14},... | collective-permute-start | bytes 491528 | tf_op jit(solution)/shard_map/swap_ctx_2/ppermute | solution.py:107
  87.2 9.1 %collective-permute-start.31 = (bf16[80,1024]{1,0:T(8,128)(2,1)S(1)}, bf16[80,1024]{1,0:T(8,128)(2,1)S(1)}, u32[]{:S(2)}, u32[]{:S(2)}) collective-permute-start(bf16[80,1024]{1,0:T(8,128)(2,1)S(1)} %get-tuple-element.381), channel_id=1, source_target_pairs={{0,4},{4,0},{8,12},{12,8},{1,5},{5,1},{9,13},{13,9},{2,6},{6,2},{1... | collective-permute-start | bytes 491528 | tf_op jit(solution)/shard_map/swap_ctx_1/ppermute | solution.py:107
  95.0 19.0 %copy-start = (s32[2]{0:T(128)S(1)}, s32[2]{0:T(128)}, u32[]{:S(2)}) copy-start(s32[2]{0:T(128)} %refs_0_.3) | copy-start | bytes 28
  95.0 5.8 %collective-permute-start.35 = (bf16[64,1024]{1,0:T(8,128)(2,1)S(1)}, bf16[64,1024]{1,0:T(8,128)(2,1)S(1)}, u32[]{:S(2)}, u32[]{:S(2)}) collective-permute-start(bf16[64,1024]{1,0:T(8,128)(2,1)S(1)} %get-tuple-element.393), channel_id=1, source_target_pairs={{0,8},{4,12},{8,0},{12,4},{16,20},{20,16},{24,28},{28,24},{1,9},{5... | collective-permute-start | bytes 393224 | tf_op jit(solution)/shard_map/swap_turn_1/ppermute | solution.py:122
  97.0 12.7 %collective-permute-start.36 = (bf16[96,512]{1,0:T(8,128)(2,1)S(1)}, bf16[96,512]{1,0:T(8,128)(2,1)S(1)}, u32[]{:S(2)}, u32[]{:S(2)}) collective-permute-start(bf16[96,512]{1,0:T(8,128)(2,1)S(1)} %get-tuple-element.395.refs_3_), channel_id=1, source_target_pairs={{0,2},{1,3},{2,0},{3,1},{4,6},{5,7},{6,4},{7,5},{8,10},{9,11},{10,... | collective-permute-start | bytes 294920 | tf_op jit(solution)/shard_map/swap_tp_2/ppermute | solution.py:107
  99.3 15.4 %collective-permute-start.34 = (bf16[256,512]{1,0:T(8,128)(2,1)S(1)}, bf16[256,512]{1,0:T(8,128)(2,1)S(1)}, u32[]{:S(2)}, u32[]{:S(2)}) collective-permute-start(bf16[256,512]{1,0:T(8,128)(2,1)S(1)} %shard_map.297.refs_3_), channel_id=1, source_target_pairs={{0,2},{1,3},{2,0},{3,1},{4,6},{5,7},{6,4},{7,5},{8,10},{9,11},{10,... | collective-permute-start | bytes 786440 | tf_op jit(solution)/shard_map/swap_tp_2/ppermute | solution.py:107
  100.7 13.1 %collective-permute-start.29 = (bf16[128,512]{1,0:T(8,128)(2,1)S(1)}, bf16[128,512]{1,0:T(8,128)(2,1)S(1)}, u32[]{:S(2)}, u32[]{:S(2)}) collective-permute-start(bf16[128,512]{1,0:T(8,128)(2,1)S(1)} %get-tuple-element.377.refs_1_), channel_id=1, source_target_pairs={{0,1},{1,0},{2,3},{3,2},{4,5},{5,4},{6,7},{7,6},{8,9},{9,8},{10,11... | collective-permute-start | bytes 393224 | tf_op jit(solution)/shard_map/swap_tp_1/ppermute | solution.py:107
  110.3 9.6 %collective-permute-start.40 = (bf16[64,1536]{1,0:T(8,128)(2,1)S(1)}, bf16[64,1536]{1,0:T(8,128)(2,1)S(1)}, u32[]{:S(2)}, u32[]{:S(2)}) collective-permute-start(bf16[64,1536]{1,0:T(8,128)(2,1)S(1)} %get-tuple-element.416.refs_0_), channel_id=1, source_target_pairs={{0,12},{4,8},{8,4},{12,0},{1,13},{5,9},{9,5},{13,1},{2,14},{6,10},... | collective-permute-start | bytes 589832 | tf_op jit(solution)/shard_map/swap_ctx_3/ppermute | solution.py:107
  111.4 9.6 %collective-permute-start.39 = (bf16[64,1536]{1,0:T(8,128)(2,1)S(1)}, bf16[64,1536]{1,0:T(8,128)(2,1)S(1)}, u32[]{:S(2)}, u32[]{:S(2)}) collective-permute-start(bf16[64,1536]{1,0:T(8,128)(2,1)S(1)} %get-tuple-element.416.refs_0_), channel_id=1, source_target_pairs={{0,8},{4,12},{8,0},{12,4},{1,9},{5,13},{9,1},{13,5},{2,10},{6,14},... | collective-permute-start | bytes 589832 | tf_op jit(solution)/shard_map/swap_ctx_2/ppermute | solution.py:107
  112.9 8.4 %collective-permute-start.38 = (bf16[64,1536]{1,0:T(8,128)(2,1)S(1)}, bf16[64,1536]{1,0:T(8,128)(2,1)S(1)}, u32[]{:S(2)}, u32[]{:S(2)}) collective-permute-start(bf16[64,1536]{1,0:T(8,128)(2,1)S(1)} %get-tuple-element.416.refs_0_), channel_id=1, source_target_pairs={{0,4},{4,0},{8,12},{12,8},{1,5},{5,1},{9,13},{13,9},{2,6},{6,2},{1... | collective-permute-start | bytes 589832 | tf_op jit(solution)/shard_map/swap_ctx_1/ppermute | solution.py:107
  113.9 4.0 %collective-permute-start.37 = (f32[16,512]{1,0:T(8,128)S(1)}, f32[16,512]{1,0:T(8,128)S(1)}, u32[]{:S(2)}, u32[]{:S(2)}) collective-permute-start(f32[16,512]{1,0:T(8,128)S(1)} %get-tuple-element.408.refs_1_), channel_id=1, source_target_pairs={{0,1},{1,0},{2,3},{3,2},{4,5},{5,4},{6,7},{7,6},{8,9},{9,8},{10,11... | collective-permute-start | bytes 98312 | tf_op jit(solution)/shard_map/swap_tp_1/ppermute | solution.py:107

commit v4 on v3

--- a/solution.py
+++ b/solution.py
@@ -71,7 +71,7 @@
     def __init__(self, spot, parts):
         self.spot, self.parts, self.cost = spot, parts, COST
 
-    def call(self, kernel, outs, operands, *, far=(), scratch=(), limit=5, cost=None):
+    def call(self, kernel, outs, operands, *, far=(), kept=(), alias=None, scratch=(), limit=5, cost=None):
         specs = [
             SMEM if operand.ndim == 1
             else pl.BlockSpec(memory_space=pltpu.HBM if i in far else pltpu.VMEM)
@@ -90,7 +90,11 @@
             body,
             out_shape=tuple(jax.ShapeDtypeStruct(shape, dtype) for shape, dtype in outs),
             in_specs=specs + [SMEM],
-            out_specs=(VMEM,) * len(outs),
+            out_specs=tuple(
+                pl.BlockSpec(memory_space=pltpu.HBM) if i in kept else VMEM
+                for i in range(len(outs))
+            ),
+            input_output_aliases=alias or {},
             scratch_shapes=list(scratch),
             compiler_params=pltpu.CompilerParams(vmem_limit_bytes=limit << 20),
             cost_estimate=pl.CostEstimate(
@@ -146,18 +150,12 @@
 
 
 def pack_kernel(
-    spot_ref, steps_ref, w_hbm, out_hbm, qv_hbm, up_bias_hbm, up_hbm, down_hbm,
-    pack_ref, rest_ref, quarter_ref,
-    w_ref, o_ref, qv_ref, up_bias_ref, up_ref, down_ref, sems,
+    spot_ref, steps_ref, w_hbm, out_hbm, qv_hbm, up_bias_hbm, pack_ref, qkv_ref, out_ref,
+    w_ref, o_ref, qv_ref, up_bias_ref, sems,
 ):
     rows, cols = w_ref.shape[1:]
-    hidden = up_ref.shape[1]
     fetch(
-        [
-            (w_hbm, w_ref), (out_hbm, o_ref), (qv_hbm, qv_ref), (up_bias_hbm, up_bias_ref),
-            (up_hbm, up_ref), (down_hbm, down_ref),
-        ],
-        sems,
+        [(w_hbm, w_ref), (out_hbm, o_ref), (qv_hbm, qv_ref), (up_bias_hbm, up_bias_ref)], sems
     )
     for i in range(3):
         pack_ref[:rows, i * cols : (i + 1) * cols] = w_ref[i].astype(BF16)
@@ -177,13 +175,40 @@
     fill = jnp.zeros((BIAS_ROWS - 9, 4 * cols), F32)
     stack = jnp.concatenate([v.astype(F32) for v in parts] + [fill], axis=0)
     pack_ref[rows:, :] = stack.astype(BF16)
+    qkv_ref[...] = pack_ref[:, : 3 * cols]
+    out_ref[...] = pack_ref[:rows, 3 * cols :]
+
+
+def pack_rest_kernel(
+    spot_ref, own_out, up_hbm, down_hbm, cotan_hbm, rest_ref, side_ref, cotan_ref,
+    up_ref, down_ref, sems,
+):
+    rows, hidden = up_ref.shape
+    cols = own_out.shape[1]
+    pair = spot_ref[2] // 2
+    fetch([(up_hbm, up_ref), (down_hbm, down_ref), (cotan_hbm.at[pair], cotan_ref)], sems)
     rest_ref[:, :hidden] = up_ref[...].astype(BF16)
     rest_ref[:, hidden:] = down_ref[...].astype(BF16)
-    quarter = rows // 4
+    if side_ref.shape[0] == rows:
+        side_ref[...] = own_out[...]
+        return
+    quarter, fold = rows // 4, rows // 8
     mine = window(spot_ref[1], quarter)
-    quarter_ref[:quarter, :hidden] = up_ref[mine, :].astype(BF16)
-    quarter_ref[:quarter, hidden:] = down_ref[mine, :].astype(BF16)
-    clear_below(quarter_ref, quarter)
+    side_ref[:quarter, :hidden] = up_ref[mine, :].astype(BF16)
+    side_ref[:quarter, hidden:] = down_ref[mine, :].astype(BF16)
+    for i in range(8):
+        block = own_out[i * fold : (i + 1) * fold, :]
+        side_ref[quarter : quarter + fold, i * cols : (i + 1) * cols] = block
+    clear_below(side_ref, quarter + fold)
+
+
+def unpack_kernel(spot_ref, side_ref, quarter_ref, out_ref):
+    rows, cols = out_ref.shape
+    quarter, fold = rows // 4, rows // 8
+    quarter_ref[...] = side_ref[:quarter, :]
+    for i in range(8):
+        block = side_ref[quarter : quarter + fold, i * cols : (i + 1) * cols]
+        out_ref[i * fold : (i + 1) * fold, :] = block
 
 
 def bias_lines(pack_ref, row):
@@ -198,22 +223,16 @@
     return ref[:size, ref.shape[1] - cols :]
 
 
-def pair_kernel(spot_ref, own_ref, got_ref, out_ref):
-    pair, span = spot_ref[2] // 2, own_ref.shape[0]
-    out_ref[window(pair, span), :] = own_ref[...].astype(F32)
-    out_ref[window(1 - pair, span), :] = got_ref[...].astype(F32)
-
-
 def add_pair_kernel(spot_ref, base_ref, own_ref, got_ref, out_ref):
     span = base_ref.shape[0]
     terms = own_ref[:span, :].astype(F32) + got_ref[:span, :].astype(F32)
     out_ref[...] = (base_ref[...] + terms).astype(BF16)
 
 
-def stream_kernel(
-    spot_ref, steps_ref, x_hbm, table_hbm, seg_hbm, cotan_hbm, g1, b1, g2, b2, bo, bd,
-    stream_ref, normed_ref, seg_ref, lines_ref, cotan_ref, x_ref, table_ref, ids_ref, line_ref,
-    sems,
+def open_kernel(
+    spot_ref, steps_ref, x_hbm, table_hbm, seg_hbm, g1, b1, g2, b2, bo, bd, one_ref, two_ref,
+    bias_ref, q_ref, kv_ref, stream_ref, normed_ref, seg_ref, lines_ref,
+    x_ref, table_ref, ids_ref, line_ref, sems, *, row,
 ):
     pair = spot_ref[2] // 2
     step = steps_ref[pair]
@@ -222,7 +241,6 @@
         (x_hbm.at[pair], x_ref),
         (table_hbm.at[pl.ds(block, 8), :], table_ref),
         (seg_hbm, ids_ref),
-        (cotan_hbm.at[pair], cotan_ref),
     ]
     vectors = (g1, b1, g2, b2, bo, bd)
     fetch(copies + [(v, line_ref.at[i]) for i, v in enumerate(vectors)], sems)
@@ -233,6 +251,7 @@
     hat, _ = norm_parts(stream)
     stream_ref[...] = stream
     normed_ref[...] = (hat * line_ref[0] + line_ref[1]).astype(BF16)
+    project_kernel(spot_ref, normed_ref, one_ref, two_ref, bias_ref, q_ref, kv_ref, row=row)
 
 
 def project_kernel(spot_ref, normed_ref, one_ref, two_ref, bias_ref, q_ref, kv_ref, *, row):
@@ -485,7 +504,7 @@
 def input_kernel(
     spot_ref, stream_ref, lines_ref, rows_ref, up_near, up_far, dq_ref, own_ref, g1, g2, g3,
     one_n, two_n, one_f, two_f, normed_ref, low_ref, near_ref, far_ref,
-    given_ref, small_ref, w_kept_ref, w_near_ref, w_far_ref, pulled_ref, terms_ref,
+    given_ref, small_ref, w_kept_ref, w_near_ref, w_far_ref, w_out_ref, pulled_ref, terms_ref,
 ):
     span, width = stream_ref.shape
     cols = dq_ref.shape[1] // 2
@@ -528,9 +547,12 @@
                 w_kept_ref[:, start : start + 3 * cols] = qkv
                 w_kept_ref[:, start + 3 * cols : start + 4 * cols] = out
             else:
-                given[side][:size, : 3 * cols] = qkv.astype(BF16)
-                given[side][:size, 3 * cols :] = out.astype(BF16)
-    w_near_ref[size:, :], w_far_ref[size:, :] = split_two(small_ref[...])
+                given[side][:size, :] = qkv.astype(BF16)
+                w_out_ref[:size, side * cols : (side + 1) * cols] = out.astype(BF16)
+    both_parts = jnp.concatenate(split_two(small_ref[...]), axis=1)
+    w_near_ref[size:, :] = both_parts[:, : 3 * cols]
+    w_far_ref[size:, :] = both_parts[:, 3 * cols : 6 * cols]
+    w_out_ref[size:, :] = both_parts[:, 6 * cols :]
 
 
 def turn_bits(spot_ref):
@@ -577,9 +599,10 @@
         at = span // 2 + i * rows
         columns = slice(width + i * half, width + (i + 1) * half)
         send_ref[at : at + rows, :] = values[:, columns].astype(BF16)
-
-
-def settle_kernel(spot_ref, near_ref, got_ref, out_ref, own_ref, send_ref):
+    clear_below(send_ref, span // 2 + width // half * rows)
+
+
+def settle_kernel(spot_ref, near_ref, got_ref, out_ref, own_ref, *sends):
     rows, width = own_ref.shape
     span = out_ref.shape[0]
     out_ref[...] = got_ref[:span, :]
@@ -588,32 +611,43 @@
         at, columns = span + 2 * i * rows, slice(i * half, (i + 1) * half)
         own_ref[:, columns] = near_ref[:rows, columns] + got_ref[at : at + rows, :].astype(F32)
         more = near_ref[rows:, columns] + got_ref[at + rows : at + 2 * rows, :].astype(F32)
-        send_ref[:, columns] = more.astype(BF16)
-
-
-def rows_kernel(spot_ref, own_ref, one_ref, two_ref, in_own, in_got, out_ref, in_ref):
+        sends[i][...] = more.astype(BF16)
+
+
+def fill_rows(spot_ref, own_ref, others, out_ref):
     pair, bit, span = spot_ref[2] // 2, spot_ref[2] % 2, own_ref.shape[0]
-    half = span // 2
     out_ref[window(pair, span), :] = own_ref[...].astype(F32)
-    out_ref[window(2 * (1 - pair) + bit, half), :] = one_ref[...].astype(F32)
-    out_ref[window(2 * (1 - pair) + 1 - bit, half), :] = two_ref[...].astype(F32)
-    in_ref[window(pair, span), :] = in_own[...].astype(F32)
-    in_ref[window(1 - pair, span), :] = in_got[...].astype(F32)
+    if len(others) == 1:
+        out_ref[window(1 - pair, span), :] = others[0][...].astype(F32)
+    else:
+        for i, other in enumerate(others):
+            at = 2 * (1 - pair) + (bit ^ i)
+            out_ref[window(at, span // 2), :] = other[: span // 2, :].astype(F32)
+
+
+def rows_kernel(spot_ref, out_own, out_one, out_two, in_own, in_far, out_ref, in_ref):
+    fill_rows(spot_ref, out_own, (out_one, out_two), out_ref)
+    fill_rows(spot_ref, in_own, (in_far,), in_ref)
 
 
 def cut_small_kernel(
-    spot_ref, kept_ref, got_near, got_far, small_ref, own_ref, o1, o2, o3, sum_ref
+    spot_ref, kept_ref, got_near, got_far, got_out, small_ref, own_ref, o1, o2, o3, sum_ref
 ):
     rows, width = own_ref.shape[0], small_ref.shape[1]
     whole = kept_ref.shape[0]
     for bits, out_ref in enumerate((own_ref, o1, o2, o3)):
         at = window(spot_ref[1] ^ bits, rows)
         for side, got_ref in enumerate((got_near, got_far)):
-            columns = slice(side * width, (side + 1) * width)
-            values = kept_ref[at, columns] + got_ref[at, :].astype(F32)
-            out_ref[:rows, columns] = values.astype(out_ref.dtype)
+            cols = got_ref.shape[1] // 3
+            got = (got_ref[at, :], got_out[at, side * cols : (side + 1) * cols])
+            for part, start, stop in ((got[0], 0, 3 * cols), (got[1], 3 * cols, 4 * cols)):
+                columns = slice(side * width + start, side * width + stop)
+                values = kept_ref[at, columns] + part.astype(F32)
+                out_ref[:rows, columns] = values.astype(out_ref.dtype)
     mine = both(*split_two(small_ref[...]))
-    high, low = split_two(mine + both(got_near[whole:, :], got_far[whole:, :]))
+    got = [piece[whole:, :].astype(F32) for piece in (got_near, got_far, got_out)]
+    got = jnp.concatenate(got, axis=1)
+    high, low = split_two(mine + (got[:, :width] + got[:, width:]))
     for out_ref in (o1, o2, o3):
         out_ref[rows:, :width] = high
         out_ref[rows:, width:] = low
@@ -634,42 +668,104 @@
 
 
 def owned_kernel(
-    spot_ref, ffn_kept, ffn_got, kept_ref, sent_ref, got_ref, out_ref, small_ref
-):
-    rows, width = ffn_kept.shape
-    out_ref[:, :width] = (ffn_kept[...] + ffn_got[...].astype(F32)).astype(BF16)
-    out_ref[:, width:] = (kept_ref[...] + got_ref[:rows, :].astype(F32)).astype(BF16)
-    count = small_ref.shape[0]
+    spot_ref, ffn_kept, ffn_one, ffn_two, kept_ref, sent_ref, got_ref, half_ref,
+    out_ref, pass_ref,
+):
+    rows, width = kept_ref.shape
+    half = half_ref.shape[0]
+    pass_ref[:half, :] = half_ref[...]
+    for i, piece in enumerate((ffn_one, ffn_two)):
+        at = slice(i * width, (i + 1) * width)
+        out_ref[:, at] = (ffn_kept[:, at] + piece[...].astype(F32)).astype(BF16)
+    out_ref[:, 2 * width :] = (kept_ref[...] + got_ref[:rows, :].astype(F32)).astype(BF16)
+    count = (sent_ref.shape[0] - rows) // 2
     top, end = slice(rows, rows + count), slice(rows + count, rows + 2 * count)
     mine = both(sent_ref[top, :], sent_ref[end, :])
-    small_ref[...] = mine + both(got_ref[top, :], got_ref[end, :])
-
-
-def own_kernel(spot_ref, p0, p1, p2, p3, up_ref, down_ref, qkv_ref, out_ref):
-    rows, hidden, cols = p0.shape[0], up_ref.shape[1], out_ref.shape[1]
-    for bits, piece in enumerate((p0, p1, p2, p3)):
-        at = window(spot_ref[1] ^ bits, rows)
-        up_ref[at, :] = piece[:, :hidden].astype(F32)
-        down_ref[at, :] = piece[:, hidden : 2 * hidden].astype(F32)
-        start = 2 * hidden
-        for i in range(3):
-            qkv_ref[i, at, :] = piece[:, start + i * cols : start + (i + 1) * cols].astype(F32)
-        out_ref[at, :] = piece[:, start + 3 * cols :].astype(F32)
-
-
-def sums_kernel(spot_ref, steps_ref, own_ref, got_ref, table_ref, up_ref, qv_ref, *refs):
-    lines, rows_ref = refs[:-1], refs[-1]
-    cols = qv_ref.shape[1]
-    shard = spot_ref[2]
-    rows_ref[...] = own_ref[...] + got_ref[...]
+    high, low = split_two(mine + both(got_ref[top, :], got_ref[end, :]))
+    pass_ref[half : half + count, :] = high
+    pass_ref[half + count :, :] = low
+
+
+def sums_out(spot_ref, rows_ref, up_ref, qv_ref, lines):
+    up_ref[...] = rows_ref[pl.ds(8 + spot_ref[2], 1), :]
+    qv_ref[...] = rows_ref[6:8, window(spot_ref[2], qv_ref.shape[1])]
+    for i, line_ref in enumerate(lines):
+        line_ref[...] = rows_ref[i : i + 1, :]
+
+
+def plain_sums_kernel(spot_ref, steps_ref, small_ref, table_ref, up_ref, qv_ref, *lines):
     table_ref[...] = jnp.zeros_like(table_ref)
     for place in range(steps_ref.shape[0]):
         at = pl.ds(steps_ref[place], 1)
-        table_ref[at, :] = table_ref[at, :] + rows_ref[12 + place : 13 + place, :]
-    up_ref[...] = rows_ref[pl.ds(8 + shard, 1), :]
-    qv_ref[...] = rows_ref[6:8, window(shard, cols)]
-    for i, line_ref in enumerate(lines):
-        line_ref[...] = rows_ref[i : i + 1, :]
+        table_ref[at, :] = table_ref[at, :] + small_ref[12 + place : 13 + place, :]
+    sums_out(spot_ref, small_ref, up_ref, qv_ref, lines)
+
+
+def zero_kernel(spot_ref, table_hbm, block_ref, sems):
+    block_ref[...] = jnp.zeros_like(block_ref)
+    rows = block_ref.shape[0]
+    fetch(
+        [
+            (block_ref, table_hbm.at[i * rows : (i + 1) * rows, :])
+            for i in range(table_hbm.shape[0] // rows)
+        ],
+        sems,
+    )
+
+
+def close_kernel(
+    spot_ref, steps_ref, p0, p1, p2, p3, out_own, out_one, out_two, in_own, in_far,
+    zero_hbm,
+    out_hbm, in_hbm, up_hbm, down_hbm, qkv_hbm, proj_hbm, table_hbm, up_ref, qv_ref, *refs,
+):
+    lines, refs = refs[:6], refs[6:]
+    out_all, in_all, up_all, down_all, qkv_all, proj_all, rows_ref, blocks_ref, sems = refs
+    copies = []
+
+    def send(source, target, alone=None):
+        copy = pltpu.make_async_copy(source, target, sems.at[len(copies)])
+        copies.append((copy, alone))
+        copy.start() if alone is None else pl.when(alone)(copy.start)
+
+    fill_rows(spot_ref, out_own, (out_one, out_two), out_all)
+    send(out_all, out_hbm)
+    start, count = out_one.shape[0] - 2 * rows_ref.shape[0], rows_ref.shape[0]
+    parts = [
+        both(ref[start : start + count, :], ref[start + count :, :]) for ref in (out_one, out_two)
+    ]
+    rows_ref[...] = parts[0] + parts[1]
+    places = range(steps_ref.shape[0])
+    at = lax.broadcasted_iota(jnp.int32, (8, 1), 0)
+    for place in places:
+        block = steps_ref[place] // 8
+        total_rows = jnp.zeros(blocks_ref.shape[1:], F32)
+        for other in places:
+            step = steps_ref[other]
+            row = jnp.where(step // 8 == block, step % 8, -1)
+            total_rows = total_rows + jnp.where(at == row, rows_ref[12 + other : 13 + other, :], 0.0)
+        blocks_ref[place] = total_rows
+        seen = [steps_ref[other] // 8 == block for other in range(place)]
+        alone = jnp.logical_not(functools.reduce(jnp.logical_or, seen)) if seen else None
+        send(blocks_ref.at[place], table_hbm.at[pl.ds(pl.multiple_of(block * 8, 8), 8), :], alone)
+    sums_out(spot_ref, rows_ref, up_ref, qv_ref, lines)
+    rows, hidden, cols = p0.shape[0], up_all.shape[1], proj_all.shape[1]
+    pieces = (p0, p1, p2, p3)
+    spots = [window(spot_ref[1] ^ bits, rows) for bits in range(4)]
+    for i, (whole, target) in enumerate(((up_all, up_hbm), (down_all, down_hbm))):
+        for spot, piece in zip(spots, pieces):
+            whole[spot, :] = piece[:, i * hidden : (i + 1) * hidden].astype(F32)
+        send(whole, target)
+    start = 2 * hidden
+    for spot, piece in zip(spots, pieces):
+        for i in range(3):
+            qkv_all[i, spot, :] = piece[:, start + i * cols : start + (i + 1) * cols].astype(F32)
+        proj_all[spot, :] = piece[:, start + 3 * cols :].astype(F32)
+    send(qkv_all, qkv_hbm)
+    send(proj_all, proj_hbm)
+    fill_rows(spot_ref, in_own, (in_far,), in_all)
+    send(in_all, in_hbm)
+    for copy, alone in copies:
+        copy.wait() if alone is None else pl.when(alone)(copy.wait)
 
 
 class Reduction:
@@ -749,65 +845,92 @@
     line = lambda values: values.reshape(1, -1)
     dma = lambda count: pltpu.SemaphoreType.DMA((count,))
 
-    pack, rest, quarter = order.call(
+    pack, qkv_part, out_part_own = order.call(
         pack_kernel,
         [
-            ((rows + BIAS_ROWS, 4 * cols), BF16), ((rows, 2 * hidden), BF16),
-            ((rows // 4 + PAD * (parts == 2), 2 * hidden), BF16),
+            ((rows + BIAS_ROWS, 4 * cols), BF16), ((rows + BIAS_ROWS, 3 * cols), BF16),
+            ((rows, cols), BF16),
         ],
-        [timesteps, w_qkv, w_out_t, b_qv, line(b_up), w_up, w_down_t],
-        far=range(7),
+        [timesteps, w_qkv, w_out_t, b_qv, line(b_up)],
+        far=range(5),
         scratch=[
             pltpu.VMEM(w_qkv.shape, F32),
             pltpu.VMEM(w_out_t.shape, F32),
             pltpu.VMEM(b_qv.shape, F32),
             pltpu.VMEM((1, hidden), F32),
-            pltpu.VMEM(w_up.shape, F32),
-            pltpu.VMEM(w_down_t.shape, F32),
-            dma(6),
+            dma(4),
         ],
     )
     near = pieces_of(order, pack, parts, rows)
-    pack_far = order.swap(pack, "tp", 2)
-    stream, normed, seg, lines, cotan = order.call(
-        stream_kernel,
-        [
+    pack_far = order.swap(qkv_part, "tp", 2)
+    projected = [((span, cols), BF16), ((span, 2 * cols), BF16)]
+    more = [((span, cols), BF16), ((span + PAD, 2 * cols), BF16)]
+    q_near, kv_near, stream, normed, seg, lines = order.call(
+        functools.partial(open_kernel, row=rows),
+        projected
+        + [
             ((span, width), F32), ((span, width), BF16), ((1, segment_ids.shape[1]), jnp.int32),
-            ((8, width), F32), ((span, width), F32),
+            ((8, width), F32),
         ],
-        [timesteps, layer_input, time_table, segment_ids, out_grad]
-        + [line(v) for v in (ln1_gain, ln1_bias, ln2_gain, ln2_bias, b_out, b_down)],
-        far=range(11),
+        [timesteps, layer_input, time_table, segment_ids]
+        + [line(v) for v in (ln1_gain, ln1_bias, ln2_gain, ln2_bias, b_out, b_down)]
+        + [*near, pack],
+        far=range(10),
         scratch=[
             pltpu.VMEM((span, width), F32),
             pltpu.VMEM((8, width), F32),
             pltpu.VMEM(segment_ids.shape, jnp.int32),
             pltpu.VMEM((6, 1, width), F32),
-            dma(10),
+            dma(9),
         ],
     )
-    projected = [((span, cols), BF16), ((span, 2 * cols), BF16)]
-    more = [((span, cols), BF16), ((span + PAD, 2 * cols), BF16)]
+    kvs_near = [kv_near] + order.swap_three(kv_near, "ctx")
     project = functools.partial(project_kernel, row=rows)
-    q_near, kv_near = order.call(project, projected, [normed, *near, pack])
-    kvs_near = [kv_near] + order.swap_three(kv_near, "ctx")
-    rest_far = order.swap(quarter if parts == 2 else rest, "tp", 2)
+
+    side_shape = (rows // 4 + rows // 8, 2 * hidden) if parts == 2 else (rows, cols)
+    rest, side, cotan = order.call(
+        pack_rest_kernel,
+        [((rows, 2 * hidden), BF16), (side_shape, BF16), ((span, width), F32)],
+        [out_part_own, w_up, w_down_t, out_grad],
+        far=(1, 2, 3),
+        scratch=[pltpu.VMEM(w_up.shape, F32), pltpu.VMEM(w_down_t.shape, F32), dma(3)],
+        cost=QUICK,
+    )
+    side_far = order.swap(side, "tp", 2)
+    if parts == 2:
+        table = order.call(
+            zero_kernel,
+            [(time_table.shape, F32)],
+            [],
+            kept=(0,),
+            scratch=[pltpu.VMEM((time_table.shape[0] // 5, width), F32), dma(5)],
+            cost=QUICK,
+        )[0]
     rest_near = pieces_of(order, rest, parts, rows)
 
     attended = [((span, cols), BF16), ((span, cols), F32)]
     pack_far, *kvs_near[1:] = hold(pack_far, *kvs_near[1:])
     far = pieces_of(order, pack_far, parts, rows)
     mixed_near, lse_near = order.call(
-        attend_one_kernel, attended, [seg, q_near, *kvs_near], cost=QUICK
+        attend_one_kernel, attended, [seg, q_near, *kvs_near], cost=COST
     )
     q_far, kv_far = order.call(project, more, [normed, *far, pack_far], cost=QUICK)
     kvs_far = [kv_far] + order.swap_three(kv_far, "ctx")
     if parts == 2:
+        rest_far, out_far = order.call(
+            unpack_kernel,
+            [((rows // 4, 2 * hidden), BF16), ((rows, cols), BF16)],
+            [side_far],
+            cost=QUICK,
+        )
         rest_turn = order.swap_turn(rest_far, 0)
+    else:
+        rest_far, out_far = order.swap(rest, "tp", 2), side_far
+    out_far = pieces_of(order, out_far, parts, rows)
     mixed_far, lse_far, given = order.call(
         attend_two_kernel,
         attended + [((span + PAD, width), BF16)],
-        [seg, q_far, *kvs_far, mixed_near, *near, *far],
+        [seg, q_far, *kvs_far, mixed_near, *near, *out_far],
     )
     got = order.swap(given, "tp", 1)
     if parts == 2:
@@ -822,7 +945,7 @@
         rest_far = pieces_of(order, rest_far, parts, rows)
 
     acts = [((span, hidden), BF16), ((span, hidden), BF16)]
-    back_near, ffn_near, out_base, resid, normed_two, act_n, pre_n, low, up_near = order.call(
+    back_near, down_near, out_base, resid, normed_two, act_n, pre_n, low, up_near = order.call(
         functools.partial(ffn_near_kernel, row=rows),
         [((span, width), F32)] * 4
         + [((span, width), BF16), *acts, ((span, width), BF16), ((1, hidden), F32)],
@@ -831,7 +954,7 @@
     act_f, pre_f, up_far, back, ffn_terms = order.call(
         functools.partial(ffn_far_kernel, row=rows),
         [*acts, ((1, hidden), F32), ((span + PAD, width), BF16), ((span, width), BF16)],
-        [normed_two, low, back_near, ffn_near, pack_far, *rest_far],
+        [normed_two, low, back_near, down_near, pack_far, *rest_far],
         scratch=[pltpu.VMEM((size, 2 * hidden), BF16)] * 2,
     )
     back_got = order.swap(back, "tp", 1)
@@ -856,7 +979,7 @@
         + [((span, width), F32), ((span, width), BF16), ((4, width), F32)],
         [
             seg, q_near, lse_near, *kvs_near, q_far, lse_far, *kvs_far, back, back_got, resid,
-            cotan, lines, *near, *far,
+            cotan, lines, *near, *out_far,
         ],
         scratch=[pltpu.VMEM((2, span, width), F32)],
         limit=6,
@@ -868,7 +991,7 @@
         ffn_near, sent, out_low = order.call(
             middle_kernel,
             [
-                ((rows // 2, 2 * hidden), F32), ((span // 2 + rows, width), BF16),
+                ((rows // 2, 2 * hidden), F32), ((span // 2 + rows + 2 * PAD, width), BF16),
                 ((span, width), BF16),
             ],
             [ffn_own, ffn_turn, out_base, ffn_terms, terms_got],
@@ -879,7 +1002,8 @@
         out_low = order.call(
             add_pair_kernel, [((span, width), BF16)], [out_base, ffn_terms, terms_got]
         )[0]
-        out_got = order.swap(out_low, "tp", 2)
+        half_rows = lax.dynamic_slice_in_dim(out_low, shard % 2 * (span // 2), span // 2, 0)
+        out_half = order.swap(half_rows, "tp", 2)
 
     seqs = 2 * parts
     small_rows = -(-(12 + seqs) // 16) * 16
@@ -887,8 +1011,8 @@
         input_kernel,
         [
             ((span, width), BF16), ((small_rows, width), F32),
-            ((size, 8 * cols), F32), ((size + small_rows, 4 * cols), BF16),
-            ((size + small_rows, 4 * cols), BF16),
+            ((size, 8 * cols), F32), ((size + small_rows, 3 * cols), BF16),
+            ((size + small_rows, 3 * cols), BF16), ((size + small_rows, 2 * cols), BF16),
         ],
         [
             stream, lines, resid_rows, up_near, up_far, dq, own, *shared, *near, *far,
@@ -901,44 +1025,35 @@
         attention_far = [order.swap(piece, "fsdp", 1) for piece in attention_sent]
     in_got = order.swap(in_terms, "tp", 1)
     if parts == 2:
-        attention_sum = Reduction(order, attention_kept, small)
-        attention_sum.cut(attention_far)
-        out_half, ffn_own, ffn_cut = order.call(
+        sums = Reduction(order, attention_kept, small)
+        sums.cut(attention_far)
+        out_half, ffn_own, *ffn_cuts = order.call(
             settle_kernel,
-            [
-                ((span // 2, width), BF16), ((rows // 4, 2 * hidden), F32),
-                ((rows // 4, 2 * hidden), BF16),
-            ],
+            [((span // 2, width), BF16), ((rows // 4, 2 * hidden), F32)]
+            + [((rows // 4, hidden), BF16)] * 2,
             [ffn_near, sent_got],
-            cost=COST,
-        )
-        ffn_turn = order.swap_turn(ffn_cut, 1)
-        out_more = order.swap(out_half, "tp", 1)
-        attention_sum.shards()
-    else:
-        output = order.call(pair_kernel, [((2 * span, width), F32)], [out_low, out_got])[0]
+        )
+        ffn_turns = [order.swap_turn(piece, 1) for piece in ffn_cuts]
+        sums.shards()
     in_low = order.call(
         add_pair_kernel, [((span, width), BF16)], [resid_grad, in_terms, in_got]
     )[0]
+    if parts == 2:
+        in_low, sums.got = hold(in_low, sums.got)
     in_far = order.swap(in_low, "tp", 2)
+    vectors = [((1, hidden), F32), ((2, cols), F32)] + [((1, width), F32)] * 6
+    large = [((2 * span, width), F32)] * 2
     if parts == 2:
-        attention = attention_sum
-        owned, small = order.call(
+        owned, passed = order.call(
             owned_kernel,
-            [((rows // 4, 2 * hidden + 4 * cols), BF16), (small.shape, F32)],
-            [ffn_own, ffn_turn, attention.own, attention.sent, attention.got],
-        )
-        small_got = order.swap(small, "tp", 1)
+            [
+                ((rows // 4, 2 * hidden + 4 * cols), BF16),
+                ((span // 2 + 2 * small_rows, width), BF16),
+            ],
+            [ffn_own, *ffn_turns, sums.own, sums.sent, sums.got, out_half],
+        )
+        passed_got = order.swap(passed, "tp", 1)
         pieces = [owned] + order.swap_three(owned, "ctx")
-    if parts == 2:
-        output, grad_input = order.call(
-            rows_kernel,
-            [((2 * span, width), F32)] * 2,
-            [out_low, out_half, out_more, in_low, in_far],
-        )
-    else:
-        grad_input = order.call(pair_kernel, [((2 * span, width), F32)], [in_low, in_far])[0]
-    if parts == 2:
         bits = near[1][rows : rows + 9 : 3, 2 * cols : 2 * cols + 2].astype(F32)
         far_steps = jnp.sum(bits, axis=0).astype(jnp.int32)
         steps = jnp.where(
@@ -946,31 +1061,42 @@
             jnp.concatenate([timesteps, far_steps]),
             jnp.concatenate([far_steps, timesteps]),
         )
+        large = large + [((rows, hidden), F32)] * 2 + [((3, rows, cols), F32), ((rows, cols), F32)]
+        output, grad_input, grads_up, grads_down, grads_qkv, grads_out, table, *rest = order.call(
+            close_kernel,
+            large + [(time_table.shape, F32)] + vectors,
+            [
+                steps, *pieces, out_low, passed, passed_got, in_low, in_far, table,
+            ],
+            far=(10,),
+            kept=range(7),
+            alias={10: 6},
+            scratch=[pltpu.VMEM(shape, dtype) for shape, dtype in large]
+            + [pltpu.VMEM((small_rows, width), F32), pltpu.VMEM((seqs, 8, width), F32)]
+            + [dma(6 + seqs)],
+            limit=8,
+        )
     else:
+        output, grad_input = order.call(
+            rows_kernel, large, [out_low, out_half, order.swap(out_half, "tp", 1), in_low, in_far]
+        )
         ffn_sent = jnp.concatenate(ffn_sent, axis=1)
         both_grads = reduce_plainly(ffn_kept, ffn_sent, chunk)
         grads_up, grads_down = both_grads[:, :hidden], both_grads[:, hidden:]
-        small = lax.psum(small, ("fsdp", "ctx", "tp"))
-        small_got = jnp.zeros_like(small)
-        steps = lax.all_gather(timesteps, "fsdp", axis=0, tiled=True)
-    table, up_line, qv_lines, *sums = order.call(
-        sums_kernel,
-        [(time_table.shape, F32), ((1, hidden), F32), ((2, cols), F32)] + [((1, width), F32)] * 6,
-        [steps, small, small_got],
-        scratch=[pltpu.VMEM(small.shape, F32)],
-    )
-    sums = [values.reshape(-1) for values in sums]
-    if parts == 2:
-        grads_up, grads_down, grads_qkv, grads_out = order.call(
-            own_kernel,
-            [((rows, hidden), F32)] * 2 + [((3, rows, cols), F32), ((rows, cols), F32)],
-            pieces,
-        )
-    else:
-        attention_sent = jnp.concatenate(attention_sent, axis=1)[:size]
+        near_part, far_part, out_columns = [piece[:size] for piece in attention_sent]
+        attention_sent = jnp.concatenate(
+            [near_part, out_columns[:, :cols], far_part, out_columns[:, cols:]], axis=1
+        )
         every = reduce_plainly(attention_kept, attention_sent, chunk)
         grads_qkv = jnp.stack([every[:, i * cols : (i + 1) * cols] for i in range(3)])
         grads_out = every[:, 3 * cols :]
+        small = lax.psum(small, ("fsdp", "ctx", "tp"))
+        steps = lax.all_gather(timesteps, "fsdp", axis=0, tiled=True)
+        table, *rest = order.call(
+            plain_sums_kernel, [(time_table.shape, F32)] + vectors, [steps, small]
+        )
+    up_line, qv_lines, *sums = rest
+    sums = [values.reshape(-1) for values in sums]
 
     shape = layer_input.shape
     return (

time: 123 us -> 119 us (0.967)
  waiting for transfers between devices: 51.2 us -> 42.6 us
  starting transfers between devices: 37.6 us -> 40.6 us
    ppermute x37 -> x38, waiting for transfers between devices: 46.3 us -> 37.7 us  [swap(): return lax.ppermute(values, axis, [(i, i ^ bits) for i in range(size)])]
    ppermute x37 -> x38, starting transfers between devices: 31.5 us -> 34 us  [swap(): return lax.ppermute(values, axis, [(i, i ^ bits) for i in range(size)])]
    ppermute x4 -> x5, starting transfers between devices: 6.07 us -> 6.59 us  [swap_turn(): return lax.ppermute(values, ('fsdp', 'ctx'), pairs)]
    ppermute x4 -> x5, waiting for transfers between devices: 4.86 us -> 4.94 us  [swap_turn(): return lax.ppermute(values, ('fsdp', 'ctx'), pairs)]
  transfers between devices with their start and end apart: 41 -> 43, of which waited for: 22 -> 18; matrix products, arithmetic and copies ran while one was open for 0% -> 0% of each run, Pallas kernels for 22% -> 23%
where the time goes in v4:
time: 119 us; the launch traced here: 118 us
  waiting for transfers between devices  42.6 us (36%)
  starting transfers between devices  40.6 us (34%)
  Pallas kernels  33.9 us (28%)
    ppermute x38, waiting for transfers between devices, swap(): return lax.ppermute(values, axis, [(i, i ^ bits) for i in range(size)])  37.7 us
    ppermute x38, starting transfers between devices, swap(): return lax.ppermute(values, axis, [(i, i ^ bits) for i in range(size)])  34 us
    pallas_call x22, Pallas kernels, call(): pl.pallas_call(body, out_shape=tuple((jax.ShapeDtypeStruct(shape, dtype)...  33.9 us
    ppermute x5, starting transfers between devices, swap_turn(): return lax.ppermute(values, ('fsdp', 'ctx'), pairs)  6.59 us
    ppermute x5, waiting for transfers between devices, swap_turn(): return lax.ppermute(values, ('fsdp', 'ctx'), pairs)  4.94 us
  transfers between devices with their start and end apart: 43, of which 18 were waited for; matrix products, arithmetic and copies ran while one was open for 0% of the time, Pallas kernels for 23%

profile of v4, /device:TPU:0, one launch (start us, length us, event | category | flops | bytes accessed | tf_op | source)
XLA Modules:
  0.0 118.4 jit_solution(4493959893771811268)
XLA Ops:
  0.7 1.8 %shard_map.280 = (bf16[272,512]{1,0:T(8,128)(2,1)S(1)}, bf16[272,384]{1,0:T(8,128)(2,1)S(1)}, bf16[256,128]{1,0:T(8,128)(2,1)S(1)}) custom-call(s32[2]{0:T(128)} %refs_0_.3, f32[3,256,128]{2,1,0:T(8,128)} %refs_1_.3, f32[256,128]{1,0:T(8,128)} %refs_2_.3, f32[2,128]{1,0:T(2,128)} %refs_3_.3, f32[1,512]{1,0:T(1,128)} %bitcast.22, ...), custom_call_target="tpu_custom_call" | custom-call | flops 8000000000 | bytes 65536 | tf_op jit(solution)/shard_map/pallas_call | solution.py:89
  2.5 0.5 collective-permute-start
  3.1 3.7 %collective-permute-start.1 = (bf16[272,384]{1,0:T(8,128)(2,1)S(1)}, bf16[272,384]{1,0:T(8,128)(2,1)S(1)}, u32[]{:S(2)}, u32[]{:S(2)}) collective-permute-start(bf16[272,384]{1,0:T(8,128)(2,1)S(1)} %get-tuple-element.243), channel_id=1, source_target_pairs={{0,2},{1,3},{2,0},{3,1},{4,6},{5,7},{6,4},{7,5},{8,10},{9,11},{10,... | collective-permute-start | bytes 626696 | tf_op jit(solution)/shard_map/swap_tp_2/ppermute | solution.py:111
  6.7 2.4 %shard_map.281 = (bf16[256,128]{1,0:T(8,128)(2,1)S(1)}, bf16[256,256]{1,0:T(8,128)(2,1)S(1)}, f32[256,512]{1,0:T(8,128)S(1)}, bf16[256,512]{1,0:T(8,128)(2,1)S(1...) custom-call(s32[2]{0:T(128)} %refs_0_.3, f32[2,256,512]{2,1,0:T(8,128)} %refs_1_.4, f32[1000,512]{1,0:T(8,128)} %refs_2_.4, ...), custom_call_target="tpu_custom_call" | custom-call | flops 8000000000 | bytes 65536 | tf_op jit(solution)/shard_map/pallas_call | solution.py:89
  9.1 2.5 %collective-permute-start.4 = (bf16[256,256]{1,0:T(8,128)(2,1)S(1)}, bf16[256,256]{1,0:T(8,128)(2,1)S(1)}, u32[]{:S(2)}, u32[]{:S(2)}) collective-permute-start(bf16[256,256]{1,0:T(8,128)(2,1)S(1)} %get-tuple-element.251.refs_2_.refs_3_), channel_id=1, source_target_pairs={{0,12},{4,8},{8,4},{12,0},{1,13},{5,9},{9,5},{13,1},{2,14},{6,10},... | collective-permute-start | bytes 393224 | tf_op jit(solution)/shard_map/swap_ctx_3/ppermute | solution.py:111
  11.6 0.5 collective-permute-start.3
  12.1 0.5 collective-permute-start.2
  12.7 2.0 %shard_map.282 = (bf16[256,1024]{1,0:T(8,128)(2,1)S(1)}, bf16[96,1024]{1,0:T(8,128)(2,1)S(1)}, f32[256,512]{1,0:T(8,128)S(1)}) custom-call(bf16[256,128]{1,0:T(8,128)(2,1)S(1)} %get-tuple-element.253.refs_0_, f32[256,512]{1,0:T(8,128)} %refs_1_.5, f32[256,512]{1,0:T(8,128)} %refs_2_.5, f32[2,256,512]{2,1,0:T(8,128)} %refs_3_.5, ...), custom_call_target="tpu_custom_call" | custom-call | flops 1000 | bytes 65536 | tf_op jit(solution)/shard_map/pallas_call | solution.py:89
  14.7 1.9 %shard_map.283.refs_10_ = f32[1000,512]{1,0:T(8,128)} custom-call(s32[4]{0:T(128)S(1)} %pad_add_fusion.refs_5_.refs_13_.refs_4_.refs_0_.refs_6_.refs_1_.refs_11_.refs_2_.refs_8_.refs_9_.refs_22_.refs_18_.refs_3_.refs_7_), custom_call_target="tpu_custom_call" | custom-call | flops 1000 | bytes 65536 | tf_op jit(solution)/shard_map/pallas_call | solution.py:89
  16.6 1.5 %collective-permute-start.9 = (bf16[96,1024]{1,0:T(8,128)(2,1)S(1)}, bf16[96,1024]{1,0:T(8,128)(2,1)S(1)}, u32[]{:S(2)}, u32[]{:S(2)}) collective-permute-start(bf16[96,1024]{1,0:T(8,128)(2,1)S(1)} %get-tuple-element.280), channel_id=1, source_target_pairs={{0,2},{1,3},{2,0},{3,1},{4,6},{5,7},{6,4},{7,5},{8,10},{9,11},{10,... | collective-permute-start | bytes 589832 | tf_op jit(solution)/shard_map/swap_tp_2/ppermute | solution.py:111
  18.5 1.9 %shard_map.284 = (bf16[256,128]{1,0:T(8,128)(2,1)S(1)}, f32[256,128]{1,0:T(8,128)S(1)}) custom-call(s32[1,1024]{1,0:T(1,128)S(1)} %get-tuple-element.241.refs_0_, bf16[256,128]{1,0:T(8,128)(2,1)S(1)} %get-tuple-element.263.refs_1_, bf16[256,256]{1,0:T(8,128)(2,1)S(1)} %get-tuple-element.251.refs_2_.refs_3_, ...), custom_call_target="tpu_custom_call" | custom-call | flops 8000000000 | bytes 65536 | tf_op jit(solution)/shard_map/pallas_call | solution.py:89
  20.5 0.8 shard_map.285
  21.3 2.2 %collective-permute-start.8 = (bf16[272,256]{1,0:T(8,128)(2,1)S(1)}, bf16[272,256]{1,0:T(8,128)(2,1)S(1)}, u32[]{:S(2)}, u32[]{:S(2)}) collective-permute-start(bf16[272,256]{1,0:T(8,128)(2,1)S(1)} %get-tuple-element.278.refs_2_.refs_9_), channel_id=1, source_target_pairs={{0,12},{4,8},{8,4},{12,0},{1,13},{5,9},{9,5},{13,1},{2,14},{6,10},... | collective-permute-start | bytes 417800 | tf_op jit(solution)/shard_map/swap_ctx_3/ppermute | solution.py:111
  23.5 0.8 collective-permute-start.7
  24.4 0.5 collective-permute-start.6
  24.9 3.0 %collective-permute-done.9.refs_0_ = bf16[96,1024]{1,0:T(8,128)(2,1)S(1)} collective-permute-done((bf16[96,1024]{1,0:T(8,128)(2,1)S(1)}, bf16[96,1024]{1,0:T(8,128)(2,1)S(1)}, u32[]{:S(2)}, u32[]{:S(2)}) %collective-permute-start.9) | collective-permute-done | bytes 196640 | tf_op jit(solution)/shard_map/swap_tp_2/ppermute | solution.py:111
  27.9 0.6 shard_map.286
  28.5 0.5 collective-permute-start.12
  29.0 0.7 collective-permute-done.10.refs_10_.refs_21_
  29.8 1.5 %collective-permute-start.13 = (bf16[64,1024]{1,0:T(8,128)(2,1)S(1)}, bf16[64,1024]{1,0:T(8,128)(2,1)S(1)}, u32[]{:S(2)}, u32[]{:S(2)}) collective-permute-start(bf16[64,1024]{1,0:T(8,128)(2,1)S(1)} %get-tuple-element.295.refs_0_), channel_id=1, source_target_pairs={{0,4},{4,0},{8,12},{12,8},{16,24},{20,28},{24,16},{28,20},{1,5},{5... | collective-permute-start | bytes 393224 | tf_op jit(solution)/shard_map/swap_turn_0/ppermute | solution.py:126
  31.4 2.2 %shard_map.287 = (bf16[256,128]{1,0:T(8,128)(2,1)S(1)}, f32[256,128]{1,0:T(8,128)S(1)}, bf16[272,512]{1,0:T(8,128)(2,1)S(1)}) custom-call(s32[1,1024]{1,0:T(1,128)S(1)} %get-tuple-element.241.refs_0_, bf16[256,128]{1,0:T(8,128)(2,1)S(1)} %get-tuple-element.271.refs_1_.refs_7_, bf16[272,256]{1,0:T(8,128)(2,1)S(1)} %get-tuple-element.278.refs_2_.refs_9_, ...), custom_call_target="tpu_custom_call" | custom-call | flops 8000000000 | bytes 65536 | tf_op jit(solution)/shard_map/pallas_call | solution.py:89
  33.6 1.7 %collective-permute-start.11 = (bf16[272,512]{1,0:T(8,128)(2,1)S(1)}, bf16[272,512]{1,0:T(8,128)(2,1)S(1)}, u32[]{:S(2)}, u32[]{:S(2)}) collective-permute-start(bf16[272,512]{1,0:T(8,128)(2,1)S(1)} %get-tuple-element.290.refs_1_), channel_id=1, source_target_pairs={{0,1},{1,0},{2,3},{3,2},{4,5},{5,4},{6,7},{7,6},{8,9},{9,8},{10,11... | collective-permute-start | bytes 835592 | tf_op jit(solution)/shard_map/swap_tp_1/ppermute | solution.py:111
  35.3 0.6 shard_map.288.refs_5_
  35.8 1.5 %collective-permute-start.14 = (bf16[128,1024]{1,0:T(8,128)(2,1)S(1)}, bf16[128,1024]{1,0:T(8,128)(2,1)S(1)}, u32[]{:S(2)}, u32[]{:S(2)}) collective-permute-start(bf16[128,1024]{1,0:T(8,128)(2,1)S(1)} %shard_map.288.refs_5_), channel_id=1, source_target_pairs={{0,8},{4,12},{8,0},{12,4},{16,20},{20,16},{24,28},{28,24},{1,9},{5... | collective-permute-start | bytes 786440 | tf_op jit(solution)/shard_map/swap_turn_1/ppermute | solution.py:126
  37.4 4.9 %collective-permute-done.14.refs_6_ = bf16[128,1024]{1,0:T(8,128)(2,1)S(1)} collective-permute-done((bf16[128,1024]{1,0:T(8,128)(2,1)S(1)}, bf16[128,1024]{1,0:T(8,128)(2,1)S(1)}, u32[]{:S(2)}, u32[]{:S(2)}) %collective-permute-start.14) | collective-permute-done | bytes 262176 | tf_op jit(solution)/shard_map/swap_turn_1/ppermute | solution.py:126
  42.3 1.9 %shard_map.289 = (f32[256,512]{1,0:T(8,128)S(1)}, f32[256,512]{1,0:T(8,128)S(1)}, f32[256,512]{1,0:T(8,128)S(1)}, f32[256,512]{1,0:T(8,128)S(1)}, bf16[256,512]{...) custom-call(f32[256,512]{1,0:T(8,128)S(1)} %get-tuple-element.240.re, ...), custom_call_target="tpu_custom_call" | custom-call | flops 8000000000 | bytes 65536 | tf_op jit(solution)/shard_map/pallas_call | solution.py:89
  44.2 1.6 %shard_map.290 = (bf16[256,512]{1,0:T(8,128)(2,1)S(1)}, bf16[256,512]{1,0:T(8,128)(2,1)S(1)}, f32[1,512]{1,0:T(1,128)S(1)}, bf16[272,512]{1,0:T(8,128)(2,1)S(1)}, bf16[256,512]{1,0:T(8,128)(2,1)S(1)}) custom-call(bf16[256,512]{1,0:T(8,128)(2,1)S(1)} %get-tuple-element.302.refs_0_, bf16[256,512]{1,0:T(8,128)(2,1)S(1)} %get-tuple-element.303.refs_1_, ...), custom_call_target="tpu_custom_call" | custom-call | flops 8000000000 | bytes 65536 | tf_op jit(solution)/shard_map/pallas_call | solution.py:89
  45.8 1.6 %collective-permute-start.22 = (bf16[272,512]{1,0:T(8,128)(2,1)S(1)}, bf16[272,512]{1,0:T(8,128)(2,1)S(1)}, u32[]{:S(2)}, u32[]{:S(2)}) collective-permute-start(bf16[272,512]{1,0:T(8,128)(2,1)S(1)} %get-tuple-element.342.refs_13_), channel_id=1, source_target_pairs={{0,1},{1,0},{2,3},{3,2},{4,5},{5,4},{6,7},{7,6},{8,9},{9,8},{10,11... | collective-permute-start | bytes 835592 | tf_op jit(solution)/shard_map/swap_tp_1/ppermute | solution.py:111
  47.4 1.3 %shard_map.291 = (f32[256,2048]{1,0:T(8,128)S(1)}, bf16[256,512]{1,0:T(8,128)(2,1)S(1)}, bf16[256,512]{1,0:T(8,128)(2,1)S(1)}, bf16[256,512]{1,0:T(8,128)(2,1)S(1)}, bf16[256,512]{1,0:T(8,128)(2,1)S(1)}) custom-call(bf16[256,512]{1,0:T(8,128)(2,1)S(1)} %get-tuple-element.302.refs_0_, bf16[256,512]{1,0:T(8,128)(2,1)S(1)} %get-tuple-element.303.refs_1_, ...), custom_call_target="tpu_custom_call" | custom-call | flops 8000000000 | bytes 65536 | tf_op jit(solution)/shard_map/pallas_call | solution.py:89
  48.7 0.5 collective-permute-start.19
  49.3 0.4 collective-permute-start.17
  49.7 0.5 collective-permute-done.20.refs_4_
  51.4 0.7 shard_map.292
  52.1 1.6 %collective-permute-start.21 = (bf16[128,2048]{1,0:T(8,128)(2,1)S(1)}, bf16[128,2048]{1,0:T(8,128)(2,1)S(1)}, u32[]{:S(2)}, u32[]{:S(2)}) collective-permute-start(bf16[128,2048]{1,0:T(8,128)(2,1)S(1)} %get-tuple-element.337), channel_id=1, source_target_pairs={{0,4},{4,0},{8,12},{12,8},{16,24},{20,28},{24,16},{28,20},{1,5},{5... | collective-permute-start | bytes 1572872 | tf_op jit(solution)/shard_map/swap_turn_0/ppermute | solution.py:126
  53.7 1.2 %collective-permute-done.22.refs_14_ = bf16[272,512]{1,0:T(8,128)(2,1)S(1)} collective-permute-done((bf16[272,512]{1,0:T(8,128)(2,1)S(1)}, bf16[272,512]{1,0:T(8,128)(2,1)S(1)}, u32[]{:S(2)}, u32[]{:S(2)}) %collective-permute-start.22) | collective-permute-done | bytes 278560 | tf_op jit(solution)/shard_map/swap_tp_1/ppermute | solution.py:111
  54.9 5.4 %shard_map.293 = (f32[256,256]{1,0:T(8,128)S(1)}, f32[256,512]{1,0:T(8,128)S(1)}, bf16[272,512]{1,0:T(8,128)(2,1)S(1)}, bf16[272,512]{1,0:T(8,128)(2,1)S(1)}, bf...) custom-call(s32[1,1024]{1,0:T(1,128)S(1)} %get-tuple-element.241.refs_, ...), custom_call_target="tpu_custom_call" | custom-call | flops 8000000000 | bytes 65536 | tf_op jit(solution)/shard_map/pallas_call | solution.py:89
  60.3 2.0 %collective-permute-start.27 = (bf16[272,512]{1,0:T(8,128)(2,1)S(1)}, bf16[272,512]{1,0:T(8,128)(2,1)S(1)}, u32[]{:S(2)}, u32[]{:S(2)}) collective-permute-start(bf16[272,512]{1,0:T(8,128)(2,1)S(1)} %get-tuple-element.367), channel_id=1, source_target_pairs={{0,12},{4,8},{8,4},{12,0},{1,13},{5,9},{9,5},{13,1},{2,14},{6,10},... | collective-permute-start | bytes 835592 | tf_op jit(solution)/shard_map/swap_ctx_3/ppermute | solution.py:111
  62.3 1.0 collective-permute-start.26
  63.4 0.5 collective-permute-start.25
  64.3 6.7 %collective-permute-done.23.refs_4_ = bf16[256,512]{1,0:T(8,128)(2,1)S(1)} collective-permute-done((bf16[256,512]{1,0:T(8,128)(2,1)S(1)}, bf16[256,512]{1,0:T(8,128)(2,1)S(1)}, u32[]{:S(2)}, u32[]{:S(2)}) %collective-permute-start.23) | collective-permute-done | bytes 262176 | tf_op jit(solution)/shard_map/swap_tp_1/ppermute | solution.py:111
  71.0 0.9 shard_map.294
  71.9 1.5 %collective-permute-start.24 = (bf16[416,512]{1,0:T(8,128)(2,1)S(1)}, bf16[416,512]{1,0:T(8,128)(2,1)S(1)}, u32[]{:S(2)}, u32[]{:S(2)}) collective-permute-start(bf16[416,512]{1,0:T(8,128)(2,1)S(1)} %get-tuple-element.359), channel_id=1, source_target_pairs={{0,2},{1,3},{2,0},{3,1},{4,6},{5,7},{6,4},{7,5},{8,10},{9,11},{10,... | collective-permute-start | bytes 1277960 | tf_op jit(solution)/shard_map/swap_tp_2/ppermute | solution.py:111
  73.3 2.2 %collective-permute-done.26.refs_8_ = bf16[272,512]{1,0:T(8,128)(2,1)S(1)} collective-permute-done((bf16[272,512]{1,0:T(8,128)(2,1)S(1)}, bf16[272,512]{1,0:T(8,128)(2,1)S(1)}, u32[]{:S(2)}, u32[]{:S(2)}) %collective-permute-start.26) | collective-permute-done | bytes 278560 | tf_op jit(solution)/shard_map/swap_ctx_2/ppermute | solution.py:111
  75.6 1.7 %shard_map.295 = (bf16[256,512]{1,0:T(8,128)(2,1)S(1)}, f32[16,512]{1,0:T(8,128)S(1)}, f32[256,1024]{1,0:T(8,128)S(1)}, bf16[272,384]{1,0:T(8,128)(2,1)S(1)}, bf...) custom-call(f32[256,512]{1,0:T(8,128)S(1)} %get-tuple-element.240.refs_0_, ...), custom_call_target="tpu_custom_call" | custom-call | flops 8000000000 | bytes 65536 | tf_op jit(solution)/shard_map/pallas_call | solution.py:89
  77.4 0.5 collective-permute-start.28
  77.9 1.4 %collective-permute-done.30.refs_3_ = bf16[272,256]{1,0:T(8,128)(2,1)S(1)} collective-permute-done((bf16[272,256]{1,0:T(8,128)(2,1)S(1)}, bf16[272,256]{1,0:T(8,128)(2,1)S(1)}, u32[]{:S(2)}, u32[]{:S(2)}) %collective-permute-start.30) | collective-permute-done | bytes 139296 | tf_op jit(solution)/shard_map/swap_fsdp_1/ppermute | solution.py:111
  79.3 0.7 shard_map.296
  80.0 1.8 %collective-permute-start.35 = (bf16[80,1024]{1,0:T(8,128)(2,1)S(1)}, bf16[80,1024]{1,0:T(8,128)(2,1)S(1)}, u32[]{:S(2)}, u32[]{:S(2)}) collective-permute-start(bf16[80,1024]{1,0:T(8,128)(2,1)S(1)} %get-tuple-element.405), channel_id=1, source_target_pairs={{0,12},{4,8},{8,4},{12,0},{1,13},{5,9},{9,5},{13,1},{2,14},{6,10},... | collective-permute-start | bytes 491528 | tf_op jit(solution)/shard_map/swap_ctx_3/ppermute | solution.py:111
  81.8 1.2 %collective-permute-start.34 = (bf16[80,1024]{1,0:T(8,128)(2,1)S(1)}, bf16[80,1024]{1,0:T(8,128)(2,1)S(1)}, u32[]{:S(2)}, u32[]{:S(2)}) collective-permute-start(bf16[80,1024]{1,0:T(8,128)(2,1)S(1)} %get-tuple-element.404), channel_id=1, source_target_pairs={{0,8},{4,12},{8,0},{12,4},{1,9},{5,13},{9,1},{13,5},{2,10},{6,14},... | collective-permute-start | bytes 491528 | tf_op jit(solution)/shard_map/swap_ctx_2/ppermute | solution.py:111
  83.0 0.5 collective-permute-start.33
  83.5 7.8 %collective-permute-done.24.refs_1_ = bf16[416,512]{1,0:T(8,128)(2,1)S(1)} collective-permute-done((bf16[416,512]{1,0:T(8,128)(2,1)S(1)}, bf16[416,512]{1,0:T(8,128)(2,1)S(1)}, u32[]{:S(2)}, u32[]{:S(2)}) %collective-permute-start.24) | collective-permute-done | bytes 426016 | tf_op jit(solution)/shard_map/swap_tp_2/ppermute | solution.py:111
  91.3 0.6 shard_map.297
  92.0 0.6 shard_map.298
  92.9 1.4 %collective-permute-start.32 = (bf16[64,512]{1,0:T(8,128)(2,1)S(1)}, bf16[64,512]{1,0:T(8,128)(2,1)S(1)}, u32[]{:S(2)}, u32[]{:S(2)}) collective-permute-start(bf16[64,512]{1,0:T(8,128)(2,1)S(1)} %get-tuple-element.401), channel_id=1, source_target_pairs={{0,8},{4,12},{8,0},{12,4},{16,20},{20,16},{24,28},{28,24},{1,9},{5... | collective-permute-start | bytes 196616 | tf_op jit(solution)/shard_map/swap_turn_1/ppermute | solution.py:126
  94.3 0.6 collective-permute-start.31
  94.9 2.1 %collective-permute-done.36.refs_2_ = bf16[256,512]{1,0:T(8,128)(2,1)S(1)} collective-permute-done((bf16[256,512]{1,0:T(8,128)(2,1)S(1)}, bf16[256,512]{1,0:T(8,128)(2,1)S(1)}, u32[]{:S(2)}, u32[]{:S(2)}) %collective-permute-start.36) | collective-permute-done | bytes 262176 | tf_op jit(solution)/shard_map/swap_tp_1/ppermute | solution.py:111
  97.0 0.6 shard_map.299.refs_8_
  97.7 1.6 %collective-permute-done.37.refs_5_ = bf16[96,512]{1,0:T(8,128)(2,1)S(1)} collective-permute-done((bf16[96,512]{1,0:T(8,128)(2,1)S(1)}, bf16[96,512]{1,0:T(8,128)(2,1)S(1)}, u32[]{:S(2)}, u32[]{:S(2)}) %collective-permute-start.37) | collective-permute-done | bytes 98336 | tf_op jit(solution)/shard_map/swap_tp_2/ppermute | solution.py:111
  99.3 0.6 shard_map.300
  99.9 2.9 %collective-permute-start.40 = (bf16[64,1536]{1,0:T(8,128)(2,1)S(1)}, bf16[64,1536]{1,0:T(8,128)(2,1)S(1)}, u32[]{:S(2)}, u32[]{:S(2)}) collective-permute-start(bf16[64,1536]{1,0:T(8,128)(2,1)S(1)} %get-tuple-element.431.refs_1_), channel_id=1, source_target_pairs={{0,12},{4,8},{8,4},{12,0},{1,13},{5,9},{9,5},{13,1},{2,14},{6,10},... | collective-permute-start | bytes 589832 | tf_op jit(solution)/shard_map/swap_ctx_3/ppermute | solution.py:111
  102.8 0.6 collective-permute-start.38
  103.5 2.8 %collective-permute-start.41 = (bf16[160,512]{1,0:T(8,128)(2,1)S(1)}, bf16[160,512]{1,0:T(8,128)(2,1)S(1)}, u32[]{:S(2)}, u32[]{:S(2)}) collective-permute-start(bf16[160,512]{1,0:T(8,128)(2,1)S(1)} %get-tuple-element.433.refs_6_), channel_id=1, source_target_pairs={{0,1},{1,0},{2,3},{3,2},{4,5},{5,4},{6,7},{7,6},{8,9},{9,8},{10,11... | collective-permute-start | bytes 491528 | tf_op jit(solution)/shard_map/swap_tp_1/ppermute | solution.py:111
  106.4 8.7 %collective-permute-done.41.refs_7_ = bf16[160,512]{1,0:T(8,128)(2,1)S(1)} collective-permute-done((bf16[160,512]{1,0:T(8,128)(2,1)S(1)}, bf16[160,512]{1,0:T(8,128)(2,1)S(1)}, u32[]{:S(2)}, u32[]{:S(2)}) %collective-permute-start.41) | collective-permute-done | bytes 163872 | tf_op jit(solution)/shard_map/swap_tp_1/ppermute | solution.py:111
  115.1 3.2 %shard_map.301 = (f32[512,512]{1,0:T(8,128)}, f32[512,512]{1,0:T(8,128)}, f32[256,512]{1,0:T(8,128)}, f32[256,512]{1,0:T(8,128)}, f32[3,256,128]{2,1,0:T(8,128)}...) custom-call(s32[4]{0:T(128)S(1)} %broadcast_select_fusion.refs_0_, ...), custom_call_target="tpu_custom_call", output_to_operand_aliasing={{6}: (10, {})} | custom-call | flops 1000 | bytes 65536 | tf_op jit(solution)/shard_map/pallas_call | solution.py:89
  (51 shorter events, 3.0 us)
Async XLA Ops:
  2.5 4.2 %collective-permute-start = (bf16[272,512]{1,0:T(8,128)(2,1)S(1)}, bf16[272,512]{1,0:T(8,128)(2,1)S(1)}, u32[]{:S(2)}, u32[]{:S(2)}) collective-permute-start(bf16[272,512]{1,0:T(8,128)(2,1)S(1)} %get-tuple-element.236.refs_10_.refs_12_.refs_7_.refs_5_.refs_18_), channel_id=1, source_target_pairs={{0,16},{16,0},{1,17},{17,1},{2,18},{18,2},{3,19},{19,3},{4,20},{20... | collective-permute-start | bytes 835592 | tf_op jit(solution)/shard_map/swap_fsdp_1/ppermute | solution.py:111
  3.1 15.1 %collective-permute-start.1 = (bf16[272,384]{1,0:T(8,128)(2,1)S(1)}, bf16[272,384]{1,0:T(8,128)(2,1)S(1)}, u32[]{:S(2)}, u32[]{:S(2)}) collective-permute-start(bf16[272,384]{1,0:T(8,128)(2,1)S(1)} %get-tuple-element.243), channel_id=1, source_target_pairs={{0,2},{1,3},{2,0},{3,1},{4,6},{5,7},{6,4},{7,5},{8,10},{9,11},{10,... | collective-permute-start | bytes 626696 | tf_op jit(solution)/shard_map/swap_tp_2/ppermute | solution.py:111
  9.1 9.0 %collective-permute-start.4 = (bf16[256,256]{1,0:T(8,128)(2,1)S(1)}, bf16[256,256]{1,0:T(8,128)(2,1)S(1)}, u32[]{:S(2)}, u32[]{:S(2)}) collective-permute-start(bf16[256,256]{1,0:T(8,128)(2,1)S(1)} %get-tuple-element.251.refs_2_.refs_3_), channel_id=1, source_target_pairs={{0,12},{4,8},{8,4},{12,0},{1,13},{5,9},{9,5},{13,1},{2,14},{6,10},... | collective-permute-start | bytes 393224 | tf_op jit(solution)/shard_map/swap_ctx_3/ppermute | solution.py:111
  11.6 6.8 %collective-permute-start.3 = (bf16[256,256]{1,0:T(8,128)(2,1)S(1)}, bf16[256,256]{1,0:T(8,128)(2,1)S(1)}, u32[]{:S(2)}, u32[]{:S(2)}) collective-permute-start(bf16[256,256]{1,0:T(8,128)(2,1)S(1)} %get-tuple-element.251.refs_2_.refs_3_), channel_id=1, source_target_pairs={{0,8},{4,12},{8,0},{12,4},{1,9},{5,13},{9,1},{13,5},{2,10},{6,14},... | collective-permute-start | bytes 393224 | tf_op jit(solution)/shard_map/swap_ctx_2/ppermute | solution.py:111
  12.1 6.4 %collective-permute-start.2 = (bf16[256,256]{1,0:T(8,128)(2,1)S(1)}, bf16[256,256]{1,0:T(8,128)(2,1)S(1)}, u32[]{:S(2)}, u32[]{:S(2)}) collective-permute-start(bf16[256,256]{1,0:T(8,128)(2,1)S(1)} %get-tuple-element.251.refs_2_.refs_3_), channel_id=1, source_target_pairs={{0,4},{4,0},{8,12},{12,8},{1,5},{5,1},{9,13},{13,9},{2,6},{6,2},{1... | collective-permute-start | bytes 393224 | tf_op jit(solution)/shard_map/swap_ctx_1/ppermute | solution.py:111
  16.6 11.3 %collective-permute-start.9 = (bf16[96,1024]{1,0:T(8,128)(2,1)S(1)}, bf16[96,1024]{1,0:T(8,128)(2,1)S(1)}, u32[]{:S(2)}, u32[]{:S(2)}) collective-permute-start(bf16[96,1024]{1,0:T(8,128)(2,1)S(1)} %get-tuple-element.280), channel_id=1, source_target_pairs={{0,2},{1,3},{2,0},{3,1},{4,6},{5,7},{6,4},{7,5},{8,10},{9,11},{10,... | collective-permute-start | bytes 589832 | tf_op jit(solution)/shard_map/swap_tp_2/ppermute | solution.py:111
  18.5 2.0 %collective-permute-start.5 = (bf16[272,384]{1,0:T(8,128)(2,1)S(1)}, bf16[272,384]{1,0:T(8,128)(2,1)S(1)}, u32[]{:S(2)}, u32[]{:S(2)}) collective-permute-start(bf16[272,384]{1,0:T(8,128)(2,1)S(1)} %collective-permute-done.1.refs_1_.refs_3_.refs_4_.refs_12_), channel_id=1, source_target_pairs={{0,16},{16,0},{1,17},{17,1},{2,18},{18,2},{3,19},{19,3},{4,20},{20... | collective-permute-start | bytes 626696 | tf_op jit(solution)/shard_map/swap_fsdp_1/ppermute | solution.py:111
  21.3 9.9 %collective-permute-start.8 = (bf16[272,256]{1,0:T(8,128)(2,1)S(1)}, bf16[272,256]{1,0:T(8,128)(2,1)S(1)}, u32[]{:S(2)}, u32[]{:S(2)}) collective-permute-start(bf16[272,256]{1,0:T(8,128)(2,1)S(1)} %get-tuple-element.278.refs_2_.refs_9_), channel_id=1, source_target_pairs={{0,12},{4,8},{8,4},{12,0},{1,13},{5,9},{9,5},{13,1},{2,14},{6,10},... | collective-permute-start | bytes 417800 | tf_op jit(solution)/shard_map/swap_ctx_3/ppermute | solution.py:111
  23.5 7.8 %collective-permute-start.7 = (bf16[272,256]{1,0:T(8,128)(2,1)S(1)}, bf16[272,256]{1,0:T(8,128)(2,1)S(1)}, u32[]{:S(2)}, u32[]{:S(2)}) collective-permute-start(bf16[272,256]{1,0:T(8,128)(2,1)S(1)} %get-tuple-element.278.refs_2_.refs_9_), channel_id=1, source_target_pairs={{0,8},{4,12},{8,0},{12,4},{1,9},{5,13},{9,1},{13,5},{2,10},{6,14},... | collective-permute-start | bytes 417800 | tf_op jit(solution)/shard_map/swap_ctx_2/ppermute | solution.py:111
  24.4 7.0 %collective-permute-start.6 = (bf16[272,256]{1,0:T(8,128)(2,1)S(1)}, bf16[272,256]{1,0:T(8,128)(2,1)S(1)}, u32[]{:S(2)}, u32[]{:S(2)}) collective-permute-start(bf16[272,256]{1,0:T(8,128)(2,1)S(1)} %get-tuple-element.278.refs_2_.refs_9_), channel_id=1, source_target_pairs={{0,4},{4,0},{8,12},{12,8},{1,5},{5,1},{9,13},{13,9},{2,6},{6,2},{1... | collective-permute-start | bytes 417800 | tf_op jit(solution)/shard_map/swap_ctx_1/ppermute | solution.py:111
  28.5 1.3 %collective-permute-start.10 = (bf16[256,128]{1,0:T(8,128)(2,1)S(1)}, bf16[256,128]{1,0:T(8,128)(2,1)S(1)}, u32[]{:S(2)}, u32[]{:S(2)}) collective-permute-start(bf16[256,128]{1,0:T(8,128)(2,1)S(1)} %get-tuple-element.285.refs_9_.refs_20_), channel_id=1, source_target_pairs={{0,16},{16,0},{1,17},{17,1},{2,18},{18,2},{3,19},{19,3},{4,20},{20... | collective-permute-start | bytes 196616 | tf_op jit(solution)/shard_map/swap_fsdp_1/ppermute | solution.py:111
  28.5 13.8 %collective-permute-start.12 = (bf16[256,1024]{1,0:T(8,128)(2,1)S(1)}, bf16[256,1024]{1,0:T(8,128)(2,1)S(1)}, u32[]{:S(2)}, u32[]{:S(2)}) collective-permute-start(bf16[256,1024]{1,0:T(8,128)(2,1)S(1)} %get-tuple-element.293.refs_6_), channel_id=1, source_target_pairs={{0,16},{16,0},{1,17},{17,1},{2,18},{18,2},{3,19},{19,3},{4,20},{20... | collective-permute-start | bytes 1572872 | tf_op jit(solution)/shard_map/swap_fsdp_1/ppermute | solution.py:111
  29.8 5.5 %collective-permute-start.13 = (bf16[64,1024]{1,0:T(8,128)(2,1)S(1)}, bf16[64,1024]{1,0:T(8,128)(2,1)S(1)}, u32[]{:S(2)}, u32[]{:S(2)}) collective-permute-start(bf16[64,1024]{1,0:T(8,128)(2,1)S(1)} %get-tuple-element.295.refs_0_), channel_id=1, source_target_pairs={{0,4},{4,0},{8,12},{12,8},{16,24},{20,28},{24,16},{28,20},{1,5},{5... | collective-permute-start | bytes 393224 | tf_op jit(solution)/shard_map/swap_turn_0/ppermute | solution.py:126
  33.6 8.7 %collective-permute-start.11 = (bf16[272,512]{1,0:T(8,128)(2,1)S(1)}, bf16[272,512]{1,0:T(8,128)(2,1)S(1)}, u32[]{:S(2)}, u32[]{:S(2)}) collective-permute-start(bf16[272,512]{1,0:T(8,128)(2,1)S(1)} %get-tuple-element.290.refs_1_), channel_id=1, source_target_pairs={{0,1},{1,0},{2,3},{3,2},{4,5},{5,4},{6,7},{7,6},{8,9},{9,8},{10,11... | collective-permute-start | bytes 835592 | tf_op jit(solution)/shard_map/swap_tp_1/ppermute | solution.py:111
  35.8 6.4 %collective-permute-start.14 = (bf16[128,1024]{1,0:T(8,128)(2,1)S(1)}, bf16[128,1024]{1,0:T(8,128)(2,1)S(1)}, u32[]{:S(2)}, u32[]{:S(2)}) collective-permute-start(bf16[128,1024]{1,0:T(8,128)(2,1)S(1)} %shard_map.288.refs_5_), channel_id=1, source_target_pairs={{0,8},{4,12},{8,0},{12,4},{16,20},{20,16},{24,28},{28,24},{1,9},{5... | collective-permute-start | bytes 786440 | tf_op jit(solution)/shard_map/swap_turn_1/ppermute | solution.py:126
  37.3 6.8 %collective-permute-start.15 = (bf16[128,1024]{1,0:T(8,128)(2,1)S(1)}, bf16[128,1024]{1,0:T(8,128)(2,1)S(1)}, u32[]{:S(2)}, u32[]{:S(2)}) collective-permute-start(bf16[128,1024]{1,0:T(8,128)(2,1)S(1)} %shard_map.288.refs_5_), channel_id=1, source_target_pairs={{0,16},{16,0},{1,17},{17,1},{2,18},{18,2},{3,19},{19,3},{4,20},{20... | collective-permute-start | bytes 786440 | tf_op jit(solution)/shard_map/swap_fsdp_1/ppermute | solution.py:111
  42.3 1.9 %collective-permute-start.16 = (bf16[128,1024]{1,0:T(8,128)(2,1)S(1)}, bf16[128,1024]{1,0:T(8,128)(2,1)S(1)}, u32[]{:S(2)}, u32[]{:S(2)}) collective-permute-start(bf16[128,1024]{1,0:T(8,128)(2,1)S(1)} %collective-permute-done.14.refs_6_), channel_id=1, source_target_pairs={{0,16},{16,0},{1,17},{17,1},{2,18},{18,2},{3,19},{19,3},{4,20},{20... | collective-permute-start | bytes 786440 | tf_op jit(solution)/shard_map/swap_fsdp_1/ppermute | solution.py:111
  45.8 9.1 %collective-permute-start.22 = (bf16[272,512]{1,0:T(8,128)(2,1)S(1)}, bf16[272,512]{1,0:T(8,128)(2,1)S(1)}, u32[]{:S(2)}, u32[]{:S(2)}) collective-permute-start(bf16[272,512]{1,0:T(8,128)(2,1)S(1)} %get-tuple-element.342.refs_13_), channel_id=1, source_target_pairs={{0,1},{1,0},{2,3},{3,2},{4,5},{5,4},{6,7},{7,6},{8,9},{9,8},{10,11... | collective-permute-start | bytes 835592 | tf_op jit(solution)/shard_map/swap_tp_1/ppermute | solution.py:111
  48.7 1.6 %collective-permute-start.20 = (bf16[256,512]{1,0:T(8,128)(2,1)S(1)}, bf16[256,512]{1,0:T(8,128)(2,1)S(1)}, u32[]{:S(2)}, u32[]{:S(2)}) collective-permute-start(bf16[256,512]{1,0:T(8,128)(2,1)S(1)} %get-tuple-element.331), channel_id=1, source_target_pairs={{0,16},{16,0},{1,17},{17,1},{2,18},{18,2},{3,19},{19,3},{4,20},{20... | collective-permute-start | bytes 786440 | tf_op jit(solution)/shard_map/swap_fsdp_1/ppermute | solution.py:111
  48.7 1.9 %collective-permute-start.19 = (bf16[256,512]{1,0:T(8,128)(2,1)S(1)}, bf16[256,512]{1,0:T(8,128)(2,1)S(1)}, u32[]{:S(2)}, u32[]{:S(2)}) collective-permute-start(bf16[256,512]{1,0:T(8,128)(2,1)S(1)} %get-tuple-element.328), channel_id=1, source_target_pairs={{0,16},{16,0},{1,17},{17,1},{2,18},{18,2},{3,19},{19,3},{4,20},{20... | collective-permute-start | bytes 786440 | tf_op jit(solution)/shard_map/swap_fsdp_1/ppermute | solution.py:111
  49.2 1.8 %collective-permute-start.18 = (bf16[256,512]{1,0:T(8,128)(2,1)S(1)}, bf16[256,512]{1,0:T(8,128)(2,1)S(1)}, u32[]{:S(2)}, u32[]{:S(2)}) collective-permute-start(bf16[256,512]{1,0:T(8,128)(2,1)S(1)} %get-tuple-element.325), channel_id=1, source_target_pairs={{0,16},{16,0},{1,17},{17,1},{2,18},{18,2},{3,19},{19,3},{4,20},{20... | collective-permute-start | bytes 786440 | tf_op jit(solution)/shard_map/swap_fsdp_1/ppermute | solution.py:111
  49.3 2.1 %collective-permute-start.17 = (bf16[256,512]{1,0:T(8,128)(2,1)S(1)}, bf16[256,512]{1,0:T(8,128)(2,1)S(1)}, u32[]{:S(2)}, u32[]{:S(2)}) collective-permute-start(bf16[256,512]{1,0:T(8,128)(2,1)S(1)} %get-tuple-element.322), channel_id=1, source_target_pairs={{0,16},{16,0},{1,17},{17,1},{2,18},{18,2},{3,19},{19,3},{4,20},{20... | collective-permute-start | bytes 786440 | tf_op jit(solution)/shard_map/swap_fsdp_1/ppermute | solution.py:111
  52.1 18.8 %collective-permute-start.21 = (bf16[128,2048]{1,0:T(8,128)(2,1)S(1)}, bf16[128,2048]{1,0:T(8,128)(2,1)S(1)}, u32[]{:S(2)}, u32[]{:S(2)}) collective-permute-start(bf16[128,2048]{1,0:T(8,128)(2,1)S(1)} %get-tuple-element.337), channel_id=1, source_target_pairs={{0,4},{4,0},{8,12},{12,8},{16,24},{20,28},{24,16},{28,20},{1,5},{5... | collective-permute-start | bytes 1572872 | tf_op jit(solution)/shard_map/swap_turn_0/ppermute | solution.py:126
  60.3 13.0 %collective-permute-start.27 = (bf16[272,512]{1,0:T(8,128)(2,1)S(1)}, bf16[272,512]{1,0:T(8,128)(2,1)S(1)}, u32[]{:S(2)}, u32[]{:S(2)}) collective-permute-start(bf16[272,512]{1,0:T(8,128)(2,1)S(1)} %get-tuple-element.367), channel_id=1, source_target_pairs={{0,12},{4,8},{8,4},{12,0},{1,13},{5,9},{9,5},{13,1},{2,14},{6,10},... | collective-permute-start | bytes 835592 | tf_op jit(solution)/shard_map/swap_ctx_3/ppermute | solution.py:111
  62.3 13.2 %collective-permute-start.26 = (bf16[272,512]{1,0:T(8,128)(2,1)S(1)}, bf16[272,512]{1,0:T(8,128)(2,1)S(1)}, u32[]{:S(2)}, u32[]{:S(2)}) collective-permute-start(bf16[272,512]{1,0:T(8,128)(2,1)S(1)} %get-tuple-element.366), channel_id=1, source_target_pairs={{0,8},{4,12},{8,0},{12,4},{1,9},{5,13},{9,1},{13,5},{2,10},{6,14},... | collective-permute-start | bytes 835592 | tf_op jit(solution)/shard_map/swap_ctx_2/ppermute | solution.py:111
  63.4 12.2 %collective-permute-start.25 = (bf16[272,512]{1,0:T(8,128)(2,1)S(1)}, bf16[272,512]{1,0:T(8,128)(2,1)S(1)}, u32[]{:S(2)}, u32[]{:S(2)}) collective-permute-start(bf16[272,512]{1,0:T(8,128)(2,1)S(1)} %get-tuple-element.365), channel_id=1, source_target_pairs={{0,4},{4,0},{8,12},{12,8},{1,5},{5,1},{9,13},{13,9},{2,6},{6,2},{1... | collective-permute-start | bytes 835592 | tf_op jit(solution)/shard_map/swap_ctx_1/ppermute | solution.py:111
  63.9 7.1 %collective-permute-start.23 = (bf16[256,512]{1,0:T(8,128)(2,1)S(1)}, bf16[256,512]{1,0:T(8,128)(2,1)S(1)}, u32[]{:S(2)}, u32[]{:S(2)}) collective-permute-start(bf16[256,512]{1,0:T(8,128)(2,1)S(1)} %get-tuple-element.353.refs_3_), channel_id=1, source_target_pairs={{0,1},{1,0},{2,3},{3,2},{4,5},{5,4},{6,7},{7,6},{8,9},{9,8},{10,11... | collective-permute-start | bytes 786440 | tf_op jit(solution)/shard_map/swap_tp_1/ppermute | solution.py:111
  71.9 19.5 %collective-permute-start.24 = (bf16[416,512]{1,0:T(8,128)(2,1)S(1)}, bf16[416,512]{1,0:T(8,128)(2,1)S(1)}, u32[]{:S(2)}, u32[]{:S(2)}) collective-permute-start(bf16[416,512]{1,0:T(8,128)(2,1)S(1)} %get-tuple-element.359), channel_id=1, source_target_pairs={{0,2},{1,3},{2,0},{3,1},{4,6},{5,7},{6,4},{7,5},{8,10},{9,11},{10,... | collective-permute-start | bytes 1277960 | tf_op jit(solution)/shard_map/swap_tp_2/ppermute | solution.py:111
  77.3 2.0 %collective-permute-start.29 = (bf16[272,384]{1,0:T(8,128)(2,1)S(1)}, bf16[272,384]{1,0:T(8,128)(2,1)S(1)}, u32[]{:S(2)}, u32[]{:S(2)}) collective-permute-start(bf16[272,384]{1,0:T(8,128)(2,1)S(1)} %get-tuple-element.378), channel_id=1, source_target_pairs={{0,16},{16,0},{1,17},{17,1},{2,18},{18,2},{3,19},{19,3},{4,20},{20... | collective-permute-start | bytes 626696 | tf_op jit(solution)/shard_map/swap_fsdp_1/ppermute | solution.py:111
  77.4 1.9 %collective-permute-start.28 = (bf16[272,384]{1,0:T(8,128)(2,1)S(1)}, bf16[272,384]{1,0:T(8,128)(2,1)S(1)}, u32[]{:S(2)}, u32[]{:S(2)}) collective-permute-start(bf16[272,384]{1,0:T(8,128)(2,1)S(1)} %get-tuple-element.375), channel_id=1, source_target_pairs={{0,16},{16,0},{1,17},{17,1},{2,18},{18,2},{3,19},{19,3},{4,20},{20... | collective-permute-start | bytes 626696 | tf_op jit(solution)/shard_map/swap_fsdp_1/ppermute | solution.py:111
  77.8 1.4 %collective-permute-start.30 = (bf16[272,256]{1,0:T(8,128)(2,1)S(1)}, bf16[272,256]{1,0:T(8,128)(2,1)S(1)}, u32[]{:S(2)}, u32[]{:S(2)}) collective-permute-start(bf16[272,256]{1,0:T(8,128)(2,1)S(1)} %get-tuple-element.381), channel_id=1, source_target_pairs={{0,16},{16,0},{1,17},{17,1},{2,18},{18,2},{3,19},{19,3},{4,20},{20... | collective-permute-start | bytes 417800 | tf_op jit(solution)/shard_map/swap_fsdp_1/ppermute | solution.py:111
  80.0 26.3 %copy-start = (s32[2]{0:T(128)S(1)}, s32[2]{0:T(128)}, u32[]{:S(2)}) copy-start(s32[2]{0:T(128)} %refs_0_.3) | copy-start | bytes 28
  80.0 12.0 %collective-permute-start.35 = (bf16[80,1024]{1,0:T(8,128)(2,1)S(1)}, bf16[80,1024]{1,0:T(8,128)(2,1)S(1)}, u32[]{:S(2)}, u32[]{:S(2)}) collective-permute-start(bf16[80,1024]{1,0:T(8,128)(2,1)S(1)} %get-tuple-element.405), channel_id=1, source_target_pairs={{0,12},{4,8},{8,4},{12,0},{1,13},{5,9},{9,5},{13,1},{2,14},{6,10},... | collective-permute-start | bytes 491528 | tf_op jit(solution)/shard_map/swap_ctx_3/ppermute | solution.py:111
  81.8 10.2 %collective-permute-start.34 = (bf16[80,1024]{1,0:T(8,128)(2,1)S(1)}, bf16[80,1024]{1,0:T(8,128)(2,1)S(1)}, u32[]{:S(2)}, u32[]{:S(2)}) collective-permute-start(bf16[80,1024]{1,0:T(8,128)(2,1)S(1)} %get-tuple-element.404), channel_id=1, source_target_pairs={{0,8},{4,12},{8,0},{12,4},{1,9},{5,13},{9,1},{13,5},{2,10},{6,14},... | collective-permute-start | bytes 491528 | tf_op jit(solution)/shard_map/swap_ctx_2/ppermute | solution.py:111
  83.0 9.0 %collective-permute-start.33 = (bf16[80,1024]{1,0:T(8,128)(2,1)S(1)}, bf16[80,1024]{1,0:T(8,128)(2,1)S(1)}, u32[]{:S(2)}, u32[]{:S(2)}) collective-permute-start(bf16[80,1024]{1,0:T(8,128)(2,1)S(1)} %get-tuple-element.403), channel_id=1, source_target_pairs={{0,4},{4,0},{8,12},{12,8},{1,5},{5,1},{9,13},{13,9},{2,6},{6,2},{1... | collective-permute-start | bytes 491528 | tf_op jit(solution)/shard_map/swap_ctx_1/ppermute | solution.py:111
  83.5 13.5 %collective-permute-start.36 = (bf16[256,512]{1,0:T(8,128)(2,1)S(1)}, bf16[256,512]{1,0:T(8,128)(2,1)S(1)}, u32[]{:S(2)}, u32[]{:S(2)}) collective-permute-start(bf16[256,512]{1,0:T(8,128)(2,1)S(1)} %get-tuple-element.412.refs_1_), channel_id=1, source_target_pairs={{0,1},{1,0},{2,3},{3,2},{4,5},{5,4},{6,7},{7,6},{8,9},{9,8},{10,11... | collective-permute-start | bytes 786440 | tf_op jit(solution)/shard_map/swap_tp_1/ppermute | solution.py:111
  92.6 6.7 %collective-permute-start.37 = (bf16[96,512]{1,0:T(8,128)(2,1)S(1)}, bf16[96,512]{1,0:T(8,128)(2,1)S(1)}, u32[]{:S(2)}, u32[]{:S(2)}) collective-permute-start(bf16[96,512]{1,0:T(8,128)(2,1)S(1)} %get-tuple-element.416.refs_4_), channel_id=1, source_target_pairs={{0,2},{1,3},{2,0},{3,1},{4,6},{5,7},{6,4},{7,5},{8,10},{9,11},{10,... | collective-permute-start | bytes 294920 | tf_op jit(solution)/shard_map/swap_tp_2/ppermute | solution.py:111
  92.9 6.4 %collective-permute-start.32 = (bf16[64,512]{1,0:T(8,128)(2,1)S(1)}, bf16[64,512]{1,0:T(8,128)(2,1)S(1)}, u32[]{:S(2)}, u32[]{:S(2)}) collective-permute-start(bf16[64,512]{1,0:T(8,128)(2,1)S(1)} %get-tuple-element.401), channel_id=1, source_target_pairs={{0,8},{4,12},{8,0},{12,4},{16,20},{20,16},{24,28},{28,24},{1,9},{5... | collective-permute-start | bytes 196616 | tf_op jit(solution)/shard_map/swap_turn_1/ppermute | solution.py:126
  94.3 5.0 %collective-permute-start.31 = (bf16[64,512]{1,0:T(8,128)(2,1)S(1)}, bf16[64,512]{1,0:T(8,128)(2,1)S(1)}, u32[]{:S(2)}, u32[]{:S(2)}) collective-permute-start(bf16[64,512]{1,0:T(8,128)(2,1)S(1)} %get-tuple-element.398), channel_id=1, source_target_pairs={{0,8},{4,12},{8,0},{12,4},{16,20},{20,16},{24,28},{28,24},{1,9},{5... | collective-permute-start | bytes 196616 | tf_op jit(solution)/shard_map/swap_turn_1/ppermute | solution.py:126
  99.3 15.8 %collective-permute-start.42 = (bf16[256,512]{1,0:T(8,128)(2,1)S(1)}, bf16[256,512]{1,0:T(8,128)(2,1)S(1)}, u32[]{:S(2)}, u32[]{:S(2)}) collective-permute-start(bf16[256,512]{1,0:T(8,128)(2,1)S(1)} %shard_map.299.refs_8_), channel_id=1, source_target_pairs={{0,2},{1,3},{2,0},{3,1},{4,6},{5,7},{6,4},{7,5},{8,10},{9,11},{10,... | collective-permute-start | bytes 786440 | tf_op jit(solution)/shard_map/swap_tp_2/ppermute | solution.py:111
  99.9 15.1 %collective-permute-start.40 = (bf16[64,1536]{1,0:T(8,128)(2,1)S(1)}, bf16[64,1536]{1,0:T(8,128)(2,1)S(1)}, u32[]{:S(2)}, u32[]{:S(2)}) collective-permute-start(bf16[64,1536]{1,0:T(8,128)(2,1)S(1)} %get-tuple-element.431.refs_1_), channel_id=1, source_target_pairs={{0,12},{4,8},{8,4},{12,0},{1,13},{5,9},{9,5},{13,1},{2,14},{6,10},... | collective-permute-start | bytes 589832 | tf_op jit(solution)/shard_map/swap_ctx_3/ppermute | solution.py:111
  102.8 12.2 %collective-permute-start.39 = (bf16[64,1536]{1,0:T(8,128)(2,1)S(1)}, bf16[64,1536]{1,0:T(8,128)(2,1)S(1)}, u32[]{:S(2)}, u32[]{:S(2)}) collective-permute-start(bf16[64,1536]{1,0:T(8,128)(2,1)S(1)} %get-tuple-element.431.refs_1_), channel_id=1, source_target_pairs={{0,8},{4,12},{8,0},{12,4},{1,9},{5,13},{9,1},{13,5},{2,10},{6,14},... | collective-permute-start | bytes 589832 | tf_op jit(solution)/shard_map/swap_ctx_2/ppermute | solution.py:111
  102.8 12.2 %collective-permute-start.38 = (bf16[64,1536]{1,0:T(8,128)(2,1)S(1)}, bf16[64,1536]{1,0:T(8,128)(2,1)S(1)}, u32[]{:S(2)}, u32[]{:S(2)}) collective-permute-start(bf16[64,1536]{1,0:T(8,128)(2,1)S(1)} %get-tuple-element.431.refs_1_), channel_id=1, source_target_pairs={{0,4},{4,0},{8,12},{12,8},{1,5},{5,1},{9,13},{13,9},{2,6},{6,2},{1... | collective-permute-start | bytes 589832 | tf_op jit(solution)/shard_map/swap_ctx_1/ppermute | solution.py:111
  103.5 11.6 %collective-permute-start.41 = (bf16[160,512]{1,0:T(8,128)(2,1)S(1)}, bf16[160,512]{1,0:T(8,128)(2,1)S(1)}, u32[]{:S(2)}, u32[]{:S(2)}) collective-permute-start(bf16[160,512]{1,0:T(8,128)(2,1)S(1)} %get-tuple-element.433.refs_6_), channel_id=1, source_target_pairs={{0,1},{1,0},{2,3},{3,2},{4,5},{5,4},{6,7},{7,6},{8,9},{9,8},{10,11... | collective-permute-start | bytes 491528 | tf_op jit(solution)/shard_map/swap_tp_1/ppermute | solution.py:111

commit v5 on v4

--- a/solution.py
+++ b/solution.py
@@ -410,6 +410,24 @@
         normed_ref, low_ref, bias_lines(pack_ref, row)[1], first, second,
         halves(spot_ref, first.shape[0]), act_ref, pre_ref, sum_ref, back_near, ffn_near,
         back_ref, ffn_ref,
+    )
+
+
+def ffn_kernel(
+    spot_ref, stream_ref, mine_ref, got_ref, cotan_ref, lines_ref, pack_ref, far_pack, first, second,
+    *refs, row,
+):
+    pieces, outs, scratch = refs[:-16], refs[-16:-4], refs[-4:]
+    back_ref, down_ref, out_ref, resid_ref, normed_ref, low_ref = outs[:6]
+    act_n, pre_n, sum_n, act_f, pre_f, sum_f = outs[6:]
+    back_near, down_near, one, two = scratch
+    ffn_near_kernel(
+        spot_ref, stream_ref, mine_ref, got_ref, cotan_ref, lines_ref, pack_ref, first, second,
+        back_near, down_near, out_ref, resid_ref, normed_ref, act_n, pre_n, low_ref, sum_n, row=row,
+    )
+    ffn_far_kernel(
+        spot_ref, normed_ref, low_ref, back_near, down_near, far_pack, *pieces,
+        act_f, pre_f, sum_f, back_ref, down_ref, one, two, row=row,
     )
 
 
@@ -713,22 +731,52 @@
     )
 
 
+class Sends:
+    def __init__(self, sems):
+        self.sems, self.copies = sems, []
+
+    def start(self, source, target, alone=None):
+        copy = pltpu.make_async_copy(source, target, self.sems.at[len(self.copies)])
+        self.copies.append((copy, alone))
+        copy.start() if alone is None else pl.when(alone)(copy.start)
+
+    def wait(self):
+        for copy, alone in self.copies:
+            copy.wait() if alone is None else pl.when(alone)(copy.wait)
+
+
+def weights_kernel(
+    spot_ref, p0, p1, p2, p3, up_hbm, down_hbm, qkv_hbm, proj_hbm,
+    up_all, down_all, qkv_all, proj_all, sems,
+):
+    sends = Sends(sems)
+    rows, hidden, cols = p0.shape[0], up_all.shape[1], proj_all.shape[1]
+    pieces = (p0, p1, p2, p3)
+    spots = [window(spot_ref[1] ^ bits, rows) for bits in range(4)]
+    for i, (whole, target) in enumerate(((up_all, up_hbm), (down_all, down_hbm))):
+        for spot, piece in zip(spots, pieces):
+            whole[spot, :] = piece[:, i * hidden : (i + 1) * hidden].astype(F32)
+        sends.start(whole, target)
+    start = 2 * hidden
+    for spot, piece in zip(spots, pieces):
+        for i in range(3):
+            qkv_all[i, spot, :] = piece[:, start + i * cols : start + (i + 1) * cols].astype(F32)
+        proj_all[spot, :] = piece[:, start + 3 * cols :].astype(F32)
+    sends.start(qkv_all, qkv_hbm)
+    sends.start(proj_all, proj_hbm)
+    sends.wait()
+
+
 def close_kernel(
-    spot_ref, steps_ref, p0, p1, p2, p3, out_own, out_one, out_two, in_own, in_far,
-    zero_hbm,
-    out_hbm, in_hbm, up_hbm, down_hbm, qkv_hbm, proj_hbm, table_hbm, up_ref, qv_ref, *refs,
-):
-    lines, refs = refs[:6], refs[6:]
-    out_all, in_all, up_all, down_all, qkv_all, proj_all, rows_ref, blocks_ref, sems = refs
-    copies = []
-
-    def send(source, target, alone=None):
-        copy = pltpu.make_async_copy(source, target, sems.at[len(copies)])
-        copies.append((copy, alone))
-        copy.start() if alone is None else pl.when(alone)(copy.start)
-
+    spot_ref, steps_ref, out_own, out_one, out_two, in_own, in_far, zero_hbm,
+    out_hbm, in_hbm, table_hbm, up_ref, qv_ref, *refs,
+):
+    lines, (out_all, in_all, rows_ref, blocks_ref, sems) = refs[:6], refs[6:]
+    sends = Sends(sems)
     fill_rows(spot_ref, out_own, (out_one, out_two), out_all)
-    send(out_all, out_hbm)
+    sends.start(out_all, out_hbm)
+    fill_rows(spot_ref, in_own, (in_far,), in_all)
+    sends.start(in_all, in_hbm)
     start, count = out_one.shape[0] - 2 * rows_ref.shape[0], rows_ref.shape[0]
     parts = [
         both(ref[start : start + count, :], ref[start + count :, :]) for ref in (out_one, out_two)
@@ -746,26 +794,10 @@
         blocks_ref[place] = total_rows
         seen = [steps_ref[other] // 8 == block for other in range(place)]
         alone = jnp.logical_not(functools.reduce(jnp.logical_or, seen)) if seen else None
-        send(blocks_ref.at[place], table_hbm.at[pl.ds(pl.multiple_of(block * 8, 8), 8), :], alone)
+        target = table_hbm.at[pl.ds(pl.multiple_of(block * 8, 8), 8), :]
+        sends.start(blocks_ref.at[place], target, alone)
     sums_out(spot_ref, rows_ref, up_ref, qv_ref, lines)
-    rows, hidden, cols = p0.shape[0], up_all.shape[1], proj_all.shape[1]
-    pieces = (p0, p1, p2, p3)
-    spots = [window(spot_ref[1] ^ bits, rows) for bits in range(4)]
-    for i, (whole, target) in enumerate(((up_all, up_hbm), (down_all, down_hbm))):
-        for spot, piece in zip(spots, pieces):
-            whole[spot, :] = piece[:, i * hidden : (i + 1) * hidden].astype(F32)
-        send(whole, target)
-    start = 2 * hidden
-    for spot, piece in zip(spots, pieces):
-        for i in range(3):
-            qkv_all[i, spot, :] = piece[:, start + i * cols : start + (i + 1) * cols].astype(F32)
-        proj_all[spot, :] = piece[:, start + 3 * cols :].astype(F32)
-    send(qkv_all, qkv_hbm)
-    send(proj_all, proj_hbm)
-    fill_rows(spot_ref, in_own, (in_far,), in_all)
-    send(in_all, in_hbm)
-    for copy, alone in copies:
-        copy.wait() if alone is None else pl.when(alone)(copy.wait)
+    sends.wait()
 
 
 class Reduction:
@@ -864,7 +896,7 @@
     near = pieces_of(order, pack, parts, rows)
     pack_far = order.swap(qkv_part, "tp", 2)
     projected = [((span, cols), BF16), ((span, 2 * cols), BF16)]
-    more = [((span, cols), BF16), ((span + PAD, 2 * cols), BF16)]
+    more = [((span, cols), BF16), ((span, 2 * cols), BF16)]
     q_near, kv_near, stream, normed, seg, lines = order.call(
         functools.partial(open_kernel, row=rows),
         projected
@@ -929,7 +961,7 @@
     out_far = pieces_of(order, out_far, parts, rows)
     mixed_far, lse_far, given = order.call(
         attend_two_kernel,
-        attended + [((span + PAD, width), BF16)],
+        attended + [((span, width), BF16)],
         [seg, q_far, *kvs_far, mixed_near, *near, *out_far],
     )
     got = order.swap(given, "tp", 1)
@@ -944,18 +976,19 @@
     else:
         rest_far = pieces_of(order, rest_far, parts, rows)
 
-    acts = [((span, hidden), BF16), ((span, hidden), BF16)]
-    back_near, down_near, out_base, resid, normed_two, act_n, pre_n, low, up_near = order.call(
-        functools.partial(ffn_near_kernel, row=rows),
-        [((span, width), F32)] * 4
-        + [((span, width), BF16), *acts, ((span, width), BF16), ((1, hidden), F32)],
-        [stream, given, got, cotan, lines, pack, *rest_near],
-    )
-    act_f, pre_f, up_far, back, ffn_terms = order.call(
-        functools.partial(ffn_far_kernel, row=rows),
-        [*acts, ((1, hidden), F32), ((span + PAD, width), BF16), ((span, width), BF16)],
-        [normed_two, low, back_near, down_near, pack_far, *rest_far],
-        scratch=[pltpu.VMEM((size, 2 * hidden), BF16)] * 2,
+    acts = [((span, hidden), BF16), ((span, hidden), BF16), ((1, hidden), F32)]
+    (
+        back, ffn_terms, out_base, resid, normed_two, low, act_n, pre_n, up_near, act_f, pre_f, up_far,
+    ) = order.call(
+        functools.partial(ffn_kernel, row=rows),
+        [
+            ((span + PAD, width), BF16), ((span, width), BF16), ((span, width), F32),
+            ((span, width), F32), ((span, width), BF16), ((span, width), BF16), *acts, *acts,
+        ],
+        [stream, given, got, cotan, lines, pack, pack_far, *rest_near, *rest_far],
+        scratch=[pltpu.VMEM((span, width), F32)] * 2
+        + [pltpu.VMEM((size, 2 * hidden), BF16)] * 2,
+        limit=8,
     )
     back_got = order.swap(back, "tp", 1)
     ffn_kept, *ffn_sent = order.call(
@@ -991,7 +1024,7 @@
         ffn_near, sent, out_low = order.call(
             middle_kernel,
             [
-                ((rows // 2, 2 * hidden), F32), ((span // 2 + rows + 2 * PAD, width), BF16),
+                ((rows // 2, 2 * hidden), F32), ((span // 2 + rows + 0 * PAD, width), BF16),
                 ((span, width), BF16),
             ],
             [ffn_own, ffn_turn, out_base, ffn_terms, terms_got],
@@ -1061,20 +1094,29 @@
             jnp.concatenate([timesteps, far_steps]),
             jnp.concatenate([far_steps, timesteps]),
         )
-        large = large + [((rows, hidden), F32)] * 2 + [((3, rows, cols), F32), ((rows, cols), F32)]
-        output, grad_input, grads_up, grads_down, grads_qkv, grads_out, table, *rest = order.call(
+        whole = [
+            ((rows, hidden), F32), ((rows, hidden), F32), ((3, rows, cols), F32),
+            ((rows, cols), F32),
+        ]
+        grads_up, grads_down, grads_qkv, grads_out = order.call(
+            weights_kernel,
+            whole,
+            pieces,
+            kept=range(4),
+            scratch=[pltpu.VMEM(shape, dtype) for shape, dtype in whole] + [dma(4)],
+        )
+        output, grad_input, table, *rest = order.call(
             close_kernel,
             large + [(time_table.shape, F32)] + vectors,
-            [
-                steps, *pieces, out_low, passed, passed_got, in_low, in_far, table,
+            [steps, out_low, passed, passed_got, in_low, in_far, table],
+            far=(6,),
+            kept=range(3),
+            alias={6: 2},
+            scratch=[pltpu.VMEM((2 * span, width), F32)] * 2
+            + [
+                pltpu.VMEM((small_rows, width), F32), pltpu.VMEM((seqs, 8, width), F32),
+                dma(2 + seqs),
             ],
-            far=(10,),
-            kept=range(7),
-            alias={10: 6},
-            scratch=[pltpu.VMEM(shape, dtype) for shape, dtype in large]
-            + [pltpu.VMEM((small_rows, width), F32), pltpu.VMEM((seqs, 8, width), F32)]
-            + [dma(6 + seqs)],
-            limit=8,
         )
     else:
         output, grad_input = order.call(

time: 119 us -> 116 us (0.975)
  waiting for transfers between devices: 42.6 us -> 37.4 us
  starting transfers between devices: 40.6 us -> 42.9 us
    ppermute x38, waiting for transfers between devices: 37.7 us -> 33.8 us  [swap(): return lax.ppermute(values, axis, [(i, i ^ bits) for i in range(size)])]
    ppermute x38, starting transfers between devices: 34 us -> 36.5 us  [swap(): return lax.ppermute(values, axis, [(i, i ^ bits) for i in range(size)])]
    ppermute x5, waiting for transfers between devices: 4.94 us -> 3.57 us  [swap_turn(): return lax.ppermute(values, ('fsdp', 'ctx'), pairs)]
  transfers between devices with their start and end apart: 43 -> 43, of which waited for: 18 -> 23; matrix products, arithmetic and copies ran while one was open for 0% -> 0% of each run, Pallas kernels for 23% -> 23%
where the time goes in v5:
time: 116 us
  starting transfers between devices  42.9 us (37%)
  waiting for transfers between devices  37.4 us (32%)
  Pallas kernels  34.2 us (29%)
    ppermute x38, starting transfers between devices, swap(): return lax.ppermute(values, axis, [(i, i ^ bits) for i in range(size)])  36.5 us
    pallas_call x22, Pallas kernels, call(): pl.pallas_call(body, out_shape=tuple((jax.ShapeDtypeStruct(shape, dtype)...  34.2 us
    ppermute x38, waiting for transfers between devices, swap(): return lax.ppermute(values, axis, [(i, i ^ bits) for i in range(size)])  33.8 us
    ppermute x5, starting transfers between devices, swap_turn(): return lax.ppermute(values, ('fsdp', 'ctx'), pairs)  6.47 us
    ppermute x5, waiting for transfers between devices, swap_turn(): return lax.ppermute(values, ('fsdp', 'ctx'), pairs)  3.57 us
  transfers between devices with their start and end apart: 43, of which 23 were waited for; matrix products, arithmetic and copies ran while one was open for 0% of the time, Pallas kernels for 23%

profile of v5, /device:TPU:0, one launch (start us, length us, event | category | flops | bytes accessed | tf_op | source)
XLA Modules:
  0.0 115.8 jit_solution(13611336163340777881)
XLA Ops:
  0.7 1.8 %shard_map.280 = (bf16[272,512]{1,0:T(8,128)(2,1)S(1)}, bf16[272,384]{1,0:T(8,128)(2,1)S(1)}, bf16[256,128]{1,0:T(8,128)(2,1)S(1)}) custom-call(s32[2]{0:T(128)} %refs_0_.3, f32[3,256,128]{2,1,0:T(8,128)} %refs_1_.3, f32[256,128]{1,0:T(8,128)} %refs_2_.3, f32[2,128]{1,0:T(2,128)} %refs_3_.3, f32[1,512]{1,0:T(1,128)} %bitcast.22, ...), custom_call_target="tpu_custom_call" | custom-call | flops 8000000000 | bytes 65536 | tf_op jit(solution)/shard_map/pallas_call | solution.py:89
  2.5 0.5 collective-permute-start
  3.1 3.7 %collective-permute-start.1 = (bf16[272,384]{1,0:T(8,128)(2,1)S(1)}, bf16[272,384]{1,0:T(8,128)(2,1)S(1)}, u32[]{:S(2)}, u32[]{:S(2)}) collective-permute-start(bf16[272,384]{1,0:T(8,128)(2,1)S(1)} %get-tuple-element.240), channel_id=1, source_target_pairs={{0,2},{1,3},{2,0},{3,1},{4,6},{5,7},{6,4},{7,5},{8,10},{9,11},{10,... | collective-permute-start | bytes 626696 | tf_op jit(solution)/shard_map/swap_tp_2/ppermute | solution.py:111
  6.7 2.4 %shard_map.281 = (bf16[256,128]{1,0:T(8,128)(2,1)S(1)}, bf16[256,256]{1,0:T(8,128)(2,1)S(1)}, f32[256,512]{1,0:T(8,128)S(1)}, bf16[256,512]{1,0:T(8,128)(2,1)S(1...) custom-call(s32[2]{0:T(128)} %refs_0_.3, f32[2,256,512]{2,1,0:T(8,128)} %refs_1_.4, f32[1000,512]{1,0:T(8,128)} %refs_2_.4, ...), custom_call_target="tpu_custom_call" | custom-call | flops 8000000000 | bytes 65536 | tf_op jit(solution)/shard_map/pallas_call | solution.py:89
  9.1 2.5 %collective-permute-start.4 = (bf16[256,256]{1,0:T(8,128)(2,1)S(1)}, bf16[256,256]{1,0:T(8,128)(2,1)S(1)}, u32[]{:S(2)}, u32[]{:S(2)}) collective-permute-start(bf16[256,256]{1,0:T(8,128)(2,1)S(1)} %get-tuple-element.248.refs_2_.refs_3_), channel_id=1, source_target_pairs={{0,12},{4,8},{8,4},{12,0},{1,13},{5,9},{9,5},{13,1},{2,14},{6,10},... | collective-permute-start | bytes 393224 | tf_op jit(solution)/shard_map/swap_ctx_3/ppermute | solution.py:111
  12.1 0.5 collective-permute-start.2
  12.7 2.0 %shard_map.282 = (bf16[256,1024]{1,0:T(8,128)(2,1)S(1)}, bf16[96,1024]{1,0:T(8,128)(2,1)S(1)}, f32[256,512]{1,0:T(8,128)S(1)}) custom-call(bf16[256,128]{1,0:T(8,128)(2,1)S(1)} %get-tuple-element.250.refs_0_, f32[256,512]{1,0:T(8,128)} %refs_1_.5, f32[256,512]{1,0:T(8,128)} %refs_2_.5, f32[2,256,512]{2,1,0:T(8,128)} %refs_3_.5, ...), custom_call_target="tpu_custom_call" | custom-call | flops 1000 | bytes 65536 | tf_op jit(solution)/shard_map/pallas_call | solution.py:89
  14.7 1.9 %shard_map.283.refs_6_ = f32[1000,512]{1,0:T(8,128)} custom-call(s32[4]{0:T(128)S(1)} %pad_add_fusion.refs_5_.refs_13_.refs_4_.refs_0_.refs_6_.refs_1_.refs_11_.refs_2_.refs_22_.refs_18_.refs_3_.refs_7_), custom_call_target="tpu_custom_call" | custom-call | flops 1000 | bytes 65536 | tf_op jit(solution)/shard_map/pallas_call | solution.py:89
  16.6 1.5 %collective-permute-start.9 = (bf16[96,1024]{1,0:T(8,128)(2,1)S(1)}, bf16[96,1024]{1,0:T(8,128)(2,1)S(1)}, u32[]{:S(2)}, u32[]{:S(2)}) collective-permute-start(bf16[96,1024]{1,0:T(8,128)(2,1)S(1)} %get-tuple-element.277), channel_id=1, source_target_pairs={{0,2},{1,3},{2,0},{3,1},{4,6},{5,7},{6,4},{7,5},{8,10},{9,11},{10,... | collective-permute-start | bytes 589832 | tf_op jit(solution)/shard_map/swap_tp_2/ppermute | solution.py:111
  18.5 1.9 %shard_map.284 = (bf16[256,128]{1,0:T(8,128)(2,1)S(1)}, f32[256,128]{1,0:T(8,128)S(1)}) custom-call(s32[1,1024]{1,0:T(1,128)S(1)} %get-tuple-element.238.refs_0_, bf16[256,128]{1,0:T(8,128)(2,1)S(1)} %get-tuple-element.260.refs_1_, bf16[256,256]{1,0:T(8,128)(2,1)S(1)} %get-tuple-element.248.refs_2_.refs_3_, ...), custom_call_target="tpu_custom_call" | custom-call | flops 8000000000 | bytes 65536 | tf_op jit(solution)/shard_map/pallas_call | solution.py:89
  20.5 0.8 shard_map.285
  21.3 2.2 %collective-permute-start.8 = (bf16[256,256]{1,0:T(8,128)(2,1)S(1)}, bf16[256,256]{1,0:T(8,128)(2,1)S(1)}, u32[]{:S(2)}, u32[]{:S(2)}) collective-permute-start(bf16[256,256]{1,0:T(8,128)(2,1)S(1)} %get-tuple-element.275.refs_2_.refs_9_), channel_id=1, source_target_pairs={{0,12},{4,8},{8,4},{12,0},{1,13},{5,9},{9,5},{13,1},{2,14},{6,10},... | collective-permute-start | bytes 393224 | tf_op jit(solution)/shard_map/swap_ctx_3/ppermute | solution.py:111
  23.5 0.8 collective-permute-start.7
  24.4 0.5 collective-permute-start.6
  24.9 3.0 %collective-permute-done.9.refs_0_ = bf16[96,1024]{1,0:T(8,128)(2,1)S(1)} collective-permute-done((bf16[96,1024]{1,0:T(8,128)(2,1)S(1)}, bf16[96,1024]{1,0:T(8,128)(2,1)S(1)}, u32[]{:S(2)}, u32[]{:S(2)}) %collective-permute-start.9) | collective-permute-done | bytes 196640 | tf_op jit(solution)/shard_map/swap_tp_2/ppermute | solution.py:111
  27.9 0.6 shard_map.286
  28.5 1.6 %collective-permute-start.13 = (bf16[64,1024]{1,0:T(8,128)(2,1)S(1)}, bf16[64,1024]{1,0:T(8,128)(2,1)S(1)}, u32[]{:S(2)}, u32[]{:S(2)}) collective-permute-start(bf16[64,1024]{1,0:T(8,128)(2,1)S(1)} %get-tuple-element.292.refs_0_), channel_id=1, source_target_pairs={{0,4},{4,0},{8,12},{12,8},{16,24},{20,28},{24,16},{28,20},{1,5},{5... | collective-permute-start | bytes 393224 | tf_op jit(solution)/shard_map/swap_turn_0/ppermute | solution.py:126
  30.1 0.9 collective-permute-done.7.refs_4_.refs_11_
  31.0 2.2 %shard_map.287 = (bf16[256,128]{1,0:T(8,128)(2,1)S(1)}, f32[256,128]{1,0:T(8,128)S(1)}, bf16[256,512]{1,0:T(8,128)(2,1)S(1)}) custom-call(s32[1,1024]{1,0:T(1,128)S(1)} %get-tuple-element.238.refs_0_, bf16[256,128]{1,0:T(8,128)(2,1)S(1)} %get-tuple-element.268.refs_1_.refs_7_, bf16[256,256]{1,0:T(8,128)(2,1)S(1)} %get-tuple-element.275.refs_2_.refs_9_, ...), custom_call_target="tpu_custom_call" | custom-call | flops 8000000000 | bytes 65536 | tf_op jit(solution)/shard_map/pallas_call | solution.py:89
  33.6 0.6 shard_map.288.refs_9_
  34.1 1.6 %collective-permute-start.14 = (bf16[128,1024]{1,0:T(8,128)(2,1)S(1)}, bf16[128,1024]{1,0:T(8,128)(2,1)S(1)}, u32[]{:S(2)}, u32[]{:S(2)}) collective-permute-start(bf16[128,1024]{1,0:T(8,128)(2,1)S(1)} %shard_map.288.refs_9_), channel_id=1, source_target_pairs={{0,8},{4,12},{8,0},{12,4},{16,20},{20,16},{24,28},{28,24},{1,9},{5... | collective-permute-start | bytes 786440 | tf_op jit(solution)/shard_map/swap_turn_1/ppermute | solution.py:126
  36.2 1.2 %collective-permute-start.11 = (bf16[256,512]{1,0:T(8,128)(2,1)S(1)}, bf16[256,512]{1,0:T(8,128)(2,1)S(1)}, u32[]{:S(2)}, u32[]{:S(2)}) collective-permute-start(bf16[256,512]{1,0:T(8,128)(2,1)S(1)} %get-tuple-element.287.refs_1_), channel_id=1, source_target_pairs={{0,1},{1,0},{2,3},{3,2},{4,5},{5,4},{6,7},{7,6},{8,9},{9,8},{10,11... | collective-permute-start | bytes 786440 | tf_op jit(solution)/shard_map/swap_tp_1/ppermute | solution.py:111
  37.4 3.2 %collective-permute-done.14.refs_10_ = bf16[128,1024]{1,0:T(8,128)(2,1)S(1)} collective-permute-done((bf16[128,1024]{1,0:T(8,128)(2,1)S(1)}, bf16[128,1024]{1,0:T(8,128)(2,1)S(1)}, u32[]{:S(2)}, u32[]{:S(2)}) %collective-permute-start.14) | collective-permute-done | bytes 262176 | tf_op jit(solution)/shard_map/swap_turn_1/ppermute | solution.py:126
  40.6 3.9 %collective-permute-done.11.refs_2_ = bf16[256,512]{1,0:T(8,128)(2,1)S(1)} collective-permute-done((bf16[256,512]{1,0:T(8,128)(2,1)S(1)}, bf16[256,512]{1,0:T(8,128)(2,1)S(1)}, u32[]{:S(2)}, u32[]{:S(2)}) %collective-permute-start.11) | collective-permute-done | bytes 262176 | tf_op jit(solution)/shard_map/swap_tp_1/ppermute | solution.py:111
  44.5 2.7 %shard_map.289 = (bf16[272,512]{1,0:T(8,128)(2,1)S(1)}, bf16[256,512]{1,0:T(8,128)(2,1)S(1)}, f32[256,512]{1,0:T(8,128)S(1)}, f32[256,512]{1,0:T(8,128)S(1)}, bf...) custom-call(f32[256,512]{1,0:T(8,128)S(1)} %get-tuple-element.237.re, ...), custom_call_target="tpu_custom_call" | custom-call | flops 8000000000 | bytes 65536 | tf_op jit(solution)/shard_map/pallas_call | solution.py:89
  47.2 1.2 %collective-permute-start.22 = (bf16[272,512]{1,0:T(8,128)(2,1)S(1)}, bf16[272,512]{1,0:T(8,128)(2,1)S(1)}, u32[]{:S(2)}, u32[]{:S(2)}) collective-permute-start(bf16[272,512]{1,0:T(8,128)(2,1)S(1)} %get-tuple-element.334.refs_13_), channel_id=1, source_target_pairs={{0,1},{1,0},{2,3},{3,2},{4,5},{5,4},{6,7},{7,6},{8,9},{9,8},{10,11... | collective-permute-start | bytes 835592 | tf_op jit(solution)/shard_map/swap_tp_1/ppermute | solution.py:111
  48.4 1.3 %shard_map.290 = (f32[256,2048]{1,0:T(8,128)S(1)}, bf16[256,512]{1,0:T(8,128)(2,1)S(1)}, bf16[256,512]{1,0:T(8,128)(2,1)S(1)}, bf16[256,512]{1,0:T(8,128)(2,1)S(1)}, bf16[256,512]{1,0:T(8,128)(2,1)S(1)}) custom-call(bf16[256,512]{1,0:T(8,128)(2,1)S(1)} %get-tuple-element.301.refs_0_, bf16[256,512]{1,0:T(8,128)(2,1)S(1)} %get-tuple-element.302.refs_1_, ...), custom_call_target="tpu_custom_call" | custom-call | flops 8000000000 | bytes 65536 | tf_op jit(solution)/shard_map/pallas_call | solution.py:89
  52.4 0.7 shard_map.291
  53.1 1.3 %collective-permute-start.21 = (bf16[128,2048]{1,0:T(8,128)(2,1)S(1)}, bf16[128,2048]{1,0:T(8,128)(2,1)S(1)}, u32[]{:S(2)}, u32[]{:S(2)}) collective-permute-start(bf16[128,2048]{1,0:T(8,128)(2,1)S(1)} %get-tuple-element.328), channel_id=1, source_target_pairs={{0,4},{4,0},{8,12},{12,8},{16,24},{20,28},{24,16},{28,20},{1,5},{5... | collective-permute-start | bytes 1572872 | tf_op jit(solution)/shard_map/swap_turn_0/ppermute | solution.py:126
  54.4 0.5 collective-permute-done.22.refs_14_
  55.0 5.3 %shard_map.292 = (f32[256,256]{1,0:T(8,128)S(1)}, f32[256,512]{1,0:T(8,128)S(1)}, bf16[272,512]{1,0:T(8,128)(2,1)S(1)}, bf16[272,512]{1,0:T(8,128)(2,1)S(1)}, bf...) custom-call(s32[1,1024]{1,0:T(1,128)S(1)} %get-tuple-element.238.refs_, ...), custom_call_target="tpu_custom_call" | custom-call | flops 8000000000 | bytes 65536 | tf_op jit(solution)/shard_map/pallas_call | solution.py:89
  60.3 1.5 %collective-permute-start.27 = (bf16[272,512]{1,0:T(8,128)(2,1)S(1)}, bf16[272,512]{1,0:T(8,128)(2,1)S(1)}, u32[]{:S(2)}, u32[]{:S(2)}) collective-permute-start(bf16[272,512]{1,0:T(8,128)(2,1)S(1)} %get-tuple-element.360), channel_id=1, source_target_pairs={{0,12},{4,8},{8,4},{12,0},{1,13},{5,9},{9,5},{13,1},{2,14},{6,10},... | collective-permute-start | bytes 835592 | tf_op jit(solution)/shard_map/swap_ctx_3/ppermute | solution.py:111
  61.8 1.5 %collective-permute-start.26 = (bf16[272,512]{1,0:T(8,128)(2,1)S(1)}, bf16[272,512]{1,0:T(8,128)(2,1)S(1)}, u32[]{:S(2)}, u32[]{:S(2)}) collective-permute-start(bf16[272,512]{1,0:T(8,128)(2,1)S(1)} %get-tuple-element.359), channel_id=1, source_target_pairs={{0,8},{4,12},{8,0},{12,4},{1,9},{5,13},{9,1},{13,5},{2,10},{6,14},... | collective-permute-start | bytes 835592 | tf_op jit(solution)/shard_map/swap_ctx_2/ppermute | solution.py:111
  63.3 0.5 collective-permute-start.25
  63.8 1.2 %collective-permute-start.23 = (bf16[256,512]{1,0:T(8,128)(2,1)S(1)}, bf16[256,512]{1,0:T(8,128)(2,1)S(1)}, u32[]{:S(2)}, u32[]{:S(2)}) collective-permute-start(bf16[256,512]{1,0:T(8,128)(2,1)S(1)} %get-tuple-element.345.refs_3_), channel_id=1, source_target_pairs={{0,1},{1,0},{2,3},{3,2},{4,5},{5,4},{6,7},{7,6},{8,9},{9,8},{10,11... | collective-permute-start | bytes 786440 | tf_op jit(solution)/shard_map/swap_tp_1/ppermute | solution.py:111
  65.0 5.2 %collective-permute-done.23.refs_4_ = bf16[256,512]{1,0:T(8,128)(2,1)S(1)} collective-permute-done((bf16[256,512]{1,0:T(8,128)(2,1)S(1)}, bf16[256,512]{1,0:T(8,128)(2,1)S(1)}, u32[]{:S(2)}, u32[]{:S(2)}) %collective-permute-start.23) | collective-permute-done | bytes 262176 | tf_op jit(solution)/shard_map/swap_tp_1/ppermute | solution.py:111
  70.2 0.9 shard_map.293
  71.1 1.7 %collective-permute-start.24 = (bf16[384,512]{1,0:T(8,128)(2,1)S(1)}, bf16[384,512]{1,0:T(8,128)(2,1)S(1)}, u32[]{:S(2)}, u32[]{:S(2)}) collective-permute-start(bf16[384,512]{1,0:T(8,128)(2,1)S(1)} %get-tuple-element.352), channel_id=1, source_target_pairs={{0,2},{1,3},{2,0},{3,1},{4,6},{5,7},{6,4},{7,5},{8,10},{9,11},{10,... | collective-permute-start | bytes 1179656 | tf_op jit(solution)/shard_map/swap_tp_2/ppermute | solution.py:111
  72.8 1.7 %collective-permute-done.26.refs_8_ = bf16[272,512]{1,0:T(8,128)(2,1)S(1)} collective-permute-done((bf16[272,512]{1,0:T(8,128)(2,1)S(1)}, bf16[272,512]{1,0:T(8,128)(2,1)S(1)}, u32[]{:S(2)}, u32[]{:S(2)}) %collective-permute-start.26) | collective-permute-done | bytes 278560 | tf_op jit(solution)/shard_map/swap_ctx_2/ppermute | solution.py:111
  74.5 1.7 %shard_map.294 = (bf16[256,512]{1,0:T(8,128)(2,1)S(1)}, f32[16,512]{1,0:T(8,128)S(1)}, f32[256,1024]{1,0:T(8,128)S(1)}, bf16[272,384]{1,0:T(8,128)(2,1)S(1)}, bf...) custom-call(f32[256,512]{1,0:T(8,128)S(1)} %get-tuple-element.237.refs_0_, ...), custom_call_target="tpu_custom_call" | custom-call | flops 8000000000 | bytes 65536 | tf_op jit(solution)/shard_map/pallas_call | solution.py:89
  76.9 1.4 %collective-permute-done.30.refs_3_ = bf16[272,256]{1,0:T(8,128)(2,1)S(1)} collective-permute-done((bf16[272,256]{1,0:T(8,128)(2,1)S(1)}, bf16[272,256]{1,0:T(8,128)(2,1)S(1)}, u32[]{:S(2)}, u32[]{:S(2)}) %collective-permute-start.30) | collective-permute-done | bytes 139296 | tf_op jit(solution)/shard_map/swap_fsdp_1/ppermute | solution.py:111
  78.2 0.7 shard_map.295
  78.9 1.8 %collective-permute-start.35 = (bf16[80,1024]{1,0:T(8,128)(2,1)S(1)}, bf16[80,1024]{1,0:T(8,128)(2,1)S(1)}, u32[]{:S(2)}, u32[]{:S(2)}) collective-permute-start(bf16[80,1024]{1,0:T(8,128)(2,1)S(1)} %get-tuple-element.398), channel_id=1, source_target_pairs={{0,12},{4,8},{8,4},{12,0},{1,13},{5,9},{9,5},{13,1},{2,14},{6,10},... | collective-permute-start | bytes 491528 | tf_op jit(solution)/shard_map/swap_ctx_3/ppermute | solution.py:111
  80.7 1.2 %collective-permute-start.34 = (bf16[80,1024]{1,0:T(8,128)(2,1)S(1)}, bf16[80,1024]{1,0:T(8,128)(2,1)S(1)}, u32[]{:S(2)}, u32[]{:S(2)}) collective-permute-start(bf16[80,1024]{1,0:T(8,128)(2,1)S(1)} %get-tuple-element.397), channel_id=1, source_target_pairs={{0,8},{4,12},{8,0},{12,4},{1,9},{5,13},{9,1},{13,5},{2,10},{6,14},... | collective-permute-start | bytes 491528 | tf_op jit(solution)/shard_map/swap_ctx_2/ppermute | solution.py:111
  81.9 0.5 collective-permute-start.33
  82.5 1.0 collective-permute-start.36
  83.5 5.1 %collective-permute-done.24.refs_1_ = bf16[384,512]{1,0:T(8,128)(2,1)S(1)} collective-permute-done((bf16[384,512]{1,0:T(8,128)(2,1)S(1)}, bf16[384,512]{1,0:T(8,128)(2,1)S(1)}, u32[]{:S(2)}, u32[]{:S(2)}) %collective-permute-start.24) | collective-permute-done | bytes 393248 | tf_op jit(solution)/shard_map/swap_tp_2/ppermute | solution.py:111
  88.6 0.6 shard_map.296
  89.7 0.6 shard_map.297
  90.3 2.0 %collective-permute-start.37 = (bf16[96,512]{1,0:T(8,128)(2,1)S(1)}, bf16[96,512]{1,0:T(8,128)(2,1)S(1)}, u32[]{:S(2)}, u32[]{:S(2)}) collective-permute-start(bf16[96,512]{1,0:T(8,128)(2,1)S(1)} %get-tuple-element.409.refs_4_), channel_id=1, source_target_pairs={{0,2},{1,3},{2,0},{3,1},{4,6},{5,7},{6,4},{7,5},{8,10},{9,11},{10,... | collective-permute-start | bytes 294920 | tf_op jit(solution)/shard_map/swap_tp_2/ppermute | solution.py:111
  92.3 1.2 %collective-permute-start.32 = (bf16[64,512]{1,0:T(8,128)(2,1)S(1)}, bf16[64,512]{1,0:T(8,128)(2,1)S(1)}, u32[]{:S(2)}, u32[]{:S(2)}) collective-permute-start(bf16[64,512]{1,0:T(8,128)(2,1)S(1)} %get-tuple-element.394), channel_id=1, source_target_pairs={{0,8},{4,12},{8,0},{12,4},{16,20},{20,16},{24,28},{28,24},{1,9},{5... | collective-permute-start | bytes 196616 | tf_op jit(solution)/shard_map/swap_turn_1/ppermute | solution.py:126
  93.6 0.8 collective-permute-start.31
  94.7 0.6 shard_map.298.refs_4_
  95.3 2.8 %collective-permute-done.37.refs_5_ = bf16[96,512]{1,0:T(8,128)(2,1)S(1)} collective-permute-done((bf16[96,512]{1,0:T(8,128)(2,1)S(1)}, bf16[96,512]{1,0:T(8,128)(2,1)S(1)}, u32[]{:S(2)}, u32[]{:S(2)}) %collective-permute-start.37) | collective-permute-done | bytes 98336 | tf_op jit(solution)/shard_map/swap_tp_2/ppermute | solution.py:111
  98.2 0.6 shard_map.299
  98.8 1.8 %collective-permute-start.42 = (bf16[64,1536]{1,0:T(8,128)(2,1)S(1)}, bf16[64,1536]{1,0:T(8,128)(2,1)S(1)}, u32[]{:S(2)}, u32[]{:S(2)}) collective-permute-start(bf16[64,1536]{1,0:T(8,128)(2,1)S(1)} %get-tuple-element.427.refs_0_), channel_id=1, source_target_pairs={{0,12},{4,8},{8,4},{12,0},{1,13},{5,9},{9,5},{13,1},{2,14},{6,10},... | collective-permute-start | bytes 589832 | tf_op jit(solution)/shard_map/swap_ctx_3/ppermute | solution.py:111
  100.6 1.2 %collective-permute-start.41 = (bf16[64,1536]{1,0:T(8,128)(2,1)S(1)}, bf16[64,1536]{1,0:T(8,128)(2,1)S(1)}, u32[]{:S(2)}, u32[]{:S(2)}) collective-permute-start(bf16[64,1536]{1,0:T(8,128)(2,1)S(1)} %get-tuple-element.427.refs_0_), channel_id=1, source_target_pairs={{0,8},{4,12},{8,0},{12,4},{1,9},{5,13},{9,1},{13,5},{2,10},{6,14},... | collective-permute-start | bytes 589832 | tf_op jit(solution)/shard_map/swap_ctx_2/ppermute | solution.py:111
  101.8 0.5 collective-permute-start.40
  102.3 2.4 %collective-permute-start.38 = (bf16[160,512]{1,0:T(8,128)(2,1)S(1)}, bf16[160,512]{1,0:T(8,128)(2,1)S(1)}, u32[]{:S(2)}, u32[]{:S(2)}) collective-permute-start(bf16[160,512]{1,0:T(8,128)(2,1)S(1)} %get-tuple-element.418.refs_2_), channel_id=1, source_target_pairs={{0,1},{1,0},{2,3},{3,2},{4,5},{5,4},{6,7},{7,6},{8,9},{9,8},{10,11... | collective-permute-start | bytes 491528 | tf_op jit(solution)/shard_map/swap_tp_1/ppermute | solution.py:111
  104.9 2.7 %collective-permute-done.42.refs_3_ = bf16[64,1536]{1,0:T(8,128)(2,1)S(1)} collective-permute-done((bf16[64,1536]{1,0:T(8,128)(2,1)S(1)}, bf16[64,1536]{1,0:T(8,128)(2,1)S(1)}, u32[]{:S(2)}, u32[]{:S(2)}) %collective-permute-start.42) | collective-permute-done | bytes 196640 | tf_op jit(solution)/shard_map/swap_ctx_3/ppermute | solution.py:111
  107.6 2.7 %collective-permute-done.41.refs_2_ = bf16[64,1536]{1,0:T(8,128)(2,1)S(1)} collective-permute-done((bf16[64,1536]{1,0:T(8,128)(2,1)S(1)}, bf16[64,1536]{1,0:T(8,128)(2,1)S(1)}, u32[]{:S(2)}, u32[]{:S(2)}) %collective-permute-start.41) | collective-permute-done | bytes 196640 | tf_op jit(solution)/shard_map/swap_ctx_2/ppermute | solution.py:111
  110.5 1.8 %shard_map.300 = (f32[256,512]{1,0:T(8,128)}, f32[256,512]{1,0:T(8,128)}, f32[3,256,128]{2,1,0:T(8,128)}, f32[256,128]{1,0:T(8,128)}) custom-call(bf16[64,1536]{1,0:T(8,128)(2,1)S(1)} %get-tuple-element.427.refs_0_, bf16[64,1536]{1,0:T(8,128)(2,1)S(1)} %collective-permute-done.40.refs_1_, bf16[64,1536]{1,0:T(8,128)(2,1)S(1)} %collective-permute-done.41.refs_2_, ...), custom_call_target="tpu_custom_call" | custom-call | flops 1000 | bytes 65536 | tf_op jit(solution)/shard_map/pallas_call | solution.py:89
  112.3 0.8 collective-permute-done.38.refs_3_
  113.0 2.6 %shard_map.301 = (f32[512,512]{1,0:T(8,128)}, f32[512,512]{1,0:T(8,128)}, f32[1000,512]{1,0:T(8,128)}, f32[1,512]{1,0:T(1,128)}, f32[2,128]{1,0:T(2,128)}, /*ind...) custom-call(s32[4]{0:T(128)S(1)} %broadcast_select_fusion.refs_0_, ...), custom_call_target="tpu_custom_call", output_to_operand_aliasing={{2}: (6, {})} | custom-call | flops 1000 | bytes 65536 | tf_op jit(solution)/shard_map/pallas_call | solution.py:89
  (51 shorter events, 6.5 us)
Async XLA Ops:
  2.5 4.2 %collective-permute-start = (bf16[272,512]{1,0:T(8,128)(2,1)S(1)}, bf16[272,512]{1,0:T(8,128)(2,1)S(1)}, u32[]{:S(2)}, u32[]{:S(2)}) collective-permute-start(bf16[272,512]{1,0:T(8,128)(2,1)S(1)} %get-tuple-element.233.refs_10_.refs_12_.refs_7_.refs_5_.refs_18_), channel_id=1, source_target_pairs={{0,16},{16,0},{1,17},{17,1},{2,18},{18,2},{3,19},{19,3},{4,20},{20... | collective-permute-start | bytes 835592 | tf_op jit(solution)/shard_map/swap_fsdp_1/ppermute | solution.py:111
  3.1 15.1 %collective-permute-start.1 = (bf16[272,384]{1,0:T(8,128)(2,1)S(1)}, bf16[272,384]{1,0:T(8,128)(2,1)S(1)}, u32[]{:S(2)}, u32[]{:S(2)}) collective-permute-start(bf16[272,384]{1,0:T(8,128)(2,1)S(1)} %get-tuple-element.240), channel_id=1, source_target_pairs={{0,2},{1,3},{2,0},{3,1},{4,6},{5,7},{6,4},{7,5},{8,10},{9,11},{10,... | collective-permute-start | bytes 626696 | tf_op jit(solution)/shard_map/swap_tp_2/ppermute | solution.py:111
  9.1 9.0 %collective-permute-start.4 = (bf16[256,256]{1,0:T(8,128)(2,1)S(1)}, bf16[256,256]{1,0:T(8,128)(2,1)S(1)}, u32[]{:S(2)}, u32[]{:S(2)}) collective-permute-start(bf16[256,256]{1,0:T(8,128)(2,1)S(1)} %get-tuple-element.248.refs_2_.refs_3_), channel_id=1, source_target_pairs={{0,12},{4,8},{8,4},{12,0},{1,13},{5,9},{9,5},{13,1},{2,14},{6,10},... | collective-permute-start | bytes 393224 | tf_op jit(solution)/shard_map/swap_ctx_3/ppermute | solution.py:111
  11.6 6.8 %collective-permute-start.3 = (bf16[256,256]{1,0:T(8,128)(2,1)S(1)}, bf16[256,256]{1,0:T(8,128)(2,1)S(1)}, u32[]{:S(2)}, u32[]{:S(2)}) collective-permute-start(bf16[256,256]{1,0:T(8,128)(2,1)S(1)} %get-tuple-element.248.refs_2_.refs_3_), channel_id=1, source_target_pairs={{0,8},{4,12},{8,0},{12,4},{1,9},{5,13},{9,1},{13,5},{2,10},{6,14},... | collective-permute-start | bytes 393224 | tf_op jit(solution)/shard_map/swap_ctx_2/ppermute | solution.py:111
  12.1 6.4 %collective-permute-start.2 = (bf16[256,256]{1,0:T(8,128)(2,1)S(1)}, bf16[256,256]{1,0:T(8,128)(2,1)S(1)}, u32[]{:S(2)}, u32[]{:S(2)}) collective-permute-start(bf16[256,256]{1,0:T(8,128)(2,1)S(1)} %get-tuple-element.248.refs_2_.refs_3_), channel_id=1, source_target_pairs={{0,4},{4,0},{8,12},{12,8},{1,5},{5,1},{9,13},{13,9},{2,6},{6,2},{1... | collective-permute-start | bytes 393224 | tf_op jit(solution)/shard_map/swap_ctx_1/ppermute | solution.py:111
  16.6 11.3 %collective-permute-start.9 = (bf16[96,1024]{1,0:T(8,128)(2,1)S(1)}, bf16[96,1024]{1,0:T(8,128)(2,1)S(1)}, u32[]{:S(2)}, u32[]{:S(2)}) collective-permute-start(bf16[96,1024]{1,0:T(8,128)(2,1)S(1)} %get-tuple-element.277), channel_id=1, source_target_pairs={{0,2},{1,3},{2,0},{3,1},{4,6},{5,7},{6,4},{7,5},{8,10},{9,11},{10,... | collective-permute-start | bytes 589832 | tf_op jit(solution)/shard_map/swap_tp_2/ppermute | solution.py:111
  18.5 1.9 %collective-permute-start.5 = (bf16[272,384]{1,0:T(8,128)(2,1)S(1)}, bf16[272,384]{1,0:T(8,128)(2,1)S(1)}, u32[]{:S(2)}, u32[]{:S(2)}) collective-permute-start(bf16[272,384]{1,0:T(8,128)(2,1)S(1)} %collective-permute-done.1.refs_1_.refs_3_.refs_6_.refs_12_), channel_id=1, source_target_pairs={{0,16},{16,0},{1,17},{17,1},{2,18},{18,2},{3,19},{19,3},{4,20},{20... | collective-permute-start | bytes 626696 | tf_op jit(solution)/shard_map/swap_fsdp_1/ppermute | solution.py:111
  21.3 8.8 %collective-permute-start.8 = (bf16[256,256]{1,0:T(8,128)(2,1)S(1)}, bf16[256,256]{1,0:T(8,128)(2,1)S(1)}, u32[]{:S(2)}, u32[]{:S(2)}) collective-permute-start(bf16[256,256]{1,0:T(8,128)(2,1)S(1)} %get-tuple-element.275.refs_2_.refs_9_), channel_id=1, source_target_pairs={{0,12},{4,8},{8,4},{12,0},{1,13},{5,9},{9,5},{13,1},{2,14},{6,10},... | collective-permute-start | bytes 393224 | tf_op jit(solution)/shard_map/swap_ctx_3/ppermute | solution.py:111
  23.5 7.5 %collective-permute-start.7 = (bf16[256,256]{1,0:T(8,128)(2,1)S(1)}, bf16[256,256]{1,0:T(8,128)(2,1)S(1)}, u32[]{:S(2)}, u32[]{:S(2)}) collective-permute-start(bf16[256,256]{1,0:T(8,128)(2,1)S(1)} %get-tuple-element.275.refs_2_.refs_9_), channel_id=1, source_target_pairs={{0,8},{4,12},{8,0},{12,4},{1,9},{5,13},{9,1},{13,5},{2,10},{6,14},... | collective-permute-start | bytes 393224 | tf_op jit(solution)/shard_map/swap_ctx_2/ppermute | solution.py:111
  24.4 6.7 %collective-permute-start.6 = (bf16[256,256]{1,0:T(8,128)(2,1)S(1)}, bf16[256,256]{1,0:T(8,128)(2,1)S(1)}, u32[]{:S(2)}, u32[]{:S(2)}) collective-permute-start(bf16[256,256]{1,0:T(8,128)(2,1)S(1)} %get-tuple-element.275.refs_2_.refs_9_), channel_id=1, source_target_pairs={{0,4},{4,0},{8,12},{12,8},{1,5},{5,1},{9,13},{13,9},{2,6},{6,2},{1... | collective-permute-start | bytes 393224 | tf_op jit(solution)/shard_map/swap_ctx_1/ppermute | solution.py:111
  28.5 1.6 %collective-permute-start.10 = (bf16[256,128]{1,0:T(8,128)(2,1)S(1)}, bf16[256,128]{1,0:T(8,128)(2,1)S(1)}, u32[]{:S(2)}, u32[]{:S(2)}) collective-permute-start(bf16[256,128]{1,0:T(8,128)(2,1)S(1)} %get-tuple-element.282.refs_9_.refs_20_), channel_id=1, source_target_pairs={{0,16},{16,0},{1,17},{17,1},{2,18},{18,2},{3,19},{19,3},{4,20},{20... | collective-permute-start | bytes 196616 | tf_op jit(solution)/shard_map/swap_fsdp_1/ppermute | solution.py:111
  28.5 5.0 %collective-permute-start.13 = (bf16[64,1024]{1,0:T(8,128)(2,1)S(1)}, bf16[64,1024]{1,0:T(8,128)(2,1)S(1)}, u32[]{:S(2)}, u32[]{:S(2)}) collective-permute-start(bf16[64,1024]{1,0:T(8,128)(2,1)S(1)} %get-tuple-element.292.refs_0_), channel_id=1, source_target_pairs={{0,4},{4,0},{8,12},{12,8},{16,24},{20,28},{24,16},{28,20},{1,5},{5... | collective-permute-start | bytes 393224 | tf_op jit(solution)/shard_map/swap_turn_0/ppermute | solution.py:126
  34.1 6.4 %collective-permute-start.14 = (bf16[128,1024]{1,0:T(8,128)(2,1)S(1)}, bf16[128,1024]{1,0:T(8,128)(2,1)S(1)}, u32[]{:S(2)}, u32[]{:S(2)}) collective-permute-start(bf16[128,1024]{1,0:T(8,128)(2,1)S(1)} %shard_map.288.refs_9_), channel_id=1, source_target_pairs={{0,8},{4,12},{8,0},{12,4},{16,20},{20,16},{24,28},{28,24},{1,9},{5... | collective-permute-start | bytes 786440 | tf_op jit(solution)/shard_map/swap_turn_1/ppermute | solution.py:126
  35.7 4.9 %collective-permute-start.12 = (bf16[256,1024]{1,0:T(8,128)(2,1)S(1)}, bf16[256,1024]{1,0:T(8,128)(2,1)S(1)}, u32[]{:S(2)}, u32[]{:S(2)}) collective-permute-start(bf16[256,1024]{1,0:T(8,128)(2,1)S(1)} %get-tuple-element.290.refs_7_), channel_id=1, source_target_pairs={{0,16},{16,0},{1,17},{17,1},{2,18},{18,2},{3,19},{19,3},{4,20},{20... | collective-permute-start | bytes 1572872 | tf_op jit(solution)/shard_map/swap_fsdp_1/ppermute | solution.py:111
  35.7 4.9 %collective-permute-start.15 = (bf16[128,1024]{1,0:T(8,128)(2,1)S(1)}, bf16[128,1024]{1,0:T(8,128)(2,1)S(1)}, u32[]{:S(2)}, u32[]{:S(2)}) collective-permute-start(bf16[128,1024]{1,0:T(8,128)(2,1)S(1)} %shard_map.288.refs_9_), channel_id=1, source_target_pairs={{0,16},{16,0},{1,17},{17,1},{2,18},{18,2},{3,19},{19,3},{4,20},{20... | collective-permute-start | bytes 786440 | tf_op jit(solution)/shard_map/swap_fsdp_1/ppermute | solution.py:111
  36.2 8.2 %collective-permute-start.11 = (bf16[256,512]{1,0:T(8,128)(2,1)S(1)}, bf16[256,512]{1,0:T(8,128)(2,1)S(1)}, u32[]{:S(2)}, u32[]{:S(2)}) collective-permute-start(bf16[256,512]{1,0:T(8,128)(2,1)S(1)} %get-tuple-element.287.refs_1_), channel_id=1, source_target_pairs={{0,1},{1,0},{2,3},{3,2},{4,5},{5,4},{6,7},{7,6},{8,9},{9,8},{10,11... | collective-permute-start | bytes 786440 | tf_op jit(solution)/shard_map/swap_tp_1/ppermute | solution.py:111
  40.6 3.9 %collective-permute-start.16 = (bf16[128,1024]{1,0:T(8,128)(2,1)S(1)}, bf16[128,1024]{1,0:T(8,128)(2,1)S(1)}, u32[]{:S(2)}, u32[]{:S(2)}) collective-permute-start(bf16[128,1024]{1,0:T(8,128)(2,1)S(1)} %collective-permute-done.14.refs_10_), channel_id=1, source_target_pairs={{0,16},{16,0},{1,17},{17,1},{2,18},{18,2},{3,19},{19,3},{4,20},{20... | collective-permute-start | bytes 786440 | tf_op jit(solution)/shard_map/swap_fsdp_1/ppermute | solution.py:111
  47.2 7.8 %collective-permute-start.22 = (bf16[272,512]{1,0:T(8,128)(2,1)S(1)}, bf16[272,512]{1,0:T(8,128)(2,1)S(1)}, u32[]{:S(2)}, u32[]{:S(2)}) collective-permute-start(bf16[272,512]{1,0:T(8,128)(2,1)S(1)} %get-tuple-element.334.refs_13_), channel_id=1, source_target_pairs={{0,1},{1,0},{2,3},{3,2},{4,5},{5,4},{6,7},{7,6},{8,9},{9,8},{10,11... | collective-permute-start | bytes 835592 | tf_op jit(solution)/shard_map/swap_tp_1/ppermute | solution.py:111
  49.7 1.6 %collective-permute-start.20 = (bf16[256,512]{1,0:T(8,128)(2,1)S(1)}, bf16[256,512]{1,0:T(8,128)(2,1)S(1)}, u32[]{:S(2)}, u32[]{:S(2)}) collective-permute-start(bf16[256,512]{1,0:T(8,128)(2,1)S(1)} %get-tuple-element.322), channel_id=1, source_target_pairs={{0,16},{16,0},{1,17},{17,1},{2,18},{18,2},{3,19},{19,3},{4,20},{20... | collective-permute-start | bytes 786440 | tf_op jit(solution)/shard_map/swap_fsdp_1/ppermute | solution.py:111
  49.8 1.9 %collective-permute-start.19 = (bf16[256,512]{1,0:T(8,128)(2,1)S(1)}, bf16[256,512]{1,0:T(8,128)(2,1)S(1)}, u32[]{:S(2)}, u32[]{:S(2)}) collective-permute-start(bf16[256,512]{1,0:T(8,128)(2,1)S(1)} %get-tuple-element.319), channel_id=1, source_target_pairs={{0,16},{16,0},{1,17},{17,1},{2,18},{18,2},{3,19},{19,3},{4,20},{20... | collective-permute-start | bytes 786440 | tf_op jit(solution)/shard_map/swap_fsdp_1/ppermute | solution.py:111
  50.3 1.8 %collective-permute-start.18 = (bf16[256,512]{1,0:T(8,128)(2,1)S(1)}, bf16[256,512]{1,0:T(8,128)(2,1)S(1)}, u32[]{:S(2)}, u32[]{:S(2)}) collective-permute-start(bf16[256,512]{1,0:T(8,128)(2,1)S(1)} %get-tuple-element.316), channel_id=1, source_target_pairs={{0,16},{16,0},{1,17},{17,1},{2,18},{18,2},{3,19},{19,3},{4,20},{20... | collective-permute-start | bytes 786440 | tf_op jit(solution)/shard_map/swap_fsdp_1/ppermute | solution.py:111
  50.3 2.1 %collective-permute-start.17 = (bf16[256,512]{1,0:T(8,128)(2,1)S(1)}, bf16[256,512]{1,0:T(8,128)(2,1)S(1)}, u32[]{:S(2)}, u32[]{:S(2)}) collective-permute-start(bf16[256,512]{1,0:T(8,128)(2,1)S(1)} %get-tuple-element.313), channel_id=1, source_target_pairs={{0,16},{16,0},{1,17},{17,1},{2,18},{18,2},{3,19},{19,3},{4,20},{20... | collective-permute-start | bytes 786440 | tf_op jit(solution)/shard_map/swap_fsdp_1/ppermute | solution.py:111
  53.1 17.1 %collective-permute-start.21 = (bf16[128,2048]{1,0:T(8,128)(2,1)S(1)}, bf16[128,2048]{1,0:T(8,128)(2,1)S(1)}, u32[]{:S(2)}, u32[]{:S(2)}) collective-permute-start(bf16[128,2048]{1,0:T(8,128)(2,1)S(1)} %get-tuple-element.328), channel_id=1, source_target_pairs={{0,4},{4,0},{8,12},{12,8},{16,24},{20,28},{24,16},{28,20},{1,5},{5... | collective-permute-start | bytes 1572872 | tf_op jit(solution)/shard_map/swap_turn_0/ppermute | solution.py:126
  60.3 12.5 %collective-permute-start.27 = (bf16[272,512]{1,0:T(8,128)(2,1)S(1)}, bf16[272,512]{1,0:T(8,128)(2,1)S(1)}, u32[]{:S(2)}, u32[]{:S(2)}) collective-permute-start(bf16[272,512]{1,0:T(8,128)(2,1)S(1)} %get-tuple-element.360), channel_id=1, source_target_pairs={{0,12},{4,8},{8,4},{12,0},{1,13},{5,9},{9,5},{13,1},{2,14},{6,10},... | collective-permute-start | bytes 835592 | tf_op jit(solution)/shard_map/swap_ctx_3/ppermute | solution.py:111
  61.8 12.7 %collective-permute-start.26 = (bf16[272,512]{1,0:T(8,128)(2,1)S(1)}, bf16[272,512]{1,0:T(8,128)(2,1)S(1)}, u32[]{:S(2)}, u32[]{:S(2)}) collective-permute-start(bf16[272,512]{1,0:T(8,128)(2,1)S(1)} %get-tuple-element.359), channel_id=1, source_target_pairs={{0,8},{4,12},{8,0},{12,4},{1,9},{5,13},{9,1},{13,5},{2,10},{6,14},... | collective-permute-start | bytes 835592 | tf_op jit(solution)/shard_map/swap_ctx_2/ppermute | solution.py:111
  63.3 11.2 %collective-permute-start.25 = (bf16[272,512]{1,0:T(8,128)(2,1)S(1)}, bf16[272,512]{1,0:T(8,128)(2,1)S(1)}, u32[]{:S(2)}, u32[]{:S(2)}) collective-permute-start(bf16[272,512]{1,0:T(8,128)(2,1)S(1)} %get-tuple-element.358), channel_id=1, source_target_pairs={{0,4},{4,0},{8,12},{12,8},{1,5},{5,1},{9,13},{13,9},{2,6},{6,2},{1... | collective-permute-start | bytes 835592 | tf_op jit(solution)/shard_map/swap_ctx_1/ppermute | solution.py:111
  63.8 6.4 %collective-permute-start.23 = (bf16[256,512]{1,0:T(8,128)(2,1)S(1)}, bf16[256,512]{1,0:T(8,128)(2,1)S(1)}, u32[]{:S(2)}, u32[]{:S(2)}) collective-permute-start(bf16[256,512]{1,0:T(8,128)(2,1)S(1)} %get-tuple-element.345.refs_3_), channel_id=1, source_target_pairs={{0,1},{1,0},{2,3},{3,2},{4,5},{5,4},{6,7},{7,6},{8,9},{9,8},{10,11... | collective-permute-start | bytes 786440 | tf_op jit(solution)/shard_map/swap_tp_1/ppermute | solution.py:111
  71.1 17.5 %collective-permute-start.24 = (bf16[384,512]{1,0:T(8,128)(2,1)S(1)}, bf16[384,512]{1,0:T(8,128)(2,1)S(1)}, u32[]{:S(2)}, u32[]{:S(2)}) collective-permute-start(bf16[384,512]{1,0:T(8,128)(2,1)S(1)} %get-tuple-element.352), channel_id=1, source_target_pairs={{0,2},{1,3},{2,0},{3,1},{4,6},{5,7},{6,4},{7,5},{8,10},{9,11},{10,... | collective-permute-start | bytes 1179656 | tf_op jit(solution)/shard_map/swap_tp_2/ppermute | solution.py:111
  76.2 2.0 %collective-permute-start.29 = (bf16[272,384]{1,0:T(8,128)(2,1)S(1)}, bf16[272,384]{1,0:T(8,128)(2,1)S(1)}, u32[]{:S(2)}, u32[]{:S(2)}) collective-permute-start(bf16[272,384]{1,0:T(8,128)(2,1)S(1)} %get-tuple-element.371), channel_id=1, source_target_pairs={{0,16},{16,0},{1,17},{17,1},{2,18},{18,2},{3,19},{19,3},{4,20},{20... | collective-permute-start | bytes 626696 | tf_op jit(solution)/shard_map/swap_fsdp_1/ppermute | solution.py:111
  76.3 1.9 %collective-permute-start.28 = (bf16[272,384]{1,0:T(8,128)(2,1)S(1)}, bf16[272,384]{1,0:T(8,128)(2,1)S(1)}, u32[]{:S(2)}, u32[]{:S(2)}) collective-permute-start(bf16[272,384]{1,0:T(8,128)(2,1)S(1)} %get-tuple-element.368), channel_id=1, source_target_pairs={{0,16},{16,0},{1,17},{17,1},{2,18},{18,2},{3,19},{19,3},{4,20},{20... | collective-permute-start | bytes 626696 | tf_op jit(solution)/shard_map/swap_fsdp_1/ppermute | solution.py:111
  76.8 1.4 %collective-permute-start.30 = (bf16[272,256]{1,0:T(8,128)(2,1)S(1)}, bf16[272,256]{1,0:T(8,128)(2,1)S(1)}, u32[]{:S(2)}, u32[]{:S(2)}) collective-permute-start(bf16[272,256]{1,0:T(8,128)(2,1)S(1)} %get-tuple-element.374), channel_id=1, source_target_pairs={{0,16},{16,0},{1,17},{17,1},{2,18},{18,2},{3,19},{19,3},{4,20},{20... | collective-permute-start | bytes 417800 | tf_op jit(solution)/shard_map/swap_fsdp_1/ppermute | solution.py:111
  78.9 25.9 %copy-start = (s32[2]{0:T(128)S(1)}, s32[2]{0:T(128)}, u32[]{:S(2)}) copy-start(s32[2]{0:T(128)} %refs_0_.3) | copy-start | bytes 28
  78.9 10.3 %collective-permute-start.35 = (bf16[80,1024]{1,0:T(8,128)(2,1)S(1)}, bf16[80,1024]{1,0:T(8,128)(2,1)S(1)}, u32[]{:S(2)}, u32[]{:S(2)}) collective-permute-start(bf16[80,1024]{1,0:T(8,128)(2,1)S(1)} %get-tuple-element.398), channel_id=1, source_target_pairs={{0,12},{4,8},{8,4},{12,0},{1,13},{5,9},{9,5},{13,1},{2,14},{6,10},... | collective-permute-start | bytes 491528 | tf_op jit(solution)/shard_map/swap_ctx_3/ppermute | solution.py:111
  80.7 9.0 %collective-permute-start.34 = (bf16[80,1024]{1,0:T(8,128)(2,1)S(1)}, bf16[80,1024]{1,0:T(8,128)(2,1)S(1)}, u32[]{:S(2)}, u32[]{:S(2)}) collective-permute-start(bf16[80,1024]{1,0:T(8,128)(2,1)S(1)} %get-tuple-element.397), channel_id=1, source_target_pairs={{0,8},{4,12},{8,0},{12,4},{1,9},{5,13},{9,1},{13,5},{2,10},{6,14},... | collective-permute-start | bytes 491528 | tf_op jit(solution)/shard_map/swap_ctx_2/ppermute | solution.py:111
  81.9 7.8 %collective-permute-start.33 = (bf16[80,1024]{1,0:T(8,128)(2,1)S(1)}, bf16[80,1024]{1,0:T(8,128)(2,1)S(1)}, u32[]{:S(2)}, u32[]{:S(2)}) collective-permute-start(bf16[80,1024]{1,0:T(8,128)(2,1)S(1)} %get-tuple-element.396), channel_id=1, source_target_pairs={{0,4},{4,0},{8,12},{12,8},{1,5},{5,1},{9,13},{13,9},{2,6},{6,2},{1... | collective-permute-start | bytes 491528 | tf_op jit(solution)/shard_map/swap_ctx_1/ppermute | solution.py:111
  82.5 12.2 %collective-permute-start.36 = (bf16[256,512]{1,0:T(8,128)(2,1)S(1)}, bf16[256,512]{1,0:T(8,128)(2,1)S(1)}, u32[]{:S(2)}, u32[]{:S(2)}) collective-permute-start(bf16[256,512]{1,0:T(8,128)(2,1)S(1)} %get-tuple-element.405.refs_1_), channel_id=1, source_target_pairs={{0,1},{1,0},{2,3},{3,2},{4,5},{5,4},{6,7},{7,6},{8,9},{9,8},{10,11... | collective-permute-start | bytes 786440 | tf_op jit(solution)/shard_map/swap_tp_1/ppermute | solution.py:111
  90.3 7.8 %collective-permute-start.37 = (bf16[96,512]{1,0:T(8,128)(2,1)S(1)}, bf16[96,512]{1,0:T(8,128)(2,1)S(1)}, u32[]{:S(2)}, u32[]{:S(2)}) collective-permute-start(bf16[96,512]{1,0:T(8,128)(2,1)S(1)} %get-tuple-element.409.refs_4_), channel_id=1, source_target_pairs={{0,2},{1,3},{2,0},{3,1},{4,6},{5,7},{6,4},{7,5},{8,10},{9,11},{10,... | collective-permute-start | bytes 294920 | tf_op jit(solution)/shard_map/swap_tp_2/ppermute | solution.py:111
  92.3 5.8 %collective-permute-start.32 = (bf16[64,512]{1,0:T(8,128)(2,1)S(1)}, bf16[64,512]{1,0:T(8,128)(2,1)S(1)}, u32[]{:S(2)}, u32[]{:S(2)}) collective-permute-start(bf16[64,512]{1,0:T(8,128)(2,1)S(1)} %get-tuple-element.394), channel_id=1, source_target_pairs={{0,8},{4,12},{8,0},{12,4},{16,20},{20,16},{24,28},{28,24},{1,9},{5... | collective-permute-start | bytes 196616 | tf_op jit(solution)/shard_map/swap_turn_1/ppermute | solution.py:126
  93.6 4.6 %collective-permute-start.31 = (bf16[64,512]{1,0:T(8,128)(2,1)S(1)}, bf16[64,512]{1,0:T(8,128)(2,1)S(1)}, u32[]{:S(2)}, u32[]{:S(2)}) collective-permute-start(bf16[64,512]{1,0:T(8,128)(2,1)S(1)} %get-tuple-element.391), channel_id=1, source_target_pairs={{0,8},{4,12},{8,0},{12,4},{16,20},{20,16},{24,28},{28,24},{1,9},{5... | collective-permute-start | bytes 196616 | tf_op jit(solution)/shard_map/swap_turn_1/ppermute | solution.py:126
  98.1 14.9 %collective-permute-start.39 = (bf16[256,512]{1,0:T(8,128)(2,1)S(1)}, bf16[256,512]{1,0:T(8,128)(2,1)S(1)}, u32[]{:S(2)}, u32[]{:S(2)}) collective-permute-start(bf16[256,512]{1,0:T(8,128)(2,1)S(1)} %shard_map.298.refs_4_), channel_id=1, source_target_pairs={{0,2},{1,3},{2,0},{3,1},{4,6},{5,7},{6,4},{7,5},{8,10},{9,11},{10,... | collective-permute-start | bytes 786440 | tf_op jit(solution)/shard_map/swap_tp_2/ppermute | solution.py:111
  98.8 8.8 %collective-permute-start.42 = (bf16[64,1536]{1,0:T(8,128)(2,1)S(1)}, bf16[64,1536]{1,0:T(8,128)(2,1)S(1)}, u32[]{:S(2)}, u32[]{:S(2)}) collective-permute-start(bf16[64,1536]{1,0:T(8,128)(2,1)S(1)} %get-tuple-element.427.refs_0_), channel_id=1, source_target_pairs={{0,12},{4,8},{8,4},{12,0},{1,13},{5,9},{9,5},{13,1},{2,14},{6,10},... | collective-permute-start | bytes 589832 | tf_op jit(solution)/shard_map/swap_ctx_3/ppermute | solution.py:111
  100.6 9.8 %collective-permute-start.41 = (bf16[64,1536]{1,0:T(8,128)(2,1)S(1)}, bf16[64,1536]{1,0:T(8,128)(2,1)S(1)}, u32[]{:S(2)}, u32[]{:S(2)}) collective-permute-start(bf16[64,1536]{1,0:T(8,128)(2,1)S(1)} %get-tuple-element.427.refs_0_), channel_id=1, source_target_pairs={{0,8},{4,12},{8,0},{12,4},{1,9},{5,13},{9,1},{13,5},{2,10},{6,14},... | collective-permute-start | bytes 589832 | tf_op jit(solution)/shard_map/swap_ctx_2/ppermute | solution.py:111
  101.8 8.7 %collective-permute-start.40 = (bf16[64,1536]{1,0:T(8,128)(2,1)S(1)}, bf16[64,1536]{1,0:T(8,128)(2,1)S(1)}, u32[]{:S(2)}, u32[]{:S(2)}) collective-permute-start(bf16[64,1536]{1,0:T(8,128)(2,1)S(1)} %get-tuple-element.427.refs_0_), channel_id=1, source_target_pairs={{0,4},{4,0},{8,12},{12,8},{1,5},{5,1},{9,13},{13,9},{2,6},{6,2},{1... | collective-permute-start | bytes 589832 | tf_op jit(solution)/shard_map/swap_ctx_1/ppermute | solution.py:111
  102.3 10.7 %collective-permute-start.38 = (bf16[160,512]{1,0:T(8,128)(2,1)S(1)}, bf16[160,512]{1,0:T(8,128)(2,1)S(1)}, u32[]{:S(2)}, u32[]{:S(2)}) collective-permute-start(bf16[160,512]{1,0:T(8,128)(2,1)S(1)} %get-tuple-element.418.refs_2_), channel_id=1, source_target_pairs={{0,1},{1,0},{2,3},{3,2},{4,5},{5,4},{6,7},{7,6},{8,9},{9,8},{10,11... | collective-permute-start | bytes 491528 | tf_op jit(solution)/shard_map/swap_tp_1/ppermute | solution.py:111

commit v6 on v5

--- a/solution.py
+++ b/solution.py
@@ -289,9 +289,9 @@
     mixed, lse = None, None
     for head in range(width // HEAD_DIM):
         mine = lane_mask((span, width), head)
-        masked = jnp.where(mine, query, jnp.zeros_like(query))
+        masked = jnp.where(mine, query * SCALE, jnp.zeros_like(query))
         scores = [
-            dot_nt(masked, kv[:span, :width]) * SCALE + bias for kv, bias in zip(kvs, biases)
+            dot_nt(masked, kv[:span, :width]) + bias for kv, bias in zip(kvs, biases)
         ]
         top = functools.reduce(
             jnp.maximum, [jnp.max(block, axis=-1, keepdims=True) for block in scores]
@@ -471,16 +471,16 @@
     dq, dks, dvs = None, [None] * 4, [None] * 4
     for head in range(width // HEAD_DIM):
         mine = lane_mask((span, width), head)
-        masked_q = jnp.where(mine, query, jnp.zeros_like(query))
+        masked_q = jnp.where(mine, query * SCALE, jnp.zeros_like(query))
         masked_g = jnp.where(mine, grad, jnp.zeros_like(grad))
         lse = lse_ref[:, head * HEAD_DIM : head * HEAD_DIM + 1]
         probs = [
-            jnp.exp(dot_nt(masked_q, kv[:span, :width]) * SCALE + bias - lse)
+            jnp.exp(dot_nt(masked_q, kv[:span, :width]) + bias - lse)
             for kv, bias in zip(kvs, biases)
         ]
         grads = [dot_nt(masked_g, kv[:span, width:]) for kv in kvs]
         inner = total([jnp.sum(p * g, axis=-1, keepdims=True) for p, g in zip(probs, grads)])
-        raws = [(p * (g - inner) * SCALE).astype(BF16) for p, g in zip(probs, grads)]
+        raws = [(p * (g - inner)).astype(BF16) for p, g in zip(probs, grads)]
         head_dq = total([dot_nn(raw, kv[:span, :width]) for raw, kv in zip(raws, kvs)])
         dq = head_dq if head == 0 else jnp.where(mine, head_dq, dq)
         for step in range(4):
@@ -488,10 +488,10 @@
             head_dv = dot_tn(probs[step].astype(BF16), grad)
             dks[step] = head_dk if head == 0 else jnp.where(mine, head_dk, dks[step])
             dvs[step] = head_dv if head == 0 else jnp.where(mine, head_dv, dvs[step])
-    dq_ref[:, side * width : (side + 1) * width] = dq
+    dq_ref[:, side * width : (side + 1) * width] = dq * SCALE
     at = 2 * side * width
     for step in range(4):
-        outs[step][:span, at : at + width] = dks[step].astype(outs[step].dtype)
+        outs[step][:span, at : at + width] = (dks[step] * SCALE).astype(outs[step].dtype)
         outs[step][:span, at + width : at + 2 * width] = dvs[step].astype(outs[step].dtype)
 
 

time: 116 us -> 116 us (level)
  no operation moved by 1% of the time
where the time goes in v6:
time: 116 us
  starting transfers between devices  43 us (37%)
  waiting for transfers between devices  37.4 us (32%)
  Pallas kernels  34 us (29%)
    ppermute x38, starting transfers between devices, swap(): return lax.ppermute(values, axis, [(i, i ^ bits) for i in range(size)])  36.5 us
    pallas_call x22, Pallas kernels, call(): pl.pallas_call(body, out_shape=tuple((jax.ShapeDtypeStruct(shape, dtype)...  34 us
    ppermute x38, waiting for transfers between devices, swap(): return lax.ppermute(values, axis, [(i, i ^ bits) for i in range(size)])  33.8 us
    ppermute x5, starting transfers between devices, swap_turn(): return lax.ppermute(values, ('fsdp', 'ctx'), pairs)  6.47 us
    ppermute x5, waiting for transfers between devices, swap_turn(): return lax.ppermute(values, ('fsdp', 'ctx'), pairs)  3.56 us
  transfers between devices with their start and end apart: 43, of which 23 were waited for; matrix products, arithmetic and copies ran while one was open for 0% of the time, Pallas kernels for 23%

profile of v6, /device:TPU:0, one launch (start us, length us, event | category | flops | bytes accessed | tf_op | source)
XLA Modules:
  0.0 115.6 jit_solution(4031348386500351069)
XLA Ops:
  0.7 1.8 %shard_map.280 = (bf16[272,512]{1,0:T(8,128)(2,1)S(1)}, bf16[272,384]{1,0:T(8,128)(2,1)S(1)}, bf16[256,128]{1,0:T(8,128)(2,1)S(1)}) custom-call(s32[2]{0:T(128)} %refs_0_.3, f32[3,256,128]{2,1,0:T(8,128)} %refs_1_.3, f32[256,128]{1,0:T(8,128)} %refs_2_.3, f32[2,128]{1,0:T(2,128)} %refs_3_.3, f32[1,512]{1,0:T(1,128)} %bitcast.22, ...), custom_call_target="tpu_custom_call" | custom-call | flops 8000000000 | bytes 65536 | tf_op jit(solution)/shard_map/pallas_call | solution.py:89
  3.1 3.7 %collective-permute-start.1 = (bf16[272,384]{1,0:T(8,128)(2,1)S(1)}, bf16[272,384]{1,0:T(8,128)(2,1)S(1)}, u32[]{:S(2)}, u32[]{:S(2)}) collective-permute-start(bf16[272,384]{1,0:T(8,128)(2,1)S(1)} %get-tuple-element.240), channel_id=1, source_target_pairs={{0,2},{1,3},{2,0},{3,1},{4,6},{5,7},{6,4},{7,5},{8,10},{9,11},{10,... | collective-permute-start | bytes 626696 | tf_op jit(solution)/shard_map/swap_tp_2/ppermute | solution.py:111
  6.7 2.4 %shard_map.281 = (bf16[256,128]{1,0:T(8,128)(2,1)S(1)}, bf16[256,256]{1,0:T(8,128)(2,1)S(1)}, f32[256,512]{1,0:T(8,128)S(1)}, bf16[256,512]{1,0:T(8,128)(2,1)S(1...) custom-call(s32[2]{0:T(128)} %refs_0_.3, f32[2,256,512]{2,1,0:T(8,128)} %refs_1_.4, f32[1000,512]{1,0:T(8,128)} %refs_2_.4, ...), custom_call_target="tpu_custom_call" | custom-call | flops 8000000000 | bytes 65536 | tf_op jit(solution)/shard_map/pallas_call | solution.py:89
  9.1 2.5 %collective-permute-start.4 = (bf16[256,256]{1,0:T(8,128)(2,1)S(1)}, bf16[256,256]{1,0:T(8,128)(2,1)S(1)}, u32[]{:S(2)}, u32[]{:S(2)}) collective-permute-start(bf16[256,256]{1,0:T(8,128)(2,1)S(1)} %get-tuple-element.248.refs_2_.refs_3_), channel_id=1, source_target_pairs={{0,12},{4,8},{8,4},{12,0},{1,13},{5,9},{9,5},{13,1},{2,14},{6,10},... | collective-permute-start | bytes 393224 | tf_op jit(solution)/shard_map/swap_ctx_3/ppermute | solution.py:111
  12.1 0.5 collective-permute-start.2
  12.7 2.0 %shard_map.282 = (bf16[256,1024]{1,0:T(8,128)(2,1)S(1)}, bf16[96,1024]{1,0:T(8,128)(2,1)S(1)}, f32[256,512]{1,0:T(8,128)S(1)}) custom-call(bf16[256,128]{1,0:T(8,128)(2,1)S(1)} %get-tuple-element.250.refs_0_, f32[256,512]{1,0:T(8,128)} %refs_1_.5, f32[256,512]{1,0:T(8,128)} %refs_2_.5, f32[2,256,512]{2,1,0:T(8,128)} %refs_3_.5, ...), custom_call_target="tpu_custom_call" | custom-call | flops 1000 | bytes 65536 | tf_op jit(solution)/shard_map/pallas_call | solution.py:89
  14.7 1.9 %shard_map.283.refs_6_ = f32[1000,512]{1,0:T(8,128)} custom-call(s32[4]{0:T(128)S(1)} %pad_add_fusion.refs_5_.refs_13_.refs_4_.refs_0_.refs_6_.refs_1_.refs_11_.refs_2_.refs_22_.refs_18_.refs_3_.refs_7_), custom_call_target="tpu_custom_call" | custom-call | flops 1000 | bytes 65536 | tf_op jit(solution)/shard_map/pallas_call | solution.py:89
  16.6 1.5 %collective-permute-start.9 = (bf16[96,1024]{1,0:T(8,128)(2,1)S(1)}, bf16[96,1024]{1,0:T(8,128)(2,1)S(1)}, u32[]{:S(2)}, u32[]{:S(2)}) collective-permute-start(bf16[96,1024]{1,0:T(8,128)(2,1)S(1)} %get-tuple-element.277), channel_id=1, source_target_pairs={{0,2},{1,3},{2,0},{3,1},{4,6},{5,7},{6,4},{7,5},{8,10},{9,11},{10,... | collective-permute-start | bytes 589832 | tf_op jit(solution)/shard_map/swap_tp_2/ppermute | solution.py:111
  18.5 1.9 %shard_map.284 = (bf16[256,128]{1,0:T(8,128)(2,1)S(1)}, f32[256,128]{1,0:T(8,128)S(1)}) custom-call(s32[1,1024]{1,0:T(1,128)S(1)} %get-tuple-element.238.refs_0_, bf16[256,128]{1,0:T(8,128)(2,1)S(1)} %get-tuple-element.260.refs_1_, bf16[256,256]{1,0:T(8,128)(2,1)S(1)} %get-tuple-element.248.refs_2_.refs_3_, ...), custom_call_target="tpu_custom_call" | custom-call | flops 8000000000 | bytes 65536 | tf_op jit(solution)/shard_map/pallas_call | solution.py:89
  20.5 0.8 shard_map.285
  21.3 2.2 %collective-permute-start.8 = (bf16[256,256]{1,0:T(8,128)(2,1)S(1)}, bf16[256,256]{1,0:T(8,128)(2,1)S(1)}, u32[]{:S(2)}, u32[]{:S(2)}) collective-permute-start(bf16[256,256]{1,0:T(8,128)(2,1)S(1)} %get-tuple-element.275.refs_2_.refs_9_), channel_id=1, source_target_pairs={{0,12},{4,8},{8,4},{12,0},{1,13},{5,9},{9,5},{13,1},{2,14},{6,10},... | collective-permute-start | bytes 393224 | tf_op jit(solution)/shard_map/swap_ctx_3/ppermute | solution.py:111
  23.5 0.8 collective-permute-start.7
  24.4 0.5 collective-permute-start.6
  24.9 3.0 %collective-permute-done.9.refs_0_ = bf16[96,1024]{1,0:T(8,128)(2,1)S(1)} collective-permute-done((bf16[96,1024]{1,0:T(8,128)(2,1)S(1)}, bf16[96,1024]{1,0:T(8,128)(2,1)S(1)}, u32[]{:S(2)}, u32[]{:S(2)}) %collective-permute-start.9) | collective-permute-done | bytes 196640 | tf_op jit(solution)/shard_map/swap_tp_2/ppermute | solution.py:111
  27.9 0.6 shard_map.286
  28.5 1.6 %collective-permute-start.13 = (bf16[64,1024]{1,0:T(8,128)(2,1)S(1)}, bf16[64,1024]{1,0:T(8,128)(2,1)S(1)}, u32[]{:S(2)}, u32[]{:S(2)}) collective-permute-start(bf16[64,1024]{1,0:T(8,128)(2,1)S(1)} %get-tuple-element.292.refs_0_), channel_id=1, source_target_pairs={{0,4},{4,0},{8,12},{12,8},{16,24},{20,28},{24,16},{28,20},{1,5},{5... | collective-permute-start | bytes 393224 | tf_op jit(solution)/shard_map/swap_turn_0/ppermute | solution.py:126
  30.1 0.9 collective-permute-done.7.refs_4_.refs_11_
  31.0 2.2 %shard_map.287 = (bf16[256,128]{1,0:T(8,128)(2,1)S(1)}, f32[256,128]{1,0:T(8,128)S(1)}, bf16[256,512]{1,0:T(8,128)(2,1)S(1)}) custom-call(s32[1,1024]{1,0:T(1,128)S(1)} %get-tuple-element.238.refs_0_, bf16[256,128]{1,0:T(8,128)(2,1)S(1)} %get-tuple-element.268.refs_1_.refs_7_, bf16[256,256]{1,0:T(8,128)(2,1)S(1)} %get-tuple-element.275.refs_2_.refs_9_, ...), custom_call_target="tpu_custom_call" | custom-call | flops 8000000000 | bytes 65536 | tf_op jit(solution)/shard_map/pallas_call | solution.py:89
  33.6 0.6 shard_map.288.refs_9_
  34.1 1.6 %collective-permute-start.14 = (bf16[128,1024]{1,0:T(8,128)(2,1)S(1)}, bf16[128,1024]{1,0:T(8,128)(2,1)S(1)}, u32[]{:S(2)}, u32[]{:S(2)}) collective-permute-start(bf16[128,1024]{1,0:T(8,128)(2,1)S(1)} %shard_map.288.refs_9_), channel_id=1, source_target_pairs={{0,8},{4,12},{8,0},{12,4},{16,20},{20,16},{24,28},{28,24},{1,9},{5... | collective-permute-start | bytes 786440 | tf_op jit(solution)/shard_map/swap_turn_1/ppermute | solution.py:126
  36.2 1.2 %collective-permute-start.11 = (bf16[256,512]{1,0:T(8,128)(2,1)S(1)}, bf16[256,512]{1,0:T(8,128)(2,1)S(1)}, u32[]{:S(2)}, u32[]{:S(2)}) collective-permute-start(bf16[256,512]{1,0:T(8,128)(2,1)S(1)} %get-tuple-element.287.refs_1_), channel_id=1, source_target_pairs={{0,1},{1,0},{2,3},{3,2},{4,5},{5,4},{6,7},{7,6},{8,9},{9,8},{10,11... | collective-permute-start | bytes 786440 | tf_op jit(solution)/shard_map/swap_tp_1/ppermute | solution.py:111
  37.4 3.2 %collective-permute-done.14.refs_10_ = bf16[128,1024]{1,0:T(8,128)(2,1)S(1)} collective-permute-done((bf16[128,1024]{1,0:T(8,128)(2,1)S(1)}, bf16[128,1024]{1,0:T(8,128)(2,1)S(1)}, u32[]{:S(2)}, u32[]{:S(2)}) %collective-permute-start.14) | collective-permute-done | bytes 262176 | tf_op jit(solution)/shard_map/swap_turn_1/ppermute | solution.py:126
  40.6 3.9 %collective-permute-done.11.refs_2_ = bf16[256,512]{1,0:T(8,128)(2,1)S(1)} collective-permute-done((bf16[256,512]{1,0:T(8,128)(2,1)S(1)}, bf16[256,512]{1,0:T(8,128)(2,1)S(1)}, u32[]{:S(2)}, u32[]{:S(2)}) %collective-permute-start.11) | collective-permute-done | bytes 262176 | tf_op jit(solution)/shard_map/swap_tp_1/ppermute | solution.py:111
  44.5 2.7 %shard_map.289 = (bf16[272,512]{1,0:T(8,128)(2,1)S(1)}, bf16[256,512]{1,0:T(8,128)(2,1)S(1)}, f32[256,512]{1,0:T(8,128)S(1)}, f32[256,512]{1,0:T(8,128)S(1)}, bf...) custom-call(f32[256,512]{1,0:T(8,128)S(1)} %get-tuple-element.237.re, ...), custom_call_target="tpu_custom_call" | custom-call | flops 8000000000 | bytes 65536 | tf_op jit(solution)/shard_map/pallas_call | solution.py:89
  47.2 1.2 %collective-permute-start.22 = (bf16[272,512]{1,0:T(8,128)(2,1)S(1)}, bf16[272,512]{1,0:T(8,128)(2,1)S(1)}, u32[]{:S(2)}, u32[]{:S(2)}) collective-permute-start(bf16[272,512]{1,0:T(8,128)(2,1)S(1)} %get-tuple-element.334.refs_13_), channel_id=1, source_target_pairs={{0,1},{1,0},{2,3},{3,2},{4,5},{5,4},{6,7},{7,6},{8,9},{9,8},{10,11... | collective-permute-start | bytes 835592 | tf_op jit(solution)/shard_map/swap_tp_1/ppermute | solution.py:111
  48.4 1.3 %shard_map.290 = (f32[256,2048]{1,0:T(8,128)S(1)}, bf16[256,512]{1,0:T(8,128)(2,1)S(1)}, bf16[256,512]{1,0:T(8,128)(2,1)S(1)}, bf16[256,512]{1,0:T(8,128)(2,1)S(1)}, bf16[256,512]{1,0:T(8,128)(2,1)S(1)}) custom-call(bf16[256,512]{1,0:T(8,128)(2,1)S(1)} %get-tuple-element.301.refs_0_, bf16[256,512]{1,0:T(8,128)(2,1)S(1)} %get-tuple-element.302.refs_1_, ...), custom_call_target="tpu_custom_call" | custom-call | flops 8000000000 | bytes 65536 | tf_op jit(solution)/shard_map/pallas_call | solution.py:89
  52.4 0.7 shard_map.291
  53.1 1.3 %collective-permute-start.21 = (bf16[128,2048]{1,0:T(8,128)(2,1)S(1)}, bf16[128,2048]{1,0:T(8,128)(2,1)S(1)}, u32[]{:S(2)}, u32[]{:S(2)}) collective-permute-start(bf16[128,2048]{1,0:T(8,128)(2,1)S(1)} %get-tuple-element.328), channel_id=1, source_target_pairs={{0,4},{4,0},{8,12},{12,8},{16,24},{20,28},{24,16},{28,20},{1,5},{5... | collective-permute-start | bytes 1572872 | tf_op jit(solution)/shard_map/swap_turn_0/ppermute | solution.py:126
  54.4 0.5 collective-permute-done.22.refs_14_
  55.0 5.1 %shard_map.292 = (f32[256,256]{1,0:T(8,128)S(1)}, f32[256,512]{1,0:T(8,128)S(1)}, bf16[272,512]{1,0:T(8,128)(2,1)S(1)}, bf16[272,512]{1,0:T(8,128)(2,1)S(1)}, bf...) custom-call(s32[1,1024]{1,0:T(1,128)S(1)} %get-tuple-element.238.refs_, ...), custom_call_target="tpu_custom_call" | custom-call | flops 8000000000 | bytes 65536 | tf_op jit(solution)/shard_map/pallas_call | solution.py:89
  60.1 1.5 %collective-permute-start.27 = (bf16[272,512]{1,0:T(8,128)(2,1)S(1)}, bf16[272,512]{1,0:T(8,128)(2,1)S(1)}, u32[]{:S(2)}, u32[]{:S(2)}) collective-permute-start(bf16[272,512]{1,0:T(8,128)(2,1)S(1)} %get-tuple-element.360), channel_id=1, source_target_pairs={{0,12},{4,8},{8,4},{12,0},{1,13},{5,9},{9,5},{13,1},{2,14},{6,10},... | collective-permute-start | bytes 835592 | tf_op jit(solution)/shard_map/swap_ctx_3/ppermute | solution.py:111
  61.6 1.5 %collective-permute-start.26 = (bf16[272,512]{1,0:T(8,128)(2,1)S(1)}, bf16[272,512]{1,0:T(8,128)(2,1)S(1)}, u32[]{:S(2)}, u32[]{:S(2)}) collective-permute-start(bf16[272,512]{1,0:T(8,128)(2,1)S(1)} %get-tuple-element.359), channel_id=1, source_target_pairs={{0,8},{4,12},{8,0},{12,4},{1,9},{5,13},{9,1},{13,5},{2,10},{6,14},... | collective-permute-start | bytes 835592 | tf_op jit(solution)/shard_map/swap_ctx_2/ppermute | solution.py:111
  63.1 0.5 collective-permute-start.25
  63.7 1.2 %collective-permute-start.23 = (bf16[256,512]{1,0:T(8,128)(2,1)S(1)}, bf16[256,512]{1,0:T(8,128)(2,1)S(1)}, u32[]{:S(2)}, u32[]{:S(2)}) collective-permute-start(bf16[256,512]{1,0:T(8,128)(2,1)S(1)} %get-tuple-element.345.refs_3_), channel_id=1, source_target_pairs={{0,1},{1,0},{2,3},{3,2},{4,5},{5,4},{6,7},{7,6},{8,9},{9,8},{10,11... | collective-permute-start | bytes 786440 | tf_op jit(solution)/shard_map/swap_tp_1/ppermute | solution.py:111
  64.8 5.2 %collective-permute-done.23.refs_4_ = bf16[256,512]{1,0:T(8,128)(2,1)S(1)} collective-permute-done((bf16[256,512]{1,0:T(8,128)(2,1)S(1)}, bf16[256,512]{1,0:T(8,128)(2,1)S(1)}, u32[]{:S(2)}, u32[]{:S(2)}) %collective-permute-start.23) | collective-permute-done | bytes 262176 | tf_op jit(solution)/shard_map/swap_tp_1/ppermute | solution.py:111
  70.0 0.9 shard_map.293
  70.9 1.7 %collective-permute-start.24 = (bf16[384,512]{1,0:T(8,128)(2,1)S(1)}, bf16[384,512]{1,0:T(8,128)(2,1)S(1)}, u32[]{:S(2)}, u32[]{:S(2)}) collective-permute-start(bf16[384,512]{1,0:T(8,128)(2,1)S(1)} %get-tuple-element.352), channel_id=1, source_target_pairs={{0,2},{1,3},{2,0},{3,1},{4,6},{5,7},{6,4},{7,5},{8,10},{9,11},{10,... | collective-permute-start | bytes 1179656 | tf_op jit(solution)/shard_map/swap_tp_2/ppermute | solution.py:111
  72.6 1.7 %collective-permute-done.26.refs_8_ = bf16[272,512]{1,0:T(8,128)(2,1)S(1)} collective-permute-done((bf16[272,512]{1,0:T(8,128)(2,1)S(1)}, bf16[272,512]{1,0:T(8,128)(2,1)S(1)}, u32[]{:S(2)}, u32[]{:S(2)}) %collective-permute-start.26) | collective-permute-done | bytes 278560 | tf_op jit(solution)/shard_map/swap_ctx_2/ppermute | solution.py:111
  74.4 1.7 %shard_map.294 = (bf16[256,512]{1,0:T(8,128)(2,1)S(1)}, f32[16,512]{1,0:T(8,128)S(1)}, f32[256,1024]{1,0:T(8,128)S(1)}, bf16[272,384]{1,0:T(8,128)(2,1)S(1)}, bf...) custom-call(f32[256,512]{1,0:T(8,128)S(1)} %get-tuple-element.237.refs_0_, ...), custom_call_target="tpu_custom_call" | custom-call | flops 8000000000 | bytes 65536 | tf_op jit(solution)/shard_map/pallas_call | solution.py:89
  76.7 1.4 %collective-permute-done.30.refs_3_ = bf16[272,256]{1,0:T(8,128)(2,1)S(1)} collective-permute-done((bf16[272,256]{1,0:T(8,128)(2,1)S(1)}, bf16[272,256]{1,0:T(8,128)(2,1)S(1)}, u32[]{:S(2)}, u32[]{:S(2)}) %collective-permute-start.30) | collective-permute-done | bytes 139296 | tf_op jit(solution)/shard_map/swap_fsdp_1/ppermute | solution.py:111
  78.1 0.7 shard_map.295
  78.8 1.7 %collective-permute-start.35 = (bf16[80,1024]{1,0:T(8,128)(2,1)S(1)}, bf16[80,1024]{1,0:T(8,128)(2,1)S(1)}, u32[]{:S(2)}, u32[]{:S(2)}) collective-permute-start(bf16[80,1024]{1,0:T(8,128)(2,1)S(1)} %get-tuple-element.398), channel_id=1, source_target_pairs={{0,12},{4,8},{8,4},{12,0},{1,13},{5,9},{9,5},{13,1},{2,14},{6,10},... | collective-permute-start | bytes 491528 | tf_op jit(solution)/shard_map/swap_ctx_3/ppermute | solution.py:111
  80.5 1.3 %collective-permute-start.34 = (bf16[80,1024]{1,0:T(8,128)(2,1)S(1)}, bf16[80,1024]{1,0:T(8,128)(2,1)S(1)}, u32[]{:S(2)}, u32[]{:S(2)}) collective-permute-start(bf16[80,1024]{1,0:T(8,128)(2,1)S(1)} %get-tuple-element.397), channel_id=1, source_target_pairs={{0,8},{4,12},{8,0},{12,4},{1,9},{5,13},{9,1},{13,5},{2,10},{6,14},... | collective-permute-start | bytes 491528 | tf_op jit(solution)/shard_map/swap_ctx_2/ppermute | solution.py:111
  81.8 0.5 collective-permute-start.33
  82.3 1.0 collective-permute-start.36
  83.4 5.1 %collective-permute-done.24.refs_1_ = bf16[384,512]{1,0:T(8,128)(2,1)S(1)} collective-permute-done((bf16[384,512]{1,0:T(8,128)(2,1)S(1)}, bf16[384,512]{1,0:T(8,128)(2,1)S(1)}, u32[]{:S(2)}, u32[]{:S(2)}) %collective-permute-start.24) | collective-permute-done | bytes 393248 | tf_op jit(solution)/shard_map/swap_tp_2/ppermute | solution.py:111
  88.4 0.6 shard_map.296
  89.0 0.5 collective-permute-done.34.refs_2_
  89.6 0.6 shard_map.297
  90.2 2.0 %collective-permute-start.37 = (bf16[96,512]{1,0:T(8,128)(2,1)S(1)}, bf16[96,512]{1,0:T(8,128)(2,1)S(1)}, u32[]{:S(2)}, u32[]{:S(2)}) collective-permute-start(bf16[96,512]{1,0:T(8,128)(2,1)S(1)} %get-tuple-element.409.refs_4_), channel_id=1, source_target_pairs={{0,2},{1,3},{2,0},{3,1},{4,6},{5,7},{6,4},{7,5},{8,10},{9,11},{10,... | collective-permute-start | bytes 294920 | tf_op jit(solution)/shard_map/swap_tp_2/ppermute | solution.py:111
  92.2 1.2 %collective-permute-start.32 = (bf16[64,512]{1,0:T(8,128)(2,1)S(1)}, bf16[64,512]{1,0:T(8,128)(2,1)S(1)}, u32[]{:S(2)}, u32[]{:S(2)}) collective-permute-start(bf16[64,512]{1,0:T(8,128)(2,1)S(1)} %get-tuple-element.394), channel_id=1, source_target_pairs={{0,8},{4,12},{8,0},{12,4},{16,20},{20,16},{24,28},{28,24},{1,9},{5... | collective-permute-start | bytes 196616 | tf_op jit(solution)/shard_map/swap_turn_1/ppermute | solution.py:126
  93.4 0.8 collective-permute-start.31
  94.5 0.6 shard_map.298.refs_4_
  95.1 2.8 %collective-permute-done.37.refs_5_ = bf16[96,512]{1,0:T(8,128)(2,1)S(1)} collective-permute-done((bf16[96,512]{1,0:T(8,128)(2,1)S(1)}, bf16[96,512]{1,0:T(8,128)(2,1)S(1)}, u32[]{:S(2)}, u32[]{:S(2)}) %collective-permute-start.37) | collective-permute-done | bytes 98336 | tf_op jit(solution)/shard_map/swap_tp_2/ppermute | solution.py:111
  98.0 0.6 shard_map.299
  98.6 1.7 %collective-permute-start.42 = (bf16[64,1536]{1,0:T(8,128)(2,1)S(1)}, bf16[64,1536]{1,0:T(8,128)(2,1)S(1)}, u32[]{:S(2)}, u32[]{:S(2)}) collective-permute-start(bf16[64,1536]{1,0:T(8,128)(2,1)S(1)} %get-tuple-element.427.refs_0_), channel_id=1, source_target_pairs={{0,12},{4,8},{8,4},{12,0},{1,13},{5,9},{9,5},{13,1},{2,14},{6,10},... | collective-permute-start | bytes 589832 | tf_op jit(solution)/shard_map/swap_ctx_3/ppermute | solution.py:111
  100.4 1.3 %collective-permute-start.41 = (bf16[64,1536]{1,0:T(8,128)(2,1)S(1)}, bf16[64,1536]{1,0:T(8,128)(2,1)S(1)}, u32[]{:S(2)}, u32[]{:S(2)}) collective-permute-start(bf16[64,1536]{1,0:T(8,128)(2,1)S(1)} %get-tuple-element.427.refs_0_), channel_id=1, source_target_pairs={{0,8},{4,12},{8,0},{12,4},{1,9},{5,13},{9,1},{13,5},{2,10},{6,14},... | collective-permute-start | bytes 589832 | tf_op jit(solution)/shard_map/swap_ctx_2/ppermute | solution.py:111
  101.7 0.5 collective-permute-start.40
  102.2 2.4 %collective-permute-start.38 = (bf16[160,512]{1,0:T(8,128)(2,1)S(1)}, bf16[160,512]{1,0:T(8,128)(2,1)S(1)}, u32[]{:S(2)}, u32[]{:S(2)}) collective-permute-start(bf16[160,512]{1,0:T(8,128)(2,1)S(1)} %get-tuple-element.418.refs_2_), channel_id=1, source_target_pairs={{0,1},{1,0},{2,3},{3,2},{4,5},{5,4},{6,7},{7,6},{8,9},{9,8},{10,11... | collective-permute-start | bytes 491528 | tf_op jit(solution)/shard_map/swap_tp_1/ppermute | solution.py:111
  104.7 2.8 %collective-permute-done.42.refs_3_ = bf16[64,1536]{1,0:T(8,128)(2,1)S(1)} collective-permute-done((bf16[64,1536]{1,0:T(8,128)(2,1)S(1)}, bf16[64,1536]{1,0:T(8,128)(2,1)S(1)}, u32[]{:S(2)}, u32[]{:S(2)}) %collective-permute-start.42) | collective-permute-done | bytes 196640 | tf_op jit(solution)/shard_map/swap_ctx_3/ppermute | solution.py:111
  107.5 2.7 %collective-permute-done.41.refs_2_ = bf16[64,1536]{1,0:T(8,128)(2,1)S(1)} collective-permute-done((bf16[64,1536]{1,0:T(8,128)(2,1)S(1)}, bf16[64,1536]{1,0:T(8,128)(2,1)S(1)}, u32[]{:S(2)}, u32[]{:S(2)}) %collective-permute-start.41) | collective-permute-done | bytes 196640 | tf_op jit(solution)/shard_map/swap_ctx_2/ppermute | solution.py:111
  110.3 1.8 %shard_map.300 = (f32[256,512]{1,0:T(8,128)}, f32[256,512]{1,0:T(8,128)}, f32[3,256,128]{2,1,0:T(8,128)}, f32[256,128]{1,0:T(8,128)}) custom-call(bf16[64,1536]{1,0:T(8,128)(2,1)S(1)} %get-tuple-element.427.refs_0_, bf16[64,1536]{1,0:T(8,128)(2,1)S(1)} %collective-permute-done.40.refs_1_, bf16[64,1536]{1,0:T(8,128)(2,1)S(1)} %collective-permute-done.41.refs_2_, ...), custom_call_target="tpu_custom_call" | custom-call | flops 1000 | bytes 65536 | tf_op jit(solution)/shard_map/pallas_call | solution.py:89
  112.1 0.7 collective-permute-done.38.refs_3_
  112.9 2.6 %shard_map.301 = (f32[512,512]{1,0:T(8,128)}, f32[512,512]{1,0:T(8,128)}, f32[1000,512]{1,0:T(8,128)}, f32[1,512]{1,0:T(1,128)}, f32[2,128]{1,0:T(2,128)}, /*ind...) custom-call(s32[4]{0:T(128)S(1)} %broadcast_select_fusion.refs_0_, ...), custom_call_target="tpu_custom_call", output_to_operand_aliasing={{2}: (6, {})} | custom-call | flops 1000 | bytes 65536 | tf_op jit(solution)/shard_map/pallas_call | solution.py:89
  (51 shorter events, 6.5 us)
Async XLA Ops:
  2.5 4.2 %collective-permute-start = (bf16[272,512]{1,0:T(8,128)(2,1)S(1)}, bf16[272,512]{1,0:T(8,128)(2,1)S(1)}, u32[]{:S(2)}, u32[]{:S(2)}) collective-permute-start(bf16[272,512]{1,0:T(8,128)(2,1)S(1)} %get-tuple-element.233.refs_10_.refs_12_.refs_7_.refs_5_.refs_18_), channel_id=1, source_target_pairs={{0,16},{16,0},{1,17},{17,1},{2,18},{18,2},{3,19},{19,3},{4,20},{20... | collective-permute-start | bytes 835592 | tf_op jit(solution)/shard_map/swap_fsdp_1/ppermute | solution.py:111
  3.1 15.1 %collective-permute-start.1 = (bf16[272,384]{1,0:T(8,128)(2,1)S(1)}, bf16[272,384]{1,0:T(8,128)(2,1)S(1)}, u32[]{:S(2)}, u32[]{:S(2)}) collective-permute-start(bf16[272,384]{1,0:T(8,128)(2,1)S(1)} %get-tuple-element.240), channel_id=1, source_target_pairs={{0,2},{1,3},{2,0},{3,1},{4,6},{5,7},{6,4},{7,5},{8,10},{9,11},{10,... | collective-permute-start | bytes 626696 | tf_op jit(solution)/shard_map/swap_tp_2/ppermute | solution.py:111
  9.1 9.0 %collective-permute-start.4 = (bf16[256,256]{1,0:T(8,128)(2,1)S(1)}, bf16[256,256]{1,0:T(8,128)(2,1)S(1)}, u32[]{:S(2)}, u32[]{:S(2)}) collective-permute-start(bf16[256,256]{1,0:T(8,128)(2,1)S(1)} %get-tuple-element.248.refs_2_.refs_3_), channel_id=1, source_target_pairs={{0,12},{4,8},{8,4},{12,0},{1,13},{5,9},{9,5},{13,1},{2,14},{6,10},... | collective-permute-start | bytes 393224 | tf_op jit(solution)/shard_map/swap_ctx_3/ppermute | solution.py:111
  11.6 6.8 %collective-permute-start.3 = (bf16[256,256]{1,0:T(8,128)(2,1)S(1)}, bf16[256,256]{1,0:T(8,128)(2,1)S(1)}, u32[]{:S(2)}, u32[]{:S(2)}) collective-permute-start(bf16[256,256]{1,0:T(8,128)(2,1)S(1)} %get-tuple-element.248.refs_2_.refs_3_), channel_id=1, source_target_pairs={{0,8},{4,12},{8,0},{12,4},{1,9},{5,13},{9,1},{13,5},{2,10},{6,14},... | collective-permute-start | bytes 393224 | tf_op jit(solution)/shard_map/swap_ctx_2/ppermute | solution.py:111
  12.1 6.4 %collective-permute-start.2 = (bf16[256,256]{1,0:T(8,128)(2,1)S(1)}, bf16[256,256]{1,0:T(8,128)(2,1)S(1)}, u32[]{:S(2)}, u32[]{:S(2)}) collective-permute-start(bf16[256,256]{1,0:T(8,128)(2,1)S(1)} %get-tuple-element.248.refs_2_.refs_3_), channel_id=1, source_target_pairs={{0,4},{4,0},{8,12},{12,8},{1,5},{5,1},{9,13},{13,9},{2,6},{6,2},{1... | collective-permute-start | bytes 393224 | tf_op jit(solution)/shard_map/swap_ctx_1/ppermute | solution.py:111
  16.6 11.3 %collective-permute-start.9 = (bf16[96,1024]{1,0:T(8,128)(2,1)S(1)}, bf16[96,1024]{1,0:T(8,128)(2,1)S(1)}, u32[]{:S(2)}, u32[]{:S(2)}) collective-permute-start(bf16[96,1024]{1,0:T(8,128)(2,1)S(1)} %get-tuple-element.277), channel_id=1, source_target_pairs={{0,2},{1,3},{2,0},{3,1},{4,6},{5,7},{6,4},{7,5},{8,10},{9,11},{10,... | collective-permute-start | bytes 589832 | tf_op jit(solution)/shard_map/swap_tp_2/ppermute | solution.py:111
  18.5 1.9 %collective-permute-start.5 = (bf16[272,384]{1,0:T(8,128)(2,1)S(1)}, bf16[272,384]{1,0:T(8,128)(2,1)S(1)}, u32[]{:S(2)}, u32[]{:S(2)}) collective-permute-start(bf16[272,384]{1,0:T(8,128)(2,1)S(1)} %collective-permute-done.1.refs_1_.refs_3_.refs_6_.refs_12_), channel_id=1, source_target_pairs={{0,16},{16,0},{1,17},{17,1},{2,18},{18,2},{3,19},{19,3},{4,20},{20... | collective-permute-start | bytes 626696 | tf_op jit(solution)/shard_map/swap_fsdp_1/ppermute | solution.py:111
  21.3 8.8 %collective-permute-start.8 = (bf16[256,256]{1,0:T(8,128)(2,1)S(1)}, bf16[256,256]{1,0:T(8,128)(2,1)S(1)}, u32[]{:S(2)}, u32[]{:S(2)}) collective-permute-start(bf16[256,256]{1,0:T(8,128)(2,1)S(1)} %get-tuple-element.275.refs_2_.refs_9_), channel_id=1, source_target_pairs={{0,12},{4,8},{8,4},{12,0},{1,13},{5,9},{9,5},{13,1},{2,14},{6,10},... | collective-permute-start | bytes 393224 | tf_op jit(solution)/shard_map/swap_ctx_3/ppermute | solution.py:111
  23.5 7.5 %collective-permute-start.7 = (bf16[256,256]{1,0:T(8,128)(2,1)S(1)}, bf16[256,256]{1,0:T(8,128)(2,1)S(1)}, u32[]{:S(2)}, u32[]{:S(2)}) collective-permute-start(bf16[256,256]{1,0:T(8,128)(2,1)S(1)} %get-tuple-element.275.refs_2_.refs_9_), channel_id=1, source_target_pairs={{0,8},{4,12},{8,0},{12,4},{1,9},{5,13},{9,1},{13,5},{2,10},{6,14},... | collective-permute-start | bytes 393224 | tf_op jit(solution)/shard_map/swap_ctx_2/ppermute | solution.py:111
  24.4 6.7 %collective-permute-start.6 = (bf16[256,256]{1,0:T(8,128)(2,1)S(1)}, bf16[256,256]{1,0:T(8,128)(2,1)S(1)}, u32[]{:S(2)}, u32[]{:S(2)}) collective-permute-start(bf16[256,256]{1,0:T(8,128)(2,1)S(1)} %get-tuple-element.275.refs_2_.refs_9_), channel_id=1, source_target_pairs={{0,4},{4,0},{8,12},{12,8},{1,5},{5,1},{9,13},{13,9},{2,6},{6,2},{1... | collective-permute-start | bytes 393224 | tf_op jit(solution)/shard_map/swap_ctx_1/ppermute | solution.py:111
  28.5 1.6 %collective-permute-start.10 = (bf16[256,128]{1,0:T(8,128)(2,1)S(1)}, bf16[256,128]{1,0:T(8,128)(2,1)S(1)}, u32[]{:S(2)}, u32[]{:S(2)}) collective-permute-start(bf16[256,128]{1,0:T(8,128)(2,1)S(1)} %get-tuple-element.282.refs_9_.refs_20_), channel_id=1, source_target_pairs={{0,16},{16,0},{1,17},{17,1},{2,18},{18,2},{3,19},{19,3},{4,20},{20... | collective-permute-start | bytes 196616 | tf_op jit(solution)/shard_map/swap_fsdp_1/ppermute | solution.py:111
  28.5 5.0 %collective-permute-start.13 = (bf16[64,1024]{1,0:T(8,128)(2,1)S(1)}, bf16[64,1024]{1,0:T(8,128)(2,1)S(1)}, u32[]{:S(2)}, u32[]{:S(2)}) collective-permute-start(bf16[64,1024]{1,0:T(8,128)(2,1)S(1)} %get-tuple-element.292.refs_0_), channel_id=1, source_target_pairs={{0,4},{4,0},{8,12},{12,8},{16,24},{20,28},{24,16},{28,20},{1,5},{5... | collective-permute-start | bytes 393224 | tf_op jit(solution)/shard_map/swap_turn_0/ppermute | solution.py:126
  34.1 6.4 %collective-permute-start.14 = (bf16[128,1024]{1,0:T(8,128)(2,1)S(1)}, bf16[128,1024]{1,0:T(8,128)(2,1)S(1)}, u32[]{:S(2)}, u32[]{:S(2)}) collective-permute-start(bf16[128,1024]{1,0:T(8,128)(2,1)S(1)} %shard_map.288.refs_9_), channel_id=1, source_target_pairs={{0,8},{4,12},{8,0},{12,4},{16,20},{20,16},{24,28},{28,24},{1,9},{5... | collective-permute-start | bytes 786440 | tf_op jit(solution)/shard_map/swap_turn_1/ppermute | solution.py:126
  35.7 4.9 %collective-permute-start.12 = (bf16[256,1024]{1,0:T(8,128)(2,1)S(1)}, bf16[256,1024]{1,0:T(8,128)(2,1)S(1)}, u32[]{:S(2)}, u32[]{:S(2)}) collective-permute-start(bf16[256,1024]{1,0:T(8,128)(2,1)S(1)} %get-tuple-element.290.refs_7_), channel_id=1, source_target_pairs={{0,16},{16,0},{1,17},{17,1},{2,18},{18,2},{3,19},{19,3},{4,20},{20... | collective-permute-start | bytes 1572872 | tf_op jit(solution)/shard_map/swap_fsdp_1/ppermute | solution.py:111
  35.7 4.9 %collective-permute-start.15 = (bf16[128,1024]{1,0:T(8,128)(2,1)S(1)}, bf16[128,1024]{1,0:T(8,128)(2,1)S(1)}, u32[]{:S(2)}, u32[]{:S(2)}) collective-permute-start(bf16[128,1024]{1,0:T(8,128)(2,1)S(1)} %shard_map.288.refs_9_), channel_id=1, source_target_pairs={{0,16},{16,0},{1,17},{17,1},{2,18},{18,2},{3,19},{19,3},{4,20},{20... | collective-permute-start | bytes 786440 | tf_op jit(solution)/shard_map/swap_fsdp_1/ppermute | solution.py:111
  36.2 8.2 %collective-permute-start.11 = (bf16[256,512]{1,0:T(8,128)(2,1)S(1)}, bf16[256,512]{1,0:T(8,128)(2,1)S(1)}, u32[]{:S(2)}, u32[]{:S(2)}) collective-permute-start(bf16[256,512]{1,0:T(8,128)(2,1)S(1)} %get-tuple-element.287.refs_1_), channel_id=1, source_target_pairs={{0,1},{1,0},{2,3},{3,2},{4,5},{5,4},{6,7},{7,6},{8,9},{9,8},{10,11... | collective-permute-start | bytes 786440 | tf_op jit(solution)/shard_map/swap_tp_1/ppermute | solution.py:111
  40.6 3.9 %collective-permute-start.16 = (bf16[128,1024]{1,0:T(8,128)(2,1)S(1)}, bf16[128,1024]{1,0:T(8,128)(2,1)S(1)}, u32[]{:S(2)}, u32[]{:S(2)}) collective-permute-start(bf16[128,1024]{1,0:T(8,128)(2,1)S(1)} %collective-permute-done.14.refs_10_), channel_id=1, source_target_pairs={{0,16},{16,0},{1,17},{17,1},{2,18},{18,2},{3,19},{19,3},{4,20},{20... | collective-permute-start | bytes 786440 | tf_op jit(solution)/shard_map/swap_fsdp_1/ppermute | solution.py:111
  47.2 7.8 %collective-permute-start.22 = (bf16[272,512]{1,0:T(8,128)(2,1)S(1)}, bf16[272,512]{1,0:T(8,128)(2,1)S(1)}, u32[]{:S(2)}, u32[]{:S(2)}) collective-permute-start(bf16[272,512]{1,0:T(8,128)(2,1)S(1)} %get-tuple-element.334.refs_13_), channel_id=1, source_target_pairs={{0,1},{1,0},{2,3},{3,2},{4,5},{5,4},{6,7},{7,6},{8,9},{9,8},{10,11... | collective-permute-start | bytes 835592 | tf_op jit(solution)/shard_map/swap_tp_1/ppermute | solution.py:111
  49.7 1.6 %collective-permute-start.20 = (bf16[256,512]{1,0:T(8,128)(2,1)S(1)}, bf16[256,512]{1,0:T(8,128)(2,1)S(1)}, u32[]{:S(2)}, u32[]{:S(2)}) collective-permute-start(bf16[256,512]{1,0:T(8,128)(2,1)S(1)} %get-tuple-element.322), channel_id=1, source_target_pairs={{0,16},{16,0},{1,17},{17,1},{2,18},{18,2},{3,19},{19,3},{4,20},{20... | collective-permute-start | bytes 786440 | tf_op jit(solution)/shard_map/swap_fsdp_1/ppermute | solution.py:111
  49.8 1.9 %collective-permute-start.19 = (bf16[256,512]{1,0:T(8,128)(2,1)S(1)}, bf16[256,512]{1,0:T(8,128)(2,1)S(1)}, u32[]{:S(2)}, u32[]{:S(2)}) collective-permute-start(bf16[256,512]{1,0:T(8,128)(2,1)S(1)} %get-tuple-element.319), channel_id=1, source_target_pairs={{0,16},{16,0},{1,17},{17,1},{2,18},{18,2},{3,19},{19,3},{4,20},{20... | collective-permute-start | bytes 786440 | tf_op jit(solution)/shard_map/swap_fsdp_1/ppermute | solution.py:111
  50.3 1.8 %collective-permute-start.18 = (bf16[256,512]{1,0:T(8,128)(2,1)S(1)}, bf16[256,512]{1,0:T(8,128)(2,1)S(1)}, u32[]{:S(2)}, u32[]{:S(2)}) collective-permute-start(bf16[256,512]{1,0:T(8,128)(2,1)S(1)} %get-tuple-element.316), channel_id=1, source_target_pairs={{0,16},{16,0},{1,17},{17,1},{2,18},{18,2},{3,19},{19,3},{4,20},{20... | collective-permute-start | bytes 786440 | tf_op jit(solution)/shard_map/swap_fsdp_1/ppermute | solution.py:111
  50.3 2.1 %collective-permute-start.17 = (bf16[256,512]{1,0:T(8,128)(2,1)S(1)}, bf16[256,512]{1,0:T(8,128)(2,1)S(1)}, u32[]{:S(2)}, u32[]{:S(2)}) collective-permute-start(bf16[256,512]{1,0:T(8,128)(2,1)S(1)} %get-tuple-element.313), channel_id=1, source_target_pairs={{0,16},{16,0},{1,17},{17,1},{2,18},{18,2},{3,19},{19,3},{4,20},{20... | collective-permute-start | bytes 786440 | tf_op jit(solution)/shard_map/swap_fsdp_1/ppermute | solution.py:111
  53.1 16.9 %collective-permute-start.21 = (bf16[128,2048]{1,0:T(8,128)(2,1)S(1)}, bf16[128,2048]{1,0:T(8,128)(2,1)S(1)}, u32[]{:S(2)}, u32[]{:S(2)}) collective-permute-start(bf16[128,2048]{1,0:T(8,128)(2,1)S(1)} %get-tuple-element.328), channel_id=1, source_target_pairs={{0,4},{4,0},{8,12},{12,8},{16,24},{20,28},{24,16},{28,20},{1,5},{5... | collective-permute-start | bytes 1572872 | tf_op jit(solution)/shard_map/swap_turn_0/ppermute | solution.py:126
  60.1 12.5 %collective-permute-start.27 = (bf16[272,512]{1,0:T(8,128)(2,1)S(1)}, bf16[272,512]{1,0:T(8,128)(2,1)S(1)}, u32[]{:S(2)}, u32[]{:S(2)}) collective-permute-start(bf16[272,512]{1,0:T(8,128)(2,1)S(1)} %get-tuple-element.360), channel_id=1, source_target_pairs={{0,12},{4,8},{8,4},{12,0},{1,13},{5,9},{9,5},{13,1},{2,14},{6,10},... | collective-permute-start | bytes 835592 | tf_op jit(solution)/shard_map/swap_ctx_3/ppermute | solution.py:111
  61.6 12.7 %collective-permute-start.26 = (bf16[272,512]{1,0:T(8,128)(2,1)S(1)}, bf16[272,512]{1,0:T(8,128)(2,1)S(1)}, u32[]{:S(2)}, u32[]{:S(2)}) collective-permute-start(bf16[272,512]{1,0:T(8,128)(2,1)S(1)} %get-tuple-element.359), channel_id=1, source_target_pairs={{0,8},{4,12},{8,0},{12,4},{1,9},{5,13},{9,1},{13,5},{2,10},{6,14},... | collective-permute-start | bytes 835592 | tf_op jit(solution)/shard_map/swap_ctx_2/ppermute | solution.py:111
  63.1 11.2 %collective-permute-start.25 = (bf16[272,512]{1,0:T(8,128)(2,1)S(1)}, bf16[272,512]{1,0:T(8,128)(2,1)S(1)}, u32[]{:S(2)}, u32[]{:S(2)}) collective-permute-start(bf16[272,512]{1,0:T(8,128)(2,1)S(1)} %get-tuple-element.358), channel_id=1, source_target_pairs={{0,4},{4,0},{8,12},{12,8},{1,5},{5,1},{9,13},{13,9},{2,6},{6,2},{1... | collective-permute-start | bytes 835592 | tf_op jit(solution)/shard_map/swap_ctx_1/ppermute | solution.py:111
  63.7 6.4 %collective-permute-start.23 = (bf16[256,512]{1,0:T(8,128)(2,1)S(1)}, bf16[256,512]{1,0:T(8,128)(2,1)S(1)}, u32[]{:S(2)}, u32[]{:S(2)}) collective-permute-start(bf16[256,512]{1,0:T(8,128)(2,1)S(1)} %get-tuple-element.345.refs_3_), channel_id=1, source_target_pairs={{0,1},{1,0},{2,3},{3,2},{4,5},{5,4},{6,7},{7,6},{8,9},{9,8},{10,11... | collective-permute-start | bytes 786440 | tf_op jit(solution)/shard_map/swap_tp_1/ppermute | solution.py:111
  70.9 17.5 %collective-permute-start.24 = (bf16[384,512]{1,0:T(8,128)(2,1)S(1)}, bf16[384,512]{1,0:T(8,128)(2,1)S(1)}, u32[]{:S(2)}, u32[]{:S(2)}) collective-permute-start(bf16[384,512]{1,0:T(8,128)(2,1)S(1)} %get-tuple-element.352), channel_id=1, source_target_pairs={{0,2},{1,3},{2,0},{3,1},{4,6},{5,7},{6,4},{7,5},{8,10},{9,11},{10,... | collective-permute-start | bytes 1179656 | tf_op jit(solution)/shard_map/swap_tp_2/ppermute | solution.py:111
  76.1 2.0 %collective-permute-start.29 = (bf16[272,384]{1,0:T(8,128)(2,1)S(1)}, bf16[272,384]{1,0:T(8,128)(2,1)S(1)}, u32[]{:S(2)}, u32[]{:S(2)}) collective-permute-start(bf16[272,384]{1,0:T(8,128)(2,1)S(1)} %get-tuple-element.371), channel_id=1, source_target_pairs={{0,16},{16,0},{1,17},{17,1},{2,18},{18,2},{3,19},{19,3},{4,20},{20... | collective-permute-start | bytes 626696 | tf_op jit(solution)/shard_map/swap_fsdp_1/ppermute | solution.py:111
  76.1 1.9 %collective-permute-start.28 = (bf16[272,384]{1,0:T(8,128)(2,1)S(1)}, bf16[272,384]{1,0:T(8,128)(2,1)S(1)}, u32[]{:S(2)}, u32[]{:S(2)}) collective-permute-start(bf16[272,384]{1,0:T(8,128)(2,1)S(1)} %get-tuple-element.368), channel_id=1, source_target_pairs={{0,16},{16,0},{1,17},{17,1},{2,18},{18,2},{3,19},{19,3},{4,20},{20... | collective-permute-start | bytes 626696 | tf_op jit(solution)/shard_map/swap_fsdp_1/ppermute | solution.py:111
  76.6 1.4 %collective-permute-start.30 = (bf16[272,256]{1,0:T(8,128)(2,1)S(1)}, bf16[272,256]{1,0:T(8,128)(2,1)S(1)}, u32[]{:S(2)}, u32[]{:S(2)}) collective-permute-start(bf16[272,256]{1,0:T(8,128)(2,1)S(1)} %get-tuple-element.374), channel_id=1, source_target_pairs={{0,16},{16,0},{1,17},{17,1},{2,18},{18,2},{3,19},{19,3},{4,20},{20... | collective-permute-start | bytes 417800 | tf_op jit(solution)/shard_map/swap_fsdp_1/ppermute | solution.py:111
  78.8 25.9 %copy-start = (s32[2]{0:T(128)S(1)}, s32[2]{0:T(128)}, u32[]{:S(2)}) copy-start(s32[2]{0:T(128)} %refs_0_.3) | copy-start | bytes 28
  78.8 10.3 %collective-permute-start.35 = (bf16[80,1024]{1,0:T(8,128)(2,1)S(1)}, bf16[80,1024]{1,0:T(8,128)(2,1)S(1)}, u32[]{:S(2)}, u32[]{:S(2)}) collective-permute-start(bf16[80,1024]{1,0:T(8,128)(2,1)S(1)} %get-tuple-element.398), channel_id=1, source_target_pairs={{0,12},{4,8},{8,4},{12,0},{1,13},{5,9},{9,5},{13,1},{2,14},{6,10},... | collective-permute-start | bytes 491528 | tf_op jit(solution)/shard_map/swap_ctx_3/ppermute | solution.py:111
  80.5 9.0 %collective-permute-start.34 = (bf16[80,1024]{1,0:T(8,128)(2,1)S(1)}, bf16[80,1024]{1,0:T(8,128)(2,1)S(1)}, u32[]{:S(2)}, u32[]{:S(2)}) collective-permute-start(bf16[80,1024]{1,0:T(8,128)(2,1)S(1)} %get-tuple-element.397), channel_id=1, source_target_pairs={{0,8},{4,12},{8,0},{12,4},{1,9},{5,13},{9,1},{13,5},{2,10},{6,14},... | collective-permute-start | bytes 491528 | tf_op jit(solution)/shard_map/swap_ctx_2/ppermute | solution.py:111
  81.8 7.8 %collective-permute-start.33 = (bf16[80,1024]{1,0:T(8,128)(2,1)S(1)}, bf16[80,1024]{1,0:T(8,128)(2,1)S(1)}, u32[]{:S(2)}, u32[]{:S(2)}) collective-permute-start(bf16[80,1024]{1,0:T(8,128)(2,1)S(1)} %get-tuple-element.396), channel_id=1, source_target_pairs={{0,4},{4,0},{8,12},{12,8},{1,5},{5,1},{9,13},{13,9},{2,6},{6,2},{1... | collective-permute-start | bytes 491528 | tf_op jit(solution)/shard_map/swap_ctx_1/ppermute | solution.py:111
  82.3 12.2 %collective-permute-start.36 = (bf16[256,512]{1,0:T(8,128)(2,1)S(1)}, bf16[256,512]{1,0:T(8,128)(2,1)S(1)}, u32[]{:S(2)}, u32[]{:S(2)}) collective-permute-start(bf16[256,512]{1,0:T(8,128)(2,1)S(1)} %get-tuple-element.405.refs_1_), channel_id=1, source_target_pairs={{0,1},{1,0},{2,3},{3,2},{4,5},{5,4},{6,7},{7,6},{8,9},{9,8},{10,11... | collective-permute-start | bytes 786440 | tf_op jit(solution)/shard_map/swap_tp_1/ppermute | solution.py:111
  90.2 7.8 %collective-permute-start.37 = (bf16[96,512]{1,0:T(8,128)(2,1)S(1)}, bf16[96,512]{1,0:T(8,128)(2,1)S(1)}, u32[]{:S(2)}, u32[]{:S(2)}) collective-permute-start(bf16[96,512]{1,0:T(8,128)(2,1)S(1)} %get-tuple-element.409.refs_4_), channel_id=1, source_target_pairs={{0,2},{1,3},{2,0},{3,1},{4,6},{5,7},{6,4},{7,5},{8,10},{9,11},{10,... | collective-permute-start | bytes 294920 | tf_op jit(solution)/shard_map/swap_tp_2/ppermute | solution.py:111
  92.2 5.8 %collective-permute-start.32 = (bf16[64,512]{1,0:T(8,128)(2,1)S(1)}, bf16[64,512]{1,0:T(8,128)(2,1)S(1)}, u32[]{:S(2)}, u32[]{:S(2)}) collective-permute-start(bf16[64,512]{1,0:T(8,128)(2,1)S(1)} %get-tuple-element.394), channel_id=1, source_target_pairs={{0,8},{4,12},{8,0},{12,4},{16,20},{20,16},{24,28},{28,24},{1,9},{5... | collective-permute-start | bytes 196616 | tf_op jit(solution)/shard_map/swap_turn_1/ppermute | solution.py:126
  93.4 4.6 %collective-permute-start.31 = (bf16[64,512]{1,0:T(8,128)(2,1)S(1)}, bf16[64,512]{1,0:T(8,128)(2,1)S(1)}, u32[]{:S(2)}, u32[]{:S(2)}) collective-permute-start(bf16[64,512]{1,0:T(8,128)(2,1)S(1)} %get-tuple-element.391), channel_id=1, source_target_pairs={{0,8},{4,12},{8,0},{12,4},{16,20},{20,16},{24,28},{28,24},{1,9},{5... | collective-permute-start | bytes 196616 | tf_op jit(solution)/shard_map/swap_turn_1/ppermute | solution.py:126
  98.0 14.9 %collective-permute-start.39 = (bf16[256,512]{1,0:T(8,128)(2,1)S(1)}, bf16[256,512]{1,0:T(8,128)(2,1)S(1)}, u32[]{:S(2)}, u32[]{:S(2)}) collective-permute-start(bf16[256,512]{1,0:T(8,128)(2,1)S(1)} %shard_map.298.refs_4_), channel_id=1, source_target_pairs={{0,2},{1,3},{2,0},{3,1},{4,6},{5,7},{6,4},{7,5},{8,10},{9,11},{10,... | collective-permute-start | bytes 786440 | tf_op jit(solution)/shard_map/swap_tp_2/ppermute | solution.py:111
  98.6 8.8 %collective-permute-start.42 = (bf16[64,1536]{1,0:T(8,128)(2,1)S(1)}, bf16[64,1536]{1,0:T(8,128)(2,1)S(1)}, u32[]{:S(2)}, u32[]{:S(2)}) collective-permute-start(bf16[64,1536]{1,0:T(8,128)(2,1)S(1)} %get-tuple-element.427.refs_0_), channel_id=1, source_target_pairs={{0,12},{4,8},{8,4},{12,0},{1,13},{5,9},{9,5},{13,1},{2,14},{6,10},... | collective-permute-start | bytes 589832 | tf_op jit(solution)/shard_map/swap_ctx_3/ppermute | solution.py:111
  100.4 9.8 %collective-permute-start.41 = (bf16[64,1536]{1,0:T(8,128)(2,1)S(1)}, bf16[64,1536]{1,0:T(8,128)(2,1)S(1)}, u32[]{:S(2)}, u32[]{:S(2)}) collective-permute-start(bf16[64,1536]{1,0:T(8,128)(2,1)S(1)} %get-tuple-element.427.refs_0_), channel_id=1, source_target_pairs={{0,8},{4,12},{8,0},{12,4},{1,9},{5,13},{9,1},{13,5},{2,10},{6,14},... | collective-permute-start | bytes 589832 | tf_op jit(solution)/shard_map/swap_ctx_2/ppermute | solution.py:111
  101.7 8.7 %collective-permute-start.40 = (bf16[64,1536]{1,0:T(8,128)(2,1)S(1)}, bf16[64,1536]{1,0:T(8,128)(2,1)S(1)}, u32[]{:S(2)}, u32[]{:S(2)}) collective-permute-start(bf16[64,1536]{1,0:T(8,128)(2,1)S(1)} %get-tuple-element.427.refs_0_), channel_id=1, source_target_pairs={{0,4},{4,0},{8,12},{12,8},{1,5},{5,1},{9,13},{13,9},{2,6},{6,2},{1... | collective-permute-start | bytes 589832 | tf_op jit(solution)/shard_map/swap_ctx_1/ppermute | solution.py:111
  102.2 10.7 %collective-permute-start.38 = (bf16[160,512]{1,0:T(8,128)(2,1)S(1)}, bf16[160,512]{1,0:T(8,128)(2,1)S(1)}, u32[]{:S(2)}, u32[]{:S(2)}) collective-permute-start(bf16[160,512]{1,0:T(8,128)(2,1)S(1)} %get-tuple-element.418.refs_2_), channel_id=1, source_target_pairs={{0,1},{1,0},{2,3},{3,2},{4,5},{5,4},{6,7},{7,6},{8,9},{9,8},{10,11... | collective-permute-start | bytes 491528 | tf_op jit(solution)/shard_map/swap_tp_1/ppermute | solution.py:111

commit v7 on v6

--- a/solution.py
+++ b/solution.py
@@ -464,9 +464,8 @@
     rows_ref[...] = jnp.concatenate([column_sum(v) for v in sums], axis=0)
 
 
-def attend_backward(spot_ref, seg_ref, q_ref, grad, lse_ref, kvs, dq_ref, outs, side):
+def attend_backward(biases, q_ref, grad, lse_ref, kvs, dq_ref, outs, side):
     span, width = q_ref.shape
-    biases = mask_biases(spot_ref, seg_ref, span)
     query = q_ref[...]
     dq, dks, dvs = None, [None] * 4, [None] * 4
     for head in range(width // HEAD_DIM):
@@ -507,13 +506,14 @@
     )
     one, two = halves(spot_ref, size)
     outs = (own_ref, out1, out2, out3)
+    biases = mask_biases(spot_ref, seg_ref, q_n.shape[0])
     near = (q_n, lse_n, (n0, n1, n2, n3), one_n, two_n)
     far = (q_f, lse_f, (f0, f1, f2, f3), one_f, two_f)
     for side, (q_ref, lse_ref, kvs, first, second) in enumerate((near, far)):
         grad = dot_nn(low_ref[:, one], out_part(first, size))
         grad = grad + dot_nn(low_ref[:, two], out_part(second, size))
         attend_backward(
-            spot_ref, seg_ref, q_ref, grad.astype(BF16), lse_ref, kvs, dq_ref, outs, side
+            biases, q_ref, grad.astype(BF16), lse_ref, kvs, dq_ref, outs, side
         )
     for out_ref in (out1, out2, out3):
         clear_below(out_ref, q_n.shape[0])

time: 116 us -> 116 us (level)
  no operation moved by 1% of the time
where the time goes in v7:
time: 116 us
  starting transfers between devices  42.9 us (37%)
  waiting for transfers between devices  37.4 us (32%)
  Pallas kernels  34 us (29%)
    ppermute x38, starting transfers between devices, swap(): return lax.ppermute(values, axis, [(i, i ^ bits) for i in range(size)])  36.5 us
    pallas_call x22, Pallas kernels, call(): pl.pallas_call(body, out_shape=tuple((jax.ShapeDtypeStruct(shape, dtype)...  34 us
    ppermute x38, waiting for transfers between devices, swap(): return lax.ppermute(values, axis, [(i, i ^ bits) for i in range(size)])  33.9 us
    ppermute x5, starting transfers between devices, swap_turn(): return lax.ppermute(values, ('fsdp', 'ctx'), pairs)  6.47 us
    ppermute x5, waiting for transfers between devices, swap_turn(): return lax.ppermute(values, ('fsdp', 'ctx'), pairs)  3.56 us
  transfers between devices with their start and end apart: 43, of which 23 were waited for; matrix products, arithmetic and copies ran while one was open for 0% of the time, Pallas kernels for 23%

profile of v7, /device:TPU:0, one launch (start us, length us, event | category | flops | bytes accessed | tf_op | source)
XLA Modules:
  0.0 115.6 jit_solution(2774379662499697123)
XLA Ops:
  0.7 1.8 %shard_map.280 = (bf16[272,512]{1,0:T(8,128)(2,1)S(1)}, bf16[272,384]{1,0:T(8,128)(2,1)S(1)}, bf16[256,128]{1,0:T(8,128)(2,1)S(1)}) custom-call(s32[2]{0:T(128)} %refs_0_.3, f32[3,256,128]{2,1,0:T(8,128)} %refs_1_.3, f32[256,128]{1,0:T(8,128)} %refs_2_.3, f32[2,128]{1,0:T(2,128)} %refs_3_.3, f32[1,512]{1,0:T(1,128)} %bitcast.22, ...), custom_call_target="tpu_custom_call" | custom-call | flops 8000000000 | bytes 65536 | tf_op jit(solution)/shard_map/pallas_call | solution.py:89
  3.1 3.7 %collective-permute-start.1 = (bf16[272,384]{1,0:T(8,128)(2,1)S(1)}, bf16[272,384]{1,0:T(8,128)(2,1)S(1)}, u32[]{:S(2)}, u32[]{:S(2)}) collective-permute-start(bf16[272,384]{1,0:T(8,128)(2,1)S(1)} %get-tuple-element.240), channel_id=1, source_target_pairs={{0,2},{1,3},{2,0},{3,1},{4,6},{5,7},{6,4},{7,5},{8,10},{9,11},{10,... | collective-permute-start | bytes 626696 | tf_op jit(solution)/shard_map/swap_tp_2/ppermute | solution.py:111
  6.7 2.4 %shard_map.281 = (bf16[256,128]{1,0:T(8,128)(2,1)S(1)}, bf16[256,256]{1,0:T(8,128)(2,1)S(1)}, f32[256,512]{1,0:T(8,128)S(1)}, bf16[256,512]{1,0:T(8,128)(2,1)S(1...) custom-call(s32[2]{0:T(128)} %refs_0_.3, f32[2,256,512]{2,1,0:T(8,128)} %refs_1_.4, f32[1000,512]{1,0:T(8,128)} %refs_2_.4, ...), custom_call_target="tpu_custom_call" | custom-call | flops 8000000000 | bytes 65536 | tf_op jit(solution)/shard_map/pallas_call | solution.py:89
  9.1 2.5 %collective-permute-start.4 = (bf16[256,256]{1,0:T(8,128)(2,1)S(1)}, bf16[256,256]{1,0:T(8,128)(2,1)S(1)}, u32[]{:S(2)}, u32[]{:S(2)}) collective-permute-start(bf16[256,256]{1,0:T(8,128)(2,1)S(1)} %get-tuple-element.248.refs_2_.refs_3_), channel_id=1, source_target_pairs={{0,12},{4,8},{8,4},{12,0},{1,13},{5,9},{9,5},{13,1},{2,14},{6,10},... | collective-permute-start | bytes 393224 | tf_op jit(solution)/shard_map/swap_ctx_3/ppermute | solution.py:111
  12.1 0.5 collective-permute-start.2
  12.7 2.0 %shard_map.282 = (bf16[256,1024]{1,0:T(8,128)(2,1)S(1)}, bf16[96,1024]{1,0:T(8,128)(2,1)S(1)}, f32[256,512]{1,0:T(8,128)S(1)}) custom-call(bf16[256,128]{1,0:T(8,128)(2,1)S(1)} %get-tuple-element.250.refs_0_, f32[256,512]{1,0:T(8,128)} %refs_1_.5, f32[256,512]{1,0:T(8,128)} %refs_2_.5, f32[2,256,512]{2,1,0:T(8,128)} %refs_3_.5, ...), custom_call_target="tpu_custom_call" | custom-call | flops 1000 | bytes 65536 | tf_op jit(solution)/shard_map/pallas_call | solution.py:89
  14.7 1.9 %shard_map.283.refs_6_ = f32[1000,512]{1,0:T(8,128)} custom-call(s32[4]{0:T(128)S(1)} %pad_add_fusion.refs_5_.refs_13_.refs_4_.refs_0_.refs_6_.refs_1_.refs_11_.refs_2_.refs_22_.refs_18_.refs_3_.refs_7_), custom_call_target="tpu_custom_call" | custom-call | flops 1000 | bytes 65536 | tf_op jit(solution)/shard_map/pallas_call | solution.py:89
  16.6 1.5 %collective-permute-start.9 = (bf16[96,1024]{1,0:T(8,128)(2,1)S(1)}, bf16[96,1024]{1,0:T(8,128)(2,1)S(1)}, u32[]{:S(2)}, u32[]{:S(2)}) collective-permute-start(bf16[96,1024]{1,0:T(8,128)(2,1)S(1)} %get-tuple-element.277), channel_id=1, source_target_pairs={{0,2},{1,3},{2,0},{3,1},{4,6},{5,7},{6,4},{7,5},{8,10},{9,11},{10,... | collective-permute-start | bytes 589832 | tf_op jit(solution)/shard_map/swap_tp_2/ppermute | solution.py:111
  18.5 1.9 %shard_map.284 = (bf16[256,128]{1,0:T(8,128)(2,1)S(1)}, f32[256,128]{1,0:T(8,128)S(1)}) custom-call(s32[1,1024]{1,0:T(1,128)S(1)} %get-tuple-element.238.refs_0_, bf16[256,128]{1,0:T(8,128)(2,1)S(1)} %get-tuple-element.260.refs_1_, bf16[256,256]{1,0:T(8,128)(2,1)S(1)} %get-tuple-element.248.refs_2_.refs_3_, ...), custom_call_target="tpu_custom_call" | custom-call | flops 8000000000 | bytes 65536 | tf_op jit(solution)/shard_map/pallas_call | solution.py:89
  20.5 0.8 shard_map.285
  21.3 2.2 %collective-permute-start.8 = (bf16[256,256]{1,0:T(8,128)(2,1)S(1)}, bf16[256,256]{1,0:T(8,128)(2,1)S(1)}, u32[]{:S(2)}, u32[]{:S(2)}) collective-permute-start(bf16[256,256]{1,0:T(8,128)(2,1)S(1)} %get-tuple-element.275.refs_2_.refs_9_), channel_id=1, source_target_pairs={{0,12},{4,8},{8,4},{12,0},{1,13},{5,9},{9,5},{13,1},{2,14},{6,10},... | collective-permute-start | bytes 393224 | tf_op jit(solution)/shard_map/swap_ctx_3/ppermute | solution.py:111
  23.5 0.8 collective-permute-start.7
  24.4 0.5 collective-permute-start.6
  24.9 3.0 %collective-permute-done.9.refs_0_ = bf16[96,1024]{1,0:T(8,128)(2,1)S(1)} collective-permute-done((bf16[96,1024]{1,0:T(8,128)(2,1)S(1)}, bf16[96,1024]{1,0:T(8,128)(2,1)S(1)}, u32[]{:S(2)}, u32[]{:S(2)}) %collective-permute-start.9) | collective-permute-done | bytes 196640 | tf_op jit(solution)/shard_map/swap_tp_2/ppermute | solution.py:111
  27.9 0.6 shard_map.286
  28.5 1.6 %collective-permute-start.13 = (bf16[64,1024]{1,0:T(8,128)(2,1)S(1)}, bf16[64,1024]{1,0:T(8,128)(2,1)S(1)}, u32[]{:S(2)}, u32[]{:S(2)}) collective-permute-start(bf16[64,1024]{1,0:T(8,128)(2,1)S(1)} %get-tuple-element.292.refs_0_), channel_id=1, source_target_pairs={{0,4},{4,0},{8,12},{12,8},{16,24},{20,28},{24,16},{28,20},{1,5},{5... | collective-permute-start | bytes 393224 | tf_op jit(solution)/shard_map/swap_turn_0/ppermute | solution.py:126
  30.1 0.9 collective-permute-done.7.refs_4_.refs_11_
  31.0 2.2 %shard_map.287 = (bf16[256,128]{1,0:T(8,128)(2,1)S(1)}, f32[256,128]{1,0:T(8,128)S(1)}, bf16[256,512]{1,0:T(8,128)(2,1)S(1)}) custom-call(s32[1,1024]{1,0:T(1,128)S(1)} %get-tuple-element.238.refs_0_, bf16[256,128]{1,0:T(8,128)(2,1)S(1)} %get-tuple-element.268.refs_1_.refs_7_, bf16[256,256]{1,0:T(8,128)(2,1)S(1)} %get-tuple-element.275.refs_2_.refs_9_, ...), custom_call_target="tpu_custom_call" | custom-call | flops 8000000000 | bytes 65536 | tf_op jit(solution)/shard_map/pallas_call | solution.py:89
  33.6 0.6 shard_map.288.refs_9_
  34.1 1.6 %collective-permute-start.14 = (bf16[128,1024]{1,0:T(8,128)(2,1)S(1)}, bf16[128,1024]{1,0:T(8,128)(2,1)S(1)}, u32[]{:S(2)}, u32[]{:S(2)}) collective-permute-start(bf16[128,1024]{1,0:T(8,128)(2,1)S(1)} %shard_map.288.refs_9_), channel_id=1, source_target_pairs={{0,8},{4,12},{8,0},{12,4},{16,20},{20,16},{24,28},{28,24},{1,9},{5... | collective-permute-start | bytes 786440 | tf_op jit(solution)/shard_map/swap_turn_1/ppermute | solution.py:126
  36.2 1.2 %collective-permute-start.11 = (bf16[256,512]{1,0:T(8,128)(2,1)S(1)}, bf16[256,512]{1,0:T(8,128)(2,1)S(1)}, u32[]{:S(2)}, u32[]{:S(2)}) collective-permute-start(bf16[256,512]{1,0:T(8,128)(2,1)S(1)} %get-tuple-element.287.refs_1_), channel_id=1, source_target_pairs={{0,1},{1,0},{2,3},{3,2},{4,5},{5,4},{6,7},{7,6},{8,9},{9,8},{10,11... | collective-permute-start | bytes 786440 | tf_op jit(solution)/shard_map/swap_tp_1/ppermute | solution.py:111
  37.4 3.2 %collective-permute-done.14.refs_10_ = bf16[128,1024]{1,0:T(8,128)(2,1)S(1)} collective-permute-done((bf16[128,1024]{1,0:T(8,128)(2,1)S(1)}, bf16[128,1024]{1,0:T(8,128)(2,1)S(1)}, u32[]{:S(2)}, u32[]{:S(2)}) %collective-permute-start.14) | collective-permute-done | bytes 262176 | tf_op jit(solution)/shard_map/swap_turn_1/ppermute | solution.py:126
  40.6 3.9 %collective-permute-done.11.refs_2_ = bf16[256,512]{1,0:T(8,128)(2,1)S(1)} collective-permute-done((bf16[256,512]{1,0:T(8,128)(2,1)S(1)}, bf16[256,512]{1,0:T(8,128)(2,1)S(1)}, u32[]{:S(2)}, u32[]{:S(2)}) %collective-permute-start.11) | collective-permute-done | bytes 262176 | tf_op jit(solution)/shard_map/swap_tp_1/ppermute | solution.py:111
  44.5 2.7 %shard_map.289 = (bf16[272,512]{1,0:T(8,128)(2,1)S(1)}, bf16[256,512]{1,0:T(8,128)(2,1)S(1)}, f32[256,512]{1,0:T(8,128)S(1)}, f32[256,512]{1,0:T(8,128)S(1)}, bf...) custom-call(f32[256,512]{1,0:T(8,128)S(1)} %get-tuple-element.237.re, ...), custom_call_target="tpu_custom_call" | custom-call | flops 8000000000 | bytes 65536 | tf_op jit(solution)/shard_map/pallas_call | solution.py:89
  47.2 1.2 %collective-permute-start.22 = (bf16[272,512]{1,0:T(8,128)(2,1)S(1)}, bf16[272,512]{1,0:T(8,128)(2,1)S(1)}, u32[]{:S(2)}, u32[]{:S(2)}) collective-permute-start(bf16[272,512]{1,0:T(8,128)(2,1)S(1)} %get-tuple-element.334.refs_13_), channel_id=1, source_target_pairs={{0,1},{1,0},{2,3},{3,2},{4,5},{5,4},{6,7},{7,6},{8,9},{9,8},{10,11... | collective-permute-start | bytes 835592 | tf_op jit(solution)/shard_map/swap_tp_1/ppermute | solution.py:111
  48.4 1.3 %shard_map.290 = (f32[256,2048]{1,0:T(8,128)S(1)}, bf16[256,512]{1,0:T(8,128)(2,1)S(1)}, bf16[256,512]{1,0:T(8,128)(2,1)S(1)}, bf16[256,512]{1,0:T(8,128)(2,1)S(1)}, bf16[256,512]{1,0:T(8,128)(2,1)S(1)}) custom-call(bf16[256,512]{1,0:T(8,128)(2,1)S(1)} %get-tuple-element.301.refs_0_, bf16[256,512]{1,0:T(8,128)(2,1)S(1)} %get-tuple-element.302.refs_1_, ...), custom_call_target="tpu_custom_call" | custom-call | flops 8000000000 | bytes 65536 | tf_op jit(solution)/shard_map/pallas_call | solution.py:89
  52.4 0.7 shard_map.291
  53.1 1.3 %collective-permute-start.21 = (bf16[128,2048]{1,0:T(8,128)(2,1)S(1)}, bf16[128,2048]{1,0:T(8,128)(2,1)S(1)}, u32[]{:S(2)}, u32[]{:S(2)}) collective-permute-start(bf16[128,2048]{1,0:T(8,128)(2,1)S(1)} %get-tuple-element.328), channel_id=1, source_target_pairs={{0,4},{4,0},{8,12},{12,8},{16,24},{20,28},{24,16},{28,20},{1,5},{5... | collective-permute-start | bytes 1572872 | tf_op jit(solution)/shard_map/swap_turn_0/ppermute | solution.py:126
  54.4 0.5 collective-permute-done.22.refs_14_
  55.0 5.1 %shard_map.292 = (f32[256,256]{1,0:T(8,128)S(1)}, f32[256,512]{1,0:T(8,128)S(1)}, bf16[272,512]{1,0:T(8,128)(2,1)S(1)}, bf16[272,512]{1,0:T(8,128)(2,1)S(1)}, bf...) custom-call(s32[1,1024]{1,0:T(1,128)S(1)} %get-tuple-element.238.refs_, ...), custom_call_target="tpu_custom_call" | custom-call | flops 8000000000 | bytes 65536 | tf_op jit(solution)/shard_map/pallas_call | solution.py:89
  60.1 1.5 %collective-permute-start.27 = (bf16[272,512]{1,0:T(8,128)(2,1)S(1)}, bf16[272,512]{1,0:T(8,128)(2,1)S(1)}, u32[]{:S(2)}, u32[]{:S(2)}) collective-permute-start(bf16[272,512]{1,0:T(8,128)(2,1)S(1)} %get-tuple-element.360), channel_id=1, source_target_pairs={{0,12},{4,8},{8,4},{12,0},{1,13},{5,9},{9,5},{13,1},{2,14},{6,10},... | collective-permute-start | bytes 835592 | tf_op jit(solution)/shard_map/swap_ctx_3/ppermute | solution.py:111
  61.6 1.5 %collective-permute-start.26 = (bf16[272,512]{1,0:T(8,128)(2,1)S(1)}, bf16[272,512]{1,0:T(8,128)(2,1)S(1)}, u32[]{:S(2)}, u32[]{:S(2)}) collective-permute-start(bf16[272,512]{1,0:T(8,128)(2,1)S(1)} %get-tuple-element.359), channel_id=1, source_target_pairs={{0,8},{4,12},{8,0},{12,4},{1,9},{5,13},{9,1},{13,5},{2,10},{6,14},... | collective-permute-start | bytes 835592 | tf_op jit(solution)/shard_map/swap_ctx_2/ppermute | solution.py:111
  63.1 0.5 collective-permute-start.25
  63.6 1.2 %collective-permute-start.23 = (bf16[256,512]{1,0:T(8,128)(2,1)S(1)}, bf16[256,512]{1,0:T(8,128)(2,1)S(1)}, u32[]{:S(2)}, u32[]{:S(2)}) collective-permute-start(bf16[256,512]{1,0:T(8,128)(2,1)S(1)} %get-tuple-element.345.refs_3_), channel_id=1, source_target_pairs={{0,1},{1,0},{2,3},{3,2},{4,5},{5,4},{6,7},{7,6},{8,9},{9,8},{10,11... | collective-permute-start | bytes 786440 | tf_op jit(solution)/shard_map/swap_tp_1/ppermute | solution.py:111
  64.8 5.2 %collective-permute-done.23.refs_4_ = bf16[256,512]{1,0:T(8,128)(2,1)S(1)} collective-permute-done((bf16[256,512]{1,0:T(8,128)(2,1)S(1)}, bf16[256,512]{1,0:T(8,128)(2,1)S(1)}, u32[]{:S(2)}, u32[]{:S(2)}) %collective-permute-start.23) | collective-permute-done | bytes 262176 | tf_op jit(solution)/shard_map/swap_tp_1/ppermute | solution.py:111
  70.0 0.9 shard_map.293
  70.9 1.7 %collective-permute-start.24 = (bf16[384,512]{1,0:T(8,128)(2,1)S(1)}, bf16[384,512]{1,0:T(8,128)(2,1)S(1)}, u32[]{:S(2)}, u32[]{:S(2)}) collective-permute-start(bf16[384,512]{1,0:T(8,128)(2,1)S(1)} %get-tuple-element.352), channel_id=1, source_target_pairs={{0,2},{1,3},{2,0},{3,1},{4,6},{5,7},{6,4},{7,5},{8,10},{9,11},{10,... | collective-permute-start | bytes 1179656 | tf_op jit(solution)/shard_map/swap_tp_2/ppermute | solution.py:111
  72.6 1.8 %collective-permute-done.26.refs_8_ = bf16[272,512]{1,0:T(8,128)(2,1)S(1)} collective-permute-done((bf16[272,512]{1,0:T(8,128)(2,1)S(1)}, bf16[272,512]{1,0:T(8,128)(2,1)S(1)}, u32[]{:S(2)}, u32[]{:S(2)}) %collective-permute-start.26) | collective-permute-done | bytes 278560 | tf_op jit(solution)/shard_map/swap_ctx_2/ppermute | solution.py:111
  74.4 1.7 %shard_map.294 = (bf16[256,512]{1,0:T(8,128)(2,1)S(1)}, f32[16,512]{1,0:T(8,128)S(1)}, f32[256,1024]{1,0:T(8,128)S(1)}, bf16[272,384]{1,0:T(8,128)(2,1)S(1)}, bf...) custom-call(f32[256,512]{1,0:T(8,128)S(1)} %get-tuple-element.237.refs_0_, ...), custom_call_target="tpu_custom_call" | custom-call | flops 8000000000 | bytes 65536 | tf_op jit(solution)/shard_map/pallas_call | solution.py:89
  76.7 1.4 %collective-permute-done.30.refs_3_ = bf16[272,256]{1,0:T(8,128)(2,1)S(1)} collective-permute-done((bf16[272,256]{1,0:T(8,128)(2,1)S(1)}, bf16[272,256]{1,0:T(8,128)(2,1)S(1)}, u32[]{:S(2)}, u32[]{:S(2)}) %collective-permute-start.30) | collective-permute-done | bytes 139296 | tf_op jit(solution)/shard_map/swap_fsdp_1/ppermute | solution.py:111
  78.1 0.7 shard_map.295
  78.8 1.7 %collective-permute-start.35 = (bf16[80,1024]{1,0:T(8,128)(2,1)S(1)}, bf16[80,1024]{1,0:T(8,128)(2,1)S(1)}, u32[]{:S(2)}, u32[]{:S(2)}) collective-permute-start(bf16[80,1024]{1,0:T(8,128)(2,1)S(1)} %get-tuple-element.398), channel_id=1, source_target_pairs={{0,12},{4,8},{8,4},{12,0},{1,13},{5,9},{9,5},{13,1},{2,14},{6,10},... | collective-permute-start | bytes 491528 | tf_op jit(solution)/shard_map/swap_ctx_3/ppermute | solution.py:111
  80.5 1.3 %collective-permute-start.34 = (bf16[80,1024]{1,0:T(8,128)(2,1)S(1)}, bf16[80,1024]{1,0:T(8,128)(2,1)S(1)}, u32[]{:S(2)}, u32[]{:S(2)}) collective-permute-start(bf16[80,1024]{1,0:T(8,128)(2,1)S(1)} %get-tuple-element.397), channel_id=1, source_target_pairs={{0,8},{4,12},{8,0},{12,4},{1,9},{5,13},{9,1},{13,5},{2,10},{6,14},... | collective-permute-start | bytes 491528 | tf_op jit(solution)/shard_map/swap_ctx_2/ppermute | solution.py:111
  81.8 0.5 collective-permute-start.33
  82.3 1.0 collective-permute-start.36
  83.4 5.0 %collective-permute-done.24.refs_1_ = bf16[384,512]{1,0:T(8,128)(2,1)S(1)} collective-permute-done((bf16[384,512]{1,0:T(8,128)(2,1)S(1)}, bf16[384,512]{1,0:T(8,128)(2,1)S(1)}, u32[]{:S(2)}, u32[]{:S(2)}) %collective-permute-start.24) | collective-permute-done | bytes 393248 | tf_op jit(solution)/shard_map/swap_tp_2/ppermute | solution.py:111
  88.4 0.6 shard_map.296
  89.0 0.6 collective-permute-done.34.refs_2_
  89.6 0.6 shard_map.297
  90.2 2.0 %collective-permute-start.37 = (bf16[96,512]{1,0:T(8,128)(2,1)S(1)}, bf16[96,512]{1,0:T(8,128)(2,1)S(1)}, u32[]{:S(2)}, u32[]{:S(2)}) collective-permute-start(bf16[96,512]{1,0:T(8,128)(2,1)S(1)} %get-tuple-element.409.refs_4_), channel_id=1, source_target_pairs={{0,2},{1,3},{2,0},{3,1},{4,6},{5,7},{6,4},{7,5},{8,10},{9,11},{10,... | collective-permute-start | bytes 294920 | tf_op jit(solution)/shard_map/swap_tp_2/ppermute | solution.py:111
  92.2 1.2 %collective-permute-start.32 = (bf16[64,512]{1,0:T(8,128)(2,1)S(1)}, bf16[64,512]{1,0:T(8,128)(2,1)S(1)}, u32[]{:S(2)}, u32[]{:S(2)}) collective-permute-start(bf16[64,512]{1,0:T(8,128)(2,1)S(1)} %get-tuple-element.394), channel_id=1, source_target_pairs={{0,8},{4,12},{8,0},{12,4},{16,20},{20,16},{24,28},{28,24},{1,9},{5... | collective-permute-start | bytes 196616 | tf_op jit(solution)/shard_map/swap_turn_1/ppermute | solution.py:126
  93.4 0.8 collective-permute-start.31
  94.5 0.6 shard_map.298.refs_4_
  95.1 2.9 %collective-permute-done.37.refs_5_ = bf16[96,512]{1,0:T(8,128)(2,1)S(1)} collective-permute-done((bf16[96,512]{1,0:T(8,128)(2,1)S(1)}, bf16[96,512]{1,0:T(8,128)(2,1)S(1)}, u32[]{:S(2)}, u32[]{:S(2)}) %collective-permute-start.37) | collective-permute-done | bytes 98336 | tf_op jit(solution)/shard_map/swap_tp_2/ppermute | solution.py:111
  98.0 0.6 shard_map.299
  98.6 1.7 %collective-permute-start.42 = (bf16[64,1536]{1,0:T(8,128)(2,1)S(1)}, bf16[64,1536]{1,0:T(8,128)(2,1)S(1)}, u32[]{:S(2)}, u32[]{:S(2)}) collective-permute-start(bf16[64,1536]{1,0:T(8,128)(2,1)S(1)} %get-tuple-element.427.refs_0_), channel_id=1, source_target_pairs={{0,12},{4,8},{8,4},{12,0},{1,13},{5,9},{9,5},{13,1},{2,14},{6,10},... | collective-permute-start | bytes 589832 | tf_op jit(solution)/shard_map/swap_ctx_3/ppermute | solution.py:111
  100.3 1.3 %collective-permute-start.41 = (bf16[64,1536]{1,0:T(8,128)(2,1)S(1)}, bf16[64,1536]{1,0:T(8,128)(2,1)S(1)}, u32[]{:S(2)}, u32[]{:S(2)}) collective-permute-start(bf16[64,1536]{1,0:T(8,128)(2,1)S(1)} %get-tuple-element.427.refs_0_), channel_id=1, source_target_pairs={{0,8},{4,12},{8,0},{12,4},{1,9},{5,13},{9,1},{13,5},{2,10},{6,14},... | collective-permute-start | bytes 589832 | tf_op jit(solution)/shard_map/swap_ctx_2/ppermute | solution.py:111
  101.7 0.5 collective-permute-start.40
  102.2 2.4 %collective-permute-start.38 = (bf16[160,512]{1,0:T(8,128)(2,1)S(1)}, bf16[160,512]{1,0:T(8,128)(2,1)S(1)}, u32[]{:S(2)}, u32[]{:S(2)}) collective-permute-start(bf16[160,512]{1,0:T(8,128)(2,1)S(1)} %get-tuple-element.418.refs_2_), channel_id=1, source_target_pairs={{0,1},{1,0},{2,3},{3,2},{4,5},{5,4},{6,7},{7,6},{8,9},{9,8},{10,11... | collective-permute-start | bytes 491528 | tf_op jit(solution)/shard_map/swap_tp_1/ppermute | solution.py:111
  104.7 2.8 %collective-permute-done.42.refs_3_ = bf16[64,1536]{1,0:T(8,128)(2,1)S(1)} collective-permute-done((bf16[64,1536]{1,0:T(8,128)(2,1)S(1)}, bf16[64,1536]{1,0:T(8,128)(2,1)S(1)}, u32[]{:S(2)}, u32[]{:S(2)}) %collective-permute-start.42) | collective-permute-done | bytes 196640 | tf_op jit(solution)/shard_map/swap_ctx_3/ppermute | solution.py:111
  107.5 2.7 %collective-permute-done.41.refs_2_ = bf16[64,1536]{1,0:T(8,128)(2,1)S(1)} collective-permute-done((bf16[64,1536]{1,0:T(8,128)(2,1)S(1)}, bf16[64,1536]{1,0:T(8,128)(2,1)S(1)}, u32[]{:S(2)}, u32[]{:S(2)}) %collective-permute-start.41) | collective-permute-done | bytes 196640 | tf_op jit(solution)/shard_map/swap_ctx_2/ppermute | solution.py:111
  110.3 1.8 %shard_map.300 = (f32[256,512]{1,0:T(8,128)}, f32[256,512]{1,0:T(8,128)}, f32[3,256,128]{2,1,0:T(8,128)}, f32[256,128]{1,0:T(8,128)}) custom-call(bf16[64,1536]{1,0:T(8,128)(2,1)S(1)} %get-tuple-element.427.refs_0_, bf16[64,1536]{1,0:T(8,128)(2,1)S(1)} %collective-permute-done.40.refs_1_, bf16[64,1536]{1,0:T(8,128)(2,1)S(1)} %collective-permute-done.41.refs_2_, ...), custom_call_target="tpu_custom_call" | custom-call | flops 1000 | bytes 65536 | tf_op jit(solution)/shard_map/pallas_call | solution.py:89
  112.1 0.7 collective-permute-done.38.refs_3_
  112.8 2.6 %shard_map.301 = (f32[512,512]{1,0:T(8,128)}, f32[512,512]{1,0:T(8,128)}, f32[1000,512]{1,0:T(8,128)}, f32[1,512]{1,0:T(1,128)}, f32[2,128]{1,0:T(2,128)}, /*ind...) custom-call(s32[4]{0:T(128)S(1)} %broadcast_select_fusion.refs_0_, ...), custom_call_target="tpu_custom_call", output_to_operand_aliasing={{2}: (6, {})} | custom-call | flops 1000 | bytes 65536 | tf_op jit(solution)/shard_map/pallas_call | solution.py:89
  (51 shorter events, 6.5 us)
Async XLA Ops:
  2.5 4.2 %collective-permute-start = (bf16[272,512]{1,0:T(8,128)(2,1)S(1)}, bf16[272,512]{1,0:T(8,128)(2,1)S(1)}, u32[]{:S(2)}, u32[]{:S(2)}) collective-permute-start(bf16[272,512]{1,0:T(8,128)(2,1)S(1)} %get-tuple-element.233.refs_10_.refs_12_.refs_7_.refs_5_.refs_18_), channel_id=1, source_target_pairs={{0,16},{16,0},{1,17},{17,1},{2,18},{18,2},{3,19},{19,3},{4,20},{20... | collective-permute-start | bytes 835592 | tf_op jit(solution)/shard_map/swap_fsdp_1/ppermute | solution.py:111
  3.1 15.1 %collective-permute-start.1 = (bf16[272,384]{1,0:T(8,128)(2,1)S(1)}, bf16[272,384]{1,0:T(8,128)(2,1)S(1)}, u32[]{:S(2)}, u32[]{:S(2)}) collective-permute-start(bf16[272,384]{1,0:T(8,128)(2,1)S(1)} %get-tuple-element.240), channel_id=1, source_target_pairs={{0,2},{1,3},{2,0},{3,1},{4,6},{5,7},{6,4},{7,5},{8,10},{9,11},{10,... | collective-permute-start | bytes 626696 | tf_op jit(solution)/shard_map/swap_tp_2/ppermute | solution.py:111
  9.1 9.0 %collective-permute-start.4 = (bf16[256,256]{1,0:T(8,128)(2,1)S(1)}, bf16[256,256]{1,0:T(8,128)(2,1)S(1)}, u32[]{:S(2)}, u32[]{:S(2)}) collective-permute-start(bf16[256,256]{1,0:T(8,128)(2,1)S(1)} %get-tuple-element.248.refs_2_.refs_3_), channel_id=1, source_target_pairs={{0,12},{4,8},{8,4},{12,0},{1,13},{5,9},{9,5},{13,1},{2,14},{6,10},... | collective-permute-start | bytes 393224 | tf_op jit(solution)/shard_map/swap_ctx_3/ppermute | solution.py:111
  11.6 6.8 %collective-permute-start.3 = (bf16[256,256]{1,0:T(8,128)(2,1)S(1)}, bf16[256,256]{1,0:T(8,128)(2,1)S(1)}, u32[]{:S(2)}, u32[]{:S(2)}) collective-permute-start(bf16[256,256]{1,0:T(8,128)(2,1)S(1)} %get-tuple-element.248.refs_2_.refs_3_), channel_id=1, source_target_pairs={{0,8},{4,12},{8,0},{12,4},{1,9},{5,13},{9,1},{13,5},{2,10},{6,14},... | collective-permute-start | bytes 393224 | tf_op jit(solution)/shard_map/swap_ctx_2/ppermute | solution.py:111
  12.1 6.4 %collective-permute-start.2 = (bf16[256,256]{1,0:T(8,128)(2,1)S(1)}, bf16[256,256]{1,0:T(8,128)(2,1)S(1)}, u32[]{:S(2)}, u32[]{:S(2)}) collective-permute-start(bf16[256,256]{1,0:T(8,128)(2,1)S(1)} %get-tuple-element.248.refs_2_.refs_3_), channel_id=1, source_target_pairs={{0,4},{4,0},{8,12},{12,8},{1,5},{5,1},{9,13},{13,9},{2,6},{6,2},{1... | collective-permute-start | bytes 393224 | tf_op jit(solution)/shard_map/swap_ctx_1/ppermute | solution.py:111
  16.6 11.3 %collective-permute-start.9 = (bf16[96,1024]{1,0:T(8,128)(2,1)S(1)}, bf16[96,1024]{1,0:T(8,128)(2,1)S(1)}, u32[]{:S(2)}, u32[]{:S(2)}) collective-permute-start(bf16[96,1024]{1,0:T(8,128)(2,1)S(1)} %get-tuple-element.277), channel_id=1, source_target_pairs={{0,2},{1,3},{2,0},{3,1},{4,6},{5,7},{6,4},{7,5},{8,10},{9,11},{10,... | collective-permute-start | bytes 589832 | tf_op jit(solution)/shard_map/swap_tp_2/ppermute | solution.py:111
  18.5 1.9 %collective-permute-start.5 = (bf16[272,384]{1,0:T(8,128)(2,1)S(1)}, bf16[272,384]{1,0:T(8,128)(2,1)S(1)}, u32[]{:S(2)}, u32[]{:S(2)}) collective-permute-start(bf16[272,384]{1,0:T(8,128)(2,1)S(1)} %collective-permute-done.1.refs_1_.refs_3_.refs_6_.refs_12_), channel_id=1, source_target_pairs={{0,16},{16,0},{1,17},{17,1},{2,18},{18,2},{3,19},{19,3},{4,20},{20... | collective-permute-start | bytes 626696 | tf_op jit(solution)/shard_map/swap_fsdp_1/ppermute | solution.py:111
  21.3 8.8 %collective-permute-start.8 = (bf16[256,256]{1,0:T(8,128)(2,1)S(1)}, bf16[256,256]{1,0:T(8,128)(2,1)S(1)}, u32[]{:S(2)}, u32[]{:S(2)}) collective-permute-start(bf16[256,256]{1,0:T(8,128)(2,1)S(1)} %get-tuple-element.275.refs_2_.refs_9_), channel_id=1, source_target_pairs={{0,12},{4,8},{8,4},{12,0},{1,13},{5,9},{9,5},{13,1},{2,14},{6,10},... | collective-permute-start | bytes 393224 | tf_op jit(solution)/shard_map/swap_ctx_3/ppermute | solution.py:111
  23.5 7.5 %collective-permute-start.7 = (bf16[256,256]{1,0:T(8,128)(2,1)S(1)}, bf16[256,256]{1,0:T(8,128)(2,1)S(1)}, u32[]{:S(2)}, u32[]{:S(2)}) collective-permute-start(bf16[256,256]{1,0:T(8,128)(2,1)S(1)} %get-tuple-element.275.refs_2_.refs_9_), channel_id=1, source_target_pairs={{0,8},{4,12},{8,0},{12,4},{1,9},{5,13},{9,1},{13,5},{2,10},{6,14},... | collective-permute-start | bytes 393224 | tf_op jit(solution)/shard_map/swap_ctx_2/ppermute | solution.py:111
  24.4 6.7 %collective-permute-start.6 = (bf16[256,256]{1,0:T(8,128)(2,1)S(1)}, bf16[256,256]{1,0:T(8,128)(2,1)S(1)}, u32[]{:S(2)}, u32[]{:S(2)}) collective-permute-start(bf16[256,256]{1,0:T(8,128)(2,1)S(1)} %get-tuple-element.275.refs_2_.refs_9_), channel_id=1, source_target_pairs={{0,4},{4,0},{8,12},{12,8},{1,5},{5,1},{9,13},{13,9},{2,6},{6,2},{1... | collective-permute-start | bytes 393224 | tf_op jit(solution)/shard_map/swap_ctx_1/ppermute | solution.py:111
  28.5 1.6 %collective-permute-start.10 = (bf16[256,128]{1,0:T(8,128)(2,1)S(1)}, bf16[256,128]{1,0:T(8,128)(2,1)S(1)}, u32[]{:S(2)}, u32[]{:S(2)}) collective-permute-start(bf16[256,128]{1,0:T(8,128)(2,1)S(1)} %get-tuple-element.282.refs_9_.refs_20_), channel_id=1, source_target_pairs={{0,16},{16,0},{1,17},{17,1},{2,18},{18,2},{3,19},{19,3},{4,20},{20... | collective-permute-start | bytes 196616 | tf_op jit(solution)/shard_map/swap_fsdp_1/ppermute | solution.py:111
  28.5 5.0 %collective-permute-start.13 = (bf16[64,1024]{1,0:T(8,128)(2,1)S(1)}, bf16[64,1024]{1,0:T(8,128)(2,1)S(1)}, u32[]{:S(2)}, u32[]{:S(2)}) collective-permute-start(bf16[64,1024]{1,0:T(8,128)(2,1)S(1)} %get-tuple-element.292.refs_0_), channel_id=1, source_target_pairs={{0,4},{4,0},{8,12},{12,8},{16,24},{20,28},{24,16},{28,20},{1,5},{5... | collective-permute-start | bytes 393224 | tf_op jit(solution)/shard_map/swap_turn_0/ppermute | solution.py:126
  34.1 6.4 %collective-permute-start.14 = (bf16[128,1024]{1,0:T(8,128)(2,1)S(1)}, bf16[128,1024]{1,0:T(8,128)(2,1)S(1)}, u32[]{:S(2)}, u32[]{:S(2)}) collective-permute-start(bf16[128,1024]{1,0:T(8,128)(2,1)S(1)} %shard_map.288.refs_9_), channel_id=1, source_target_pairs={{0,8},{4,12},{8,0},{12,4},{16,20},{20,16},{24,28},{28,24},{1,9},{5... | collective-permute-start | bytes 786440 | tf_op jit(solution)/shard_map/swap_turn_1/ppermute | solution.py:126
  35.7 4.9 %collective-permute-start.12 = (bf16[256,1024]{1,0:T(8,128)(2,1)S(1)}, bf16[256,1024]{1,0:T(8,128)(2,1)S(1)}, u32[]{:S(2)}, u32[]{:S(2)}) collective-permute-start(bf16[256,1024]{1,0:T(8,128)(2,1)S(1)} %get-tuple-element.290.refs_7_), channel_id=1, source_target_pairs={{0,16},{16,0},{1,17},{17,1},{2,18},{18,2},{3,19},{19,3},{4,20},{20... | collective-permute-start | bytes 1572872 | tf_op jit(solution)/shard_map/swap_fsdp_1/ppermute | solution.py:111
  35.7 4.9 %collective-permute-start.15 = (bf16[128,1024]{1,0:T(8,128)(2,1)S(1)}, bf16[128,1024]{1,0:T(8,128)(2,1)S(1)}, u32[]{:S(2)}, u32[]{:S(2)}) collective-permute-start(bf16[128,1024]{1,0:T(8,128)(2,1)S(1)} %shard_map.288.refs_9_), channel_id=1, source_target_pairs={{0,16},{16,0},{1,17},{17,1},{2,18},{18,2},{3,19},{19,3},{4,20},{20... | collective-permute-start | bytes 786440 | tf_op jit(solution)/shard_map/swap_fsdp_1/ppermute | solution.py:111
  36.2 8.2 %collective-permute-start.11 = (bf16[256,512]{1,0:T(8,128)(2,1)S(1)}, bf16[256,512]{1,0:T(8,128)(2,1)S(1)}, u32[]{:S(2)}, u32[]{:S(2)}) collective-permute-start(bf16[256,512]{1,0:T(8,128)(2,1)S(1)} %get-tuple-element.287.refs_1_), channel_id=1, source_target_pairs={{0,1},{1,0},{2,3},{3,2},{4,5},{5,4},{6,7},{7,6},{8,9},{9,8},{10,11... | collective-permute-start | bytes 786440 | tf_op jit(solution)/shard_map/swap_tp_1/ppermute | solution.py:111
  40.6 3.9 %collective-permute-start.16 = (bf16[128,1024]{1,0:T(8,128)(2,1)S(1)}, bf16[128,1024]{1,0:T(8,128)(2,1)S(1)}, u32[]{:S(2)}, u32[]{:S(2)}) collective-permute-start(bf16[128,1024]{1,0:T(8,128)(2,1)S(1)} %collective-permute-done.14.refs_10_), channel_id=1, source_target_pairs={{0,16},{16,0},{1,17},{17,1},{2,18},{18,2},{3,19},{19,3},{4,20},{20... | collective-permute-start | bytes 786440 | tf_op jit(solution)/shard_map/swap_fsdp_1/ppermute | solution.py:111
  47.2 7.8 %collective-permute-start.22 = (bf16[272,512]{1,0:T(8,128)(2,1)S(1)}, bf16[272,512]{1,0:T(8,128)(2,1)S(1)}, u32[]{:S(2)}, u32[]{:S(2)}) collective-permute-start(bf16[272,512]{1,0:T(8,128)(2,1)S(1)} %get-tuple-element.334.refs_13_), channel_id=1, source_target_pairs={{0,1},{1,0},{2,3},{3,2},{4,5},{5,4},{6,7},{7,6},{8,9},{9,8},{10,11... | collective-permute-start | bytes 835592 | tf_op jit(solution)/shard_map/swap_tp_1/ppermute | solution.py:111
  49.7 1.6 %collective-permute-start.20 = (bf16[256,512]{1,0:T(8,128)(2,1)S(1)}, bf16[256,512]{1,0:T(8,128)(2,1)S(1)}, u32[]{:S(2)}, u32[]{:S(2)}) collective-permute-start(bf16[256,512]{1,0:T(8,128)(2,1)S(1)} %get-tuple-element.322), channel_id=1, source_target_pairs={{0,16},{16,0},{1,17},{17,1},{2,18},{18,2},{3,19},{19,3},{4,20},{20... | collective-permute-start | bytes 786440 | tf_op jit(solution)/shard_map/swap_fsdp_1/ppermute | solution.py:111
  49.8 1.9 %collective-permute-start.19 = (bf16[256,512]{1,0:T(8,128)(2,1)S(1)}, bf16[256,512]{1,0:T(8,128)(2,1)S(1)}, u32[]{:S(2)}, u32[]{:S(2)}) collective-permute-start(bf16[256,512]{1,0:T(8,128)(2,1)S(1)} %get-tuple-element.319), channel_id=1, source_target_pairs={{0,16},{16,0},{1,17},{17,1},{2,18},{18,2},{3,19},{19,3},{4,20},{20... | collective-permute-start | bytes 786440 | tf_op jit(solution)/shard_map/swap_fsdp_1/ppermute | solution.py:111
  50.3 1.8 %collective-permute-start.18 = (bf16[256,512]{1,0:T(8,128)(2,1)S(1)}, bf16[256,512]{1,0:T(8,128)(2,1)S(1)}, u32[]{:S(2)}, u32[]{:S(2)}) collective-permute-start(bf16[256,512]{1,0:T(8,128)(2,1)S(1)} %get-tuple-element.316), channel_id=1, source_target_pairs={{0,16},{16,0},{1,17},{17,1},{2,18},{18,2},{3,19},{19,3},{4,20},{20... | collective-permute-start | bytes 786440 | tf_op jit(solution)/shard_map/swap_fsdp_1/ppermute | solution.py:111
  50.3 2.1 %collective-permute-start.17 = (bf16[256,512]{1,0:T(8,128)(2,1)S(1)}, bf16[256,512]{1,0:T(8,128)(2,1)S(1)}, u32[]{:S(2)}, u32[]{:S(2)}) collective-permute-start(bf16[256,512]{1,0:T(8,128)(2,1)S(1)} %get-tuple-element.313), channel_id=1, source_target_pairs={{0,16},{16,0},{1,17},{17,1},{2,18},{18,2},{3,19},{19,3},{4,20},{20... | collective-permute-start | bytes 786440 | tf_op jit(solution)/shard_map/swap_fsdp_1/ppermute | solution.py:111
  53.1 16.9 %collective-permute-start.21 = (bf16[128,2048]{1,0:T(8,128)(2,1)S(1)}, bf16[128,2048]{1,0:T(8,128)(2,1)S(1)}, u32[]{:S(2)}, u32[]{:S(2)}) collective-permute-start(bf16[128,2048]{1,0:T(8,128)(2,1)S(1)} %get-tuple-element.328), channel_id=1, source_target_pairs={{0,4},{4,0},{8,12},{12,8},{16,24},{20,28},{24,16},{28,20},{1,5},{5... | collective-permute-start | bytes 1572872 | tf_op jit(solution)/shard_map/swap_turn_0/ppermute | solution.py:126
  60.1 12.5 %collective-permute-start.27 = (bf16[272,512]{1,0:T(8,128)(2,1)S(1)}, bf16[272,512]{1,0:T(8,128)(2,1)S(1)}, u32[]{:S(2)}, u32[]{:S(2)}) collective-permute-start(bf16[272,512]{1,0:T(8,128)(2,1)S(1)} %get-tuple-element.360), channel_id=1, source_target_pairs={{0,12},{4,8},{8,4},{12,0},{1,13},{5,9},{9,5},{13,1},{2,14},{6,10},... | collective-permute-start | bytes 835592 | tf_op jit(solution)/shard_map/swap_ctx_3/ppermute | solution.py:111
  61.6 12.8 %collective-permute-start.26 = (bf16[272,512]{1,0:T(8,128)(2,1)S(1)}, bf16[272,512]{1,0:T(8,128)(2,1)S(1)}, u32[]{:S(2)}, u32[]{:S(2)}) collective-permute-start(bf16[272,512]{1,0:T(8,128)(2,1)S(1)} %get-tuple-element.359), channel_id=1, source_target_pairs={{0,8},{4,12},{8,0},{12,4},{1,9},{5,13},{9,1},{13,5},{2,10},{6,14},... | collective-permute-start | bytes 835592 | tf_op jit(solution)/shard_map/swap_ctx_2/ppermute | solution.py:111
  63.1 11.3 %collective-permute-start.25 = (bf16[272,512]{1,0:T(8,128)(2,1)S(1)}, bf16[272,512]{1,0:T(8,128)(2,1)S(1)}, u32[]{:S(2)}, u32[]{:S(2)}) collective-permute-start(bf16[272,512]{1,0:T(8,128)(2,1)S(1)} %get-tuple-element.358), channel_id=1, source_target_pairs={{0,4},{4,0},{8,12},{12,8},{1,5},{5,1},{9,13},{13,9},{2,6},{6,2},{1... | collective-permute-start | bytes 835592 | tf_op jit(solution)/shard_map/swap_ctx_1/ppermute | solution.py:111
  63.6 6.4 %collective-permute-start.23 = (bf16[256,512]{1,0:T(8,128)(2,1)S(1)}, bf16[256,512]{1,0:T(8,128)(2,1)S(1)}, u32[]{:S(2)}, u32[]{:S(2)}) collective-permute-start(bf16[256,512]{1,0:T(8,128)(2,1)S(1)} %get-tuple-element.345.refs_3_), channel_id=1, source_target_pairs={{0,1},{1,0},{2,3},{3,2},{4,5},{5,4},{6,7},{7,6},{8,9},{9,8},{10,11... | collective-permute-start | bytes 786440 | tf_op jit(solution)/shard_map/swap_tp_1/ppermute | solution.py:111
  70.9 17.5 %collective-permute-start.24 = (bf16[384,512]{1,0:T(8,128)(2,1)S(1)}, bf16[384,512]{1,0:T(8,128)(2,1)S(1)}, u32[]{:S(2)}, u32[]{:S(2)}) collective-permute-start(bf16[384,512]{1,0:T(8,128)(2,1)S(1)} %get-tuple-element.352), channel_id=1, source_target_pairs={{0,2},{1,3},{2,0},{3,1},{4,6},{5,7},{6,4},{7,5},{8,10},{9,11},{10,... | collective-permute-start | bytes 1179656 | tf_op jit(solution)/shard_map/swap_tp_2/ppermute | solution.py:111
  76.1 2.0 %collective-permute-start.29 = (bf16[272,384]{1,0:T(8,128)(2,1)S(1)}, bf16[272,384]{1,0:T(8,128)(2,1)S(1)}, u32[]{:S(2)}, u32[]{:S(2)}) collective-permute-start(bf16[272,384]{1,0:T(8,128)(2,1)S(1)} %get-tuple-element.371), channel_id=1, source_target_pairs={{0,16},{16,0},{1,17},{17,1},{2,18},{18,2},{3,19},{19,3},{4,20},{20... | collective-permute-start | bytes 626696 | tf_op jit(solution)/shard_map/swap_fsdp_1/ppermute | solution.py:111
  76.1 1.9 %collective-permute-start.28 = (bf16[272,384]{1,0:T(8,128)(2,1)S(1)}, bf16[272,384]{1,0:T(8,128)(2,1)S(1)}, u32[]{:S(2)}, u32[]{:S(2)}) collective-permute-start(bf16[272,384]{1,0:T(8,128)(2,1)S(1)} %get-tuple-element.368), channel_id=1, source_target_pairs={{0,16},{16,0},{1,17},{17,1},{2,18},{18,2},{3,19},{19,3},{4,20},{20... | collective-permute-start | bytes 626696 | tf_op jit(solution)/shard_map/swap_fsdp_1/ppermute | solution.py:111
  76.6 1.4 %collective-permute-start.30 = (bf16[272,256]{1,0:T(8,128)(2,1)S(1)}, bf16[272,256]{1,0:T(8,128)(2,1)S(1)}, u32[]{:S(2)}, u32[]{:S(2)}) collective-permute-start(bf16[272,256]{1,0:T(8,128)(2,1)S(1)} %get-tuple-element.374), channel_id=1, source_target_pairs={{0,16},{16,0},{1,17},{17,1},{2,18},{18,2},{3,19},{19,3},{4,20},{20... | collective-permute-start | bytes 417800 | tf_op jit(solution)/shard_map/swap_fsdp_1/ppermute | solution.py:111
  78.8 25.8 %copy-start = (s32[2]{0:T(128)S(1)}, s32[2]{0:T(128)}, u32[]{:S(2)}) copy-start(s32[2]{0:T(128)} %refs_0_.3) | copy-start | bytes 28
  78.8 10.2 %collective-permute-start.35 = (bf16[80,1024]{1,0:T(8,128)(2,1)S(1)}, bf16[80,1024]{1,0:T(8,128)(2,1)S(1)}, u32[]{:S(2)}, u32[]{:S(2)}) collective-permute-start(bf16[80,1024]{1,0:T(8,128)(2,1)S(1)} %get-tuple-element.398), channel_id=1, source_target_pairs={{0,12},{4,8},{8,4},{12,0},{1,13},{5,9},{9,5},{13,1},{2,14},{6,10},... | collective-permute-start | bytes 491528 | tf_op jit(solution)/shard_map/swap_ctx_3/ppermute | solution.py:111
  80.5 9.1 %collective-permute-start.34 = (bf16[80,1024]{1,0:T(8,128)(2,1)S(1)}, bf16[80,1024]{1,0:T(8,128)(2,1)S(1)}, u32[]{:S(2)}, u32[]{:S(2)}) collective-permute-start(bf16[80,1024]{1,0:T(8,128)(2,1)S(1)} %get-tuple-element.397), channel_id=1, source_target_pairs={{0,8},{4,12},{8,0},{12,4},{1,9},{5,13},{9,1},{13,5},{2,10},{6,14},... | collective-permute-start | bytes 491528 | tf_op jit(solution)/shard_map/swap_ctx_2/ppermute | solution.py:111
  81.8 7.8 %collective-permute-start.33 = (bf16[80,1024]{1,0:T(8,128)(2,1)S(1)}, bf16[80,1024]{1,0:T(8,128)(2,1)S(1)}, u32[]{:S(2)}, u32[]{:S(2)}) collective-permute-start(bf16[80,1024]{1,0:T(8,128)(2,1)S(1)} %get-tuple-element.396), channel_id=1, source_target_pairs={{0,4},{4,0},{8,12},{12,8},{1,5},{5,1},{9,13},{13,9},{2,6},{6,2},{1... | collective-permute-start | bytes 491528 | tf_op jit(solution)/shard_map/swap_ctx_1/ppermute | solution.py:111
  82.3 12.1 %collective-permute-start.36 = (bf16[256,512]{1,0:T(8,128)(2,1)S(1)}, bf16[256,512]{1,0:T(8,128)(2,1)S(1)}, u32[]{:S(2)}, u32[]{:S(2)}) collective-permute-start(bf16[256,512]{1,0:T(8,128)(2,1)S(1)} %get-tuple-element.405.refs_1_), channel_id=1, source_target_pairs={{0,1},{1,0},{2,3},{3,2},{4,5},{5,4},{6,7},{7,6},{8,9},{9,8},{10,11... | collective-permute-start | bytes 786440 | tf_op jit(solution)/shard_map/swap_tp_1/ppermute | solution.py:111
  90.2 7.8 %collective-permute-start.37 = (bf16[96,512]{1,0:T(8,128)(2,1)S(1)}, bf16[96,512]{1,0:T(8,128)(2,1)S(1)}, u32[]{:S(2)}, u32[]{:S(2)}) collective-permute-start(bf16[96,512]{1,0:T(8,128)(2,1)S(1)} %get-tuple-element.409.refs_4_), channel_id=1, source_target_pairs={{0,2},{1,3},{2,0},{3,1},{4,6},{5,7},{6,4},{7,5},{8,10},{9,11},{10,... | collective-permute-start | bytes 294920 | tf_op jit(solution)/shard_map/swap_tp_2/ppermute | solution.py:111
  92.2 5.8 %collective-permute-start.32 = (bf16[64,512]{1,0:T(8,128)(2,1)S(1)}, bf16[64,512]{1,0:T(8,128)(2,1)S(1)}, u32[]{:S(2)}, u32[]{:S(2)}) collective-permute-start(bf16[64,512]{1,0:T(8,128)(2,1)S(1)} %get-tuple-element.394), channel_id=1, source_target_pairs={{0,8},{4,12},{8,0},{12,4},{16,20},{20,16},{24,28},{28,24},{1,9},{5... | collective-permute-start | bytes 196616 | tf_op jit(solution)/shard_map/swap_turn_1/ppermute | solution.py:126
  93.4 4.6 %collective-permute-start.31 = (bf16[64,512]{1,0:T(8,128)(2,1)S(1)}, bf16[64,512]{1,0:T(8,128)(2,1)S(1)}, u32[]{:S(2)}, u32[]{:S(2)}) collective-permute-start(bf16[64,512]{1,0:T(8,128)(2,1)S(1)} %get-tuple-element.391), channel_id=1, source_target_pairs={{0,8},{4,12},{8,0},{12,4},{16,20},{20,16},{24,28},{28,24},{1,9},{5... | collective-permute-start | bytes 196616 | tf_op jit(solution)/shard_map/swap_turn_1/ppermute | solution.py:126
  98.0 14.8 %collective-permute-start.39 = (bf16[256,512]{1,0:T(8,128)(2,1)S(1)}, bf16[256,512]{1,0:T(8,128)(2,1)S(1)}, u32[]{:S(2)}, u32[]{:S(2)}) collective-permute-start(bf16[256,512]{1,0:T(8,128)(2,1)S(1)} %shard_map.298.refs_4_), channel_id=1, source_target_pairs={{0,2},{1,3},{2,0},{3,1},{4,6},{5,7},{6,4},{7,5},{8,10},{9,11},{10,... | collective-permute-start | bytes 786440 | tf_op jit(solution)/shard_map/swap_tp_2/ppermute | solution.py:111
  98.6 8.8 %collective-permute-start.42 = (bf16[64,1536]{1,0:T(8,128)(2,1)S(1)}, bf16[64,1536]{1,0:T(8,128)(2,1)S(1)}, u32[]{:S(2)}, u32[]{:S(2)}) collective-permute-start(bf16[64,1536]{1,0:T(8,128)(2,1)S(1)} %get-tuple-element.427.refs_0_), channel_id=1, source_target_pairs={{0,12},{4,8},{8,4},{12,0},{1,13},{5,9},{9,5},{13,1},{2,14},{6,10},... | collective-permute-start | bytes 589832 | tf_op jit(solution)/shard_map/swap_ctx_3/ppermute | solution.py:111
  100.3 9.9 %collective-permute-start.41 = (bf16[64,1536]{1,0:T(8,128)(2,1)S(1)}, bf16[64,1536]{1,0:T(8,128)(2,1)S(1)}, u32[]{:S(2)}, u32[]{:S(2)}) collective-permute-start(bf16[64,1536]{1,0:T(8,128)(2,1)S(1)} %get-tuple-element.427.refs_0_), channel_id=1, source_target_pairs={{0,8},{4,12},{8,0},{12,4},{1,9},{5,13},{9,1},{13,5},{2,10},{6,14},... | collective-permute-start | bytes 589832 | tf_op jit(solution)/shard_map/swap_ctx_2/ppermute | solution.py:111
  101.7 8.7 %collective-permute-start.40 = (bf16[64,1536]{1,0:T(8,128)(2,1)S(1)}, bf16[64,1536]{1,0:T(8,128)(2,1)S(1)}, u32[]{:S(2)}, u32[]{:S(2)}) collective-permute-start(bf16[64,1536]{1,0:T(8,128)(2,1)S(1)} %get-tuple-element.427.refs_0_), channel_id=1, source_target_pairs={{0,4},{4,0},{8,12},{12,8},{1,5},{5,1},{9,13},{13,9},{2,6},{6,2},{1... | collective-permute-start | bytes 589832 | tf_op jit(solution)/shard_map/swap_ctx_1/ppermute | solution.py:111
  102.2 10.6 %collective-permute-start.38 = (bf16[160,512]{1,0:T(8,128)(2,1)S(1)}, bf16[160,512]{1,0:T(8,128)(2,1)S(1)}, u32[]{:S(2)}, u32[]{:S(2)}) collective-permute-start(bf16[160,512]{1,0:T(8,128)(2,1)S(1)} %get-tuple-element.418.refs_2_), channel_id=1, source_target_pairs={{0,1},{1,0},{2,3},{3,2},{4,5},{5,4},{6,7},{7,6},{8,9},{9,8},{10,11... | collective-permute-start | bytes 491528 | tf_op jit(solution)/shard_map/swap_tp_1/ppermute | solution.py:111
